TPU v7x, 32 devices: a whole 2x2x4 slice. The times are simulated.
32 devices in a mesh: batch: 8 (over y, x, core), head: 4 (over z).
Axes of the slice: x: 2, y: 2, z: 4, core: 2. Of those that a mesh axis runs over, the one named last changes fastest.
Arguments:
- hidden: bfloat16 [8, 512, 3, 1024], P('batch', 'head'), may hold values from -6 to 6
- memory: bfloat16 [8, 1024, 1024], P('batch', 'head'), may hold values from -6 to 6
- grad_out: float32 [8, 512, 3, 1024], P('batch'), may hold values from -6 to 6
- lengths: int32 [8, 4], P('batch'), may hold values from 1 to 256, 512 in all within a row
- key_mask: int32 [8, 512], P('batch'), may hold values 0 or 1
- buckets: int32 [512], replicated, may hold values from 0 to 31, as said below
- self_weight: float32 [1024, 3, 1024], P('batch', None, 'head'), may hold values from -0.1875 to 0.1875
- relpos_weight: float32 [1024, 512], P('batch', 'head'), may hold values from -0.1875 to 0.1875
- selfout_weight: float32 [1024, 1024], P('batch', 'head'), may hold values from -1 to 1
- crossq_weight: float32 [1024, 1024], P('batch', 'head'), may hold values from -0.1875 to 0.1875
- crosskv_weight: float32 [1024, 2, 1024], P('batch', None, 'head'), may hold values from -0.1875 to 0.1875
- crossout_weight: float32 [1024, 1024], P('batch', 'head'), may hold values from -3 to 3
- up_weight: float32 [1024, 4096], P('batch', 'head'), may hold values from -0.1875 to 0.1875
- down_weight: float32 [1024, 4096], P('batch', 'head'), may hold values from -0.09375 to 0.09375
- self_bias: float32 [2, 1024], replicated, may hold values from -1.8 to 1.8
- relpos_bias: float32 [512], replicated, may hold values from -3 to 3
- cross_bias: float32 [2, 1024], replicated, may hold values from -1.8 to 1.8
- up_bias: float32 [4096], replicated, may hold values from -1.8 to 1.8
- norm_gain: float32 [3, 1024], replicated, may hold values from 0.5 to 1.5
- norm_bias: float32 [3, 1024], replicated, may hold values from -1.8 to 1.8
- out_bias: float32 [3, 1024], replicated, may hold values from -1.8 to 1.8
Outputs:
- layer_out: bfloat16 [8, 512, 3, 1024], P('batch')
- grad_hidden: float32 [8, 512, 3, 1024], P('batch', 'head')
- grad_memory: float32 [8, 1024, 1024], P('batch', 'head')
- self_weight_grad: float32 [1024, 3, 1024], P('batch', None, 'head')
- relpos_weight_grad: float32 [1024, 512], P('batch', 'head')
- selfout_weight_grad: float32 [1024, 1024], P('batch', 'head')
- crossq_weight_grad: float32 [1024, 1024], P('batch', 'head')
- crosskv_weight_grad: float32 [1024, 2, 1024], P('batch', None, 'head')
- crossout_weight_grad: float32 [1024, 1024], P('batch', 'head')
- up_weight_grad: float32 [1024, 4096], P('batch', 'head')
- down_weight_grad: float32 [1024, 4096], P('batch', 'head')
- self_bias_grad: float32 [2, 1024], replicated
- relpos_bias_grad: float32 [512], replicated
- cross_bias_grad: float32 [2, 1024], replicated
- up_bias_grad: float32 [4096], replicated
- norm_gain_grad: float32 [3, 1024], replicated
- norm_bias_grad: float32 [3, 1024], replicated
- out_bias_grad: float32 [3, 1024], replicated
Inputs may be any that keep to these rules, and one draw needn't show every extreme that they name: The 4 document lengths of a row sum to 512. `key_mask`: 1 marks a key that queries may attend to. buckets[d] is the bucket of a key d positions before its query; it never falls as d grows, and buckets[0] is 0.
All inputs are finite; a program needn't handle non-finite values. No bound on the sum of `key_mask` on one device may be relied on, other than what follows from the above.
Results may differ from a plain program's by a relative error of at most 0.025.
Values may be sent and summed in bfloat16 or wider, within the bound.
No kernel may reach another device: no remote copies, remote signals or barrier semaphores. Data moves between devices by JAX's collectives and lax.ppermute only.
A program may use at most 256 MiB of HBM per device.

v0:
```python
import jax
import jax.numpy as jnp
from jax import lax
from jax.sharding import PartitionSpec as P

HEADS = 16
HEAD_DIM = 64
BUCKETS = 32
FF = 4096
ROW_LEN = 512


epsilon = 1e-05
masked_score = -1e30


def matmul(pattern, former, latter):
    return jnp.einsum(pattern, former, latter, preferred_element_type=jnp.float32)


def normalize(inputs, gain_row, shift_row):
    centered = inputs - jnp.mean(inputs, -1, keepdims=True)
    spread = lax.rsqrt(jnp.mean(centered * centered, -1, keepdims=True) + epsilon)
    unitary = centered * spread
    return (unitary * gain_row + shift_row, unitary, spread)


def normalize_back(gradient, unitary, spread, gain_row):
    scaled = gradient * gain_row
    return spread * (
        scaled
        - jnp.mean(scaled, -1, keepdims=True)
        - unitary * jnp.mean(scaled * unitary, -1, keepdims=True)
    )


def gelu_slope(inputs):
    normal_cdf = 0.5 * (1.0 + lax.erf(inputs * 0.7071067811865476))
    return normal_cdf + inputs * jnp.exp(-0.5 * inputs * inputs) * 0.3989422804014327


def widen(section, columns, member):
    zeroed = jnp.zeros(section.shape[:-1] + (columns,), jnp.float32)
    return lax.dynamic_update_slice_in_dim(
        zeroed, section, member * section.shape[-1], section.ndim - 1
    )


def by_distance(relpos_track, bucket_table):
    return jnp.einsum("rthb,bd->rhtd", relpos_track, bucket_table, precision=lax.Precision.HIGHEST)


def skew_grid(distance):
    length = distance.shape[-1]
    lead = distance.shape[:-2]
    flipped = distance[..., ::-1]
    padded = jnp.concatenate([flipped, jnp.zeros(flipped.shape, flipped.dtype)], -1)
    flat = padded.reshape(lead + (2 * length * length,))[..., : length * (2 * length - 1)]
    return flat.reshape(lead + (length, 2 * length - 1))[..., length - 1 :]


def unskew_grid(grid):
    length = grid.shape[-1]
    lead = grid.shape[:-2]
    placed = jnp.concatenate([jnp.zeros(lead + (length, length - 1), grid.dtype), grid], -1)
    flat = placed.reshape(lead + (length * (2 * length - 1),))
    flat = jnp.concatenate([flat, jnp.zeros(lead + (length,), grid.dtype)], -1)
    return flat.reshape(lead + (length, 2 * length))[..., :length][..., ::-1]


def self_scores(queries_in, keys_main, keys_own, distance, allowed):
    main_part = matmul("rthc,rshc->rhts", queries_in, keys_main) + skew_grid(distance)
    main_part = jnp.where(allowed[:, None], main_part, masked_score)
    if keys_own is None:
        return (main_part, None)
    own_part = matmul("rthc,rthc->rht", queries_in, keys_own) + distance[..., 0]
    return (main_part, own_part)


def log_total(main_part, own_part):
    largest = jnp.max(main_part, -1)
    if own_part is not None:
        largest = jnp.maximum(largest, own_part)
    totals = jnp.sum(jnp.exp(main_part - largest[..., None]), -1)
    if own_part is not None:
        totals = totals + jnp.exp(own_part - largest)
    return largest + jnp.log(totals)


def branch_total(term):
    return lax.psum(term, "head")


def per_device(
    hidden,
    memory,
    grad_out,
    lengths,
    key_mask,
    buckets,
    self_weight,
    relpos_weight,
    selfout_weight,
    crossq_weight,
    crosskv_weight,
    crossout_weight,
    up_weight,
    down_weight,
    self_bias,
    relpos_bias,
    cross_bias,
    up_bias,
    norm_gain,
    norm_bias,
    out_bias,
):
    groups = lax.axis_size("head")
    member = lax.axis_index("head")
    local_heads = HEADS // groups
    head_width = local_heads * HEAD_DIM
    share_rows = ROW_LEN // groups
    local_rows = hidden.shape[0]

    def own_rows(array_in):
        return lax.dynamic_slice_in_dim(array_in, member * share_rows, share_rows, 1)

    def own_cols(vector, columns):
        return lax.dynamic_slice_in_dim(vector, member * columns, columns, vector.ndim - 1)

    def split_heads(array_in):
        return array_in.reshape(array_in.shape[:-1] + (local_heads, HEAD_DIM))

    def flat_heads(array_in):
        return array_in.reshape(array_in.shape[:-2] + (head_width,))

    halves = tuple(
        (
            weight.astype(jnp.bfloat16)
            for weight in (
                self_weight,
                relpos_weight,
                selfout_weight,
                crossq_weight,
                crosskv_weight,
                crossout_weight,
                up_weight,
                down_weight,
            )
        )
    )
    gathered = (
        lax.all_gather(halves[0], "batch", axis=0, tiled=True),
        lax.all_gather(halves[1], "batch", axis=0, tiled=True),
        lax.all_gather(halves[2], "batch", axis=0, tiled=True),
        lax.all_gather(halves[3], "batch", axis=0, tiled=True),
        lax.all_gather(halves[4], "batch", axis=0, tiled=True),
        lax.all_gather(halves[5], "batch", axis=0, tiled=True),
        lax.all_gather(halves[6], "batch", axis=0, tiled=True),
        lax.all_gather(halves[7], "batch", axis=0, tiled=True),
    )
    (
        self_full,
        relpos_full,
        selfout_full,
        crossq_full,
        crosskv_full,
        crossout_full,
        up_full,
        down_full,
    ) = gathered
    self_part = own_cols(self_bias, head_width)
    relpos_part = own_cols(relpos_bias, local_heads * BUCKETS)
    cross_part = own_cols(cross_bias, head_width)
    up_part = own_cols(up_bias, FF // groups)
    places = lax.iota(jnp.int32, ROW_LEN)
    doc_ends = jnp.cumsum(lengths, axis=-1)
    segment = jnp.sum((places[None, :, None] >= doc_ends[:, None, :]).astype(jnp.int32), -1)
    diagonal = places[:, None] == places[None, :]
    joined = (segment[:, :, None] == segment[:, None, :]) & (
        (key_mask[:, None, :] == 1) | diagonal[None]
    )
    allowed_main = joined & (places[None, :] <= places[:, None])[None]
    allowed_pred = joined & (places[None, :] < places[:, None])[None]
    bucket_ids = lax.iota(jnp.int32, BUCKETS)
    bucket_table = (bucket_ids[:, None] == buckets[None, :]).astype(jnp.float32)
    bucket_low = bucket_table.astype(jnp.bfloat16)
    own_hot = bucket_table[:, 0]
    rows_full, memory_full = (
        lax.all_gather(hidden, "head", axis=1, tiled=True),
        lax.all_gather(memory, "head", axis=1, tiled=True),
    )
    projected = matmul("rsnd,dkc->rsnkc", rows_full, self_full)
    queries = split_heads(((projected[:, :, :, 0] + self_part[0]) * 0.125).astype(jnp.bfloat16))
    keys_all = split_heads(projected[:, :, :, 1].astype(jnp.bfloat16))
    values_all = split_heads((projected[:, :, :, 2] + self_part[1]).astype(jnp.bfloat16))
    relpos = (matmul("rsnd,dc->rsnc", rows_full, relpos_full) + relpos_part).reshape(
        local_rows, ROW_LEN, 3, local_heads, BUCKETS
    )
    distances = [by_distance(relpos[:, :, which_track], bucket_table) for which_track in range(3)]

    def track_scores(which_track):
        keys_own = None if which_track == 0 else keys_all[:, :, which_track]
        allowed = allowed_main if which_track == 0 else allowed_pred
        return self_scores(
            queries[:, :, which_track], keys_all[:, :, 0], keys_own, distances[which_track], allowed
        )

    contexts = []
    self_totals = []
    for which_track in range(3):
        main_part, own_part = track_scores(which_track)
        totals = log_total(main_part, own_part)
        softmaxed = jnp.exp(main_part - totals[..., None]).astype(jnp.bfloat16)
        mixture = matmul("rhts,rshc->rthc", softmaxed, values_all[:, :, 0])
        if own_part is not None:
            own_probs = jnp.exp(own_part - totals).astype(jnp.bfloat16).astype(jnp.float32)
            mixture = (
                mixture
                + jnp.transpose(own_probs, (0, 2, 1))[..., None] * values_all[:, :, which_track]
            )
        contexts.append(mixture.astype(jnp.bfloat16))
        self_totals.append(totals)
    context = flat_heads(jnp.stack(contexts, 2))
    self_term = matmul("rsnc,dc->rsnd", context, selfout_full)
    attended = branch_total(self_term) + out_bias[0]
    normed1, unitary1, spread1 = normalize(rows_full + attended, norm_gain[0], norm_bias[0])
    normed1_low = normed1.astype(jnp.bfloat16)
    unitary1_share = own_rows(unitary1)
    spread1_share = own_rows(spread1)
    cross_queries = split_heads(
        ((matmul("rsnd,dc->rsnc", normed1_low, crossq_full) + cross_part[0]) * 0.125).astype(
            jnp.bfloat16
        )
    )
    cross_kv = matmul("rmd,dkc->rmkc", memory_full, crosskv_full)
    cross_keys = split_heads(cross_kv[:, :, 0].astype(jnp.bfloat16))
    cross_values = split_heads((cross_kv[:, :, 1] + cross_part[1]).astype(jnp.bfloat16))
    cross_contexts = []
    cross_totals = []
    for which_track in range(3):
        scores = matmul("rthc,rmhc->rhtm", cross_queries[:, :, which_track], cross_keys)
        totals = log_total(scores, None)
        softmaxed = jnp.exp(scores - totals[..., None]).astype(jnp.bfloat16)
        cross_contexts.append(
            matmul("rhtm,rmhc->rthc", softmaxed, cross_values).astype(jnp.bfloat16)
        )
        cross_totals.append(totals)
    cross_context = flat_heads(jnp.stack(cross_contexts, 2))
    cross_term = matmul("rsnc,dc->rsnd", cross_context, crossout_full)
    crossed = branch_total(cross_term) + out_bias[1]
    normed2, unitary2, spread2 = normalize(normed1 + crossed, norm_gain[1], norm_bias[1])
    normed2_low = normed2.astype(jnp.bfloat16)
    unitary2_share = own_rows(unitary2)
    spread2_share = own_rows(spread2)
    upper_in = matmul("rsnd,df->rsnf", normed2_low, up_full) + up_part
    active = jax.nn.gelu(upper_in, approximate=False).astype(jnp.bfloat16)
    ffn_term = matmul("rsnf,df->rsnd", active, down_full)
    grad_out_share = own_rows(grad_out)
    ffn_out = branch_total(ffn_term) + out_bias[2]
    normed3, unitary3, spread3 = normalize(normed2 + ffn_out, norm_gain[2], norm_bias[2])
    layer_out = normed3.astype(jnp.bfloat16)
    grad_third = normalize_back(grad_out, unitary3, spread3, norm_gain[2])
    third_low = grad_third.astype(jnp.bfloat16)
    third_share = own_rows(grad_third)
    unitary3_share = own_rows(unitary3)
    reloaded = (
        lax.all_gather(halves[0], "batch", axis=0, tiled=True),
        lax.all_gather(halves[1], "batch", axis=0, tiled=True),
        lax.all_gather(halves[2], "batch", axis=0, tiled=True),
        lax.all_gather(halves[3], "batch", axis=0, tiled=True),
        lax.all_gather(halves[4], "batch", axis=0, tiled=True),
        lax.all_gather(halves[5], "batch", axis=0, tiled=True),
        lax.all_gather(halves[6], "batch", axis=0, tiled=True),
        lax.all_gather(halves[7], "batch", axis=0, tiled=True),
    )
    (
        self_back,
        relpos_back,
        selfout_back,
        crossq_back,
        crosskv_back,
        crossout_back,
        up_back,
        down_back,
    ) = reloaded
    gain_third = jnp.sum(grad_out_share * unitary3_share, (0, 1, 2))
    shift_third = jnp.sum(grad_out_share, (0, 1, 2))
    bias_third = jnp.sum(third_share, (0, 1, 2))
    down_grad = matmul("rsnd,rsnf->df", third_low, active)
    grad_upper = matmul("rsnd,df->rsnf", third_low, down_back) * gelu_slope(upper_in)
    up_bias_local = jnp.sum(grad_upper, (0, 1, 2))
    upper_low = grad_upper.astype(jnp.bfloat16)
    up_grad = matmul("rsnd,rsnf->df", normed2_low, upper_low)
    grad_norm2 = (
        lax.psum_scatter(
            matmul("rsnf,df->rsnd", upper_low, up_back), "head", scatter_dimension=1, tiled=True
        )
        + third_share
    )
    gain_second = jnp.sum(grad_norm2 * unitary2_share, (0, 1, 2))
    shift_second = jnp.sum(grad_norm2, (0, 1, 2))
    grad_second = normalize_back(grad_norm2, unitary2_share, spread2_share, norm_gain[1])
    bias_second = jnp.sum(grad_second, (0, 1, 2))
    second_full = lax.all_gather(grad_second.astype(jnp.bfloat16), "head", axis=1, tiled=True)
    crossout_grad = matmul("rsnd,rsnc->dc", second_full, cross_context)
    grad_cross_ctx = split_heads(
        matmul("rsnd,dc->rsnc", second_full, crossout_back).astype(jnp.bfloat16)
    )
    cross_query_list = []
    grad_cross_keys = jnp.zeros(cross_keys.shape, jnp.float32)
    grad_cross_values = jnp.zeros(cross_values.shape, jnp.float32)
    for which_track in range(3):
        query_track = cross_queries[:, :, which_track]
        scores = matmul("rthc,rmhc->rhtm", query_track, cross_keys)
        softmaxed = jnp.exp(scores - cross_totals[which_track][..., None])
        ctx_track = grad_cross_ctx[:, :, which_track]
        grad_probs = matmul("rthc,rmhc->rhtm", ctx_track, cross_values)
        grad_scores = (
            softmaxed * (grad_probs - jnp.sum(softmaxed * grad_probs, -1, keepdims=True))
        ).astype(jnp.bfloat16)
        cross_query_list.append(matmul("rhtm,rmhc->rthc", grad_scores, cross_keys))
        grad_cross_keys = grad_cross_keys + matmul("rhtm,rthc->rmhc", grad_scores, query_track)
        grad_cross_values = grad_cross_values + matmul(
            "rhtm,rthc->rmhc", softmaxed.astype(jnp.bfloat16), ctx_track
        )
    grad_cross_query = flat_heads(jnp.stack(cross_query_list, 2)) * 0.125
    grad_cross_keys = flat_heads(grad_cross_keys)
    grad_cross_values = flat_heads(grad_cross_values)
    cross_bias_local = jnp.stack(
        [jnp.sum(grad_cross_query, (0, 1, 2)), jnp.sum(grad_cross_values, (0, 1))]
    )
    query_low = grad_cross_query.astype(jnp.bfloat16)
    crossq_grad = matmul("rsnd,rsnc->dc", normed1_low, query_low)
    grad_kv_low = jnp.stack([grad_cross_keys, grad_cross_values], 2).astype(jnp.bfloat16)
    crosskv_grad = matmul("rmd,rmkc->dkc", memory_full, grad_kv_low)
    memory_part = matmul("rmkc,dkc->rmd", grad_kv_low, crosskv_back)
    grad_norm1 = (
        lax.psum_scatter(
            matmul("rsnc,dc->rsnd", query_low, crossq_back), "head", scatter_dimension=1, tiled=True
        )
        + grad_second
    )
    gain_first = jnp.sum(grad_norm1 * unitary1_share, (0, 1, 2))
    shift_first = jnp.sum(grad_norm1, (0, 1, 2))
    grad_first = normalize_back(grad_norm1, unitary1_share, spread1_share, norm_gain[0])
    bias_first = jnp.sum(grad_first, (0, 1, 2))
    first_full = lax.all_gather(grad_first.astype(jnp.bfloat16), "head", axis=1, tiled=True)
    selfout_grad = matmul("rsnd,rsnc->dc", first_full, context)
    grad_context = split_heads(
        matmul("rsnd,dc->rsnc", first_full, selfout_back).astype(jnp.bfloat16)
    )
    grad_keys_main = jnp.zeros(keys_all[:, :, 0].shape, jnp.float32)
    grad_values_main = jnp.zeros(values_all[:, :, 0].shape, jnp.float32)
    query_list = []
    keys_own_list = []
    values_own_list = []
    relpos_list = []
    for which_track in range(3):
        main_part, own_part = track_scores(which_track)
        totals = self_totals[which_track]
        softmaxed = jnp.exp(main_part - totals[..., None])
        ctx_track = grad_context[:, :, which_track]
        grad_probs = matmul("rthc,rshc->rhts", ctx_track, values_all[:, :, 0])
        row_dot = jnp.sum(softmaxed * grad_probs, -1)
        if own_part is not None:
            own_probs = jnp.exp(own_part - totals)
            own_grad = matmul("rthc,rthc->rht", ctx_track, values_all[:, :, which_track])
            row_dot = row_dot + own_probs * own_grad
        grad_main = (softmaxed * (grad_probs - row_dot[..., None])).astype(jnp.bfloat16)
        query_track = queries[:, :, which_track]
        grad_query = matmul("rhts,rshc->rthc", grad_main, keys_all[:, :, 0])
        grad_keys_main = grad_keys_main + matmul("rhts,rthc->rshc", grad_main, query_track)
        grad_values_main = grad_values_main + matmul(
            "rhts,rthc->rshc", softmaxed.astype(jnp.bfloat16), ctx_track
        )
        grad_dist = unskew_grid(grad_main)
        grad_rel = matmul("rhtd,bd->rthb", grad_dist, bucket_low)
        if own_part is not None:
            grad_own = jnp.transpose(
                (own_probs * (own_grad - row_dot)).astype(jnp.bfloat16).astype(jnp.float32),
                (0, 2, 1),
            )[..., None]
            grad_query = grad_query + grad_own * keys_all[:, :, which_track]
            keys_own_list.append(grad_own * query_track)
            prob_own = jnp.transpose(own_probs.astype(jnp.bfloat16).astype(jnp.float32), (0, 2, 1))[
                ..., None
            ]
            values_own_list.append(prob_own * ctx_track)
            grad_rel = grad_rel + grad_own * own_hot
        query_list.append(grad_query)
        relpos_list.append(grad_rel)
    grad_queries = flat_heads(jnp.stack(query_list, 2)) * 0.125
    grad_keys = flat_heads(jnp.stack([grad_keys_main] + keys_own_list, 2))
    grad_values = flat_heads(jnp.stack([grad_values_main] + values_own_list, 2))
    grad_relpos = jnp.stack(relpos_list, 2).reshape(local_rows, ROW_LEN, 3, local_heads * BUCKETS)
    self_bias_local = jnp.stack([jnp.sum(grad_queries, (0, 1, 2)), jnp.sum(grad_values, (0, 1, 2))])
    relpos_bias_local = jnp.sum(grad_relpos, (0, 1, 2))
    grad_qkv_low = jnp.stack([grad_queries, grad_keys, grad_values], 3).astype(jnp.bfloat16)
    grad_rel_low = grad_relpos.astype(jnp.bfloat16)
    self_grad = matmul("rsnd,rsnkc->dkc", rows_full, grad_qkv_low)
    relpos_grad = matmul("rsnd,rsnc->dc", rows_full, grad_rel_low)
    input_part = matmul("rsnkc,dkc->rsnd", grad_qkv_low, self_back) + matmul(
        "rsnc,dc->rsnd", grad_rel_low, relpos_back
    )
    input_share, memory_share = (
        lax.psum_scatter(
            input_part.astype(jnp.bfloat16), "head", scatter_dimension=1, tiled=True
        ).astype(jnp.float32),
        lax.psum_scatter(
            memory_part.astype(jnp.bfloat16), "head", scatter_dimension=1, tiled=True
        ).astype(jnp.float32),
    )
    grad_hidden = input_share + grad_first
    weight_grads = (
        lax.psum_scatter(self_grad, "batch", scatter_dimension=0, tiled=True),
        lax.psum_scatter(relpos_grad, "batch", scatter_dimension=0, tiled=True),
        lax.psum_scatter(selfout_grad, "batch", scatter_dimension=0, tiled=True),
        lax.psum_scatter(crossq_grad, "batch", scatter_dimension=0, tiled=True),
        lax.psum_scatter(crosskv_grad, "batch", scatter_dimension=0, tiled=True),
        lax.psum_scatter(crossout_grad, "batch", scatter_dimension=0, tiled=True),
        lax.psum_scatter(up_grad, "batch", scatter_dimension=0, tiled=True),
        lax.psum_scatter(down_grad, "batch", scatter_dimension=0, tiled=True),
    )
    small_sums = lax.psum(
        (
            widen(self_bias_local, HEADS * HEAD_DIM, member),
            widen(relpos_bias_local, HEADS * BUCKETS, member),
            widen(cross_bias_local, HEADS * HEAD_DIM, member),
            widen(up_bias_local, FF, member),
            jnp.stack([gain_first, gain_second, gain_third]),
            jnp.stack([shift_first, shift_second, shift_third]),
            jnp.stack([bias_first, bias_second, bias_third]),
        ),
        ("batch", "head"),
    )
    return (layer_out, grad_hidden, memory_share) + tuple(weight_grads) + tuple(small_sums)


def solution(mesh):
    in_specs = (
        P("batch", "head", None, None),
        P("batch", "head", None),
        P("batch", None, None, None),
        P("batch", None),
        P("batch", None),
        P(),
        P("batch", None, "head"),
        P("batch", "head"),
        P("batch", "head"),
        P("batch", "head"),
        P("batch", None, "head"),
        P("batch", "head"),
        P("batch", "head"),
        P("batch", "head"),
        P(),
        P(),
        P(),
        P(),
        P(),
        P(),
        P(),
    )
    out_specs = (
        P("batch", None, None, None),
        P("batch", "head", None, None),
        P("batch", "head", None),
        P("batch", None, "head"),
        P("batch", "head"),
        P("batch", "head"),
        P("batch", "head"),
        P("batch", None, "head"),
        P("batch", "head"),
        P("batch", "head"),
        P("batch", "head"),
        P(),
        P(),
        P(),
        P(),
        P(),
        P(),
        P(),
    )
    return jax.shard_map(
        per_device, mesh=mesh, in_specs=in_specs, out_specs=out_specs, check_vma=False
    )
```

profile of v0, /device:TPU:0, one launch (start us, length us, event | category | flops | bytes accessed | tf_op | source)
XLA Modules:
  0.0 2382.5 jit_solution(5094770194783179505)
XLA Ops:
  16.7 10.8 all_gather.46
  27.6 10.8 all_gather.47
  40.1 35.6 %all-gather.9.cloned.1.call-done = bf16[1,512,3,1024]{3,1,2,0:T(8,128)(2,1)} async-done(((bf16[1,128,3,1024]{3,1,2,0:T(8,128)(2,1)}), bf16[1,512,3,1024]{3,1,2,0:T(8,128)(2,1)}) %all-gather.9.cloned.1.call-update) | async-done | bytes 3145744 | tf_op jit(solution)/shard_map/all_gather | solution.py:189
  86.6 33.0 %rev.22 = f32[1,4,512,512]{2,3,1,0:T(8,128)} reverse(f32[1,4,512,512]{2,3,1,0:T(8,128)} %copy-done.26), dimensions={3} | reverse | bytes 8388608 | tf_op jit(solution)/shard_map/rev | solution.py:56
  138.5 12.5 reshape.1757
  151.0 7.5 slice.256
  158.5 15.8 reshape.1758
  200.3 32.6 %rev.23 = f32[1,4,512,512]{2,3,1,0:T(8,128)} reverse(f32[1,4,512,512]{2,3,1,0:T(8,128)} %convolution_bitcast_fusion.6), dimensions={3} | reverse | bytes 8388608 | tf_op jit(solution)/shard_map/rev | solution.py:56
  238.2 6.6 concatenate.82.clone
  244.8 12.4 reshape.1763
  257.2 7.3 slice.263
  264.5 15.7 reshape.1764
  291.2 32.6 %rev.21 = f32[1,4,512,512]{2,3,1,0:T(8,128)} reverse(f32[1,4,512,512]{2,3,1,0:T(8,128)} %convolution_bitcast_fusion.8), dimensions={3} | reverse | bytes 8388608 | tf_op jit(solution)/shard_map/rev | solution.py:56
  329.5 6.7 concatenate.80.clone
  336.1 12.4 reshape.1752
  348.5 7.3 slice.252
  355.8 15.7 reshape.1753
  405.6 11.0 all_gather.51
  416.7 10.8 all_gather.50
  432.7 194.0 %all-reduce.15.cloned.1.call-done = f32[1,512,3,1024]{3,1,2,0:T(8,128)} async-done(((f32[1,512,3,1024]{3,1,2,0:T(8,128)}), f32[1,512,3,1024]{3,1,2,0:T(8,128)}) %all-reduce.15.cloned.1.call-update) | async-done | bytes 6291472 | tf_op jit(solution)/shard_map/psum | solution.py:91
  677.8 218.6 %all-reduce.17.cloned.1.call-done = f32[1,512,3,1024]{3,1,2,0:T(8,128)} async-done(((f32[1,512,3,1024]{3,1,2,0:T(8,128)}), f32[1,512,3,1024]{3,1,2,0:T(8,128)}) %all-reduce.17.cloned.1.call-update) | async-done | bytes 6291472 | tf_op jit(solution)/shard_map/psum | solution.py:91
  907.7 18.0 all-gather.17.cloned.1.call-done
  925.7 8.3 fusion.115
  936.7 15.3 fusion.5
  956.1 8.6 convolution_bitcast_fusion.4
  964.8 223.0 %all-reduce.19.cloned.1.call-done = f32[1,512,3,1024]{3,1,2,0:T(8,128)} async-done(((f32[1,512,3,1024]{3,1,2,0:T(8,128)}), f32[1,512,3,1024]{3,1,2,0:T(8,128)}) %all-reduce.19.cloned.1.call-update) | async-done | bytes 6291472 | tf_op jit(solution)/shard_map/psum | solution.py:91
  1200.7 8.8 fusion.293
  1216.8 109.8 %reduce-scatter.13.cloned.1.call-done = f32[1,128,3,1024]{3,1,2,0:T(8,128)} async-done(((f32[1,512,3,1024]{3,1,2,0:T(8,128)}), f32[1,128,3,1024]{3,1,2,0:T(8,128)}) %reduce-scatter.13.cloned.1.call-update) | async-done | bytes 1572880 | tf_op jit(solution)/shard_map/reduce_scatter | solution.py:295
  1333.9 64.1 %all-gather.21.cloned.1.call-done = bf16[1,512,3,1024]{3,1,2,0:T(8,128)(2,1)} async-done(((bf16[1,128,3,1024]{3,1,2,0:T(8,128)(2,1)}), bf16[1,512,3,1024]{3,1,2,0:T(8,128)(2,1)}) %all-gather.21.cloned.1.call-update) | async-done | bytes 3145744 | tf_op jit(solution)/shard_map/all_gather | solution.py:304
  1401.0 8.0 multiply_reduce_fusion
  1441.6 109.5 %reduce-scatter.15.cloned.1.call-done = f32[1,128,3,1024]{3,1,2,0:T(8,128)} async-done(((f32[1,512,3,1024]{3,1,2,0:T(8,128)}), f32[1,128,3,1024]{3,1,2,0:T(8,128)}) %reduce-scatter.15.cloned.1.call-update) | async-done | bytes 1572880 | tf_op jit(solution)/shard_map/reduce_scatter | solution.py:338
  1587.0 36.0 %all-gather.23.cloned.1.call-done = bf16[1,512,3,1024]{3,1,2,0:T(8,128)(2,1)} async-done(((bf16[1,128,3,1024]{3,1,2,0:T(8,128)(2,1)}), bf16[1,512,3,1024]{3,1,2,0:T(8,128)(2,1)}) %all-gather.23.cloned.1.call-update) | async-done | bytes 3145744 | tf_op jit(solution)/shard_map/all_gather | solution.py:347
  1654.9 8.5 reshape.1869
  1676.0 27.5 %rev.26 = bf16[1,4,512,512]{3,2,1,0:T(8,128)(2,1)S(1)} reverse(bf16[1,4,512,512]{3,2,1,0:T(8,128)(2,1)} %slice.282), dimensions={3} | reverse | bytes 4194304 | tf_op jit(solution)/shard_map/rev | solution.py:68
  1721.3 8.8 reshape.1871
  1742.6 27.4 %rev.25 = bf16[1,4,512,512]{3,2,1,0:T(8,128)(2,1)S(1)} reverse(bf16[1,4,512,512]{3,2,1,0:T(8,128)(2,1)} %slice.280), dimensions={3} | reverse | bytes 4194304 | tf_op jit(solution)/shard_map/rev | solution.py:68
  1790.5 8.7 reshape.1873
  1811.7 32.0 %rev.24 = bf16[1,4,512,512]{3,2,1,0:T(8,128)(2,1)} reverse(bf16[1,4,512,512]{3,2,1,0:T(8,128)(2,1)} %slice.279), dimensions={3} | reverse | bytes 4194304 | tf_op jit(solution)/shard_map/rev | solution.py:68
  1883.2 7.9 fusion.60
  1893.0 7.9 convolution_bitcast_fusion.5
  1927.4 13.5 reduce-scatter.21.cloned.1.call-done
  1942.8 60.5 %reduce-scatter.17.cloned.1.call-done = bf16[1,128,3,1024]{3,1,2,0:T(8,128)(2,1)} async-done(((bf16[1,512,3,1024]{3,1,2,0:T(8,128)(2,1)}), bf16[1,128,3,1024]{3,1,2,0:T(8,128)(2,1)}) %reduce-scatter.17.cloned.1.call-update) | async-done | bytes 786448 | tf_op jit(solution)/shard_map/reduce_scatter | solution.py:406
  2005.8 52.8 %reduce-scatter.35.cloned.1.call-done = f32[128,1024]{1,0:T(8,128)} async-done(((f32[1024,1024]{1,0:T(8,128)}), f32[128,1024]{1,0:T(8,128)}) %reduce-scatter.35.cloned.1.call-update) | async-done | bytes 524304 | tf_op jit(solution)/shard_map/reduce_scatter | solution.py:422
  2058.6 55.5 %reduce-scatter.33.cloned.1.call-done = f32[128,1024]{1,0:T(8,128)} async-done(((f32[1024,1024]{1,0:T(8,128)}), f32[128,1024]{1,0:T(8,128)}) %reduce-scatter.33.cloned.1.call-update) | async-done | bytes 524304 | tf_op jit(solution)/shard_map/reduce_scatter | solution.py:421
  2114.1 39.8 %reduce-scatter.31.cloned.1.call-done = f32[128,256]{1,0:T(8,128)} async-done(((f32[1024,256]{1,0:T(8,128)}), f32[128,256]{1,0:T(8,128)}) %reduce-scatter.31.cloned.1.call-update) | async-done | bytes 131088 | tf_op jit(solution)/shard_map/reduce_scatter | solution.py:420
  2153.9 39.8 %reduce-scatter.27.cloned.1.call-done = f32[128,256]{1,0:T(8,128)} async-done(((f32[1024,256]{1,0:T(8,128)}), f32[128,256]{1,0:T(8,128)}) %reduce-scatter.27.cloned.1.call-update) | async-done | bytes 131088 | tf_op jit(solution)/shard_map/reduce_scatter | solution.py:418
  2193.7 131.4 %all-reduce.21.cloned.1.call-done = (f32[2,1024]{1,0:T(2,128)}, f32[512]{0:T(512)}, f32[2,1024]{1,0:T(2,128)}, f32[4096]{0:T(1024)}, f32[3,1024]{1,0:T(4,128)}, /*index=5*/f32[3,1024]{1,0:T(4,128)}, f32[3,1024]{1,0:T(4,128)}) async-done(((f32[2,1024]{1,0:T(2,128)}, f32[512]{0:T(512)}, f32[2,1024]{1,0:T(2,128)}, f32[4096]{0:T(1024)}, f32[3,1024]{1,0:T(4,128)}, /*index=5*/f32[3,1024]{1,0:T(4,128)}, ...) | async-done | bytes 71696 | tf_op jit(solution)/shard_map/psum | solution.py:424
  2325.1 41.2 %reduce-scatter.25.cloned.1.call-done = f32[128,256]{1,0:T(8,128)} async-done(((f32[1024,256]{1,0:T(8,128)}), f32[128,256]{1,0:T(8,128)}) %reduce-scatter.25.cloned.1.call-update) | async-done | bytes 131088 | tf_op jit(solution)/shard_map/reduce_scatter | solution.py:417
  (587 shorter events, 483.3 us)
Async XLA Ops:
  7.2 68.6 %all-gather.9.cloned.1.call-start = ((), (), s32[]{:S(2)}) async-start(), calls=%async_computation.12 | async-start | bytes 3932160 | tf_op jit(solution)/shard_map/all_gather | solution.py:189
  7.9 111.7 %all-gather.11.cloned.1.call-start = ((), (), s32[]{:S(2)}) async-start(), calls=%async_computation.13 | async-start | bytes 1769472 | tf_op jit(solution)/shard_map/all_gather | solution.py:152
  9.8 69.1 %copy-start.88 = (s32[512]{0:T(512)S(1)}, s32[512]{0:T(512)}, u32[]{:S(2)}) copy-start(s32[512]{0:T(512)} %param.26) | copy-start | bytes 6148
  9.8 417.8 %all-gather.15.cloned.1.call-start = ((), (), s32[]{:S(2)}) async-start(), calls=%async_computation.16 | async-start | bytes 1179648 | tf_op jit(solution)/shard_map/all_gather | solution.py:156
  11.6 416.1 %all-gather.13.cloned.1.call-start = ((), (), s32[]{:S(2)}) async-start(), calls=%async_computation.15 | async-start | bytes 2621440 | tf_op jit(solution)/shard_map/all_gather | solution.py:190
  12.2 614.5 %all-reduce.15.cloned.1.call-start = ((), (), s32[]{:S(2)}) async-start(), calls=%async_computation.14 | async-start | bytes 12582912 | tf_op jit(solution)/shard_map/psum | solution.py:91
  27.6 55.2 %copy-start.54 = (bf16[1024,128]{0,1:T(8,128)(2,1)}, bf16[1024,128]{0,1:T(8,128)(2,1)S(1)}, u32[]{:S(2)}) copy-start(bf16[1024,128]{0,1:T(8,128)(2,1)S(1)} %all_gather.46) | copy-start | bytes 786436
  86.6 33.0 %copy-start.9 = (bf16[1,512,3,1024]{3,1,2,0:T(8,128)(2,1)S(1)}, bf16[1,512,3,1024]{3,1,2,0:T(8,128)(2,1)}, u32[]{:S(2)}) copy-start(bf16[1,512,3,1024]{3,1,2,0:T(8,128)(2,1)} %all-gather.9.cloned.1.call-done) | copy-start | bytes 9437188
  404.6 491.7 %all-reduce.17.cloned.1.call-start = ((), (), s32[]{:S(2)}) async-start(), calls=%async_computation.17 | async-start | bytes 12582912 | tf_op jit(solution)/shard_map/psum | solution.py:91
  427.5 902.7 %copy-start.103 = (f32[1,1024]{1,0:T(1,128)}, f32[1,1024]{1,0:T(1,128)S(1)}, u32[]{:S(2)}) copy-start(f32[1,1024]{1,0:T(1,128)S(1)} %get-tuple-element.185) | copy-start | bytes 12292
  427.6 1126.7 %copy-start.101 = (f32[1,1024]{1,0:T(1,128)}, f32[1,1024]{1,0:T(1,128)S(1)}, u32[]{:S(2)}) copy-start(f32[1,1024]{1,0:T(1,128)S(1)} %get-tuple-element.186) | copy-start | bytes 12292
  427.6 468.8 %copy-start.109 = (f32[1,1024]{1,0:T(1,128)}, f32[1,1024]{1,0:T(1,128)S(1)}, u32[]{:S(2)}) copy-start(f32[1,1024]{1,0:T(1,128)S(1)} %get-tuple-element.180) | copy-start | bytes 12292
  427.6 760.2 %copy-start.116 = (f32[1,1024]{1,0:T(1,128)}, f32[1,1024]{1,0:T(1,128)S(1)}, u32[]{:S(2)}) copy-start(f32[1,1024]{1,0:T(1,128)S(1)} %get-tuple-element.181) | copy-start | bytes 12292
  674.4 251.3 %all-gather.17.cloned.1.call-start = ((), (), s32[]{:S(2)}) async-start(), calls=%async_computation.18 | async-start | bytes 2359296 | tf_op jit(solution)/shard_map/all_gather | solution.py:158
  676.2 279.9 %all-gather.19.cloned.1.call-start = ((), (), s32[]{:S(2)}) async-start(), calls=%async_computation.19 | async-start | bytes 2359296 | tf_op jit(solution)/shard_map/all_gather | solution.py:159
  677.0 510.7 %all-reduce.19.cloned.1.call-start = ((), (), s32[]{:S(2)}) async-start(), calls=%async_computation.20 | async-start | bytes 12582912 | tf_op jit(solution)/shard_map/psum | solution.py:91
  964.7 361.8 %reduce-scatter.13.cloned.1.call-start = ((), (), s32[]{:S(2)}) async-start(), calls=%async_computation.21 | async-start | bytes 7864320 | tf_op jit(solution)/shard_map/reduce_scatter | solution.py:295
  1216.7 181.2 %all-gather.21.cloned.1.call-start = ((), (), s32[]{:S(2)}) async-start(), calls=%async_computation.22 | async-start | bytes 3932160 | tf_op jit(solution)/shard_map/all_gather | solution.py:304
  1332.6 76.4 %copy-start.32 = (f32[1,128,3,1024]{3,1,2,0:T(8,128)}, f32[1,128,3,1024]{3,1,2,0:T(8,128)S(1)}, u32[]{:S(2)}) copy-start(f32[1,128,3,1024]{3,1,2,0:T(8,128)S(1)} %get-tuple-element.140) | copy-start | bytes 4718596
  1333.8 217.3 %reduce-scatter.15.cloned.1.call-start = ((), (), s32[]{:S(2)}) async-start(), calls=%async_computation.23 | async-start | bytes 7864320 | tf_op jit(solution)/shard_map/reduce_scatter | solution.py:338
  1441.5 109.6 %copy-start.33 = (f32[1,128,3,1024]{3,1,2,0:T(8,128)S(1)}, f32[1,128,3,1024]{3,1,2,0:T(8,128)}, u32[]{:S(2)}) copy-start(f32[1,128,3,1024]{3,1,2,0:T(8,128)} %copy-done.32) | copy-start | bytes 4718596
  1441.5 181.5 %all-gather.23.cloned.1.call-start = ((), (), s32[]{:S(2)}) async-start(), calls=%async_computation.24 | async-start | bytes 3932160 | tf_op jit(solution)/shard_map/all_gather | solution.py:347
  1558.9 362.9 %reduce-scatter.29.cloned.1.call-start = ((), (), s32[]{:S(2)}) async-start(), calls=%async_computation.31 | async-start | bytes 2359296 | tf_op jit(solution)/shard_map/reduce_scatter | solution.py:419
  1582.8 340.8 %reduce-scatter.19.cloned.1.call-start = ((), (), s32[]{:S(2)}) async-start(), calls=%async_computation.26 | async-start | bytes 2621440 | tf_op jit(solution)/shard_map/reduce_scatter | solution.py:409
  1583.0 120.5 %copy-start.129 = (f32[32]{0:T(128)}, f32[32]{0:T(128)S(1)}, u32[]{:S(2)}) copy-start(f32[32]{0:T(128)S(1)} %slice_reduce_fusion) | copy-start | bytes 388
  1583.0 40.0 %copy-start.58 = (bf16[1024,256]{1,0:T(8,128)(2,1)S(1)}, bf16[1024,256]{1,0:T(8,128)(2,1)}, u32[]{:S(2)}) copy-start(bf16[1024,256]{1,0:T(8,128)(2,1)} %all_gather.47) | copy-start | bytes 1572868
  1586.9 39.2 %copy-start.35 = (bf16[1,512,3,4,64]{1,4,3,2,0:T(8,128)(2,1)S(1)}, bf16[1,512,3,4,64]{1,4,3,2,0:T(8,128)(2,1)}, u32[]{:S(2)}) copy-start(bf16[1,512,3,4,64]{1,4,3,2,0:T(8,128)(2,1)} %copy-done.34) | copy-start | bytes 2359300
  1586.9 39.4 %copy-start.93 = (f32[512,4]{0,1:T(4,128)S(1)}, f32[512,4]{0,1:T(4,128)}, u32[]{:S(2)}) copy-start(f32[512,4]{0,1:T(4,128)} %copy-done.92) | copy-start | bytes 24580
  1586.9 39.4 %copy-start.95 = (f32[512,4]{0,1:T(4,128)S(1)}, f32[512,4]{0,1:T(4,128)}, u32[]{:S(2)}) copy-start(f32[512,4]{0,1:T(4,128)} %copy-done.94) | copy-start | bytes 24580
  1586.9 40.2 %copy-start.80 = (f32[4,512]{1,0:T(4,128)S(1)}, f32[4,512]{1,0:T(4,128)}, u32[]{:S(2)}) copy-start(f32[4,512]{1,0:T(4,128)} %copy-done.79) | copy-start | bytes 24580
  1586.9 338.9 %reduce-scatter.23.cloned.1.call-start = ((), (), s32[]{:S(2)}) async-start(), calls=%async_computation.28 | async-start | bytes 589824 | tf_op jit(solution)/shard_map/reduce_scatter | solution.py:416
  1642.3 61.2 %copy-start.81 = (f32[512,4]{0,1:T(4,128)}, f32[512,4]{0,1:T(4,128)S(1)}, u32[]{:S(2)}) copy-start(f32[512,4]{0,1:T(4,128)S(1)} %get-tuple-element.177) | copy-start | bytes 24580
  1676.0 29.0 %copy-start.97 = (f32[4,512]{1,0:T(4,128)S(1)}, f32[4,512]{1,0:T(4,128)}, u32[]{:S(2)}) copy-start(f32[4,512]{1,0:T(4,128)} %copy-done.96) | copy-start | bytes 24580
  1676.0 30.3 %copy-start.29 = (bf16[1,512,3,4,64]{1,4,3,2,0:T(8,128)(2,1)S(1)}, bf16[1,512,3,4,64]{1,4,3,2,0:T(8,128)(2,1)}, u32[]{:S(2)}) copy-start(bf16[1,512,3,4,64]{1,4,3,2,0:T(8,128)(2,1)} %copy-done.28) | copy-start | bytes 2359300
  1741.1 29.0 %copy-start.84 = (f32[512,4]{0,1:T(4,128)S(1)}, f32[512,4]{0,1:T(4,128)}, u32[]{:S(2)}) copy-start(f32[512,4]{0,1:T(4,128)} %copy-done.83) | copy-start | bytes 24580
  1741.1 29.0 %copy-start.90 = (s32[512]{0:T(512)S(1)}, s32[512]{0:T(512)}, u32[]{:S(2)}) copy-start(s32[512]{0:T(512)} %param.26) | copy-start | bytes 6148
  1771.6 76.7 %copy-start.60 = (bf16[512,1,128]{2,0,1:T(8,128)(2,1)}, bf16[512,1,128]{2,0,1:T(8,128)(2,1)S(1)}, u32[]{:S(2)}) copy-start(bf16[512,1,128]{2,0,1:T(8,128)(2,1)S(1)} %copy.350) | copy-start | bytes 393220
  1810.1 33.6 %copy-start.91 = (s32[512]{0:T(512)S(1)}, s32[512]{0:T(512)}, u32[]{:S(2)}) copy-start(s32[512]{0:T(512)} %param.26) | copy-start | bytes 6148
  1811.7 36.6 %copy-start.10 = (bf16[1,512,3,1024]{3,1,2,0:T(8,128)(2,1)S(1)}, bf16[1,512,3,1024]{3,1,2,0:T(8,128)(2,1)}, u32[]{:S(2)}) copy-start(bf16[1,512,3,1024]{3,1,2,0:T(8,128)(2,1)} %all-gather.9.cloned.1.call-done) | copy-start | bytes 9437188
  1858.1 82.8 %reduce-scatter.21.cloned.1.call-start = ((), (), s32[]{:S(2)}) async-start(), calls=%async_computation.27 | async-start | bytes 3538944 | tf_op jit(solution)/shard_map/reduce_scatter | solution.py:415
  1876.6 126.7 %reduce-scatter.17.cloned.1.call-start = ((), (), s32[]{:S(2)}) async-start(), calls=%async_computation.25 | async-start | bytes 3932160 | tf_op jit(solution)/shard_map/reduce_scatter | solution.py:406
  1883.1 175.5 %reduce-scatter.35.cloned.1.call-start = ((), (), s32[]{:S(2)}) async-start(), calls=%async_computation.34 | async-start | bytes 4718592 | tf_op jit(solution)/shard_map/reduce_scatter | solution.py:422
  1891.1 223.0 %reduce-scatter.33.cloned.1.call-start = ((), (), s32[]{:S(2)}) async-start(), calls=%async_computation.33 | async-start | bytes 4718592 | tf_op jit(solution)/shard_map/reduce_scatter | solution.py:421
  1901.0 252.9 %reduce-scatter.31.cloned.1.call-start = ((), (), s32[]{:S(2)}) async-start(), calls=%async_computation.32 | async-start | bytes 1179648 | tf_op jit(solution)/shard_map/reduce_scatter | solution.py:420
  1906.2 287.5 %reduce-scatter.27.cloned.1.call-start = ((), (), s32[]{:S(2)}) async-start(), calls=%async_computation.30 | async-start | bytes 1179648 | tf_op jit(solution)/shard_map/reduce_scatter | solution.py:418
  1911.5 413.6 %all-reduce.21.cloned.1.call-start = ((), (), s32[]{:S(2)}) async-start(), calls=%async_computation.35 | async-start | bytes 167936 | tf_op jit(solution)/shard_map/psum | solution.py:424
  1917.7 448.6 %reduce-scatter.25.cloned.1.call-start = ((), (), s32[]{:S(2)}) async-start(), calls=%async_computation.29 | async-start | bytes 1179648 | tf_op jit(solution)/shard_map/reduce_scatter | solution.py:417
  1921.7 81.6 %copy-start.31 = (f32[1,128,3,1024]{3,1,2,0:T(8,128)S(1)}, f32[1,128,3,1024]{3,1,2,0:T(8,128)}, u32[]{:S(2)}) copy-start(f32[1,128,3,1024]{3,1,2,0:T(8,128)} %copy-done.30) | copy-start | bytes 4718596
  (124 other events, 653.3 us)
Sparse Core Ops, SparseCore 0:
  9.6 66.1 all-gather.8
  78.2 24.5 all-gather.10
  105.3 23.5 all-gather.14
  130.3 45.9 all-gather.12
  404.8 221.8 all-reduce.14
  674.5 221.7 all-reduce.16
  898.8 26.8 all-gather.16
  928.1 27.8 all-gather.18
  964.9 222.8 all-reduce.18
  1216.8 109.6 reduce-scatter.12
  1333.9 63.9 all-gather.20
  1441.6 109.4 reduce-scatter.14
  1559.0 63.9 all-gather.22
  1626.1 39.9 reduce-scatter.28
  1668.3 43.8 reduce-scatter.18
  1858.2 32.7 reduce-scatter.22
  1894.6 46.2 reduce-scatter.20
  1943.0 60.2 reduce-scatter.16
  2007.2 51.3 reduce-scatter.34
  2062.7 51.3 reduce-scatter.32
  2117.9 35.9 reduce-scatter.30
  2157.6 35.9 reduce-scatter.26
  2201.2 123.7 all-reduce.20
  2329.0 37.2 reduce-scatter.24
where the time goes:
time: 2410 us; the launch traced here: 2380 us
  waiting for transfers between devices  1450 us (60%)
  local copies, waits for them, and re-layouts  518 us (21%)
  matrix products  232 us (10%)
  other arithmetic  123 us (5%)
  blocking collectives  43.5 us (2%)
    psum x3, waiting for transfers between devices, branch_total(): return lax.psum(term, 'head')  636 us
    dot_general x63, matrix products, matmul(): jnp.einsum(pattern, former, latter, preferred_element_type=jnp.float32)  221 us
    psum x1, waiting for transfers between devices, per_device(): lax.psum((widen(self_bias_local, HEADS * HEAD_DIM, member), widen(relpos_...  131 us
    unnamed x325, local copies, waits for them, and re-layouts  116 us
    reduce_scatter x1, waiting for transfers between devices, per_device(): lax.psum_scatter(matmul('rsnf,df->rsnd', upper_low, up_back), 'head', sca...  110 us
    reduce_scatter x1, waiting for transfers between devices, per_device(): lax.psum_scatter(matmul('rsnc,dc->rsnd', query_low, crossq_back), 'head',...  110 us
    rev x3, local copies, waits for them, and re-layouts, skew_grid(): flipped = distance[..., ::-1]  98.2 us
    rev x3, local copies, waits for them, and re-layouts, unskew_grid(): return flat.reshape(lead + (length, 2 * length))[..., :length][..., ::-1]  86.9 us
  transfers between devices with their start and end apart: 24, of which 18 were waited for; matrix products, arithmetic and copies ran while one was open for 29% of the time, Pallas kernels for 0%

commit v1 on v0

v1 whole, which is shorter than its diff:
```python
import functools

import jax
import jax.numpy as jnp
from jax import lax
from jax.experimental import pallas as pl
from jax.experimental.pallas import tpu as pltpu
from jax.sharding import PartitionSpec as P

BUCKETS = 32
HEAD_DIM = 64
WIDEST_DOC = 256
EPSILON = 1e-05
MASKED = -1e30
BF = jnp.bfloat16
F32 = jnp.float32
VMEM_BYTES = 56 * 1024 * 1024


def params():
    return pltpu.CompilerParams(vmem_limit_bytes=VMEM_BYTES)


def dot(a, b, ca, cb):
    return lax.dot_general(a, b, (((ca,), (cb,)), ((), ())), preferred_element_type=F32)


def whole(shape):
    return pl.BlockSpec(shape, lambda *_: (0,) * len(shape))


def swap(array_in, axis, bit):
    count = lax.axis_size(axis)
    return lax.ppermute(array_in, axis, [(i, i ^ bit) for i in range(count)])


def bits_of(axis):
    return (lax.axis_size(axis) - 1).bit_length()


def gather_pieces(shard, batch_order):
    nb, nz = bits_of("batch"), bits_of("head")
    blk, cols = shard.shape
    buf = shard.reshape((1,) * (nb + nz) + (blk, cols))
    for bit in range(nz):
        axis = nb + nz - 1 - bit
        buf = jnp.concatenate([buf, swap(buf, "head", 1 << bit)], axis)
    for bit in batch_order:
        buf = jnp.concatenate([buf, swap(buf, "batch", 1 << bit)], bit)
    last = swap(buf, "batch", 1)
    shape = (1 << (nb - 1), 1 << nz, blk, cols)
    return (buf.reshape(shape), last.reshape(shape))


def scatter_pieces(kept, batch_order):
    nb, nz = bits_of("batch"), bits_of("head")
    blk, cols = kept.shape[2:]
    buf = kept.reshape((2,) * (nb - 1 + nz) + (blk, cols))
    live = list(batch_order)
    axes = sorted(live)
    steps = [("batch", bit) for bit in live] + [("head", bit) for bit in reversed(range(nz))]
    names = [("batch", bit) for bit in axes] + [("head", bit) for bit in reversed(range(nz))]
    for number, (axis_name, bit) in enumerate(steps):
        axis = names.index((axis_name, bit))
        names.pop(axis)
        mine = lax.index_in_dim(buf, 0, axis, keepdims=False)
        theirs = lax.index_in_dim(buf, 1, axis, keepdims=False)
        total = mine.astype(F32) + swap(theirs, axis_name, 1 << bit).astype(F32)
        buf = total if number == len(steps) - 1 else total.astype(BF)
    return buf.reshape(blk, cols)


def bit_reverse(number, width):
    turned = 0
    for bit in range(width):
        turned |= ((number >> bit) & 1) << (width - 1 - bit)
    return turned


def reorder_blocks(array_in, table):
    count = table.shape[0]
    rows, features = array_in.shape
    blk = features // count
    if blk % 128:
        return jnp.take(array_in.reshape(rows, count, blk), table, axis=1).reshape(rows, features)

    def body(table_ref, in_ref, out_ref):
        out_ref[...] = in_ref[...]

    return pl.pallas_call(
        body,
        out_shape=jax.ShapeDtypeStruct(array_in.shape, array_in.dtype),
        grid_spec=pltpu.PrefetchScalarGridSpec(
            num_scalar_prefetch=1,
            grid=(count,),
            in_specs=[pl.BlockSpec((rows, blk), lambda p, table_ref: (0, table_ref[p]))],
            out_specs=pl.BlockSpec((rows, blk), lambda p, table_ref: (0, p)),
        ),
        name="reorder",
    )(table, array_in)


def piece_specs(pieces, cols, col_block, step=None):
    count, _, blk, _ = pieces[0].shape
    return [
        pl.BlockSpec((count, 1, blk, cols), lambda j, *c: (0, j, 0, col_block + (c[0] if c else 0)))
        for _ in pieces
    ]


def flat_piece(ref):
    count, _, blk, cols = ref.shape
    return ref[...].reshape(count * blk, cols)


def over_features(x, piece_refs):
    depth = x.shape[1] // len(piece_refs)
    total = None
    for number, ref in enumerate(piece_refs):
        term = dot(x[:, number * depth : (number + 1) * depth], flat_piece(ref), 1, 0)
        total = term if total is None else total + term
    return total


def project(x, pieces, first_col, cols, tile, affine, out_dtype, name):
    rows, features = x.shape
    groups = pieces[0].shape[1]
    per = cols // tile

    def body(x_ref, *refs):
        *piece_refs, affine_ref, out_ref = refs
        acc = over_features(x_ref[...], piece_refs)
        out_ref[...] = ((acc + affine_ref[0:1]) * affine_ref[1:2]).astype(out_ref.dtype)

    return pl.pallas_call(
        body,
        grid=(groups, per),
        in_specs=[whole((rows, features))]
        + piece_specs(pieces, tile, first_col // tile)
        + [pl.BlockSpec((2, tile), lambda j, c: (0, j * per + c))],
        out_specs=pl.BlockSpec((rows, tile), lambda j, c: (0, j * per + c)),
        out_shape=jax.ShapeDtypeStruct((rows, groups * cols), out_dtype),
        compiler_params=params(),
        name=name,
    )(x, *pieces, affine)


def project_plain(x, pieces, first_col, cols, name):
    groups = pieces[0].shape[1]
    affine = jnp.stack([jnp.zeros((groups * cols,), F32), jnp.ones((groups * cols,), F32)])
    return project(x, pieces, first_col, cols, cols, affine, BF, name)


def add_rows(acc_ref, left, piece_refs):
    depth = acc_ref.shape[1] // len(piece_refs)
    for number, ref in enumerate(piece_refs):
        where = slice(number * depth, (number + 1) * depth)
        acc_ref[:, where] += dot(left, flat_piece(ref), 1, 1)


def row_mean(v):
    return jnp.mean(v, -1, keepdims=True)


def column_sum(v):
    return jnp.sum(v, 0, keepdims=True)


def normalize(v):
    centered = v - row_mean(v)
    spread = lax.rsqrt(row_mean(centered * centered) + EPSILON)
    return centered * spread, spread


def normalize_back(upstream, unit, spread, gain):
    a = upstream * gain
    return spread * (a - row_mean(a) - unit * row_mean(a * unit))


def close_sublayer(left, pieces, first_col, cols, residual, vectors, name):
    rows, features = residual.shape
    groups = pieces[0].shape[1]
    count = len(pieces)

    def body(left_ref, *refs):
        piece_refs = refs[:count]
        residual_ref, vectors_ref, normed_ref, low_ref, unit_ref, spread_ref, acc_ref = refs[count:]
        step = pl.program_id(0)

        @pl.when(step == 0)
        def _():
            acc_ref[...] = jnp.zeros_like(acc_ref)

        add_rows(acc_ref, left_ref[...], piece_refs)

        @pl.when(step == groups - 1)
        def _():
            v = residual_ref[...].astype(F32) + (acc_ref[...] + vectors_ref[2:3])
            unit, spread = normalize(v)
            normed = unit * vectors_ref[0:1] + vectors_ref[1:2]
            normed_ref[...] = normed
            low_ref[...] = normed.astype(BF)
            unit_ref[...] = unit
            spread_ref[...] = spread

    return pl.pallas_call(
        body,
        grid=(groups,),
        in_specs=[pl.BlockSpec((rows, cols), lambda j: (0, j))]
        + piece_specs(pieces, cols, first_col // cols)
        + [whole((rows, features)), whole((3, features))],
        out_specs=[whole((rows, features))] * 3 + [whole((rows, 1))],
        out_shape=[
            jax.ShapeDtypeStruct((rows, features), F32),
            jax.ShapeDtypeStruct((rows, features), BF),
            jax.ShapeDtypeStruct((rows, features), F32),
            jax.ShapeDtypeStruct((rows, 1), F32),
        ],
        scratch_shapes=[pltpu.VMEM((rows, features), F32)],
        compiler_params=params(),
        name=name,
    )(left, *pieces, residual, vectors)


def feed_forward(low, normed, up_pieces, down_pieces, up_bias, vectors, grad_out):
    rows, features = normed.shape
    groups, cols = up_pieces[0].shape[1], up_pieces[0].shape[3]
    count = len(up_pieces)

    def body(low_ref, normed_ref, *refs):
        ups, downs = refs[:count], refs[count : 2 * count]
        bias_ref, vectors_ref, grad_ref = refs[2 * count : 2 * count + 3]
        active_ref, slope_ref, out_ref, third_ref, third_low_ref, sums_ref, acc_ref = refs[
            2 * count + 3 :
        ]
        step = pl.program_id(0)

        @pl.when(step == 0)
        def _():
            acc_ref[...] = jnp.zeros_like(acc_ref)

        upper = over_features(low_ref[...], ups) + bias_ref[...]
        cdf = 0.5 * (1.0 + lax.erf(upper * 0.7071067811865476))
        active = (upper * cdf).astype(BF)
        slope = cdf + upper * jnp.exp(-0.5 * upper * upper) * 0.3989422804014327
        active_ref[...] = active
        slope_ref[...] = slope.astype(BF)
        add_rows(acc_ref, active, downs)

        @pl.when(step == groups - 1)
        def _():
            v = normed_ref[...] + (acc_ref[...] + vectors_ref[2:3])
            unit, spread = normalize(v)
            gain = vectors_ref[0:1]
            out_ref[...] = (unit * gain + vectors_ref[1:2]).astype(BF)
            upstream = grad_ref[...]
            third = normalize_back(upstream, unit, spread, gain)
            third_ref[...] = third
            third_low_ref[...] = third.astype(BF)
            sums_ref[0:1] = column_sum(upstream * unit)
            sums_ref[1:2] = column_sum(upstream)
            sums_ref[2:3] = column_sum(third)

    return pl.pallas_call(
        body,
        grid=(groups,),
        in_specs=[whole((rows, features)), whole((rows, features))]
        + piece_specs(up_pieces, cols, 0)
        + piece_specs(down_pieces, cols, 0)
        + [
            pl.BlockSpec((1, cols), lambda j: (0, j)),
            whole((3, features)),
            whole((rows, features)),
        ],
        out_specs=[
            pl.BlockSpec((rows, cols), lambda j: (0, j)),
            pl.BlockSpec((rows, cols), lambda j: (0, j)),
            whole((rows, features)),
            whole((rows, features)),
            whole((rows, features)),
            whole((3, features)),
        ],
        out_shape=[
            jax.ShapeDtypeStruct((rows, groups * cols), BF),
            jax.ShapeDtypeStruct((rows, groups * cols), BF),
            jax.ShapeDtypeStruct((rows, features), BF),
            jax.ShapeDtypeStruct((rows, features), F32),
            jax.ShapeDtypeStruct((rows, features), BF),
            jax.ShapeDtypeStruct((3, features), F32),
        ],
        scratch_shapes=[pltpu.VMEM((rows, features), F32)],
        compiler_params=params(),
        name="feed_forward",
    )(low, normed, *up_pieces, *down_pieces, up_bias, vectors, grad_out)


def norm_back_outputs(upstream, unit, spread, gain, grad_ref, grad_low_ref, sums_ref):
    grad = normalize_back(upstream, unit, spread, gain)
    grad_ref[...] = grad
    grad_low_ref[...] = grad.astype(BF)
    sums_ref[0:1] = column_sum(upstream * unit)
    sums_ref[1:2] = column_sum(upstream)
    sums_ref[2:3] = column_sum(grad)


def feed_forward_back(third_low, third, slope, up_pieces, down_pieces, unit, spread, gain):
    rows, features = third.shape
    groups, cols = up_pieces[0].shape[1], up_pieces[0].shape[3]
    count = len(up_pieces)

    def body(third_low_ref, third_ref, slope_ref, *refs):
        ups, downs = refs[:count], refs[count : 2 * count]
        unit_ref, spread_ref, gain_ref = refs[2 * count : 2 * count + 3]
        upper_ref, bias_ref, grad_ref, grad_low_ref, sums_ref, acc_ref = refs[2 * count + 3 :]
        step = pl.program_id(0)

        @pl.when(step == 0)
        def _():
            acc_ref[...] = jnp.zeros_like(acc_ref)

        grad_upper = over_features(third_low_ref[...], downs) * slope_ref[...].astype(F32)
        bias_ref[...] = column_sum(grad_upper)
        low = grad_upper.astype(BF)
        upper_ref[...] = low
        add_rows(acc_ref, low, ups)

        @pl.when(step == groups - 1)
        def _():
            norm_back_outputs(
                acc_ref[...] + third_ref[...],
                unit_ref[...],
                spread_ref[...],
                gain_ref[...],
                grad_ref,
                grad_low_ref,
                sums_ref,
            )

    return pl.pallas_call(
        body,
        grid=(groups,),
        in_specs=[
            whole((rows, features)),
            whole((rows, features)),
            pl.BlockSpec((rows, cols), lambda j: (0, j)),
        ]
        + piece_specs(up_pieces, cols, 0)
        + piece_specs(down_pieces, cols, 0)
        + [whole((rows, features)), whole((rows, 1)), whole((1, features))],
        out_specs=[
            pl.BlockSpec((rows, cols), lambda j: (0, j)),
            pl.BlockSpec((1, cols), lambda j: (0, j)),
            whole((rows, features)),
            whole((rows, features)),
            whole((3, features)),
        ],
        out_shape=[
            jax.ShapeDtypeStruct((rows, groups * cols), BF),
            jax.ShapeDtypeStruct((1, groups * cols), F32),
            jax.ShapeDtypeStruct((rows, features), F32),
            jax.ShapeDtypeStruct((rows, features), BF),
            jax.ShapeDtypeStruct((3, features), F32),
        ],
        scratch_shapes=[pltpu.VMEM((rows, features), F32)],
        compiler_params=params(),
        name="feed_forward_back",
    )(third_low, third, slope, *up_pieces, *down_pieces, unit, spread, gain)


def cross_query_back(grad_query, pieces, first_col, cols, second, unit, spread, gain):
    rows, features = second.shape
    groups = pieces[0].shape[1]
    count = len(pieces)

    def body(left_ref, *refs):
        piece_refs = refs[:count]
        second_ref, unit_ref, spread_ref, gain_ref, grad_ref, grad_low_ref, sums_ref, acc_ref = refs[
            count:
        ]
        step = pl.program_id(0)

        @pl.when(step == 0)
        def _():
            acc_ref[...] = second_ref[...]

        add_rows(acc_ref, left_ref[...], piece_refs)

        @pl.when(step == groups - 1)
        def _():
            norm_back_outputs(
                acc_ref[...],
                unit_ref[...],
                spread_ref[...],
                gain_ref[...],
                grad_ref,
                grad_low_ref,
                sums_ref,
            )

    return pl.pallas_call(
        body,
        grid=(groups,),
        in_specs=[pl.BlockSpec((rows, cols), lambda j: (0, j))]
        + piece_specs(pieces, cols, first_col // cols)
        + [whole((rows, features)), whole((rows, features)), whole((rows, 1)), whole((1, features))],
        out_specs=[whole((rows, features)), whole((rows, features)), whole((3, features))],
        out_shape=[
            jax.ShapeDtypeStruct((rows, features), F32),
            jax.ShapeDtypeStruct((rows, features), BF),
            jax.ShapeDtypeStruct((3, features), F32),
        ],
        scratch_shapes=[pltpu.VMEM((rows, features), F32)],
        compiler_params=params(),
        name="cross_query_back",
    )(grad_query, *pieces, second, unit, spread, gain)


def rows_back(left, pieces, first_col, cols, name):
    rows = left.shape[0]
    count = len(pieces)
    groups = pieces[0].shape[1]
    features = count * pieces[0].shape[0] * pieces[0].shape[2]

    def body(left_ref, *refs):
        piece_refs = refs[:count]
        out_ref, acc_ref = refs[count:]
        step = pl.program_id(0)

        @pl.when(step == 0)
        def _():
            acc_ref[...] = jnp.zeros_like(acc_ref)

        add_rows(acc_ref, left_ref[...], piece_refs)

        @pl.when(step == groups - 1)
        def _():
            out_ref[...] = acc_ref[...].astype(BF)

    return pl.pallas_call(
        body,
        grid=(groups,),
        in_specs=[pl.BlockSpec((rows, cols), lambda j: (0, j))]
        + piece_specs(pieces, cols, first_col // cols),
        out_specs=whole((rows, features)),
        out_shape=jax.ShapeDtypeStruct((rows, features), BF),
        scratch_shapes=[pltpu.VMEM((rows, features), F32)],
        compiler_params=params(),
        name=name,
    )(left, *pieces)


def input_back(grad_query, grad_kv, grad_rel, pieces, first):
    rows, features = first.shape
    long_rows = grad_kv.shape[0]
    halo = long_rows - rows
    groups = pieces[0].shape[1]
    count = len(pieces)
    width = grad_query.shape[1] // groups
    rel_width = grad_rel.shape[1] // groups

    def body(query_ref, kv_ref, rel_ref, *refs):
        parts = [refs[count * k : count * (k + 1)] for k in range(4)]
        first_ref, halo_ref, own_ref, acc_ref = refs[4 * count :]
        step = pl.program_id(0)

        @pl.when(step == 0)
        def _():
            acc_ref[0:halo] = jnp.zeros((halo, features), F32)
            acc_ref[halo:] = first_ref[...]

        own_acc = acc_ref.at[halo:]
        add_rows(own_acc, query_ref[...], parts[0])
        add_rows(acc_ref, kv_ref[:, 0:width], parts[1])
        add_rows(acc_ref, kv_ref[:, width : 2 * width], parts[2])
        add_rows(own_acc, rel_ref[...], parts[3])

        @pl.when(step == groups - 1)
        def _():
            halo_ref[...] = acc_ref[0:halo].astype(BF)
            own_ref[...] = acc_ref[halo:]

    return pl.pallas_call(
        body,
        grid=(groups,),
        in_specs=[
            pl.BlockSpec((rows, width), lambda j: (0, j)),
            pl.BlockSpec((long_rows, 2 * width), lambda j: (0, j)),
            pl.BlockSpec((rows, rel_width), lambda j: (0, j)),
        ]
        + piece_specs(pieces, width, 0)
        + piece_specs(pieces, width, 1)
        + piece_specs(pieces, width, 2)
        + piece_specs(pieces, rel_width, 3 * width // rel_width)
        + [whole((rows, features))],
        out_specs=[whole((halo, features)), whole((rows, features))],
        out_shape=[
            jax.ShapeDtypeStruct((halo, features), BF),
            jax.ShapeDtypeStruct((rows, features), F32),
        ],
        scratch_shapes=[pltpu.VMEM((long_rows, features), F32)],
        compiler_params=params(),
        name="input_back",
    )(grad_query, grad_kv, grad_rel, *pieces, *pieces, *pieces, *pieces, first)


def weight_products(entries, half, extra, pieces, groups, name):
    features = entries[0][0].shape[1]
    depth = features // 2
    blk = depth // pieces
    widths = [right.shape[1] // groups for _, right in entries]
    total = sum(widths)
    count = len(entries)

    def body(*refs):
        lefts, rights = refs[:count], refs[count : 2 * count]
        out_ref = refs[-1]
        at = 0
        for left_ref, right_ref, width in zip(lefts, rights, widths):
            term = dot(left_ref[...], right_ref[...], 0, 0).reshape(pieces, 1, blk, width)
            if extra is not None:
                term = term + refs[2 * count][:, :, :, at : at + width].astype(F32)
            out_ref[:, :, :, at : at + width] = term.astype(BF)
            at += width

    out_spec = pl.BlockSpec((pieces, 1, blk, total), lambda j: (0, j, 0, 0))
    in_specs = [pl.BlockSpec((left.shape[0], depth), lambda j: (0, half)) for left, _ in entries]
    in_specs += [
        pl.BlockSpec((right.shape[0], width), lambda j: (0, j))
        for (_, right), width in zip(entries, widths)
    ]
    operands = [left for left, _ in entries] + [right for _, right in entries]
    if extra is not None:
        in_specs.append(out_spec)
        operands.append(extra)
    return pl.pallas_call(
        body,
        grid=(groups,),
        in_specs=in_specs,
        out_specs=out_spec,
        out_shape=jax.ShapeDtypeStruct((pieces, groups, blk, total), BF),
        compiler_params=params(),
        name=name,
    )(*operands)


def weight_gradient(entries, batch_order, name):
    groups = lax.axis_size("head")
    pieces = lax.axis_size("batch") // 2
    sent = weight_products(entries, 1, None, pieces, groups, name + "_send")
    came = swap(sent, "batch", 1)
    kept = weight_products(entries, 0, came, pieces, groups, name + "_keep")
    return scatter_pieces(kept, batch_order)


def half_masks(rows):
    lane = lax.broadcasted_iota(jnp.int32, (rows, 128), 1)
    return [
        jnp.where((lane >= 64 * half) & (lane < 64 * half + 64), 1.0, 0.0).astype(F32)
        for half in range(2)
    ]


def skew(array_in, share):
    rows, width = array_in.shape
    parts = [
        pltpu.roll(array_in[n * share : (n + 1) * share], width - share + 1, 1, stride=1, stride_axis=0)
        for n in range(rows // share)
    ]
    return jnp.concatenate(parts, 0)


def self_attention(qkv, relpos, mask, turned, share):
    rows, window = 3 * share, 3 * share
    groups = qkv.shape[1] // 768
    halo = qkv.shape[0] - rows

    def body(q_ref, k_ref, v_ref, rel_ref, mask_ref, turned_ref, ctx_ref, probs_ref, own_ref):
        halves = half_masks(rows)
        lane = lax.broadcasted_iota(jnp.int32, (rows, 128), 1)
        rel = rel_ref[...]
        high = rel.astype(BF)
        split = jnp.concatenate([high, (rel - high.astype(F32)).astype(BF)], 1)
        row_id = lax.broadcasted_iota(jnp.int32, (256, window), 0) & 127
        own_all = jnp.zeros((rows, 128), F32)
        for pair in range(2):
            cols = slice(128 * pair, 128 * pair + 128)
            q = q_ref[halo:, cols]
            k, v = k_ref[0:window, cols], v_ref[0:window, cols]
            own_k = k_ref[halo:, cols].astype(F32)
            own_v = v_ref[halo:, cols].astype(F32)
            product = q.astype(F32) * own_k
            mixed = jnp.zeros((rows, 128), F32)
            for half in range(2):
                head = 2 * pair + half
                scores = dot(q * halves[half].astype(BF), k, 1, 1)
                table = jnp.where(row_id == turned_ref[...] + 32 * head, 1.0, 0.0).astype(BF)
                scores = scores + skew(dot(split, table, 1, 0), share) + mask_ref[...]
                own = jnp.sum(
                    product * halves[half] + jnp.where(lane == 32 * head, rel, 0.0), -1, keepdims=True
                )
                track = lax.broadcasted_iota(jnp.int32, (rows, 1), 0) >= share
                own = jnp.where(track, own, MASKED)
                top = jnp.maximum(jnp.max(scores, -1, keepdims=True), own)
                raised = jnp.exp(scores - top)
                own_raised = jnp.exp(own - top)
                scale = 1.0 / (jnp.sum(raised, -1, keepdims=True) + own_raised)
                probs = (raised * scale).astype(BF)
                own_probs = (own_raised * scale).astype(BF).astype(F32)
                probs_ref[head] = probs
                own_all = jnp.where(lane == head, own_probs, own_all)
                mixed = mixed + (dot(probs, v, 1, 0) + own_probs * own_v) * halves[half]
            ctx_ref[:, cols] = mixed.astype(BF)
        own_ref[...] = own_all

    long_rows = qkv.shape[0]
    return pl.pallas_call(
        body,
        grid=(groups,),
        in_specs=[
            pl.BlockSpec((long_rows, 256), lambda j: (0, 3 * j)),
            pl.BlockSpec((long_rows, 256), lambda j: (0, 3 * j + 1)),
            pl.BlockSpec((long_rows, 256), lambda j: (0, 3 * j + 2)),
            pl.BlockSpec((rows, 128), lambda j: (0, j)),
            whole((rows, window)),
            whole((1, window)),
        ],
        out_specs=[
            pl.BlockSpec((rows, 256), lambda j: (0, j)),
            pl.BlockSpec((4, rows, window), lambda j: (j, 0, 0)),
            pl.BlockSpec((rows, 128), lambda j: (0, j)),
        ],
        out_shape=[
            jax.ShapeDtypeStruct((rows, groups * 256), BF),
            jax.ShapeDtypeStruct((4 * groups, rows, window), BF),
            jax.ShapeDtypeStruct((rows, groups * 128), F32),
        ],
        compiler_params=params(),
        name="self_attention",
    )(qkv, qkv, qkv, relpos, mask, turned)


def self_attention_back(qkv, probs, own_probs, grad_ctx, straight, share):
    rows, window = 3 * share, 3 * share
    groups = qkv.shape[1] // 768
    halo = qkv.shape[0] - rows
    long_rows = qkv.shape[0]

    def body(
        q_ref, k_ref, v_ref, probs_ref, own_ref, grad_ref, straight_ref,
        gq_ref, gkv_ref, grel_ref, sums_ref, rel_sums_ref,
    ):
        halves = half_masks(rows)
        lane = lax.broadcasted_iota(jnp.int32, (rows, 128), 1)
        turn = jnp.where(
            lax.broadcasted_iota(jnp.int32, (window, window), 0)
            + lax.broadcasted_iota(jnp.int32, (window, window), 1)
            == window - 1,
            1.0,
            0.0,
        ).astype(BF)
        column = lax.broadcasted_iota(jnp.int32, (window, 128), 1)
        grel = jnp.zeros((rows, 128), F32)
        for pair in range(2):
            cols = slice(128 * pair, 128 * pair + 128)
            q = q_ref[halo:, cols]
            k, v = k_ref[0:window, cols], v_ref[0:window, cols]
            own_k = k_ref[halo:, cols].astype(F32)
            own_v = v_ref[halo:, cols].astype(F32)
            grad = grad_ref[:, cols]
            grad_wide = grad.astype(F32)
            own_product = grad_wide * own_v
            gq = jnp.zeros((rows, 128), F32)
            own_spread = jnp.zeros((rows, 128), F32)
            own_weight = jnp.zeros((rows, 128), F32)
            score_parts, prob_parts, q_parts, g_parts = [], [], [], []
            for half in range(2):
                head = 2 * pair + half
                low_half = halves[half].astype(BF)
                p = probs_ref[head]
                p_wide = p.astype(F32)
                grad_half = grad * low_half
                grad_probs = dot(grad_half, v, 1, 1)
                own_p = jnp.sum(jnp.where(lane == head, own_ref[...], 0.0), -1, keepdims=True)
                own_grad = jnp.sum(own_product * halves[half], -1, keepdims=True)
                row_dot = jnp.sum(p_wide * grad_probs, -1, keepdims=True) + own_p * own_grad
                grad_scores = (p_wide * (grad_probs - row_dot)).astype(BF)
                grad_own = (own_p * (own_grad - row_dot)).astype(BF).astype(F32)
                gq = gq + (dot(grad_scores, k, 1, 0) + grad_own * own_k) * halves[half]
                own_spread = own_spread + grad_own * halves[half]
                own_weight = own_weight + own_p * halves[half]
                score_parts.append(grad_scores)
                prob_parts.append(p)
                q_parts.append(q * low_half)
                g_parts.append(grad_half)
                turned = skew(dot(grad_scores, turn, 1, 0), share).astype(BF)
                table = jnp.where(column == straight_ref[...] + 32 * head, 1.0, 0.0).astype(BF)
                grel = grel + dot(turned, table, 1, 0) + jnp.where(lane == 32 * head, grad_own, 0.0)
            gk = dot(
                jnp.concatenate(q_parts, 0), jnp.concatenate(score_parts, 0), 0, 0
            ).T
            gv = dot(
                jnp.concatenate(g_parts, 0), jnp.concatenate(prob_parts, 0), 0, 0
            ).T
            gq = gq * 0.125
            gq_ref[:, cols] = gq.astype(BF)
            own_gk = own_spread * q.astype(F32)
            own_gv = own_weight * grad_wide
            vcols = slice(256 + 128 * pair, 256 + 128 * pair + 128)
            gkv_ref[0:window, cols] = gk.astype(BF)
            gkv_ref[0:window, vcols] = gv.astype(BF)
            gkv_ref[window:, cols] = own_gk[share:].astype(BF)
            gkv_ref[window:, vcols] = own_gv[share:].astype(BF)
            sums_ref[0:1, cols] = column_sum(gq)
            sums_ref[1:2, cols] = column_sum(gv) + column_sum(own_gv[share:])
        grel_ref[...] = grel.astype(BF)
        rel_sums_ref[...] = column_sum(grel)

    return pl.pallas_call(
        body,
        grid=(groups,),
        in_specs=[
            pl.BlockSpec((long_rows, 256), lambda j: (0, 3 * j)),
            pl.BlockSpec((long_rows, 256), lambda j: (0, 3 * j + 1)),
            pl.BlockSpec((long_rows, 256), lambda j: (0, 3 * j + 2)),
            pl.BlockSpec((4, rows, window), lambda j: (j, 0, 0)),
            pl.BlockSpec((rows, 128), lambda j: (0, j)),
            pl.BlockSpec((rows, 256), lambda j: (0, j)),
            whole((window, 1)),
        ],
        out_specs=[
            pl.BlockSpec((rows, 256), lambda j: (0, j)),
            pl.BlockSpec((long_rows, 512), lambda j: (0, j)),
            pl.BlockSpec((rows, 128), lambda j: (0, j)),
            pl.BlockSpec((2, 256), lambda j: (0, j)),
            pl.BlockSpec((1, 128), lambda j: (0, j)),
        ],
        out_shape=[
            jax.ShapeDtypeStruct((rows, groups * 256), BF),
            jax.ShapeDtypeStruct((long_rows, groups * 512), BF),
            jax.ShapeDtypeStruct((rows, groups * 128), BF),
            jax.ShapeDtypeStruct((2, groups * 256), F32),
            jax.ShapeDtypeStruct((1, groups * 128), F32),
        ],
        compiler_params=params(),
        name="self_attention_back",
    )(qkv, qkv, qkv, probs, own_probs, grad_ctx, straight)


def cross_attention(queries, kv):
    rows, places = queries.shape[0], kv.shape[0]
    groups = queries.shape[1] // 256

    def body(q_ref, k_ref, v_ref, ctx_ref, probs_ref):
        halves = half_masks(rows)
        for pair in range(2):
            cols = slice(128 * pair, 128 * pair + 128)
            q, k, v = q_ref[:, cols], k_ref[:, cols], v_ref[:, cols]
            mixed = jnp.zeros((rows, 128), F32)
            for half in range(2):
                scores = dot(q * halves[half].astype(BF), k, 1, 1)
                raised = jnp.exp(scores - jnp.max(scores, -1, keepdims=True))
                probs = (raised * (1.0 / jnp.sum(raised, -1, keepdims=True))).astype(BF)
                probs_ref[2 * pair + half] = probs
                mixed = mixed + dot(probs, v, 1, 0) * halves[half]
            ctx_ref[:, cols] = mixed.astype(BF)

    return pl.pallas_call(
        body,
        grid=(groups,),
        in_specs=[
            pl.BlockSpec((rows, 256), lambda j: (0, j)),
            pl.BlockSpec((places, 256), lambda j: (0, 2 * j)),
            pl.BlockSpec((places, 256), lambda j: (0, 2 * j + 1)),
        ],
        out_specs=[
            pl.BlockSpec((rows, 256), lambda j: (0, j)),
            pl.BlockSpec((4, rows, places), lambda j: (j, 0, 0)),
        ],
        out_shape=[
            jax.ShapeDtypeStruct((rows, groups * 256), BF),
            jax.ShapeDtypeStruct((4 * groups, rows, places), BF),
        ],
        compiler_params=params(),
        name="cross_attention",
    )(queries, kv, kv)


def cross_attention_back(queries, kv, probs, grad_ctx):
    rows, places = queries.shape[0], kv.shape[0]
    groups = queries.shape[1] // 256

    def body(q_ref, k_ref, v_ref, probs_ref, grad_ref, gq_ref, gkv_ref, sums_ref):
        halves = half_masks(rows)
        for pair in range(2):
            cols = slice(128 * pair, 128 * pair + 128)
            q, k, v, grad = q_ref[:, cols], k_ref[:, cols], v_ref[:, cols], grad_ref[:, cols]
            gq = jnp.zeros((rows, 128), F32)
            score_parts, prob_parts, q_parts, g_parts = [], [], [], []
            for half in range(2):
                low_half = halves[half].astype(BF)
                p = probs_ref[2 * pair + half]
                p_wide = p.astype(F32)
                grad_half = grad * low_half
                grad_probs = dot(grad_half, v, 1, 1)
                row_dot = jnp.sum(p_wide * grad_probs, -1, keepdims=True)
                grad_scores = (p_wide * (grad_probs - row_dot)).astype(BF)
                gq = gq + dot(grad_scores, k, 1, 0) * halves[half]
                score_parts.append(grad_scores)
                prob_parts.append(p)
                q_parts.append(q * low_half)
                g_parts.append(grad_half)
            gk = dot(
                jnp.concatenate(q_parts, 0), jnp.concatenate(score_parts, 0), 0, 0
            ).T
            gv = dot(
                jnp.concatenate(g_parts, 0), jnp.concatenate(prob_parts, 0), 0, 0
            ).T
            gq = gq * 0.125
            gq_ref[:, cols] = gq.astype(BF)
            vcols = slice(256 + 128 * pair, 256 + 128 * pair + 128)
            gkv_ref[:, cols] = gk.astype(BF)
            gkv_ref[:, vcols] = gv.astype(BF)
            sums_ref[0:1, cols] = column_sum(gq)
            sums_ref[1:2, cols] = column_sum(gv)

    return pl.pallas_call(
        body,
        grid=(groups,),
        in_specs=[
            pl.BlockSpec((rows, 256), lambda j: (0, j)),
            pl.BlockSpec((places, 256), lambda j: (0, 2 * j)),
            pl.BlockSpec((places, 256), lambda j: (0, 2 * j + 1)),
            pl.BlockSpec((4, rows, places), lambda j: (j, 0, 0)),
            pl.BlockSpec((rows, 256), lambda j: (0, j)),
        ],
        out_specs=[
            pl.BlockSpec((rows, 256), lambda j: (0, j)),
            pl.BlockSpec((places, 512), lambda j: (0, j)),
            pl.BlockSpec((2, 256), lambda j: (0, j)),
        ],
        out_shape=[
            jax.ShapeDtypeStruct((rows, groups * 256), BF),
            jax.ShapeDtypeStruct((places, groups * 512), BF),
            jax.ShapeDtypeStruct((2, groups * 256), F32),
        ],
        compiler_params=params(),
        name="cross_attention_back",
    )(queries, kv, kv, probs, grad_ctx)


def per_device(
    hidden,
    memory,
    grad_out,
    lengths,
    key_mask,
    buckets,
    self_weight,
    relpos_weight,
    selfout_weight,
    crossq_weight,
    crosskv_weight,
    crossout_weight,
    up_weight,
    down_weight,
    self_bias,
    relpos_bias,
    cross_bias,
    up_bias,
    norm_gain,
    norm_bias,
    out_bias,
):
    batches, groups = lax.axis_size("batch"), lax.axis_size("head")
    b, z = lax.axis_index("batch"), lax.axis_index("head")
    nb = bits_of("batch")
    share, features = hidden.shape[1], hidden.shape[3]
    length = share * groups
    rows, window = 3 * share, 3 * share
    assert share == 128 and hidden.shape[0] == 1 and WIDEST_DOC <= 2 * share
    assert batches == 1 << nb and features % batches == 0 and groups == 4
    near, far = list(range(1, nb)), list(reversed(range(1, nb)))

    turned_ids = jnp.array([bit_reverse(p, nb) for p in range(batches)], jnp.int32)
    to_exchange = b ^ turned_ids
    natural = lax.iota(jnp.int32, batches) ^ b
    to_natural = jnp.zeros_like(natural)
    for bit in range(nb):
        to_natural = to_natural | (((natural >> bit) & 1) << (nb - 1 - bit))
    group_order = z ^ lax.iota(jnp.int32, groups)

    def small_features(stack):
        count = stack.shape[0]
        blocks = stack.reshape(count, batches, features // batches)
        return jnp.take(blocks, to_exchange, axis=1).reshape(count, features)

    def by_group(vector):
        return jnp.take(vector.reshape(groups, -1), group_order, axis=0)

    blk = self_weight.shape[0]
    weights_self = gather_pieces(
        jnp.concatenate([self_weight.reshape(blk, -1), relpos_weight], 1).astype(BF), near
    )
    weights_cross = gather_pieces(
        jnp.concatenate(
            [selfout_weight, crossq_weight, crosskv_weight.reshape(blk, -1), crossout_weight], 1
        ).astype(BF),
        far,
    )
    weights_up = gather_pieces(up_weight.astype(BF), near)
    weights_down = gather_pieces(down_weight.astype(BF), far)

    own = jnp.transpose(hidden[0], (1, 0, 2)).reshape(rows, features)
    own = reorder_blocks(own, to_exchange)
    main = own[0:share]
    chain = list(range(groups))
    before_one = lax.ppermute(main, "head", [(i, i + 1) for i in chain[:-1]])
    before_two = lax.ppermute(main, "head", [(i, i + 2) for i in chain[:-2]])
    extended = jnp.concatenate([before_two, before_one, own], 0)
    memory_all = reorder_blocks(memory[0], to_exchange)
    memory_all = jnp.concatenate([memory_all, swap(memory_all, "head", 1)], 0)
    memory_all = jnp.concatenate([memory_all, swap(memory_all, "head", 2)], 0)
    upstream = lax.dynamic_slice_in_dim(grad_out[0], z * share, share, 0)
    upstream = jnp.transpose(upstream, (1, 0, 2)).reshape(rows, features)
    upstream = reorder_blocks(upstream, to_exchange)

    vectors = small_features(jnp.concatenate([norm_gain, norm_bias, out_bias], 0))
    vectors = vectors.reshape(3, 3, features).transpose(1, 0, 2)
    ones = jnp.ones((groups, 256), F32)
    none = jnp.zeros((groups, 256), F32)
    query_bias, value_bias = by_group(self_bias[0]), by_group(self_bias[1])
    qkv_affine = jnp.stack(
        [
            jnp.concatenate([query_bias, none, value_bias], 1).reshape(-1),
            jnp.concatenate([0.125 * ones, ones, ones], 1).reshape(-1),
        ]
    )
    rel_affine = jnp.stack([by_group(relpos_bias).reshape(-1), jnp.ones((groups * 128,), F32)])
    cross_query_affine = jnp.stack(
        [by_group(cross_bias[0]).reshape(-1), jnp.full((groups * 256,), 0.125, F32)]
    )
    cross_kv_affine = jnp.stack(
        [
            jnp.concatenate([none, by_group(cross_bias[1])], 1).reshape(-1),
            jnp.ones((groups * 512,), F32),
        ]
    )
    up_row = by_group(up_bias).reshape(1, -1)

    places = lax.iota(jnp.int32, length)
    doc_ends = jnp.cumsum(lengths[0])
    segment = jnp.sum((places[:, None] >= doc_ends[None, :]).astype(jnp.int32), -1)
    lead = window - share
    padded_segment = jnp.concatenate([jnp.full((lead,), -1, jnp.int32), segment])
    padded_mask = jnp.concatenate([jnp.zeros((lead,), jnp.int32), key_mask[0]])
    key_segment = lax.dynamic_slice_in_dim(padded_segment, z * share, window)
    key_open = lax.dynamic_slice_in_dim(padded_mask, z * share, window)
    query_segment = lax.dynamic_slice_in_dim(segment, z * share, share)
    query_at = lax.iota(jnp.int32, share)[:, None] + lead
    key_at = lax.iota(jnp.int32, window)[None, :]
    joined = (query_segment[:, None] == key_segment[None, :]) & (
        (key_open[None, :] == 1) | (query_at == key_at)
    )
    allowed_main = joined & (key_at <= query_at)
    allowed_pred = joined & (key_at < query_at)
    mask = jnp.where(jnp.stack([allowed_main, allowed_pred, allowed_pred]), 0.0, MASKED)
    mask = mask.reshape(rows, window).astype(F32)
    straight = buckets[0:window]
    turned = straight[::-1]

    qkv = project(extended, weights_self, 0, 768, 256, qkv_affine, BF, "self_qkv")
    relpos = project(own, weights_self, 768, 128, 128, rel_affine, F32, "self_rel")
    context, self_probs, self_own = self_attention(qkv, relpos, mask, turned.reshape(1, -1), share)
    normed1, normed1_low, unit1, spread1 = close_sublayer(
        context, weights_cross, 0, 256, own, vectors[0], "self_out"
    )
    cross_kv = project(memory_all, weights_cross, 512, 512, 512, cross_kv_affine, BF, "cross_kv")
    cross_q = project(
        normed1_low, weights_cross, 256, 256, 256, cross_query_affine, BF, "cross_q"
    )
    cross_context, cross_probs = cross_attention(cross_q, cross_kv)
    normed2, normed2_low, unit2, spread2 = close_sublayer(
        cross_context, weights_cross, 1024, 256, normed1, vectors[1], "cross_out"
    )
    active, slope, out_low, third, third_low, sums_third = feed_forward(
        normed2_low, normed2, weights_up, weights_down, up_row, vectors[2], upstream
    )
    out_low = reorder_blocks(out_low, to_natural).reshape(3, share, features)
    layer_out = lax.all_gather(jnp.transpose(out_low, (1, 0, 2)), "head", axis=0, tiled=True)[None]

    grad_down = weight_gradient([(third_low, active)], far, "down_grad")
    upper_low, up_sums, second, second_low, sums_second = feed_forward_back(
        third_low, third, slope, weights_up, weights_down, unit2, spread2, vectors[1][0:1]
    )
    grad_up = weight_gradient([(normed2_low, upper_low)], near, "up_grad")
    grad_cross_ctx = project_plain(second_low, weights_cross, 1024, 256, "cross_ctx_back")
    grad_cross_q, grad_cross_kv, cross_sums = cross_attention_back(
        cross_q, cross_kv, cross_probs, grad_cross_ctx
    )
    grads_cross = weight_gradient(
        [
            (normed1_low, grad_cross_q),
            (memory_all, grad_cross_kv),
            (second_low, cross_context),
        ],
        far,
        "cross_grad",
    )
    memory_part = rows_back(grad_cross_kv, weights_cross, 512, 512, "memory_back")
    first, first_low, sums_first = cross_query_back(
        grad_cross_q, weights_cross, 256, 256, second, unit1, spread1, vectors[0][0:1]
    )
    grad_context = project_plain(first_low, weights_cross, 0, 256, "self_ctx_back")
    grad_q, grad_kv, grad_rel, self_sums, rel_sums = self_attention_back(
        qkv, self_probs, self_own, grad_context, straight.reshape(-1, 1), share
    )
    grads_self = weight_gradient(
        [
            (own, grad_q),
            (extended, grad_kv),
            (own, grad_rel),
            (first_low, context),
        ],
        near,
        "self_grad",
    )
    halo_grad, own_grad = input_back(grad_q, grad_kv, grad_rel, weights_self, first)

    from_two = lax.ppermute(halo_grad[0:share], "head", [(i + 2, i) for i in chain[:-2]])
    from_one = lax.ppermute(halo_grad[share:], "head", [(i + 1, i) for i in chain[:-1]])
    main_grad = own_grad[0:share] + from_one.astype(F32) + from_two.astype(F32)
    own_grad = jnp.concatenate([main_grad, own_grad[share:]], 0)
    own_grad = reorder_blocks(own_grad, to_natural).reshape(3, share, features)
    grad_hidden = jnp.transpose(own_grad, (1, 0, 2))[None]
    span = memory.shape[1]
    pairs = memory_part.reshape(2, 2 * span, features)
    memory_half = pairs[0].astype(F32) + swap(pairs[1], "head", 2).astype(F32)
    memory_half = memory_half.astype(BF)
    memory_grad = memory_half[:span].astype(F32) + swap(memory_half[span:], "head", 1).astype(F32)
    grad_memory = reorder_blocks(memory_grad, to_natural)[None]

    def natural_groups(block):
        return jnp.take(block.reshape(-1, groups, block.shape[1] // groups), group_order, axis=1)

    feature_sums = jnp.concatenate([sums_first, sums_second, sums_third], 0)
    feature_sums = jnp.take(
        feature_sums.reshape(9, batches, features // batches), to_natural, axis=1
    ).reshape(3, 3, features)
    packed = jnp.concatenate(
        [
            natural_groups(self_sums).reshape(-1),
            natural_groups(rel_sums).reshape(-1),
            natural_groups(cross_sums).reshape(-1),
            natural_groups(up_sums).reshape(-1),
            feature_sums.reshape(-1),
        ]
    )
    for bit in range(nb):
        packed = packed + swap(packed, "batch", 1 << bit)
    for bit in range(bits_of("head")):
        packed = packed + swap(packed, "head", 1 << bit)
    ends = [0]
    for size in (2 * features, groups * 128, 2 * features, up_bias.shape[0], 9 * features):
        ends.append(ends[-1] + size)
    self_bias_grad = packed[ends[0] : ends[1]].reshape(2, -1)
    relpos_bias_grad = packed[ends[1] : ends[2]]
    cross_bias_grad = packed[ends[2] : ends[3]].reshape(2, -1)
    up_bias_grad = packed[ends[3] : ends[4]]
    feature_sums = packed[ends[4] : ends[5]].reshape(3, 3, features)

    return (
        layer_out,
        grad_hidden,
        grad_memory,
        jnp.concatenate(
            [
                grads_self[:, 0:256].reshape(blk, 1, 256),
                grads_self[:, 256:768].reshape(blk, 2, 256),
            ],
            1,
        ),
        grads_self[:, 768:896],
        grads_self[:, 896:1152],
        grads_cross[:, 0:256],
        grads_cross[:, 256:768].reshape(blk, 2, 256),
        grads_cross[:, 768:1024],
        grad_up,
        grad_down,
        self_bias_grad,
        relpos_bias_grad,
        cross_bias_grad,
        up_bias_grad,
        feature_sums[:, 0],
        feature_sums[:, 1],
        feature_sums[:, 2],
    )


def solution(mesh):
    in_specs = (
        P("batch", "head", None, None),
        P("batch", "head", None),
        P("batch", None, None, None),
        P("batch", None),
        P("batch", None),
        P(),
        P("batch", None, "head"),
        P("batch", "head"),
        P("batch", "head"),
        P("batch", "head"),
        P("batch", None, "head"),
        P("batch", "head"),
        P("batch", "head"),
        P("batch", "head"),
        P(),
        P(),
        P(),
        P(),
        P(),
        P(),
        P(),
    )
    out_specs = (
        P("batch", None, None, None),
        P("batch", "head", None, None),
        P("batch", "head", None),
        P("batch", None, "head"),
        P("batch", "head"),
        P("batch", "head"),
        P("batch", "head"),
        P("batch", None, "head"),
        P("batch", "head"),
        P("batch", "head"),
        P("batch", "head"),
        P(),
        P(),
        P(),
        P(),
        P(),
        P(),
        P(),
    )
    return jax.shard_map(
        per_device, mesh=mesh, in_specs=in_specs, out_specs=out_specs, check_vma=False
    )
```

time: 2410 us -> 966 us (0.40)
  waiting for transfers between devices: 1450 us -> 473 us
  local copies, waits for them, and re-layouts: 518 us -> 62.8 us
  Pallas kernels: 0 us -> 272 us
  matrix products: 232 us -> 0 us
  starting transfers between devices: 0.99 us -> 69.3 us
  other arithmetic: 123 us -> 65.1 us
  blocking collectives: 43.5 us -> 0 us
    psum x4 -> x0, waiting for transfers between devices: 767 us -> none  [the longest x3 636 us: branch_total(): return lax.psum(term, 'head')]
    reduce_scatter x12 -> x0, waiting for transfers between devices: 522 us -> none  [the longest x1 110 us: per_device(): lax.psum_scatter(matmul('rsnf,df->rsnd', upper_low, up_back), 'head', sca...]
    ppermute x0 -> x53, waiting for transfers between devices: none -> 473 us  [the longest x49 400 us: swap(): return lax.ppermute(array_in, axis, [(i, i ^ bit) for i in range(count)])]
    pallas_call x0 -> x31, Pallas kernels: none -> 272 us  [the longest x8 59.3 us: weight_products(): pl.pallas_call(body, grid=(groups,), in_specs=in_specs, out_specs=out_spe...]
    dot_general x66 -> x0, matrix products: 232 us -> none  [the longest x63 221 us: matmul(): jnp.einsum(pattern, former, latter, preferred_element_type=jnp.float32)]
    rev x6 -> x1, local copies, waits for them, and re-layouts: 185 us -> 0.1 us  [per_device(): turned = straight[::-1]]
    all_gather x8 -> x1, waiting for transfers between devices: 158 us -> 0.02 us  [per_device(): lax.all_gather(jnp.transpose(out_low, (1, 0, 2)), 'head', axis=0, tiled=T...]
    unnamed x325 -> x102, local copies, waits for them, and re-layouts: 116 us -> 6.53 us
  transfers between devices with their start and end apart: 24 -> 54, of which waited for: 18 -> 29; matrix products, arithmetic and copies ran while one was open for 29% -> 12% of each run, Pallas kernels for 0% -> 26%
where the time goes in v1:
time: 966 us; the launch traced here: 958 us
  waiting for transfers between devices  473 us (49%)
  Pallas kernels  272 us (28%)
  starting transfers between devices  69.3 us (7%)
  other arithmetic  65.1 us (7%)
  local copies, waits for them, and re-layouts  62.8 us (7%)
  between operations  15.7 us (2%)
    ppermute x49, waiting for transfers between devices, swap(): return lax.ppermute(array_in, axis, [(i, i ^ bit) for i in range(count)])  400 us
    ppermute x49, starting transfers between devices, swap(): return lax.ppermute(array_in, axis, [(i, i ^ bit) for i in range(count)])  60.6 us
    pallas_call x8, Pallas kernels, weight_products(): pl.pallas_call(body, grid=(groups,), in_specs=in_specs, out_specs=out_spe...  59.3 us
    ppermute x1, waiting for transfers between devices, per_device(): lax.ppermute(halo_grad[0:share], 'head', [(i + 2, i) for i in chain[:-2]])  51.1 us
    pallas_call x6, Pallas kernels, project(): pl.pallas_call(body, grid=(groups, per), in_specs=[whole((rows, features)...  38.8 us
    pallas_call x6, Pallas kernels, reorder_blocks(): pl.pallas_call(body, out_shape=jax.ShapeDtypeStruct(array_in.shape, array...  35.4 us
    ppermute x1, waiting for transfers between devices, per_device(): lax.ppermute(halo_grad[share:], 'head', [(i + 1, i) for i in chain[:-1]])  21.7 us
    concatenate x8, other arithmetic, gather_pieces(): buf = jnp.concatenate([buf, swap(buf, 'batch', 1 << bit)], bit)  20.9 us
  transfers between devices with their start and end apart: 54, of which 29 were waited for; matrix products, arithmetic and copies ran while one was open for 12% of the time, Pallas kernels for 26%

profile of v1, /device:TPU:0, one launch (start us, length us, event | category | flops | bytes accessed | tf_op | source)
XLA Modules:
  0.0 957.7 jit_solution(10166531018851512117)
XLA Ops:
  13.4 7.7 collective-permute-done.7
  24.0 28.1 %collective-permute-done.8 = bf16[1,1,1,1,2,128,1280]{6,5,4,3,2,1,0:T(8,128)(2,1)S(1)} collective-permute-done((bf16[1,1,1,1,2,128,1280]{6,5,4,3,2,1,0:T(8,128)(2,1)S(1)}, bf16[1,1,1,1,2,128,1280]{6,5,4,3,2,1,0:T(8,128)(2,1)S(1)}, u32[]{:S(2)}, u32[]{:S(2)}) %collective-permute-start.8) | collective-permute-done | bytes 655392 | tf_op jit(solution)/shard_map/ppermute | solution.py:34
  59.2 24.1 %collective-permute-done.9 = bf16[1,1,1,2,2,128,1280]{6,5,4,3,2,1,0:T(8,128)(2,1)S(1)} collective-permute-done((bf16[1,1,1,2,2,128,1280]{6,5,4,3,2,1,0:T(8,128)(2,1)}, bf16[1,1,1,2,2,128,1280]{6,5,4,3,2,1,0:T(8,128)(2,1)S(1)}, u32[]{:S(2)}, u32[]{:S(2)}) %collective-permute-start.9) | collective-permute-done | bytes 1310752 | tf_op jit(solution)/shard_map/ppermute | solution.py:34
  93.0 11.2 %collective-permute-done.19 = bf16[1,1,1,1,1,128,1024]{6,5,4,3,2,1,0:T(8,128)(2,1)S(1)} collective-permute-done((bf16[1,1,1,1,1,128,1024]{6,5,4,3,2,1,0:T(8,128)(2,1)S(1)}, bf16[1,1,1,1,1,128,1024]{6,5,4,3,2,1,0:T(8,128)(2,1)S(1)}, u32[]{:S(2)}, u32[]{:S(2)}) %collective-permute-start.19) | collective-permute-done | bytes 262176 | tf_op jit(solution)/shard_map/ppermute | solution.py:34
  110.6 23.5 %collective-permute-done.15 = bf16[1,1,1,1,2,128,1024]{6,5,4,3,2,1,0:T(8,128)(2,1)S(1)} collective-permute-done((bf16[1,1,1,1,2,128,1024]{6,5,4,3,2,1,0:T(8,128)(2,1)S(1)}, bf16[1,1,1,1,2,128,1024]{6,5,4,3,2,1,0:T(8,128)(2,1)S(1)}, u32[]{:S(2)}, u32[]{:S(2)}) %collective-permute-start.15) | collective-permute-done | bytes 524320 | tf_op jit(solution)/shard_map/ppermute | solution.py:34
  136.6 7.5 collective-permute-done.3
  170.3 13.9 %collective-permute-done.4 = bf16[1,1,1,2,2,128,896]{5,6,4,3,2,1,0:T(8,128)(2,1)} collective-permute-done((bf16[1,1,1,2,2,128,896]{5,6,4,3,2,1,0:T(8,128)(2,1)}, bf16[1,1,1,2,2,128,896]{5,6,4,3,2,1,0:T(8,128)(2,1)}, u32[]{:S(2)}, u32[]{:S(2)}) %collective-permute-start.4) | collective-permute-done | bytes 917536 | tf_op jit(solution)/shard_map/ppermute | solution.py:34
  194.7 30.8 %collective-permute-done.17 = bf16[1,2,1,2,2,128,1024]{6,5,4,3,2,1,0:T(8,128)(2,1)S(1)} collective-permute-done((bf16[1,2,1,2,2,128,1024]{6,5,4,3,2,1,0:T(8,128)(2,1)S(1)}, bf16[1,2,1,2,2,128,1024]{6,5,4,3,2,1,0:T(8,128)(2,1)S(1)}, u32[]{:S(2)}, u32[]{:S(2)}) %collective-permute-start.17) | collective-permute-done | bytes 2097184 | tf_op jit(solution)/shard_map/ppermute | solution.py:34
  236.3 24.4 %collective-permute-done.5 = bf16[1,2,1,2,2,128,896]{5,6,4,3,2,1,0:T(8,128)(2,1)S(1)} collective-permute-done((bf16[1,2,1,2,2,128,896]{5,6,4,3,2,1,0:T(8,128)(2,1)S(1)}, bf16[1,2,1,2,2,128,896]{5,6,4,3,2,1,0:T(8,128)(2,1)S(1)}, u32[]{:S(2)}, u32[]{:S(2)}) %collective-permute-start.5) | collective-permute-done | bytes 1835040 | tf_op jit(solution)/shard_map/ppermute | solution.py:34
  278.7 12.9 %collective-permute-done.12 = bf16[256,1024]{1,0:T(8,128)(2,1)S(1)} collective-permute-done((bf16[256,1024]{1,0:T(8,128)(2,1)}, bf16[256,1024]{1,0:T(8,128)(2,1)S(1)}, u32[]{:S(2)}, u32[]{:S(2)}) %collective-permute-start.12) | collective-permute-done | bytes 524320 | tf_op jit(solution)/shard_map/ppermute | solution.py:34
  297.7 6.3 reorder.8.refs_6_
  313.2 40.8 %collective-permute-done.13 = bf16[512,1024]{1,0:T(8,128)(2,1)S(1)} collective-permute-done((bf16[512,1024]{1,0:T(8,128)(2,1)S(1)}, bf16[512,1024]{1,0:T(8,128)(2,1)S(1)}, u32[]{:S(2)}, u32[]{:S(2)}) %collective-permute-start.13) | collective-permute-done | bytes 1048608 | tf_op jit(solution)/shard_map/ppermute | solution.py:34
  355.6 6.0 copy.81
  361.6 6.1 copy.82
  372.0 12.0 %self_qkv.1.q_ref.k_ref.v_ref = bf16[640,3072]{1,0:T(8,128)(2,1)} custom-call(bf16[640,1024]{1,0:T(8,128)(2,1)} %pad_maximum_fusion.10.x_ref.refs_1_, bf16[4,4,128,896]{3,2,1,0:T(8,128)(2,1)} %bitcast.255, bf16[4,4,128,896]{3,2,1,0:T(8,128)(2,1)} %bitcast.261, f32[2,3072]{1,0:T(2,128)} %pad_maximum_fusion.25.refs_2_), custom_call_target="tpu_custom_call" | custom-call | tf_op jit(solution)/shard_map/self_qkv/pallas_call | solution.py:135
  384.1 18.0 %self_attention.1 = (bf16[384,1024]{1,0:T(8,128)(2,1)}, bf16[16,384,384]{2,1,0:T(8,128)(2,1)}, f32[384,512]{1,0:T(8,128)}) custom-call(bf16[640,3072]{1,0:T(8,128)(2,1)} %self_qkv.1.q_ref.k_ref.v_ref, bf16[640,3072]{1,0:T(8,128)(2,1)} %self_qkv.1.q_ref.k_ref.v_ref, bf16[640,3072]{1,0:T(8,128)(2,1)} %self_qkv.1.q_ref.k_ref.v_ref, ...), custom_call_target="tpu_custom_call" | custom-call | tf_op jit(solution)/shard_map/self_attention/pallas_call | solution.py:616
  402.1 8.5 cross_kv.1.k_ref.v_ref
  410.6 6.7 self_out.1
  421.8 14.4 %cross_attention.1 = (bf16[384,1024]{1,0:T(8,128)(2,1)}, bf16[16,384,1024]{2,1,0:T(8,128)(2,1)}) custom-call(bf16[384,1024]{1,0:T(8,128)(2,1)} %cross_q.1.q_ref, bf16[1024,2048]{1,0:T(8,128)(2,1)} %cross_kv.1.k_ref.v_ref, bf16[1024,2048]{1,0:T(8,128)(2,1)} %cross_kv.1.k_ref.v_ref), custom_call_target="tpu_custom_call" | custom-call | tf_op jit(solution)/shard_map/cross_attention/pallas_call | solution.py:767
  436.2 6.9 cross_out.1
  443.1 16.7 %feed_forward.1 = (bf16[384,4096]{1,0:T(8,128)(2,1)}, bf16[384,4096]{1,0:T(8,128)(2,1)}, bf16[384,1024]{1,0:T(8,128)(2,1)}, f32[384,1024]{1,0:T(8,128)}, bf16[384,1024]{1,0:T(8,128)(2,1)}, /*index=5*/f32[3,1024]{1,0:T(4,128)}) custom-call(bf16[384,1024]{1,0:T(8,128)(2,1)} %get-tuple-element.62.low_ref.refs_0_, f32[384,1024]{1,0:T(8,128)} %get-tuple-element.63.normed_ref, ...), custom_call_target="tpu_custom_call" | custom-call | tf_op jit(solution)/shard_map/feed_forward/pallas_call | solution.py:264
  459.8 6.0 down_grad_send.1
  467.2 14.9 %feed_forward_back.1 = (bf16[384,4096]{1,0:T(8,128)(2,1)}, f32[1,4096]{1,0:T(1,128)}, f32[384,1024]{1,0:T(8,128)}, bf16[384,1024]{1,0:T(8,128)(2,1)}, f32[3,1024]{1,0:T(4,128)}) custom-call(bf16[384,1024]{1,0:T(8,128)(2,1)} %get-tuple-element.68.third_low_ref.refs_0_, f32[384,1024]{1,0:T(8,128)} %get-tuple-element.69.third_ref, ...), custom_call_target="tpu_custom_call" | custom-call | tf_op jit(solution)/shard_map/feed_forward_back/pallas_call | solution.py:339
  482.1 6.0 up_grad_send.1
  493.2 16.9 %cross_attention_back.1 = (bf16[384,1024]{1,0:T(8,128)(2,1)}, bf16[1024,2048]{1,0:T(8,128)(2,1)}, f32[2,1024]{1,0:T(2,128)}) custom-call(bf16[384,1024]{1,0:T(8,128)(2,1)} %cross_q.1.q_ref, bf16[1024,2048]{1,0:T(8,128)(2,1)} %cross_kv.1.k_ref.v_ref, bf16[1024,2048]{1,0:T(8,128)(2,1)} %cross_kv.1.k_ref.v_ref, ...), custom_call_target="tpu_custom_call" | custom-call | tf_op jit(solution)/shard_map/cross_attention_back/pallas_call | solution.py:826
  510.1 7.0 cross_query_back.1
  521.9 18.1 %self_attention_back.1 = (bf16[384,1024]{1,0:T(8,128)(2,1)}, bf16[640,2048]{1,0:T(8,128)(2,1)}, bf16[384,512]{1,0:T(8,128)(2,1)}, f32[2,1024]{1,0:T(2,128)}, f32[1,512]{1,0:T(1,128)}) custom-call(bf16[640,3072]{1,0:T(8,128)(2,1)} %self_qkv.1.q_ref.k_ref.v_ref, bf16[640,3072]{1,0:T(8,128)(2,1)} %self_qkv.1.q_ref.k_ref.v_ref, ...), custom_call_target="tpu_custom_call" | custom-call | tf_op jit(solution)/shard_map/self_attention_back/pallas_call | solution.py:718
  540.0 7.9 self_grad_send.1
  548.5 8.2 cross_grad_send.1
  560.8 5.8 reorder.9
  569.8 10.1 %input_back.1 = (bf16[256,1024]{1,0:T(8,128)(2,1)}, f32[384,1024]{1,0:T(8,128)}) custom-call(bf16[384,1024]{1,0:T(8,128)(2,1)} %get-tuple-element.79.query_ref.refs_4_, bf16[640,2048]{1,0:T(8,128)(2,1)} %get-tuple-element.80.kv_ref.refs_5_, bf16[384,512]{1,0:T(8,128)(2,1)} %get-tuple-element.81.rel_ref.refs_6_, bf16[4,4,128,896]{3,2,1,0:T(8,128)(2,1)} %bitcast.256, ...), custom_call_target="tpu_custom_call" | custom-call | tf_op jit(solution)/shard_map/input_back/pallas_call | solution.py:482
  585.6 21.7 %collective-permute-done.24 = bf16[128,1024]{1,0:T(8,128)(2,1)S(1)} collective-permute-done((bf16[128,1024]{1,0:T(8,128)(2,1)S(1)}, bf16[128,1024]{1,0:T(8,128)(2,1)S(1)}, u32[]{:S(2)}, u32[]{:S(2)}) %collective-permute-start.24) | collective-permute-done | bytes 262176 | tf_op jit(solution)/shard_map/ppermute | solution.py:1030
  607.4 8.6 collective-permute-done.51
  617.3 51.1 %collective-permute-done.25 = bf16[128,1024]{1,0:T(8,128)(2,1)S(1)} collective-permute-done((bf16[128,1024]{1,0:T(8,128)(2,1)S(1)}, bf16[128,1024]{1,0:T(8,128)(2,1)S(1)}, u32[]{:S(2)}, u32[]{:S(2)}) %collective-permute-start.25) | collective-permute-done | bytes 262176 | tf_op jit(solution)/shard_map/ppermute | solution.py:1029
  668.4 9.1 memory_back.1
  683.4 6.1 reorder.10
  689.6 7.1 down_grad_keep.1
  706.3 7.0 up_grad_keep.1
  719.5 8.6 cross_grad_keep.1
  732.6 8.6 self_grad_keep.1
  752.5 6.1 reorder.11
  771.2 22.5 %collective-permute-done.34 = bf16[2,2,2,128,1024]{4,3,2,1,0:T(8,128)(2,1)} collective-permute-done((bf16[2,2,2,128,1024]{4,3,2,1,0:T(8,128)(2,1)}, bf16[2,2,2,128,1024]{4,3,2,1,0:T(8,128)(2,1)}, u32[]{:S(2)}, u32[]{:S(2)}) %collective-permute-start.34) | collective-permute-done | bytes 2097184 | tf_op jit(solution)/shard_map/ppermute | solution.py:34
  797.7 19.8 %collective-permute-done.29 = bf16[2,2,2,128,1152]{4,3,2,1,0:T(8,128)(2,1)} collective-permute-done((bf16[2,2,2,128,1152]{4,3,2,1,0:T(8,128)(2,1)}, bf16[2,2,2,128,1152]{4,3,2,1,0:T(8,128)(2,1)}, u32[]{:S(2)}, u32[]{:S(2)}) %collective-permute-start.29) | collective-permute-done | bytes 2359328 | tf_op jit(solution)/shard_map/ppermute | solution.py:34
  821.5 18.3 %collective-permute-done.45 = bf16[2,2,128,1024]{3,2,1,0:T(8,128)(2,1)S(1)} collective-permute-done((bf16[2,2,128,1024]{3,2,1,0:T(8,128)(2,1)S(1)}, bf16[2,2,128,1024]{3,2,1,0:T(8,128)(2,1)S(1)}, u32[]{:S(2)}, u32[]{:S(2)}) %collective-permute-start.45) | collective-permute-done | bytes 1048608 | tf_op jit(solution)/shard_map/ppermute | solution.py:34
  843.0 17.5 %collective-permute-done.35 = bf16[2,2,128,1024]{3,2,1,0:T(8,128)(2,1)S(1)} collective-permute-done((bf16[2,2,128,1024]{3,2,1,0:T(8,128)(2,1)S(1)}, bf16[2,2,128,1024]{3,2,1,0:T(8,128)(2,1)S(1)}, u32[]{:S(2)}, u32[]{:S(2)}) %collective-permute-start.35) | collective-permute-done | bytes 1048608 | tf_op jit(solution)/shard_map/ppermute | solution.py:34
  866.6 31.1 %collective-permute-done.36 = bf16[2,128,1024]{2,1,0:T(8,128)(2,1)S(1)} collective-permute-done((bf16[2,128,1024]{2,1,0:T(8,128)(2,1)S(1)}, bf16[2,128,1024]{2,1,0:T(8,128)(2,1)S(1)}, u32[]{:S(2)}, u32[]{:S(2)}) %collective-permute-start.36) | collective-permute-done | bytes 524320 | tf_op jit(solution)/shard_map/ppermute | solution.py:34
  898.0 10.0 %collective-permute-done.41 = bf16[2,128,1024]{2,1,0:T(8,128)(2,1)S(1)} collective-permute-done((bf16[2,128,1024]{2,1,0:T(8,128)(2,1)S(1)}, bf16[2,128,1024]{2,1,0:T(8,128)(2,1)S(1)}, u32[]{:S(2)}, u32[]{:S(2)}) %collective-permute-start.41) | collective-permute-done | bytes 524320 | tf_op jit(solution)/shard_map/ppermute | solution.py:34
  914.9 21.5 %collective-permute-done.31 = bf16[2,128,1152]{2,1,0:T(8,128)(2,1)S(1)} collective-permute-done((bf16[2,128,1152]{2,1,0:T(8,128)(2,1)S(1)}, bf16[2,128,1152]{2,1,0:T(8,128)(2,1)S(1)}, u32[]{:S(2)}, u32[]{:S(2)}) %collective-permute-start.31) | collective-permute-done | bytes 589856 | tf_op jit(solution)/shard_map/ppermute | solution.py:34
  (358 shorter events, 240.3 us)
Async XLA Ops:
  7.2 751.5 %all-gather.2.cloned.1.call-start = ((), (), s32[]{:S(2)}) async-start(), calls=%async_computation | async-start | bytes 3932160 | tf_op jit(solution)/shard_map/all_gather | solution.py:989
  21.2 30.9 %collective-permute-start.8 = (bf16[1,1,1,1,2,128,1280]{6,5,4,3,2,1,0:T(8,128)(2,1)S(1)}, bf16[1,1,1,1,2,128,1280]{6,5,4,3,2,1,0:T(8,128)(2,1)S(1)}, u32[]{:S(2)}, u32[]{:S(2)}) collective-permute-start(bf16[1,1,1,1,2,128,1280]{6,5,4,3,2,1,0:T(8,128)(2,1)S(1)} %pad_maximum_fusion.16), channel_id=1, source_target_pairs={{0,2},{1,3},{2,0},{3,1},{4,6},{5,7},{6,4},{7,5},{8,10},{9,11},{10,... | collective-permute-start | bytes 1966088 | tf_op jit(solution)/shard_map/ppermute | solution.py:34
  53.3 30.0 %collective-permute-start.9 = (bf16[1,1,1,2,2,128,1280]{6,5,4,3,2,1,0:T(8,128)(2,1)}, bf16[1,1,1,2,2,128,1280]{6,5,4,3,2,1,0:T(8,128)(2,1)S(1)}, u32[]{:S(2)}, u32[]{:S(2)}) collective-permute-start(bf16[1,1,1,2,2,128,1280]{6,5,4,3,2,1,0:T(8,128)(2,1)} %pad_maximum_fusion.11), channel_id=1, source_target_pairs={{0,16},{4,20},{8,24},{12,28},{16,0},{20,4},{24,8},{28,12},{1,17},{... | collective-permute-start | bytes 3932168 | tf_op jit(solution)/shard_map/ppermute | solution.py:34
  55.9 35.4 %collective-permute-start.2 = (bf16[1,1,1,1,1,128,896]{5,6,4,3,2,1,0:T(8,128)(2,1)S(1)}, bf16[1,1,1,1,1,128,896]{5,6,4,3,2,1,0:T(8,128)(2,1)S(1)}, u32[]{:S(2)}, u32[]{:S(2)}) collective-permute-start(bf16[1,1,1,1,1,128,896]{5,6,4,3,2,1,0:T(8,128)(2,1)S(1)} %pad_maximum_fusion.22), channel_id=1, source_target_pairs={{0,1},{1,0},{2,3},{3,2},{4,5},{5,4},{6,7},{7,6},{8,9},{9,8},{10,11... | collective-permute-start | bytes 688136 | tf_op jit(solution)/shard_map/ppermute | solution.py:34
  57.8 28.3 %collective-permute-start.14 = (bf16[1,1,1,1,1,128,1024]{6,5,4,3,2,1,0:T(8,128)(2,1)S(1)}, bf16[1,1,1,1,1,128,1024]{6,5,4,3,2,1,0:T(8,128)(2,1)S(1)}, u32[]{:S(2)}, u32[]{:S(2)}) collective-permute-start(bf16[1,1,1,1,1,128,1024]{6,5,4,3,2,1,0:T(8,128)(2,1)S(1)} %convert_bitcast_fusion.1), channel_id=1, source_target_pairs={{0,1},{1,0},{2,3},{3,2},{4,5},{5,4},{6,7},{7,6},{8,9},{9,8},{10,11... | collective-permute-start | bytes 786440 | tf_op jit(solution)/shard_map/ppermute | solution.py:34
  84.8 105.1 %collective-permute-start.10 = (bf16[1,1,2,2,2,128,1280]{6,5,4,3,2,1,0:T(8,128)(2,1)}, bf16[1,1,2,2,2,128,1280]{6,5,4,3,2,1,0:T(8,128)(2,1)}, u32[]{:S(2)}, u32[]{:S(2)}) collective-permute-start(bf16[1,1,2,2,2,128,1280]{6,5,4,3,2,1,0:T(8,128)(2,1)} %pad_maximum_fusion.4), channel_id=1, source_target_pairs={{0,8},{4,12},{8,0},{12,4},{16,24},{20,28},{24,16},{28,20},{1,9},{5... | collective-permute-start | bytes 7864328 | tf_op jit(solution)/shard_map/ppermute | solution.py:34
  86.1 48.1 %collective-permute-start.15 = (bf16[1,1,1,1,2,128,1024]{6,5,4,3,2,1,0:T(8,128)(2,1)S(1)}, bf16[1,1,1,1,2,128,1024]{6,5,4,3,2,1,0:T(8,128)(2,1)S(1)}, u32[]{:S(2)}, u32[]{:S(2)}) collective-permute-start(bf16[1,1,1,1,2,128,1024]{6,5,4,3,2,1,0:T(8,128)(2,1)S(1)} %pad_maximum_fusion.17), channel_id=1, source_target_pairs={{0,2},{1,3},{2,0},{3,1},{4,6},{5,7},{6,4},{7,5},{8,10},{9,11},{10,... | collective-permute-start | bytes 1572872 | tf_op jit(solution)/shard_map/ppermute | solution.py:34
  86.2 18.0 %collective-permute-start.19 = (bf16[1,1,1,1,1,128,1024]{6,5,4,3,2,1,0:T(8,128)(2,1)S(1)}, bf16[1,1,1,1,1,128,1024]{6,5,4,3,2,1,0:T(8,128)(2,1)S(1)}, u32[]{:S(2)}, u32[]{:S(2)}) collective-permute-start(bf16[1,1,1,1,1,128,1024]{6,5,4,3,2,1,0:T(8,128)(2,1)S(1)} %convert_bitcast_fusion), channel_id=1, source_target_pairs={{0,1},{1,0},{2,3},{3,2},{4,5},{5,4},{6,7},{7,6},{8,9},{9,8},{10,11... | collective-permute-start | bytes 786440 | tf_op jit(solution)/shard_map/ppermute | solution.py:34
  92.9 51.1 %collective-permute-start.3 = (bf16[1,1,1,1,2,128,896]{5,6,4,3,2,1,0:T(8,128)(2,1)}, bf16[1,1,1,1,2,128,896]{5,6,4,3,2,1,0:T(8,128)(2,1)}, u32[]{:S(2)}, u32[]{:S(2)}) collective-permute-start(bf16[1,1,1,1,2,128,896]{5,6,4,3,2,1,0:T(8,128)(2,1)} %pad_maximum_fusion.19), channel_id=1, source_target_pairs={{0,2},{1,3},{2,0},{3,1},{4,6},{5,7},{6,4},{7,5},{8,10},{9,11},{10,... | collective-permute-start | bytes 1376264 | tf_op jit(solution)/shard_map/ppermute | solution.py:34
  105.1 47.0 %collective-permute-start.20 = (bf16[1,1,1,1,2,128,1024]{6,5,4,3,2,1,0:T(8,128)(2,1)}, bf16[1,1,1,1,2,128,1024]{6,5,4,3,2,1,0:T(8,128)(2,1)}, u32[]{:S(2)}, u32[]{:S(2)}) collective-permute-start(bf16[1,1,1,1,2,128,1024]{6,5,4,3,2,1,0:T(8,128)(2,1)} %pad_maximum_fusion.18), channel_id=1, source_target_pairs={{0,2},{1,3},{2,0},{3,1},{4,6},{5,7},{6,4},{7,5},{8,10},{9,11},{10,... | collective-permute-start | bytes 1572872 | tf_op jit(solution)/shard_map/ppermute | solution.py:34
  136.0 31.8 %collective-permute-start.16 = (bf16[1,1,1,2,2,128,1024]{6,5,4,3,2,1,0:T(8,128)(2,1)}, bf16[1,1,1,2,2,128,1024]{6,5,4,3,2,1,0:T(8,128)(2,1)}, u32[]{:S(2)}, u32[]{:S(2)}) collective-permute-start(bf16[1,1,1,2,2,128,1024]{6,5,4,3,2,1,0:T(8,128)(2,1)} %pad_maximum_fusion.13), channel_id=1, source_target_pairs={{0,8},{4,12},{8,0},{12,4},{16,24},{20,28},{24,16},{28,20},{1,9},{5... | collective-permute-start | bytes 3145736 | tf_op jit(solution)/shard_map/ppermute | solution.py:34
  146.2 38.0 %collective-permute-start.4 = (bf16[1,1,1,2,2,128,896]{5,6,4,3,2,1,0:T(8,128)(2,1)}, bf16[1,1,1,2,2,128,896]{5,6,4,3,2,1,0:T(8,128)(2,1)}, u32[]{:S(2)}, u32[]{:S(2)}) collective-permute-start(bf16[1,1,1,2,2,128,896]{5,6,4,3,2,1,0:T(8,128)(2,1)} %pad_maximum_fusion.15), channel_id=1, source_target_pairs={{0,8},{4,12},{8,0},{12,4},{16,24},{20,28},{24,16},{28,20},{1,9},{5... | collective-permute-start | bytes 2752520 | tf_op jit(solution)/shard_map/ppermute | solution.py:34
  154.3 32.6 %collective-permute-start.21 = (bf16[1,1,1,2,2,128,1024]{6,5,4,3,2,1,0:T(8,128)(2,1)}, bf16[1,1,1,2,2,128,1024]{6,5,4,3,2,1,0:T(8,128)(2,1)}, u32[]{:S(2)}, u32[]{:S(2)}) collective-permute-start(bf16[1,1,1,2,2,128,1024]{6,5,4,3,2,1,0:T(8,128)(2,1)} %pad_maximum_fusion.14), channel_id=1, source_target_pairs={{0,16},{4,20},{8,24},{12,28},{16,0},{20,4},{24,8},{28,12},{1,17},{... | collective-permute-start | bytes 3145736 | tf_op jit(solution)/shard_map/ppermute | solution.py:34
  163.7 113.2 %collective-permute-start = (bf16[128,1024]{1,0:T(8,128)(2,1)}, bf16[128,1024]{1,0:T(8,128)(2,1)}, u32[]{:S(2)}, u32[]{:S(2)}) collective-permute-start(bf16[128,1024]{1,0:T(8,128)(2,1)} %slice.306), channel_id=1, source_target_pairs={{0,2},{1,3},{4,6},{5,7},{8,10},{9,11},{12,14},{13,15},{16,18},{17,... | collective-permute-start | bytes 786440 | tf_op jit(solution)/shard_map/ppermute | solution.py:918
  169.4 56.1 %collective-permute-start.17 = (bf16[1,2,1,2,2,128,1024]{6,5,4,3,2,1,0:T(8,128)(2,1)S(1)}, bf16[1,2,1,2,2,128,1024]{6,5,4,3,2,1,0:T(8,128)(2,1)S(1)}, u32[]{:S(2)}, u32[]{:S(2)}) collective-permute-start(bf16[1,2,1,2,2,128,1024]{6,5,4,3,2,1,0:T(8,128)(2,1)S(1)} %pad_maximum_fusion.6), channel_id=1, source_target_pairs={{0,16},{4,20},{8,24},{12,28},{16,0},{20,4},{24,8},{28,12},{1,17},{... | collective-permute-start | bytes 6291464 | tf_op jit(solution)/shard_map/ppermute | solution.py:34
  185.7 75.0 %collective-permute-start.5 = (bf16[1,2,1,2,2,128,896]{5,6,4,3,2,1,0:T(8,128)(2,1)S(1)}, bf16[1,2,1,2,2,128,896]{5,6,4,3,2,1,0:T(8,128)(2,1)S(1)}, u32[]{:S(2)}, u32[]{:S(2)}) collective-permute-start(bf16[1,2,1,2,2,128,896]{5,6,4,3,2,1,0:T(8,128)(2,1)S(1)} %pad_maximum_fusion.8), channel_id=1, source_target_pairs={{0,16},{4,20},{8,24},{12,28},{16,0},{20,4},{24,8},{28,12},{1,17},{... | collective-permute-start | bytes 5505032 | tf_op jit(solution)/shard_map/ppermute | solution.py:34
  188.4 44.4 %collective-permute-start.22 = (bf16[1,1,2,2,2,128,1024]{6,5,4,3,2,1,0:T(8,128)(2,1)S(1)}, bf16[1,1,2,2,2,128,1024]{6,5,4,3,2,1,0:T(8,128)(2,1)S(1)}, u32[]{:S(2)}, u32[]{:S(2)}) collective-permute-start(bf16[1,1,2,2,2,128,1024]{6,5,4,3,2,1,0:T(8,128)(2,1)S(1)} %pad_maximum_fusion.7), channel_id=1, source_target_pairs={{0,8},{4,12},{8,0},{12,4},{16,24},{20,28},{24,16},{28,20},{1,9},{5... | collective-permute-start | bytes 6291464 | tf_op jit(solution)/shard_map/ppermute | solution.py:34
  194.7 207.3 %collective-permute-start.11 = (bf16[1,2,2,2,2,128,1280]{6,5,4,3,2,1,0:T(8,128)(2,1)}, bf16[1,2,2,2,2,128,1280]{6,5,4,3,2,1,0:T(8,128)(2,1)}, u32[]{:S(2)}, u32[]{:S(2)}) collective-permute-start(bf16[1,2,2,2,2,128,1280]{6,5,4,3,2,1,0:T(8,128)(2,1)} %pad_maximum_fusion), channel_id=1, source_target_pairs={{0,4},{4,0},{8,12},{12,8},{16,20},{20,16},{24,28},{28,24},{1,5},{5... | collective-permute-start | bytes 15728648 | tf_op jit(solution)/shard_map/ppermute | solution.py:34
  228.8 214.3 %collective-permute-start.18 = (bf16[1,2,2,2,2,128,1024]{6,5,4,3,2,1,0:T(8,128)(2,1)}, bf16[1,2,2,2,2,128,1024]{6,5,4,3,2,1,0:T(8,128)(2,1)}, u32[]{:S(2)}, u32[]{:S(2)}) collective-permute-start(bf16[1,2,2,2,2,128,1024]{6,5,4,3,2,1,0:T(8,128)(2,1)} %pad_maximum_fusion.1), channel_id=1, source_target_pairs={{0,4},{4,0},{8,12},{12,8},{16,20},{20,16},{24,28},{28,24},{1,5},{5... | collective-permute-start | bytes 12582920 | tf_op jit(solution)/shard_map/ppermute | solution.py:34
  236.2 206.9 %collective-permute-start.23 = (bf16[1,2,2,2,2,128,1024]{6,5,4,3,2,1,0:T(8,128)(2,1)}, bf16[1,2,2,2,2,128,1024]{6,5,4,3,2,1,0:T(8,128)(2,1)}, u32[]{:S(2)}, u32[]{:S(2)}) collective-permute-start(bf16[1,2,2,2,2,128,1024]{6,5,4,3,2,1,0:T(8,128)(2,1)} %pad_maximum_fusion.2), channel_id=1, source_target_pairs={{0,4},{4,0},{8,12},{12,8},{16,20},{20,16},{24,28},{28,24},{1,5},{5... | collective-permute-start | bytes 12582920 | tf_op jit(solution)/shard_map/ppermute | solution.py:34
  264.1 97.5 %collective-permute-start.6 = (bf16[1,2,2,2,2,128,896]{5,6,4,3,2,1,0:T(8,128)(2,1)}, bf16[1,2,2,2,2,128,896]{5,6,4,3,2,1,0:T(8,128)(2,1)}, u32[]{:S(2)}, u32[]{:S(2)}) collective-permute-start(bf16[1,2,2,2,2,128,896]{5,6,4,3,2,1,0:T(8,128)(2,1)} %pad_maximum_fusion.3), channel_id=1, source_target_pairs={{0,4},{4,0},{8,12},{12,8},{16,20},{20,16},{24,28},{28,24},{1,5},{5... | collective-permute-start | bytes 11010056 | tf_op jit(solution)/shard_map/ppermute | solution.py:34
  276.9 14.6 %collective-permute-start.12 = (bf16[256,1024]{1,0:T(8,128)(2,1)}, bf16[256,1024]{1,0:T(8,128)(2,1)S(1)}, u32[]{:S(2)}, u32[]{:S(2)}) collective-permute-start(bf16[256,1024]{1,0:T(8,128)(2,1)} %reorder.7), channel_id=1, source_target_pairs={{0,1},{1,0},{2,3},{3,2},{4,5},{5,4},{6,7},{7,6},{8,9},{9,8},{10,11... | collective-permute-start | bytes 1572872 | tf_op jit(solution)/shard_map/ppermute | solution.py:34
  291.5 13.8 %collective-permute-start.1 = (bf16[128,1024]{1,0:T(8,128)(2,1)}, bf16[128,1024]{1,0:T(8,128)(2,1)S(1)}, u32[]{:S(2)}, u32[]{:S(2)}) collective-permute-start(bf16[128,1024]{1,0:T(8,128)(2,1)} %slice.306), channel_id=1, source_target_pairs={{0,1},{1,2},{2,3},{4,5},{5,6},{6,7},{8,9},{9,10},{10,11},{12,13},{... | collective-permute-start | bytes 786440 | tf_op jit(solution)/shard_map/ppermute | solution.py:917
  305.4 48.7 %collective-permute-start.13 = (bf16[512,1024]{1,0:T(8,128)(2,1)S(1)}, bf16[512,1024]{1,0:T(8,128)(2,1)S(1)}, u32[]{:S(2)}, u32[]{:S(2)}) collective-permute-start(bf16[512,1024]{1,0:T(8,128)(2,1)S(1)} %pad_maximum_fusion.12), channel_id=1, source_target_pairs={{0,2},{1,3},{2,0},{3,1},{4,6},{5,7},{6,4},{7,5},{8,10},{9,11},{10,... | collective-permute-start | bytes 3145736 | tf_op jit(solution)/shard_map/ppermute | solution.py:34
  465.8 223.9 %collective-permute-start.43 = (bf16[4,4,128,1024]{3,2,1,0:T(8,128)(2,1)}, bf16[4,4,128,1024]{3,2,1,0:T(8,128)(2,1)}, u32[]{:S(2)}, u32[]{:S(2)}) collective-permute-start(bf16[4,4,128,1024]{3,2,1,0:T(8,128)(2,1)} %down_grad_send.1), channel_id=1, source_target_pairs={{0,4},{4,0},{8,12},{12,8},{16,20},{20,16},{24,28},{28,24},{1,5},{5... | collective-permute-start | bytes 12582920 | tf_op jit(solution)/shard_map/ppermute | solution.py:34
  488.2 218.1 %collective-permute-start.38 = (bf16[4,4,128,1024]{3,2,1,0:T(8,128)(2,1)}, bf16[4,4,128,1024]{3,2,1,0:T(8,128)(2,1)}, u32[]{:S(2)}, u32[]{:S(2)}) collective-permute-start(bf16[4,4,128,1024]{3,2,1,0:T(8,128)(2,1)} %up_grad_send.1), channel_id=1, source_target_pairs={{0,4},{4,0},{8,12},{12,8},{16,20},{20,16},{24,28},{28,24},{1,5},{5... | collective-permute-start | bytes 12582920 | tf_op jit(solution)/shard_map/ppermute | solution.py:34
  547.8 184.8 %collective-permute-start.28 = (bf16[4,4,128,1152]{3,2,1,0:T(8,128)(2,1)}, bf16[4,4,128,1152]{3,2,1,0:T(8,128)(2,1)}, u32[]{:S(2)}, u32[]{:S(2)}) collective-permute-start(bf16[4,4,128,1152]{3,2,1,0:T(8,128)(2,1)} %self_grad_send.1), channel_id=1, source_target_pairs={{0,4},{4,0},{8,12},{12,8},{16,20},{20,16},{24,28},{28,24},{1,5},{5... | collective-permute-start | bytes 14155784 | tf_op jit(solution)/shard_map/ppermute | solution.py:34
  556.6 162.9 %collective-permute-start.33 = (bf16[4,4,128,1024]{3,2,1,0:T(8,128)(2,1)}, bf16[4,4,128,1024]{3,2,1,0:T(8,128)(2,1)}, u32[]{:S(2)}, u32[]{:S(2)}) collective-permute-start(bf16[4,4,128,1024]{3,2,1,0:T(8,128)(2,1)} %cross_grad_send.1), channel_id=1, source_target_pairs={{0,4},{4,0},{8,12},{12,8},{16,20},{20,16},{24,28},{28,24},{1,5},{5... | collective-permute-start | bytes 12582920 | tf_op jit(solution)/shard_map/ppermute | solution.py:34
  568.7 11.1 %collective-permute-start.49 = (f32[17920]{0:T(1024)S(1)}, f32[17920]{0:T(1024)S(1)}, u32[]{:S(2)}, u32[]{:S(2)}) collective-permute-start(f32[17920]{0:T(1024)S(1)} %add.166), channel_id=1, source_target_pairs={{0,8},{4,12},{8,0},{12,4},{16,24},{20,28},{24,16},{28,20},{1,9},{5... | collective-permute-start | bytes 215048 | tf_op jit(solution)/shard_map/ppermute | solution.py:34
  584.3 23.1 %collective-permute-start.24 = (bf16[128,1024]{1,0:T(8,128)(2,1)S(1)}, bf16[128,1024]{1,0:T(8,128)(2,1)S(1)}, u32[]{:S(2)}, u32[]{:S(2)}) collective-permute-start(bf16[128,1024]{1,0:T(8,128)(2,1)S(1)} %get-tuple-element.109), channel_id=1, source_target_pairs={{1,0},{2,1},{3,2},{5,4},{6,5},{7,6},{9,8},{10,9},{11,10},{13,12},{... | collective-permute-start | bytes 786440 | tf_op jit(solution)/shard_map/ppermute | solution.py:1030
  616.0 52.4 %collective-permute-start.25 = (bf16[128,1024]{1,0:T(8,128)(2,1)S(1)}, bf16[128,1024]{1,0:T(8,128)(2,1)S(1)}, u32[]{:S(2)}, u32[]{:S(2)}) collective-permute-start(bf16[128,1024]{1,0:T(8,128)(2,1)S(1)} %get-tuple-element.110), channel_id=1, source_target_pairs={{2,0},{3,1},{6,4},{7,5},{10,8},{11,9},{14,12},{15,13},{18,16},{19,... | collective-permute-start | bytes 786440 | tf_op jit(solution)/shard_map/ppermute | solution.py:1029
  678.9 26.1 %collective-permute-start.26 = (bf16[512,1024]{1,0:T(8,128)(2,1)S(1)}, bf16[512,1024]{1,0:T(8,128)(2,1)S(1)}, u32[]{:S(2)}, u32[]{:S(2)}) collective-permute-start(bf16[512,1024]{1,0:T(8,128)(2,1)S(1)} %slice.313), channel_id=1, source_target_pairs={{0,2},{1,3},{2,0},{3,1},{4,6},{5,7},{6,4},{7,5},{8,10},{9,11},{10,... | collective-permute-start | bytes 3145736 | tf_op jit(solution)/shard_map/ppermute | solution.py:34
  699.9 58.8 %collective-permute-start.44 = (bf16[2,2,2,128,1024]{4,3,2,1,0:T(8,128)(2,1)}, bf16[2,2,2,128,1024]{4,3,2,1,0:T(8,128)(2,1)}, u32[]{:S(2)}, u32[]{:S(2)}) collective-permute-start(bf16[2,2,2,128,1024]{4,3,2,1,0:T(8,128)(2,1)} %slice_bitcast_fusion), channel_id=1, source_target_pairs={{0,16},{4,20},{8,24},{12,28},{16,0},{20,4},{24,8},{28,12},{1,17},{... | collective-permute-start | bytes 6291464 | tf_op jit(solution)/shard_map/ppermute | solution.py:34
  706.2 44.0 %collective-permute-start.27 = (bf16[256,1024]{1,0:T(8,128)(2,1)}, bf16[256,1024]{1,0:T(8,128)(2,1)}, u32[]{:S(2)}, u32[]{:S(2)}) collective-permute-start(bf16[256,1024]{1,0:T(8,128)(2,1)} %slice.315), channel_id=1, source_target_pairs={{0,1},{1,0},{2,3},{3,2},{4,5},{5,4},{6,7},{7,6},{8,9},{9,8},{10,11... | collective-permute-start | bytes 1572872 | tf_op jit(solution)/shard_map/ppermute | solution.py:34
  718.1 48.9 %collective-permute-start.39 = (bf16[2,2,2,128,1024]{4,3,2,1,0:T(8,128)(2,1)}, bf16[2,2,2,128,1024]{4,3,2,1,0:T(8,128)(2,1)}, u32[]{:S(2)}, u32[]{:S(2)}) collective-permute-start(bf16[2,2,2,128,1024]{4,3,2,1,0:T(8,128)(2,1)} %bitcast.62), channel_id=1, source_target_pairs={{0,8},{4,12},{8,0},{12,4},{16,24},{20,28},{24,16},{28,20},{1,9},{5... | collective-permute-start | bytes 6291464 | tf_op jit(solution)/shard_map/ppermute | solution.py:34
  731.2 62.6 %collective-permute-start.34 = (bf16[2,2,2,128,1024]{4,3,2,1,0:T(8,128)(2,1)}, bf16[2,2,2,128,1024]{4,3,2,1,0:T(8,128)(2,1)}, u32[]{:S(2)}, u32[]{:S(2)}) collective-permute-start(bf16[2,2,2,128,1024]{4,3,2,1,0:T(8,128)(2,1)} %slice_bitcast_fusion.2), channel_id=1, source_target_pairs={{0,16},{4,20},{8,24},{12,28},{16,0},{20,4},{24,8},{28,12},{1,17},{... | collective-permute-start | bytes 6291464 | tf_op jit(solution)/shard_map/ppermute | solution.py:34
  745.5 72.0 %collective-permute-start.29 = (bf16[2,2,2,128,1152]{4,3,2,1,0:T(8,128)(2,1)}, bf16[2,2,2,128,1152]{4,3,2,1,0:T(8,128)(2,1)}, u32[]{:S(2)}, u32[]{:S(2)}) collective-permute-start(bf16[2,2,2,128,1152]{4,3,2,1,0:T(8,128)(2,1)} %bitcast.44), channel_id=1, source_target_pairs={{0,8},{4,12},{8,0},{12,4},{16,24},{20,28},{24,16},{28,20},{1,9},{5... | collective-permute-start | bytes 7077896 | tf_op jit(solution)/shard_map/ppermute | solution.py:34
  762.0 77.8 %collective-permute-start.45 = (bf16[2,2,128,1024]{3,2,1,0:T(8,128)(2,1)S(1)}, bf16[2,2,128,1024]{3,2,1,0:T(8,128)(2,1)S(1)}, u32[]{:S(2)}, u32[]{:S(2)}) collective-permute-start(bf16[2,2,128,1024]{3,2,1,0:T(8,128)(2,1)S(1)} %slice_bitcast_fusion.6), channel_id=1, source_target_pairs={{0,8},{4,12},{8,0},{12,4},{16,24},{20,28},{24,16},{28,20},{1,9},{5... | collective-permute-start | bytes 3145736 | tf_op jit(solution)/shard_map/ppermute | solution.py:34
  769.8 93.7 %collective-permute-start.40 = (bf16[2,2,128,1024]{3,2,1,0:T(8,128)(2,1)S(1)}, bf16[2,2,128,1024]{3,2,1,0:T(8,128)(2,1)S(1)}, u32[]{:S(2)}, u32[]{:S(2)}) collective-permute-start(bf16[2,2,128,1024]{3,2,1,0:T(8,128)(2,1)S(1)} %slice_bitcast_fusion.8), channel_id=1, source_target_pairs={{0,16},{4,20},{8,24},{12,28},{16,0},{20,4},{24,8},{28,12},{1,17},{... | collective-permute-start | bytes 3145736 | tf_op jit(solution)/shard_map/ppermute | solution.py:34
  796.4 64.2 %collective-permute-start.35 = (bf16[2,2,128,1024]{3,2,1,0:T(8,128)(2,1)S(1)}, bf16[2,2,128,1024]{3,2,1,0:T(8,128)(2,1)S(1)}, u32[]{:S(2)}, u32[]{:S(2)}) collective-permute-start(bf16[2,2,128,1024]{3,2,1,0:T(8,128)(2,1)S(1)} %slice_bitcast_fusion.10), channel_id=1, source_target_pairs={{0,8},{4,12},{8,0},{12,4},{16,24},{20,28},{24,16},{28,20},{1,9},{5... | collective-permute-start | bytes 3145736 | tf_op jit(solution)/shard_map/ppermute | solution.py:34
  820.1 88.1 %collective-permute-start.30 = (bf16[2,2,128,1152]{3,2,1,0:T(8,128)(2,1)S(1)}, bf16[2,2,128,1152]{3,2,1,0:T(8,128)(2,1)S(1)}, u32[]{:S(2)}, u32[]{:S(2)}) collective-permute-start(bf16[2,2,128,1152]{3,2,1,0:T(8,128)(2,1)S(1)} %slice_bitcast_fusion.4), channel_id=1, source_target_pairs={{0,16},{4,20},{8,24},{12,28},{16,0},{20,4},{24,8},{28,12},{1,17},{... | collective-permute-start | bytes 3538952 | tf_op jit(solution)/shard_map/ppermute | solution.py:34
  840.3 24.2 %collective-permute-start.46 = (bf16[2,128,1024]{2,1,0:T(8,128)(2,1)S(1)}, bf16[2,128,1024]{2,1,0:T(8,128)(2,1)S(1)}, u32[]{:S(2)}, u32[]{:S(2)}) collective-permute-start(bf16[2,128,1024]{2,1,0:T(8,128)(2,1)S(1)} %slice_bitcast_fusion.14), channel_id=1, source_target_pairs={{0,2},{1,3},{2,0},{3,1},{4,6},{5,7},{6,4},{7,5},{8,10},{9,11},{10,... | collective-permute-start | bytes 1572872 | tf_op jit(solution)/shard_map/ppermute | solution.py:34
  861.0 36.6 %collective-permute-start.36 = (bf16[2,128,1024]{2,1,0:T(8,128)(2,1)S(1)}, bf16[2,128,1024]{2,1,0:T(8,128)(2,1)S(1)}, u32[]{:S(2)}, u32[]{:S(2)}) collective-permute-start(bf16[2,128,1024]{2,1,0:T(8,128)(2,1)S(1)} %slice_bitcast_fusion.18), channel_id=1, source_target_pairs={{0,2},{1,3},{2,0},{3,1},{4,6},{5,7},{6,4},{7,5},{8,10},{9,11},{10,... | collective-permute-start | bytes 1572872 | tf_op jit(solution)/shard_map/ppermute | solution.py:34
  863.9 44.1 %collective-permute-start.41 = (bf16[2,128,1024]{2,1,0:T(8,128)(2,1)S(1)}, bf16[2,128,1024]{2,1,0:T(8,128)(2,1)S(1)}, u32[]{:S(2)}, u32[]{:S(2)}) collective-permute-start(bf16[2,128,1024]{2,1,0:T(8,128)(2,1)S(1)} %slice_bitcast_fusion.16), channel_id=1, source_target_pairs={{0,2},{1,3},{2,0},{3,1},{4,6},{5,7},{6,4},{7,5},{8,10},{9,11},{10,... | collective-permute-start | bytes 1572872 | tf_op jit(solution)/shard_map/ppermute | solution.py:34
  864.8 48.0 %collective-permute-start.47 = (bf16[128,1024]{1,0:T(8,128)(2,1)S(1)}, bf16[128,1024]{1,0:T(8,128)(2,1)S(1)}, u32[]{:S(2)}, u32[]{:S(2)}) collective-permute-start(bf16[128,1024]{1,0:T(8,128)(2,1)S(1)} %slice_bitcast_fusion.22), channel_id=1, source_target_pairs={{0,1},{1,0},{2,3},{3,2},{4,5},{5,4},{6,7},{7,6},{8,9},{9,8},{10,11... | collective-permute-start | bytes 786440 | tf_op jit(solution)/shard_map/ppermute | solution.py:34
  897.9 16.9 %collective-permute-start.37 = (bf16[128,1024]{1,0:T(8,128)(2,1)S(1)}, bf16[128,1024]{1,0:T(8,128)(2,1)S(1)}, u32[]{:S(2)}, u32[]{:S(2)}) collective-permute-start(bf16[128,1024]{1,0:T(8,128)(2,1)S(1)} %slice_bitcast_fusion.26), channel_id=1, source_target_pairs={{0,1},{1,0},{2,3},{3,2},{4,5},{5,4},{6,7},{7,6},{8,9},{9,8},{10,11... | collective-permute-start | bytes 786440 | tf_op jit(solution)/shard_map/ppermute | solution.py:34
  908.5 27.9 %collective-permute-start.31 = (bf16[2,128,1152]{2,1,0:T(8,128)(2,1)S(1)}, bf16[2,128,1152]{2,1,0:T(8,128)(2,1)S(1)}, u32[]{:S(2)}, u32[]{:S(2)}) collective-permute-start(bf16[2,128,1152]{2,1,0:T(8,128)(2,1)S(1)} %slice_bitcast_fusion.12), channel_id=1, source_target_pairs={{0,2},{1,3},{2,0},{3,1},{4,6},{5,7},{6,4},{7,5},{8,10},{9,11},{10,... | collective-permute-start | bytes 1769480 | tf_op jit(solution)/shard_map/ppermute | solution.py:34
  909.3 29.7 %collective-permute-start.42 = (bf16[128,1024]{1,0:T(8,128)(2,1)}, bf16[128,1024]{1,0:T(8,128)(2,1)}, u32[]{:S(2)}, u32[]{:S(2)}) collective-permute-start(bf16[128,1024]{1,0:T(8,128)(2,1)} %slice_bitcast_fusion.24), channel_id=1, source_target_pairs={{0,1},{1,0},{2,3},{3,2},{4,5},{5,4},{6,7},{7,6},{8,9},{9,8},{10,11... | collective-permute-start | bytes 786440 | tf_op jit(solution)/shard_map/ppermute | solution.py:34
  (48 other events, 1109.4 us)
Sparse Core Ops, SparseCore 0:
  566.7 102.5 all-gather.1

commit v2 on v1

--- a/solution.py
+++ b/solution.py
@@ -4,6 +4,7 @@
 import jax.numpy as jnp
 from jax import lax
 from jax.experimental import pallas as pl
+from jax.experimental.layout import Layout, with_layout_constraint
 from jax.experimental.pallas import tpu as pltpu
 from jax.sharding import PartitionSpec as P
 
@@ -38,36 +39,101 @@
     return (lax.axis_size(axis) - 1).bit_length()
 
 
-def gather_pieces(shard, batch_order):
-    nb, nz = bits_of("batch"), bits_of("head")
-    blk, cols = shard.shape
-    buf = shard.reshape((1,) * (nb + nz) + (blk, cols))
-    for bit in range(nz):
-        axis = nb + nz - 1 - bit
-        buf = jnp.concatenate([buf, swap(buf, "head", 1 << bit)], axis)
-    for bit in batch_order:
-        buf = jnp.concatenate([buf, swap(buf, "batch", 1 << bit)], bit)
-    last = swap(buf, "batch", 1)
-    shape = (1 << (nb - 1), 1 << nz, blk, cols)
-    return (buf.reshape(shape), last.reshape(shape))
-
-
-def scatter_pieces(kept, batch_order):
-    nb, nz = bits_of("batch"), bits_of("head")
-    blk, cols = kept.shape[2:]
-    buf = kept.reshape((2,) * (nb - 1 + nz) + (blk, cols))
-    live = list(batch_order)
-    axes = sorted(live)
-    steps = [("batch", bit) for bit in live] + [("head", bit) for bit in reversed(range(nz))]
-    names = [("batch", bit) for bit in axes] + [("head", bit) for bit in reversed(range(nz))]
-    for number, (axis_name, bit) in enumerate(steps):
-        axis = names.index((axis_name, bit))
-        names.pop(axis)
-        mine = lax.index_in_dim(buf, 0, axis, keepdims=False)
-        theirs = lax.index_in_dim(buf, 1, axis, keepdims=False)
-        total = mine.astype(F32) + swap(theirs, axis_name, 1 << bit).astype(F32)
-        buf = total if number == len(steps) - 1 else total.astype(BF)
-    return buf.reshape(blk, cols)
+def after(value, *earlier):
+    return lax.optimization_barrier((value,) + earlier)[0]
+
+
+def pin(value):
+    return with_layout_constraint(value, Layout(tuple(range(value.ndim))))
+
+
+class Line:
+    def __init__(self):
+        self.last = ()
+
+    def tie(self, value):
+        return after(value, *self.last) if self.last else value
+
+    def mark(self, *values):
+        self.last = values
+        return values[0]
+
+
+class Gather:
+    def __init__(self, line, shard):
+        self.line = line
+        self.nb, self.nz = bits_of("batch"), bits_of("head")
+        self.buf = pin(shard).reshape((1,) * (self.nb + self.nz) + shard.shape)
+
+    def send(self, axis_name, bit):
+        self.axis = self.nb + self.nz - 1 - bit if axis_name == "head" else bit
+        self.came = swap(self.line.tie(self.buf), axis_name, 1 << bit)
+
+    def take(self):
+        mine = self.line.tie(self.buf)
+        self.buf = self.line.mark(jnp.concatenate([mine, self.came], self.axis))
+
+    def columns(self, first, count):
+        part = Gather.__new__(Gather)
+        part.line, part.nb, part.nz = self.line, self.nb, self.nz
+        part.buf = pin(self.buf[..., first : first + count])
+        return part
+
+    def close(self):
+        shape = (1 << (self.nb - 1), 1 << self.nz) + self.buf.shape[-2:]
+        return (self.buf.reshape(shape), self.came.reshape(shape))
+
+
+class Scatter:
+    def __init__(self, line, parts, orders):
+        nb, self.nz = bits_of("batch"), bits_of("head")
+        self.line = line
+        self.groups = parts[0][1].shape[1]
+        self.blk = parts[0][1].shape[2]
+        self.left = [list(order) for order in orders]
+        self.names = [sorted(order) for order in orders]
+        self.heads = list(range(self.nz))
+        self.mine, self.came = [None] * len(parts), [None] * len(parts)
+        for number, (theirs, mine) in enumerate(parts):
+            self.send(number, theirs, mine)
+
+    def send(self, number, theirs, mine):
+        bit = self.left[number].pop(0)
+        self.names[number].remove(bit)
+        self.mine[number] = mine
+        self.came[number] = swap(theirs, "batch", 1 << bit)
+
+    def step(self):
+        tied = [self.line.tie(mine) for mine in self.mine]
+        came = [after(came, mine) for came, mine in zip(self.came, tied)]
+        if self.left[0]:
+            halves = []
+            for number, (old, new) in enumerate(zip(tied, came)):
+                inner = (2,) * len(self.names[number]) + (self.groups, self.blk, old.shape[-1])
+                axis = self.names[number].index(self.left[number][0])
+
+                def added(side):
+                    one = lax.index_in_dim(old.reshape(inner), side, axis, keepdims=False)
+                    two = lax.index_in_dim(new.reshape(inner), side, axis, keepdims=False)
+                    total = (one.astype(F32) + two.astype(F32)).astype(BF)
+                    return pin(total.reshape(-1, self.groups, self.blk, old.shape[-1]))
+
+                halves.append((added(1), added(0)))
+            self.line.mark(*[half for pair in halves for half in pair])
+            for number, (theirs, mine) in enumerate(halves):
+                self.send(number, theirs, mine)
+            return
+        sums = [one.astype(F32) + two.astype(F32) for one, two in zip(tied, came)]
+        total = sums[0] if len(sums) == 1 else jnp.concatenate(sums, -1)
+        if not self.heads:
+            self.total = self.line.mark(pin(total.reshape(self.blk, -1)))
+            return
+        bit = self.heads.pop(0)
+        total = total.astype(BF).reshape((-1, 2, self.blk, total.shape[-1]))
+        theirs, mine = pin(total[:, 1]), pin(total[:, 0])
+        self.line.mark(theirs, mine)
+        self.mine = [mine]
+        self.came = [swap(theirs, "head", 1 << bit)]
 
 
 def bit_reverse(number, width):
@@ -85,16 +151,18 @@
         return jnp.take(array_in.reshape(rows, count, blk), table, axis=1).reshape(rows, features)
 
     def body(table_ref, in_ref, out_ref):
-        out_ref[...] = in_ref[...]
+        for p in range(count):
+            start = pl.multiple_of(table_ref[p] * blk, blk)
+            out_ref[:, p * blk : (p + 1) * blk] = in_ref[:, pl.ds(start, blk)]
 
     return pl.pallas_call(
         body,
         out_shape=jax.ShapeDtypeStruct(array_in.shape, array_in.dtype),
         grid_spec=pltpu.PrefetchScalarGridSpec(
             num_scalar_prefetch=1,
-            grid=(count,),
-            in_specs=[pl.BlockSpec((rows, blk), lambda p, table_ref: (0, table_ref[p]))],
-            out_specs=pl.BlockSpec((rows, blk), lambda p, table_ref: (0, p)),
+            grid=(1,),
+            in_specs=[pl.BlockSpec((rows, features), lambda p, table_ref: (0, 0))],
+            out_specs=pl.BlockSpec((rows, features), lambda p, table_ref: (0, 0)),
         ),
         name="reorder",
     )(table, array_in)
@@ -222,34 +290,58 @@
     )(left, *pieces, residual, vectors)
 
 
-def feed_forward(low, normed, up_pieces, down_pieces, up_bias, vectors, grad_out):
+def natural_from_exchange(order_ref, first, from_ref, to_ref, blk):
+    if blk % 128:
+        to_ref[...] = from_ref[...]
+        return
+    for p in range(from_ref.shape[1] // blk):
+        start = pl.multiple_of(order_ref[first + p] * blk, blk)
+        to_ref[:, pl.ds(start, blk)] = from_ref[:, p * blk : (p + 1) * blk]
+
+
+def exchange_from_natural(order_ref, first, from_ref, to_ref, blk):
+    if blk % 128:
+        to_ref[...] = from_ref[...]
+        return
+    for p in range(from_ref.shape[1] // blk):
+        start = pl.multiple_of(order_ref[first + p] * blk, blk)
+        to_ref[:, p * blk : (p + 1) * blk] = from_ref[:, pl.ds(start, blk)]
+
+
+def flat_natural(ref):
+    count, _, blk, cols = ref.shape
+    return ref[...].reshape(count * blk, cols)
+
+
+def feed_forward(order, low, normed, weights, up_bias, vectors, grad_out):
     rows, features = normed.shape
-    groups, cols = up_pieces[0].shape[1], up_pieces[0].shape[3]
-    count = len(up_pieces)
-
-    def body(low_ref, normed_ref, *refs):
-        ups, downs = refs[:count], refs[count : 2 * count]
-        bias_ref, vectors_ref, grad_ref = refs[2 * count : 2 * count + 3]
-        active_ref, slope_ref, out_ref, third_ref, third_low_ref, sums_ref, acc_ref = refs[
-            2 * count + 3 :
-        ]
+    batches, groups, blk, both = weights.shape
+    cols = both // 2
+
+    def body(
+        order_ref, low_ref, normed_ref, up_ref, down_ref, bias_ref, vectors_ref, grad_ref,
+        active_ref, slope_ref, out_ref, third_ref, third_low_ref, sums_ref,
+        natural_ref, acc_ref, turned_ref,
+    ):
         step = pl.program_id(0)
 
         @pl.when(step == 0)
         def _():
+            natural_from_exchange(order_ref, groups, low_ref, natural_ref, blk)
             acc_ref[...] = jnp.zeros_like(acc_ref)
 
-        upper = over_features(low_ref[...], ups) + bias_ref[...]
+        upper = dot(natural_ref[...], flat_natural(up_ref), 1, 0) + bias_ref[...]
         cdf = 0.5 * (1.0 + lax.erf(upper * 0.7071067811865476))
         active = (upper * cdf).astype(BF)
         slope = cdf + upper * jnp.exp(-0.5 * upper * upper) * 0.3989422804014327
         active_ref[...] = active
         slope_ref[...] = slope.astype(BF)
-        add_rows(acc_ref, active, downs)
+        acc_ref[...] += dot(active, flat_natural(down_ref), 1, 1)
 
         @pl.when(step == groups - 1)
         def _():
-            v = normed_ref[...] + (acc_ref[...] + vectors_ref[2:3])
+            exchange_from_natural(order_ref, groups, acc_ref, turned_ref, blk)
+            v = normed_ref[...] + (turned_ref[...] + vectors_ref[2:3])
             unit, spread = normalize(v)
             gain = vectors_ref[0:1]
             out_ref[...] = (unit * gain + vectors_ref[1:2]).astype(BF)
@@ -263,23 +355,32 @@
 
     return pl.pallas_call(
         body,
-        grid=(groups,),
-        in_specs=[whole((rows, features)), whole((rows, features))]
-        + piece_specs(up_pieces, cols, 0)
-        + piece_specs(down_pieces, cols, 0)
-        + [
-            pl.BlockSpec((1, cols), lambda j: (0, j)),
-            whole((3, features)),
-            whole((rows, features)),
-        ],
-        out_specs=[
-            pl.BlockSpec((rows, cols), lambda j: (0, j)),
-            pl.BlockSpec((rows, cols), lambda j: (0, j)),
-            whole((rows, features)),
-            whole((rows, features)),
-            whole((rows, features)),
-            whole((3, features)),
-        ],
+        grid_spec=pltpu.PrefetchScalarGridSpec(
+            num_scalar_prefetch=1,
+            grid=(groups,),
+            in_specs=[
+                whole((rows, features)),
+                whole((rows, features)),
+                pl.BlockSpec((batches, 1, blk, cols), lambda j, order: (0, j, 0, 0)),
+                pl.BlockSpec((batches, 1, blk, cols), lambda j, order: (0, j, 0, 1)),
+                pl.BlockSpec((1, cols), lambda j, order: (0, j)),
+                whole((3, features)),
+                whole((rows, features)),
+            ],
+            out_specs=[
+                pl.BlockSpec((rows, cols), lambda j, order: (0, j)),
+                pl.BlockSpec((rows, cols), lambda j, order: (0, j)),
+                whole((rows, features)),
+                whole((rows, features)),
+                whole((rows, features)),
+                whole((3, features)),
+            ],
+            scratch_shapes=[
+                pltpu.VMEM((rows, features), BF),
+                pltpu.VMEM((rows, features), F32),
+                pltpu.VMEM((rows, features), F32),
+            ],
+        ),
         out_shape=[
             jax.ShapeDtypeStruct((rows, groups * cols), BF),
             jax.ShapeDtypeStruct((rows, groups * cols), BF),
@@ -288,10 +389,9 @@
             jax.ShapeDtypeStruct((rows, features), BF),
             jax.ShapeDtypeStruct((3, features), F32),
         ],
-        scratch_shapes=[pltpu.VMEM((rows, features), F32)],
         compiler_params=params(),
         name="feed_forward",
-    )(low, normed, *up_pieces, *down_pieces, up_bias, vectors, grad_out)
+    )(order, low, normed, weights, weights, up_bias, vectors, grad_out)
 
 
 def norm_back_outputs(upstream, unit, spread, gain, grad_ref, grad_low_ref, sums_ref):
@@ -303,31 +403,35 @@
     sums_ref[2:3] = column_sum(grad)
 
 
-def feed_forward_back(third_low, third, slope, up_pieces, down_pieces, unit, spread, gain):
+def feed_forward_back(order, third_low, third, slope, weights, unit, spread, gain):
     rows, features = third.shape
-    groups, cols = up_pieces[0].shape[1], up_pieces[0].shape[3]
-    count = len(up_pieces)
-
-    def body(third_low_ref, third_ref, slope_ref, *refs):
-        ups, downs = refs[:count], refs[count : 2 * count]
-        unit_ref, spread_ref, gain_ref = refs[2 * count : 2 * count + 3]
-        upper_ref, bias_ref, grad_ref, grad_low_ref, sums_ref, acc_ref = refs[2 * count + 3 :]
+    batches, groups, blk, both = weights.shape
+    cols = both // 2
+
+    def body(
+        order_ref, third_low_ref, third_ref, slope_ref, up_ref, down_ref, unit_ref, spread_ref, gain_ref,
+        upper_ref, bias_ref, grad_ref, grad_low_ref, sums_ref,
+        natural_ref, acc_ref, turned_ref,
+    ):
         step = pl.program_id(0)
 
         @pl.when(step == 0)
         def _():
+            natural_from_exchange(order_ref, groups, third_low_ref, natural_ref, blk)
             acc_ref[...] = jnp.zeros_like(acc_ref)
 
-        grad_upper = over_features(third_low_ref[...], downs) * slope_ref[...].astype(F32)
+        grad_upper = dot(natural_ref[...], flat_natural(down_ref), 1, 0)
+        grad_upper = grad_upper * slope_ref[...].astype(F32)
         bias_ref[...] = column_sum(grad_upper)
         low = grad_upper.astype(BF)
         upper_ref[...] = low
-        add_rows(acc_ref, low, ups)
+        acc_ref[...] += dot(low, flat_natural(up_ref), 1, 1)
 
         @pl.when(step == groups - 1)
         def _():
+            exchange_from_natural(order_ref, groups, acc_ref, turned_ref, blk)
             norm_back_outputs(
-                acc_ref[...] + third_ref[...],
+                turned_ref[...] + third_ref[...],
                 unit_ref[...],
                 spread_ref[...],
                 gain_ref[...],
@@ -338,22 +442,32 @@
 
     return pl.pallas_call(
         body,
-        grid=(groups,),
-        in_specs=[
-            whole((rows, features)),
-            whole((rows, features)),
-            pl.BlockSpec((rows, cols), lambda j: (0, j)),
-        ]
-        + piece_specs(up_pieces, cols, 0)
-        + piece_specs(down_pieces, cols, 0)
-        + [whole((rows, features)), whole((rows, 1)), whole((1, features))],
-        out_specs=[
-            pl.BlockSpec((rows, cols), lambda j: (0, j)),
-            pl.BlockSpec((1, cols), lambda j: (0, j)),
-            whole((rows, features)),
-            whole((rows, features)),
-            whole((3, features)),
-        ],
+        grid_spec=pltpu.PrefetchScalarGridSpec(
+            num_scalar_prefetch=1,
+            grid=(groups,),
+            in_specs=[
+                whole((rows, features)),
+                whole((rows, features)),
+                pl.BlockSpec((rows, cols), lambda j, order: (0, j)),
+                pl.BlockSpec((batches, 1, blk, cols), lambda j, order: (0, j, 0, 0)),
+                pl.BlockSpec((batches, 1, blk, cols), lambda j, order: (0, j, 0, 1)),
+                whole((rows, features)),
+                whole((rows, 1)),
+                whole((1, features)),
+            ],
+            out_specs=[
+                pl.BlockSpec((rows, cols), lambda j, order: (0, j)),
+                pl.BlockSpec((1, cols), lambda j, order: (0, j)),
+                whole((rows, features)),
+                whole((rows, features)),
+                whole((3, features)),
+            ],
+            scratch_shapes=[
+                pltpu.VMEM((rows, features), BF),
+                pltpu.VMEM((rows, features), F32),
+                pltpu.VMEM((rows, features), F32),
+            ],
+        ),
         out_shape=[
             jax.ShapeDtypeStruct((rows, groups * cols), BF),
             jax.ShapeDtypeStruct((1, groups * cols), F32),
@@ -361,10 +475,9 @@
             jax.ShapeDtypeStruct((rows, features), BF),
             jax.ShapeDtypeStruct((3, features), F32),
         ],
-        scratch_shapes=[pltpu.VMEM((rows, features), F32)],
         compiler_params=params(),
         name="feed_forward_back",
-    )(third_low, third, slope, *up_pieces, *down_pieces, unit, spread, gain)
+    )(order, third_low, third, slope, weights, weights, unit, spread, gain)
 
 
 def cross_query_back(grad_query, pieces, first_col, cols, second, unit, spread, gain):
@@ -449,7 +562,7 @@
     )(left, *pieces)
 
 
-def input_back(grad_query, grad_kv, grad_rel, pieces, first):
+def input_back(grad_query, grad_kv, grad_rel, pieces, others, first):
     rows, features = first.shape
     long_rows = grad_kv.shape[0]
     halo = long_rows - rows
@@ -489,8 +602,8 @@
         ]
         + piece_specs(pieces, width, 0)
         + piece_specs(pieces, width, 1)
-        + piece_specs(pieces, width, 2)
-        + piece_specs(pieces, rel_width, 3 * width // rel_width)
+        + piece_specs(others, width, 0)
+        + piece_specs(others, rel_width, width // rel_width)
         + [whole((rows, features))],
         out_specs=[whole((halo, features)), whole((rows, features))],
         out_shape=[
@@ -500,29 +613,48 @@
         scratch_shapes=[pltpu.VMEM((long_rows, features), F32)],
         compiler_params=params(),
         name="input_back",
-    )(grad_query, grad_kv, grad_rel, *pieces, *pieces, *pieces, *pieces, first)
-
-
-def weight_products(entries, half, extra, pieces, groups, name):
+    )(grad_query, grad_kv, grad_rel, *pieces, *pieces, *others, *others, first)
+
+
+def weight_products(entries, half, extra, parts, pieces, groups, name):
     features = entries[0][0].shape[1]
     depth = features // 2
     blk = depth // pieces
     widths = [right.shape[1] // groups for _, right in entries]
     total = sum(widths)
     count = len(entries)
+    outs = []
+    if parts is None:
+        outs.append((0, total, list(range(pieces))))
+    else:
+        at = 0
+        for width, bit in parts:
+            for side in (1, 0):
+                outs.append((at, width, [p for p in range(pieces) if (p >> bit & 1) == side]))
+            at += width
 
     def body(*refs):
         lefts, rights = refs[:count], refs[count : 2 * count]
-        out_ref = refs[-1]
+        out_refs = refs[len(refs) - len(outs) :]
         at = 0
         for left_ref, right_ref, width in zip(lefts, rights, widths):
-            term = dot(left_ref[...], right_ref[...], 0, 0).reshape(pieces, 1, blk, width)
+            term = dot(left_ref[...], right_ref[...], 0, 0).reshape(pieces, blk, width)
             if extra is not None:
-                term = term + refs[2 * count][:, :, :, at : at + width].astype(F32)
-            out_ref[:, :, :, at : at + width] = term.astype(BF)
+                term = term + refs[2 * count][:, 0, :, at : at + width].astype(F32)
+            term = term.astype(BF)
+            for out_ref, (first, size, members) in zip(out_refs, outs):
+                low, high = max(at, first), min(at + width, first + size)
+                if low >= high:
+                    continue
+                for place, piece in enumerate(members):
+                    out_ref[place, 0, :, low - first : high - first] = term[
+                        piece, :, low - at : high - at
+                    ]
             at += width
 
-    out_spec = pl.BlockSpec((pieces, 1, blk, total), lambda j: (0, j, 0, 0))
+    def block(number, width):
+        return pl.BlockSpec((number, 1, blk, width), lambda j: (0, j, 0, 0))
+
     in_specs = [pl.BlockSpec((left.shape[0], depth), lambda j: (0, half)) for left, _ in entries]
     in_specs += [
         pl.BlockSpec((right.shape[0], width), lambda j: (0, j))
@@ -530,26 +662,20 @@
     ]
     operands = [left for left, _ in entries] + [right for _, right in entries]
     if extra is not None:
-        in_specs.append(out_spec)
+        in_specs.append(block(pieces, total))
         operands.append(extra)
     return pl.pallas_call(
         body,
         grid=(groups,),
         in_specs=in_specs,
-        out_specs=out_spec,
-        out_shape=jax.ShapeDtypeStruct((pieces, groups, blk, total), BF),
+        out_specs=[block(len(members), width) for _, width, members in outs],
+        out_shape=[
+            jax.ShapeDtypeStruct((len(members), groups, blk, width), BF)
+            for _, width, members in outs
+        ],
         compiler_params=params(),
         name=name,
     )(*operands)
-
-
-def weight_gradient(entries, batch_order, name):
-    groups = lax.axis_size("head")
-    pieces = lax.axis_size("batch") // 2
-    sent = weight_products(entries, 1, None, pieces, groups, name + "_send")
-    came = swap(sent, "batch", 1)
-    kept = weight_products(entries, 0, came, pieces, groups, name + "_keep")
-    return scatter_pieces(kept, batch_order)
 
 
 def half_masks(rows):
@@ -569,10 +695,11 @@
     return jnp.concatenate(parts, 0)
 
 
-def self_attention(qkv, relpos, mask, turned, share):
+def self_attention(qk, values, relpos, mask, turned, share):
     rows, window = 3 * share, 3 * share
-    groups = qkv.shape[1] // 768
-    halo = qkv.shape[0] - rows
+    groups = values.shape[1] // 256
+    long_rows = qk.shape[0]
+    halo = long_rows - rows
 
     def body(q_ref, k_ref, v_ref, rel_ref, mask_ref, turned_ref, ctx_ref, probs_ref, own_ref):
         halves = half_masks(rows)
@@ -612,14 +739,13 @@
             ctx_ref[:, cols] = mixed.astype(BF)
         own_ref[...] = own_all
 
-    long_rows = qkv.shape[0]
     return pl.pallas_call(
         body,
         grid=(groups,),
         in_specs=[
-            pl.BlockSpec((long_rows, 256), lambda j: (0, 3 * j)),
-            pl.BlockSpec((long_rows, 256), lambda j: (0, 3 * j + 1)),
-            pl.BlockSpec((long_rows, 256), lambda j: (0, 3 * j + 2)),
+            pl.BlockSpec((long_rows, 256), lambda j: (0, 2 * j)),
+            pl.BlockSpec((long_rows, 256), lambda j: (0, 2 * j + 1)),
+            pl.BlockSpec((long_rows, 256), lambda j: (0, j)),
             pl.BlockSpec((rows, 128), lambda j: (0, j)),
             whole((rows, window)),
             whole((1, window)),
@@ -636,14 +762,14 @@
         ],
         compiler_params=params(),
         name="self_attention",
-    )(qkv, qkv, qkv, relpos, mask, turned)
-
-
-def self_attention_back(qkv, probs, own_probs, grad_ctx, straight, share):
+    )(qk, qk, values, relpos, mask, turned)
+
+
+def self_attention_back(qk, values, probs, own_probs, grad_ctx, straight, share):
     rows, window = 3 * share, 3 * share
-    groups = qkv.shape[1] // 768
-    halo = qkv.shape[0] - rows
-    long_rows = qkv.shape[0]
+    groups = values.shape[1] // 256
+    long_rows = qk.shape[0]
+    halo = long_rows - rows
 
     def body(
         q_ref, k_ref, v_ref, probs_ref, own_ref, grad_ref, straight_ref,
@@ -719,9 +845,9 @@
         body,
         grid=(groups,),
         in_specs=[
-            pl.BlockSpec((long_rows, 256), lambda j: (0, 3 * j)),
-            pl.BlockSpec((long_rows, 256), lambda j: (0, 3 * j + 1)),
-            pl.BlockSpec((long_rows, 256), lambda j: (0, 3 * j + 2)),
+            pl.BlockSpec((long_rows, 256), lambda j: (0, 2 * j)),
+            pl.BlockSpec((long_rows, 256), lambda j: (0, 2 * j + 1)),
+            pl.BlockSpec((long_rows, 256), lambda j: (0, j)),
             pl.BlockSpec((4, rows, window), lambda j: (j, 0, 0)),
             pl.BlockSpec((rows, 128), lambda j: (0, j)),
             pl.BlockSpec((rows, 256), lambda j: (0, j)),
@@ -743,7 +869,7 @@
         ],
         compiler_params=params(),
         name="self_attention_back",
-    )(qkv, qkv, qkv, probs, own_probs, grad_ctx, straight)
+    )(qk, qk, values, probs, own_probs, grad_ctx, straight)
 
 
 def cross_attention(queries, kv):
@@ -894,58 +1020,51 @@
         blocks = stack.reshape(count, batches, features // batches)
         return jnp.take(blocks, to_exchange, axis=1).reshape(count, features)
 
-    def by_group(vector):
-        return jnp.take(vector.reshape(groups, -1), group_order, axis=0)
-
     blk = self_weight.shape[0]
-    weights_self = gather_pieces(
-        jnp.concatenate([self_weight.reshape(blk, -1), relpos_weight], 1).astype(BF), near
-    )
-    weights_cross = gather_pieces(
-        jnp.concatenate(
-            [selfout_weight, crossq_weight, crosskv_weight.reshape(blk, -1), crossout_weight], 1
-        ).astype(BF),
-        far,
-    )
-    weights_up = gather_pieces(up_weight.astype(BF), near)
-    weights_down = gather_pieces(down_weight.astype(BF), far)
-
-    own = jnp.transpose(hidden[0], (1, 0, 2)).reshape(rows, features)
-    own = reorder_blocks(own, to_exchange)
-    main = own[0:share]
+    line = Line()
+    self_shard = jnp.concatenate([self_weight.reshape(blk, -1), relpos_weight], 1).astype(BF)
+    gather_self = Gather(line, line.mark(pin(self_shard)))
+    gather_self.send("head", 1)
+
+    columns = jnp.concatenate(
+        [
+            self_bias[0].reshape(groups, -1),
+            self_bias[1].reshape(groups, -1),
+            cross_bias[0].reshape(groups, -1),
+            cross_bias[1].reshape(groups, -1),
+            relpos_bias.reshape(groups, -1),
+            up_bias.reshape(groups, -1),
+        ],
+        1,
+    )
+    columns = jnp.take(columns, group_order, axis=0)
+    query_bias, value_bias = columns[:, 0:256], columns[:, 256:512]
+    cross_query_bias, cross_value_bias = columns[:, 512:768], columns[:, 768:1024]
+    rel_row = columns[:, 1024:1152].reshape(1, -1)
+    up_row = columns[:, 1152:].reshape(1, -1)
+
+    memory_own = line.mark(reorder_blocks(line.tie(memory[0]), to_exchange))
+    ffn_shard = jnp.concatenate([up_weight, down_weight], 1).astype(BF)
+    own = jnp.transpose(line.tie(hidden[0]), (1, 0, 2)).reshape(rows, features)
+    own = line.mark(reorder_blocks(own, to_exchange))
+    upstream = lax.dynamic_slice_in_dim(line.tie(grad_out[0]), z * share, share, 0)
+    upstream = jnp.transpose(upstream, (1, 0, 2)).reshape(rows, features)
+    upstream = line.mark(reorder_blocks(upstream, to_exchange))
     chain = list(range(groups))
-    before_one = lax.ppermute(main, "head", [(i, i + 1) for i in chain[:-1]])
-    before_two = lax.ppermute(main, "head", [(i, i + 2) for i in chain[:-2]])
-    extended = jnp.concatenate([before_two, before_one, own], 0)
-    memory_all = reorder_blocks(memory[0], to_exchange)
-    memory_all = jnp.concatenate([memory_all, swap(memory_all, "head", 1)], 0)
-    memory_all = jnp.concatenate([memory_all, swap(memory_all, "head", 2)], 0)
-    upstream = lax.dynamic_slice_in_dim(grad_out[0], z * share, share, 0)
-    upstream = jnp.transpose(upstream, (1, 0, 2)).reshape(rows, features)
-    upstream = reorder_blocks(upstream, to_exchange)
 
     vectors = small_features(jnp.concatenate([norm_gain, norm_bias, out_bias], 0))
     vectors = vectors.reshape(3, 3, features).transpose(1, 0, 2)
-    ones = jnp.ones((groups, 256), F32)
     none = jnp.zeros((groups, 256), F32)
-    query_bias, value_bias = by_group(self_bias[0]), by_group(self_bias[1])
-    qkv_affine = jnp.stack(
-        [
-            jnp.concatenate([query_bias, none, value_bias], 1).reshape(-1),
-            jnp.concatenate([0.125 * ones, ones, ones], 1).reshape(-1),
-        ]
-    )
-    rel_affine = jnp.stack([by_group(relpos_bias).reshape(-1), jnp.ones((groups * 128,), F32)])
-    cross_query_affine = jnp.stack(
-        [by_group(cross_bias[0]).reshape(-1), jnp.full((groups * 256,), 0.125, F32)]
-    )
-    cross_kv_affine = jnp.stack(
-        [
-            jnp.concatenate([none, by_group(cross_bias[1])], 1).reshape(-1),
-            jnp.ones((groups * 512,), F32),
-        ]
-    )
-    up_row = by_group(up_bias).reshape(1, -1)
+
+    def affine(bias, scale):
+        return jnp.stack([bias, jnp.full(bias.shape, scale, F32)])
+
+    scales = jnp.concatenate([none + 0.125, none + 1.0], 1).reshape(-1)
+    qk_affine = jnp.stack([jnp.concatenate([query_bias, none], 1).reshape(-1), scales])
+    value_affine = affine(value_bias.reshape(-1), 1.0)
+    rel_affine = affine(rel_row[0], 1.0)
+    cross_query_affine = affine(cross_query_bias.reshape(-1), 0.125)
+    cross_kv_affine = affine(jnp.concatenate([none, cross_value_bias], 1).reshape(-1), 1.0)
 
     places = lax.iota(jnp.int32, length)
     doc_ends = jnp.cumsum(lengths[0])
@@ -968,97 +1087,229 @@
     straight = buckets[0:window]
     turned = straight[::-1]
 
-    qkv = project(extended, weights_self, 0, 768, 256, qkv_affine, BF, "self_qkv")
-    relpos = project(own, weights_self, 768, 128, 128, rel_affine, F32, "self_rel")
-    context, self_probs, self_own = self_attention(qkv, relpos, mask, turned.reshape(1, -1), share)
+    mask = line.mark(line.tie(mask))
+    assert nb >= 2 and bits_of("head") == 2
+    gather_cross = Gather(
+        line,
+        jnp.concatenate(
+            [selfout_weight, crossq_weight, crosskv_weight.reshape(blk, -1), crossout_weight], 1
+        ).astype(BF),
+    )
+    gather_self.take()
+    gather_self.send("head", 0)
+    gather_cross.send("head", 1)
+    gather_self.take()
+    parts_self = [gather_self.columns(0, 512), gather_self.columns(512, 384)]
+    orders_self = [near, far]
+    for part, part_order in zip(parts_self, orders_self):
+        part.send("batch", part_order[0])
+    main = line.tie(own[0:share])
+    before_one = lax.ppermute(main, "head", [(i, i + 1) for i in chain[:-1]])
+    before_two = lax.ppermute(main, "head", [(i, i + 2) for i in chain[:-2]])
+    gather_cross.take()
+    gather_cross.send("head", 0)
+    for number in range(1, nb - 1):
+        for part, part_order in zip(parts_self, orders_self):
+            part.take()
+            part.send("batch", part_order[number])
+    extended = line.mark(jnp.concatenate([before_two, before_one, line.tie(own)], 0))
+    gather_cross.take()
+    parts_cross = [gather_cross.columns(0, 512), gather_cross.columns(512, 768)]
+    orders_cross = [far, near]
+    gather_ffn = Gather(line, ffn_shard)
+    gather_ffn.send("head", 1)
+    for part in parts_self:
+        part.take()
+        part.send("batch", 0)
+    for part, part_order in zip(parts_cross, orders_cross):
+        part.send("batch", part_order[0])
+    gather_ffn.take()
+    gather_ffn.send("head", 0)
+    memory_came = swap(line.tie(memory_own), "head", 2)
+    weights_qk, weights_vr = [part.close() for part in parts_self]
+
+    order = jnp.concatenate([group_order, to_exchange]).astype(jnp.int32)
+    values = line.mark(
+        project(line.tie(extended), weights_vr, 0, 256, 256, value_affine, BF, "self_v")
+    )
+    relpos = line.mark(
+        project(line.tie(own), weights_vr, 256, 128, 128, rel_affine, F32, "self_rel")
+    )
+    for number in range(1, nb - 1):
+        for part, part_order in zip(parts_cross, orders_cross):
+            part.take()
+            part.send("batch", part_order[number])
+    gather_ffn.take()
+    weights_ffn = gather_ffn.buf.reshape((groups,) + ffn_shard.shape)
+    weights_ffn = lax.all_gather(weights_ffn, "batch", axis=0)
+    if blk % 128:
+        weights_ffn = jnp.take(weights_ffn, to_exchange, axis=0)
+    qk = line.mark(project(line.tie(extended), weights_qk, 0, 512, 256, qk_affine, BF, "self_qk"))
+    memory_half = line.mark(jnp.concatenate([line.tie(memory_own), memory_came], 0))
+    memory_came = swap(memory_half, "head", 1)
+    context, self_probs, self_own = self_attention(
+        line.tie(qk), values, relpos, mask, turned.reshape(1, -1), share
+    )
+    line.mark(context)
+    for part in parts_cross:
+        part.take()
+        part.send("batch", 0)
+    memory_all = line.mark(jnp.concatenate([line.tie(memory_half), memory_came], 0))
+    weights_out, weights_kv = [part.close() for part in parts_cross]
     normed1, normed1_low, unit1, spread1 = close_sublayer(
-        context, weights_cross, 0, 256, own, vectors[0], "self_out"
-    )
-    cross_kv = project(memory_all, weights_cross, 512, 512, 512, cross_kv_affine, BF, "cross_kv")
-    cross_q = project(
-        normed1_low, weights_cross, 256, 256, 256, cross_query_affine, BF, "cross_q"
-    )
-    cross_context, cross_probs = cross_attention(cross_q, cross_kv)
+        line.tie(context), weights_out, 0, 256, own, vectors[0], "self_out"
+    )
+    line.mark(normed1)
+    cross_q = line.mark(
+        project(
+            line.tie(normed1_low), weights_out, 256, 256, 256, cross_query_affine, BF, "cross_q"
+        )
+    )
+    cross_kv = line.mark(
+        project(line.tie(memory_all), weights_kv, 0, 512, 256, cross_kv_affine, BF, "cross_kv")
+    )
+    cross_context, cross_probs = cross_attention(line.tie(cross_q), cross_kv)
+    line.mark(cross_context)
     normed2, normed2_low, unit2, spread2 = close_sublayer(
-        cross_context, weights_cross, 1024, 256, normed1, vectors[1], "cross_out"
-    )
+        line.tie(cross_context), weights_kv, 512, 256, normed1, vectors[1], "cross_out"
+    )
+    line.mark(normed2)
     active, slope, out_low, third, third_low, sums_third = feed_forward(
-        normed2_low, normed2, weights_up, weights_down, up_row, vectors[2], upstream
-    )
-    out_low = reorder_blocks(out_low, to_natural).reshape(3, share, features)
+        order, line.tie(normed2_low), normed2, weights_ffn, up_row, vectors[2], upstream
+    )
+    line.mark(third)
+
+    def send(entries, name):
+        left, right = entries[0]
+        entries = [(line.tie(left), right)] + entries[1:]
+        (sent,) = weight_products(entries, 1, None, None, batches // 2, groups, name + "_send")
+        return swap(line.mark(sent), "batch", 1)
+
+    def keep(entries, came, widths, name):
+        left, right = entries[0]
+        entries = [(line.tie(left), right)] + entries[1:]
+        orders = (near, far)
+        parts = [(width, nb - 1 - order[0]) for width, order in zip(widths, orders)]
+        outs = weight_products(entries, 0, came, parts, batches // 2, groups, name + "_keep")
+        line.mark(outs[0])
+        return Scatter(line, [outs[0:2], outs[2:4]], orders)
+
+    def natural_groups(block):
+        return jnp.take(block.reshape(-1, groups, block.shape[1] // groups), group_order, axis=1)
+
+    def pack_sums(earlier):
+        feature_sums = jnp.concatenate([after(sums_first, earlier), sums_second, sums_third], 0)
+        feature_sums = jnp.take(
+            feature_sums.reshape(9, batches, features // batches), to_natural, axis=1
+        )
+        return jnp.concatenate(
+            [
+                natural_groups(self_sums).reshape(-1),
+                natural_groups(rel_sums).reshape(-1),
+                natural_groups(cross_sums).reshape(-1),
+                natural_groups(up_sums).reshape(-1),
+                feature_sums.reshape(-1),
+            ]
+        )
+
+    down_entries = [(third_low, active)]
+    down_came = send(down_entries, "down_grad")
+    upper_low, up_sums, second, second_low, sums_second = feed_forward_back(
+        order, line.tie(third_low), third, slope, weights_ffn, unit2, spread2, vectors[1][0:1]
+    )
+    line.mark(second)
+    out_low = line.mark(reorder_blocks(line.tie(out_low), to_natural))
+    out_low = out_low.reshape(3, share, features)
     layer_out = lax.all_gather(jnp.transpose(out_low, (1, 0, 2)), "head", axis=0, tiled=True)[None]
-
-    grad_down = weight_gradient([(third_low, active)], far, "down_grad")
-    upper_low, up_sums, second, second_low, sums_second = feed_forward_back(
-        third_low, third, slope, weights_up, weights_down, unit2, spread2, vectors[1][0:1]
-    )
-    grad_up = weight_gradient([(normed2_low, upper_low)], near, "up_grad")
-    grad_cross_ctx = project_plain(second_low, weights_cross, 1024, 256, "cross_ctx_back")
+    scatter_down = keep(down_entries, down_came, (512, 512), "down_grad")
+    up_entries = [(normed2_low, upper_low)]
+    up_came = send(up_entries, "up_grad")
+    grad_cross_ctx = project_plain(line.tie(second_low), weights_kv, 512, 256, "cross_ctx_back")
+    line.mark(grad_cross_ctx)
     grad_cross_q, grad_cross_kv, cross_sums = cross_attention_back(
-        cross_q, cross_kv, cross_probs, grad_cross_ctx
-    )
-    grads_cross = weight_gradient(
-        [
-            (normed1_low, grad_cross_q),
-            (memory_all, grad_cross_kv),
-            (second_low, cross_context),
-        ],
-        far,
-        "cross_grad",
-    )
-    memory_part = rows_back(grad_cross_kv, weights_cross, 512, 512, "memory_back")
+        cross_q, cross_kv, cross_probs, line.tie(grad_cross_ctx)
+    )
+    line.mark(grad_cross_q)
+    scatter_up = keep(up_entries, up_came, (512, 512), "up_grad")
+    scatter_down.step()
+    cross_entries = [
+        (normed1_low, grad_cross_q),
+        (memory_all, grad_cross_kv),
+        (second_low, cross_context),
+    ]
+    cross_came = send(cross_entries, "cross_grad")
     first, first_low, sums_first = cross_query_back(
-        grad_cross_q, weights_cross, 256, 256, second, unit1, spread1, vectors[0][0:1]
-    )
-    grad_context = project_plain(first_low, weights_cross, 0, 256, "self_ctx_back")
+        line.tie(grad_cross_q), weights_out, 256, 256, second, unit1, spread1, vectors[0][0:1]
+    )
+    line.mark(first)
+    grad_context = project_plain(line.tie(first_low), weights_out, 0, 256, "self_ctx_back")
+    line.mark(grad_context)
     grad_q, grad_kv, grad_rel, self_sums, rel_sums = self_attention_back(
-        qkv, self_probs, self_own, grad_context, straight.reshape(-1, 1), share
-    )
-    grads_self = weight_gradient(
-        [
-            (own, grad_q),
-            (extended, grad_kv),
-            (own, grad_rel),
-            (first_low, context),
-        ],
-        near,
-        "self_grad",
-    )
-    halo_grad, own_grad = input_back(grad_q, grad_kv, grad_rel, weights_self, first)
-
+        qk, values, self_probs, self_own, line.tie(grad_context), straight.reshape(-1, 1), share
+    )
+    line.mark(grad_q)
+    scatter_cross = keep(cross_entries, cross_came, (512, 512), "cross_grad")
+    layer_out = line.mark(line.tie(layer_out))
+    scatter_up.step()
+    scatter_down.step()
+    self_entries = [(own, grad_q), (first_low, context), (extended, grad_kv), (own, grad_rel)]
+    self_came = send(self_entries, "self_grad")
+    halo_grad, own_grad = input_back(
+        line.tie(grad_q), grad_kv, grad_rel, weights_qk, weights_vr, first
+    )
+    line.mark(own_grad)
     from_two = lax.ppermute(halo_grad[0:share], "head", [(i + 2, i) for i in chain[:-2]])
     from_one = lax.ppermute(halo_grad[share:], "head", [(i + 1, i) for i in chain[:-1]])
-    main_grad = own_grad[0:share] + from_one.astype(F32) + from_two.astype(F32)
+    memory_part = rows_back(line.tie(grad_cross_kv), weights_kv, 0, 512, "memory_back")
+    span = memory.shape[1]
+    memory_part = line.mark(memory_part).reshape(2, 2, span, features)
+    memory_came = swap(memory_part[1], "head", 1)
+    scatter_self = keep(self_entries, self_came, (512, 640), "self_grad")
+    scatter_cross.step()
+    scatter_up.step()
+    scatter_down.step()
+    packed = pack_sums(line.last[0])
+    packed_bits = [("batch", bit) for bit in range(nb)] + [("head", 0), ("head", 1)]
+
+    def add_packed(packed):
+        axis_name, bit = packed_bits.pop(0)
+        came = swap(packed, axis_name, 1 << bit)
+        packed = line.tie(packed)
+        return line.mark(packed + after(came, packed))
+
+    main_grad = line.tie(own_grad[0:share]) + from_one.astype(F32) + from_two.astype(F32)
     own_grad = jnp.concatenate([main_grad, own_grad[share:]], 0)
-    own_grad = reorder_blocks(own_grad, to_natural).reshape(3, share, features)
+    own_grad = line.mark(reorder_blocks(own_grad, to_natural)).reshape(3, share, features)
     grad_hidden = jnp.transpose(own_grad, (1, 0, 2))[None]
-    span = memory.shape[1]
-    pairs = memory_part.reshape(2, 2 * span, features)
-    memory_half = pairs[0].astype(F32) + swap(pairs[1], "head", 2).astype(F32)
-    memory_half = memory_half.astype(BF)
-    memory_grad = memory_half[:span].astype(F32) + swap(memory_half[span:], "head", 1).astype(F32)
-    grad_memory = reorder_blocks(memory_grad, to_natural)[None]
-
-    def natural_groups(block):
-        return jnp.take(block.reshape(-1, groups, block.shape[1] // groups), group_order, axis=1)
-
-    feature_sums = jnp.concatenate([sums_first, sums_second, sums_third], 0)
-    feature_sums = jnp.take(
-        feature_sums.reshape(9, batches, features // batches), to_natural, axis=1
-    ).reshape(3, 3, features)
-    packed = jnp.concatenate(
-        [
-            natural_groups(self_sums).reshape(-1),
-            natural_groups(rel_sums).reshape(-1),
-            natural_groups(cross_sums).reshape(-1),
-            natural_groups(up_sums).reshape(-1),
-            feature_sums.reshape(-1),
-        ]
-    )
-    for bit in range(nb):
-        packed = packed + swap(packed, "batch", 1 << bit)
-    for bit in range(bits_of("head")):
-        packed = packed + swap(packed, "head", 1 << bit)
+    packed = add_packed(packed)
+    scatter_down.step()
+    scatter_up.step()
+    memory_part, memory_came = line.tie(memory_part), after(memory_came, *line.last)
+    memory_mine = (memory_part[0].astype(F32) + memory_came.astype(F32)).astype(BF)
+    memory_mine = line.mark(memory_mine)
+    memory_came = swap(pin(memory_mine[1]), "head", 2)
+    scatter_cross.step()
+    scatter_self.step()
+    packed = add_packed(packed)
+    scatter_up.step()
+    scatter_cross.step()
+    memory_mine, memory_came = line.tie(memory_mine), after(memory_came, *line.last)
+    memory_grad = memory_mine[0].astype(F32) + memory_came.astype(F32)
+    grad_memory = line.mark(reorder_blocks(memory_grad, to_natural))[None]
+    scatter_self.step()
+    packed = add_packed(packed)
+    scatter_cross.step()
+    scatter_self.step()
+    packed = add_packed(packed)
+    scatter_self.step()
+    while packed_bits:
+        packed = add_packed(packed)
+    scatters = (scatter_down, scatter_up, scatter_cross, scatter_self)
+    for scatter in scatters:
+        while not hasattr(scatter, "total"):
+            scatter.step()
+    grad_down, grad_up, grads_cross, grads_self = [scatter.total for scatter in scatters]
+
     ends = [0]
     for size in (2 * features, groups * 128, 2 * features, up_bias.shape[0], 9 * features):
         ends.append(ends[-1] + size)
@@ -1072,15 +1323,9 @@
         layer_out,
         grad_hidden,
         grad_memory,
-        jnp.concatenate(
-            [
-                grads_self[:, 0:256].reshape(blk, 1, 256),
-                grads_self[:, 256:768].reshape(blk, 2, 256),
-            ],
-            1,
-        ),
-        grads_self[:, 768:896],
-        grads_self[:, 896:1152],
+        jnp.concatenate([grads_self[:, 0:256], grads_self[:, 512:1024]], 1).reshape(blk, 3, 256),
+        grads_self[:, 1024:1152],
+        grads_self[:, 256:512],
         grads_cross[:, 0:256],
         grads_cross[:, 256:768].reshape(blk, 2, 256),
         grads_cross[:, 768:1024],

time: 966 us -> 639 us (0.66)
  waiting for transfers between devices: 473 us -> 161 us
  other arithmetic: 65.1 us -> 39.7 us
  starting transfers between devices: 69.3 us -> 86.7 us
  Pallas kernels: 272 us -> 262 us
    ppermute x49 -> x55, waiting for transfers between devices: 400 us -> 156 us  [swap(): return lax.ppermute(array_in, axis, [(i, i ^ bit) for i in range(count)])]
    ppermute x1, waiting for transfers between devices: 51.1 us -> 5.53 us  [per_device(): lax.ppermute(halo_grad[0:share], 'head', [(i + 2, i) for i in chain[:-2]])]
    concatenate x25 -> x3, other arithmetic: 36.5 us -> 1.61 us  [the longest x1 1.01 us: per_device(): jnp.concatenate([grads_self[:, 0:256], grads_self[:, 512:1024]], 1)]
    ppermute x1, waiting for transfers between devices: 21.7 us -> 0.01 us  [per_device(): lax.ppermute(halo_grad[share:], 'head', [(i + 1, i) for i in chain[:-1]])]
    unnamed x102 -> x154, local copies, waits for them, and re-layouts: 6.53 us -> 24.6 us
    ppermute x49 -> x55, starting transfers between devices: 60.6 us -> 77.7 us  [swap(): return lax.ppermute(array_in, axis, [(i, i ^ bit) for i in range(count)])]
    pallas_call x6, Pallas kernels: 35.4 us -> 18.7 us  [reorder_blocks(): pl.pallas_call(body, out_shape=jax.ShapeDtypeStruct(array_in.shape, array...]
    pallas_call x6 -> x7, Pallas kernels: 38.8 us -> 42.5 us  [project(): pl.pallas_call(body, grid=(groups, per), in_specs=[whole((rows, features)...]
  transfers between devices with their start and end apart: 54 -> 61, of which waited for: 29 -> 21; matrix products, arithmetic and copies ran while one was open for 12% -> 12% of each run, Pallas kernels for 26% -> 35%
where the time goes in v2:
time: 639 us; the launch traced here: 631 us
  Pallas kernels  262 us (41%)
  waiting for transfers between devices  161 us (25%)
  starting transfers between devices  86.7 us (14%)
  local copies, waits for them, and re-layouts  65.5 us (10%)
  other arithmetic  39.7 us (6%)
  between operations  15.9 us (2%)
    ppermute x55, waiting for transfers between devices, swap(): return lax.ppermute(array_in, axis, [(i, i ^ bit) for i in range(count)])  156 us
    ppermute x55, starting transfers between devices, swap(): return lax.ppermute(array_in, axis, [(i, i ^ bit) for i in range(count)])  77.7 us
    pallas_call x8, Pallas kernels, weight_products(): pl.pallas_call(body, grid=(groups,), in_specs=in_specs, out_specs=[block(...  59.8 us
    pallas_call x7, Pallas kernels, project(): pl.pallas_call(body, grid=(groups, per), in_specs=[whole((rows, features)...  42.5 us
    unnamed x154, local copies, waits for them, and re-layouts  24.6 us
    pallas_call x6, Pallas kernels, reorder_blocks(): pl.pallas_call(body, out_shape=jax.ShapeDtypeStruct(array_in.shape, array...  18.7 us
    pallas_call x1, Pallas kernels, self_attention_back(): pl.pallas_call(body, grid=(groups,), in_specs=[pl.BlockSpec((long_rows, 2...  18.1 us
    pallas_call x1, Pallas kernels, self_attention(): pl.pallas_call(body, grid=(groups,), in_specs=[pl.BlockSpec((long_rows, 2...  17.9 us
  transfers between devices with their start and end apart: 61, of which 21 were waited for; matrix products, arithmetic and copies ran while one was open for 12% of the time, Pallas kernels for 35%

profile of v2, /device:TPU:0, one launch (start us, length us, event | category | flops | bytes accessed | tf_op | source)
XLA Modules:
  0.0 631.1 jit_solution(4483038156661378916)
XLA Ops:
  9.4 4.1 collective-permute-start
  24.5 3.6 reorder.8.grad_ref
  33.2 16.9 %collective-permute-done.1 = bf16[1,1,1,2,1,128,896]{6,5,4,3,2,1,0:T(8,128)(2,1)S(1)} collective-permute-done((bf16[1,1,1,2,1,128,896]{6,5,4,3,2,1,0:T(8,128)(2,1)S(1)}, bf16[1,1,1,2,1,128,896]{6,5,4,3,2,1,0:T(8,128)(2,1)S(1)}, u32[]{:S(2)}, u32[]{:S(2)}) %collective-permute-start.1) | collective-permute-done | bytes 458784 | tf_op jit(solution)/shard_map/ppermute | solution.py:35
  51.6 4.4 collective-permute-start.3
  59.3 10.1 %collective-permute-done.5 = bf16[1,1,1,2,2,128,512]{6,5,4,3,2,1,0:T(8,128)(2,1)S(1)} collective-permute-done((bf16[1,1,1,2,2,128,512]{6,5,4,3,2,1,0:T(8,128)(2,1)S(1)}, bf16[1,1,1,2,2,128,512]{6,5,4,3,2,1,0:T(8,128)(2,1)S(1)}, u32[]{:S(2)}, u32[]{:S(2)}) %collective-permute-start.5) | collective-permute-done | bytes 524320 | tf_op jit(solution)/shard_map/ppermute | solution.py:35
  71.8 4.0 collective-permute-done.7
  76.9 3.7 collective-permute-start.10
  80.6 11.0 %collective-permute-done.8 = bf16[1,2,1,2,2,128,512]{6,5,4,3,2,1,0:T(8,128)(2,1)S(1)} collective-permute-done((bf16[1,2,1,2,2,128,512]{6,5,4,3,2,1,0:T(8,128)(2,1)S(1)}, bf16[1,2,1,2,2,128,512]{6,5,4,3,2,1,0:T(8,128)(2,1)S(1)}, u32[]{:S(2)}, u32[]{:S(2)}) %collective-permute-start.8) | collective-permute-done | bytes 1048608 | tf_op jit(solution)/shard_map/ppermute | solution.py:35
  106.5 5.1 self_v.1.v_ref
  111.6 4.4 self_rel.1.rel_ref
  119.1 8.2 %collective-permute-done.14 = bf16[1,1,1,2,1,128,2048]{6,5,4,3,2,1,0:T(8,128)(2,1)S(1)} collective-permute-done((bf16[1,1,1,2,1,128,2048]{6,5,4,3,2,1,0:T(8,128)(2,1)S(1)}, bf16[1,1,1,2,1,128,2048]{6,5,4,3,2,1,0:T(8,128)(2,1)S(1)}, u32[]{:S(2)}, u32[]{:S(2)}) %collective-permute-start.14) | collective-permute-done | bytes 1048608 | tf_op jit(solution)/shard_map/ppermute | solution.py:35
  137.8 9.1 %self_qk.1.q_ref.k_ref = bf16[640,2048]{1,0:T(8,128)(2,1)} custom-call(bf16[640,1024]{1,0:T(8,128)(2,1)} %copy-done.7, bf16[4,4,128,512]{3,2,1,0:T(8,128)(2,1)} %bitcast.223, bf16[4,4,128,512]{3,2,1,0:T(8,128)(2,1)} %bitcast.21.refs_1_.refs_3_, f32[2,2048]{1,0:T(2,128)} %pad_maximum_fusion.9.refs_2_), custom_call_target="tpu_custom_call" | custom-call | tf_op jit(solution)/shard_map/self_qk/pallas_call | solution.py:203
  147.7 12.3 %collective-permute-done.16 = bf16[256,1024]{1,0:T(8,128)(2,1)} collective-permute-done((bf16[256,1024]{1,0:T(8,128)(2,1)}, bf16[256,1024]{1,0:T(8,128)(2,1)}, u32[]{:S(2)}, u32[]{:S(2)}) %collective-permute-start.16) | collective-permute-done | bytes 524320 | tf_op jit(solution)/shard_map/ppermute | solution.py:35
  161.9 17.9 %self_attention.1 = (bf16[384,1024]{1,0:T(8,128)(2,1)}, bf16[16,384,384]{2,1,0:T(8,128)(2,1)}, f32[384,512]{1,0:T(8,128)}) custom-call(bf16[640,2048]{1,0:T(8,128)(2,1)} %self_qk.1.q_ref.k_ref, bf16[640,2048]{1,0:T(8,128)(2,1)} %self_qk.1.q_ref.k_ref, bf16[640,1024]{1,0:T(8,128)(2,1)} %self_v.1.v_ref, f32[384,512]{1,0:T(8,128)} %self_rel.1.rel_ref, ...), custom_call_target="tpu_custom_call" | custom-call | tf_op jit(solution)/shard_map/self_attention/pallas_call | solution.py:742
  184.8 4.9 collective-permute-done.18
  198.8 19.2 %collective-permute-done.19 = bf16[512,1024]{1,0:T(8,128)(2,1)} collective-permute-done((bf16[512,1024]{1,0:T(8,128)(2,1)}, bf16[512,1024]{1,0:T(8,128)(2,1)}, u32[]{:S(2)}, u32[]{:S(2)}) %collective-permute-start.19) | collective-permute-done | bytes 1048608 | tf_op jit(solution)/shard_map/ppermute | solution.py:35
  219.3 7.4 %self_out.1 = (f32[384,1024]{1,0:T(8,128)}, bf16[384,1024]{1,0:T(8,128)(2,1)}, f32[384,1024]{1,0:T(8,128)}, f32[384,1]{1,0:T(8,128)}) custom-call(bf16[384,1024]{1,0:T(8,128)(2,1)} %get-tuple-element.246.left_ref.refs_5_, bf16[4,4,128,512]{3,2,1,0:T(8,128)(2,1)} %bitcast.22.refs_0_, bf16[4,4,128,512]{3,2,1,0:T(8,128)(2,1)} %bitcast.23.refs_1_, ...), custom_call_target="tpu_custom_call" | custom-call | tf_op jit(solution)/shard_map/self_out/pallas_call | solution.py:274
  226.7 4.6 cross_q.1.q_ref
  231.2 10.1 %cross_kv.1.k_ref.v_ref = bf16[1024,2048]{1,0:T(8,128)(2,1)} custom-call(bf16[1024,1024]{1,0:T(8,128)(2,1)} %copy-done.5, bf16[4,4,128,768]{3,2,1,0:T(8,128)(2,1)} %bitcast.215, bf16[4,4,128,768]{3,2,1,0:T(8,128)(2,1)} %bitcast.28.refs_1_, f32[2,2048]{1,0:T(2,128)} %stack.26.refs_2_), custom_call_target="tpu_custom_call" | custom-call | tf_op jit(solution)/shard_map/cross_kv/pallas_call | solution.py:203
  241.4 14.5 %cross_attention.1 = (bf16[384,1024]{1,0:T(8,128)(2,1)}, bf16[16,384,1024]{2,1,0:T(8,128)(2,1)}) custom-call(bf16[384,1024]{1,0:T(8,128)(2,1)} %cross_q.1.q_ref, bf16[1024,2048]{1,0:T(8,128)(2,1)} %cross_kv.1.k_ref.v_ref, bf16[1024,2048]{1,0:T(8,128)(2,1)} %cross_kv.1.k_ref.v_ref), custom_call_target="tpu_custom_call" | custom-call | tf_op jit(solution)/shard_map/cross_attention/pallas_call | solution.py:893
  255.9 7.0 %cross_out.1 = (f32[384,1024]{1,0:T(8,128)}, bf16[384,1024]{1,0:T(8,128)(2,1)}, f32[384,1024]{1,0:T(8,128)}, f32[384,1]{1,0:T(8,128)}) custom-call(bf16[384,1024]{1,0:T(8,128)(2,1)} %get-tuple-element.255.left_ref.refs_5_, bf16[4,4,128,768]{3,2,1,0:T(8,128)(2,1)} %bitcast.216, bf16[4,4,128,768]{3,2,1,0:T(8,128)(2,1)} %bitcast.28.refs_1_, ...), custom_call_target="tpu_custom_call" | custom-call | tf_op jit(solution)/shard_map/cross_out/pallas_call | solution.py:274
  262.9 17.3 %feed_forward.1 = (bf16[384,4096]{1,0:T(8,128)(2,1)}, bf16[384,4096]{1,0:T(8,128)(2,1)}, bf16[384,1024]{1,0:T(8,128)(2,1)}, f32[384,1024]{1,0:T(8,128)}, bf16[384,1024]{1,0:T(8,128)(2,1)}, /*index=5*/f32[3,1024]{1,0:T(4,128)}) custom-call(s32[12]{0:T(128)} %pad_add_fusion.order_ref, bf16[384,1024]{1,0:T(8,128)(2,1)} %get-tuple-element.281.low_ref.refs_0_, ...), custom_call_target="tpu_custom_call" | custom-call | tf_op jit(solution)/shard_map/feed_forward/pallas_call | solution.py:356
  280.2 6.0 down_grad_send.1
  287.4 16.0 %feed_forward_back.1 = (bf16[384,4096]{1,0:T(8,128)(2,1)}, f32[1,4096]{1,0:T(1,128)}, f32[384,1024]{1,0:T(8,128)}, bf16[384,1024]{1,0:T(8,128)(2,1)}, f32[3,1024]{1,0:T(4,128)}) custom-call(s32[12]{0:T(128)} %pad_add_fusion.order_ref, bf16[384,1024]{1,0:T(8,128)(2,1)} %get-tuple-element.274.refs_0_.third_low_ref, f32[384,1024]{1,0:T(8,128)} %get-tuple-element.261.third_ref, ...), custom_call_target="tpu_custom_call" | custom-call | tf_op jit(solution)/shard_map/feed_forward_back/pallas_call | solution.py:443
  306.2 7.0 %down_grad_keep.1 = (bf16[2,4,128,512]{3,2,1,0:T(8,128)(2,1)}, bf16[2,4,128,512]{3,2,1,0:T(8,128)(2,1)}, bf16[2,4,128,512]{3,2,1,0:T(8,128)(2,1)}, bf16[2,4,128,512]{3,2,1,0:T(8,128)(2,1)}) custom-call(bf16[384,1024]{1,0:T(8,128)(2,1)} %get-tuple-element.274.refs_0_.third_low_ref, bf16[384,4096]{1,0:T(8,128)(2,1)} %get-tuple-element.263.refs_1_, ...), custom_call_target="tpu_custom_call" | custom-call | tf_op jit(solution)/shard_map/down_grad_keep/pallas_call | solution.py:667
  313.3 6.1 up_grad_send.1
  323.2 4.5 cross_ctx_back.1.grad_ref
  327.8 17.1 %cross_attention_back.1 = (bf16[384,1024]{1,0:T(8,128)(2,1)}, bf16[1024,2048]{1,0:T(8,128)(2,1)}, f32[2,1024]{1,0:T(2,128)}) custom-call(bf16[384,1024]{1,0:T(8,128)(2,1)} %cross_q.1.q_ref, bf16[1024,2048]{1,0:T(8,128)(2,1)} %cross_kv.1.k_ref.v_ref, bf16[1024,2048]{1,0:T(8,128)(2,1)} %cross_kv.1.k_ref.v_ref, ...), custom_call_target="tpu_custom_call" | custom-call | tf_op jit(solution)/shard_map/cross_attention_back/pallas_call | solution.py:952
  344.9 7.1 %up_grad_keep.1 = (bf16[2,4,128,512]{3,2,1,0:T(8,128)(2,1)}, bf16[2,4,128,512]{3,2,1,0:T(8,128)(2,1)}, bf16[2,4,128,512]{3,2,1,0:T(8,128)(2,1)}, bf16[2,4,128,512]{3,2,1,0:T(8,128)(2,1)}) custom-call(bf16[384,1024]{1,0:T(8,128)(2,1)} %get-tuple-element.281.low_ref.refs_0_, bf16[384,4096]{1,0:T(8,128)(2,1)} %get-tuple-element.277.refs_1_, ...), custom_call_target="tpu_custom_call" | custom-call | tf_op jit(solution)/shard_map/up_grad_keep/pallas_call | solution.py:667
  357.7 8.2 %cross_grad_send.1 = bf16[4,4,128,1024]{3,2,1,0:T(8,128)(2,1)} custom-call(bf16[384,1024]{1,0:T(8,128)(2,1)} %get-tuple-element.298.x_ref.refs_0_, bf16[1024,1024]{1,0:T(8,128)(2,1)} %copy-done.5, bf16[384,1024]{1,0:T(8,128)(2,1)} %get-tuple-element.278.x_ref.refs_2_, bf16[384,1024]{1,0:T(8,128)(2,1)} %get-tuple-element.291.refs_3_.left_ref, ...), custom_call_target="tpu_custom_call" | custom-call | tf_op jit(solution)/shard_map/cross_grad_send/pallas_call | solution.py:667
  370.8 7.0 %cross_query_back.1 = (f32[384,1024]{1,0:T(8,128)}, bf16[384,1024]{1,0:T(8,128)(2,1)}, f32[3,1024]{1,0:T(4,128)}) custom-call(bf16[384,1024]{1,0:T(8,128)(2,1)} %get-tuple-element.291.refs_3_.left_ref, bf16[4,4,128,512]{3,2,1,0:T(8,128)(2,1)} %bitcast.22.refs_0_, bf16[4,4,128,512]{3,2,1,0:T(8,128)(2,1)} %bitcast.23.refs_1_, ...), custom_call_target="tpu_custom_call" | custom-call | tf_op jit(solution)/shard_map/cross_query_back/pallas_call | solution.py:513
  377.7 4.5 self_ctx_back.1.grad_ref
  382.3 18.1 %self_attention_back.1 = (bf16[384,1024]{1,0:T(8,128)(2,1)}, bf16[640,2048]{1,0:T(8,128)(2,1)}, bf16[384,512]{1,0:T(8,128)(2,1)}, f32[2,1024]{1,0:T(2,128)}, f32[1,512]{1,0:T(1,128)}) custom-call(bf16[640,2048]{1,0:T(8,128)(2,1)} %self_qk.1.q_ref.k_ref, bf16[640,2048]{1,0:T(8,128)(2,1)} %self_qk.1.q_ref.k_ref, bf16[640,1024]{1,0:T(8,128)(2,1)} %self_v.1.v_ref, ...), custom_call_target="tpu_custom_call" | custom-call | tf_op jit(solution)/shard_map/self_attention_back/pallas_call | solution.py:844
  402.4 8.7 %cross_grad_keep.1 = (bf16[2,4,128,512]{3,2,1,0:T(8,128)(2,1)}, bf16[2,4,128,512]{3,2,1,0:T(8,128)(2,1)}, bf16[2,4,128,512]{3,2,1,0:T(8,128)(2,1)}, bf16[2,4,128,512]{3,2,1,0:T(8,128)(2,1)}) custom-call(bf16[384,1024]{1,0:T(8,128)(2,1)} %get-tuple-element.298.x_ref.refs_0_, bf16[1024,1024]{1,0:T(8,128)(2,1)} %copy-done.5, ...), custom_call_target="tpu_custom_call" | custom-call | tf_op jit(solution)/shard_map/cross_grad_keep/pallas_call | solution.py:667
  420.5 7.8 %self_grad_send.1 = bf16[4,4,128,1152]{3,2,1,0:T(8,128)(2,1)} custom-call(bf16[384,1024]{1,0:T(8,128)(2,1)} %reorder.7.x_ref.refs_2_.refs_0_.refs_3_, bf16[384,1024]{1,0:T(8,128)(2,1)} %get-tuple-element.296.x_ref.refs_1_, bf16[640,1024]{1,0:T(8,128)(2,1)} %copy-done.7, bf16[384,1024]{1,0:T(8,128)(2,1)} %reorder.7.x_ref.refs_2_.refs_0_.refs_3_, ...), custom_call_target="tpu_custom_call" | custom-call | tf_op jit(solution)/shard_map/self_grad_send/pallas_call | solution.py:667
  436.3 10.0 %input_back.1 = (bf16[256,1024]{1,0:T(8,128)(2,1)}, f32[384,1024]{1,0:T(8,128)}) custom-call(bf16[384,1024]{1,0:T(8,128)(2,1)} %get-tuple-element.315.refs_4_.query_ref, bf16[640,2048]{1,0:T(8,128)(2,1)} %get-tuple-element.313.refs_6_.kv_ref, bf16[384,512]{1,0:T(8,128)(2,1)} %get-tuple-element.314.refs_7_.rel_ref, bf16[4,4,128,512]{3,2,1,0:T(8,128)(2,1)} %bitcast.224, ...), custom_call_target="tpu_custom_call" | custom-call | tf_op jit(solution)/shard_map/input_back/pallas_call | solution.py:595
  448.7 8.8 %memory_back.1 = bf16[1024,1024]{1,0:T(8,128)(2,1)} custom-call(bf16[1024,2048]{1,0:T(8,128)(2,1)} %get-tuple-element.318.refs_4_.left_ref, bf16[4,4,128,768]{3,2,1,0:T(8,128)(2,1)} %bitcast.218, bf16[4,4,128,768]{3,2,1,0:T(8,128)(2,1)} %bitcast.28.refs_1_), custom_call_target="tpu_custom_call" | custom-call | tf_op jit(solution)/shard_map/memory_back/pallas_call | solution.py:552
  462.1 8.8 %self_grad_keep.1 = (bf16[2,4,128,512]{3,2,1,0:T(8,128)(2,1)}, bf16[2,4,128,512]{3,2,1,0:T(8,128)(2,1)}, bf16[2,4,128,640]{3,2,1,0:T(8,128)(2,1)}, bf16[2,4,128,640]{3,2,1,0:T(8,128)(2,1)}) custom-call(bf16[384,1024]{1,0:T(8,128)(2,1)} %reorder.7.x_ref.refs_2_.refs_0_.refs_3_, bf16[384,1024]{1,0:T(8,128)(2,1)} %get-tuple-element.296.x_ref.refs_1_, ...), custom_call_target="tpu_custom_call" | custom-call | tf_op jit(solution)/shard_map/self_grad_keep/pallas_call | solution.py:667
  483.5 4.9 collective-permute-start.40
  489.7 5.5 collective-permute-done.38
  497.6 3.6 reorder.10
  501.5 18.4 %collective-permute-done.40 = bf16[1,128,1024]{2,1,0:T(8,128)(2,1)} collective-permute-done((bf16[1,128,1024]{2,1,0:T(8,128)(2,1)}, bf16[1,128,1024]{2,1,0:T(8,128)(2,1)}, u32[]{:S(2)}, u32[]{:S(2)}) %collective-permute-start.40) | collective-permute-done | bytes 262176 | tf_op jit(solution)/shard_map/ppermute | solution.py:35
  531.0 5.8 collective-permute-start.49
  536.8 7.0 %collective-permute-done.45 = bf16[2,4,128,512]{3,2,1,0:T(8,128)(2,1)S(1)} collective-permute-done((bf16[2,4,128,512]{3,2,1,0:T(8,128)(2,1)}, bf16[2,4,128,512]{3,2,1,0:T(8,128)(2,1)S(1)}, u32[]{:S(2)}, u32[]{:S(2)}) %collective-permute-start.45) | collective-permute-done | bytes 1048608 | tf_op jit(solution)/shard_map/ppermute | solution.py:35
  548.4 7.0 %collective-permute-done.46 = bf16[2,4,128,640]{3,2,1,0:T(8,128)(2,1)S(1)} collective-permute-done((bf16[2,4,128,640]{3,2,1,0:T(8,128)(2,1)}, bf16[2,4,128,640]{3,2,1,0:T(8,128)(2,1)S(1)}, u32[]{:S(2)}, u32[]{:S(2)}) %collective-permute-start.46) | collective-permute-done | bytes 1310752 | tf_op jit(solution)/shard_map/ppermute | solution.py:35
  558.5 8.5 %collective-permute-done.50 = bf16[256,1024]{1,0:T(8,128)(2,1)S(1)} collective-permute-done((bf16[256,1024]{1,0:T(8,128)(2,1)S(1)}, bf16[256,1024]{1,0:T(8,128)(2,1)S(1)}, u32[]{:S(2)}, u32[]{:S(2)}) %collective-permute-start.50) | collective-permute-done | bytes 524320 | tf_op jit(solution)/shard_map/ppermute | solution.py:35
  581.9 10.6 %collective-permute-done.54 = bf16[1,128,1024]{2,1,0:T(8,128)(2,1)S(1)} collective-permute-done((bf16[1,128,1024]{2,1,0:T(8,128)(2,1)S(1)}, bf16[1,128,1024]{2,1,0:T(8,128)(2,1)S(1)}, u32[]{:S(2)}, u32[]{:S(2)}) %collective-permute-start.54) | collective-permute-done | bytes 262176 | tf_op jit(solution)/shard_map/ppermute | solution.py:35
  603.3 4.9 collective-permute-start.58
  (425 shorter events, 193.2 us)
Async XLA Ops:
  7.2 255.7 %all-gather.3.cloned.1.call-start = ((), (), s32[]{:S(2)}) async-start(), calls=%async_computation | async-start | bytes 18874368 | tf_op jit(solution)/shard_map/all_gather | solution.py:1144
  9.4 21.6 %collective-permute-start = (bf16[1,1,1,1,1,128,896]{6,5,4,3,2,1,0:T(8,128)(2,1)S(1)}, bf16[1,1,1,1,1,128,896]{6,5,4,3,2,1,0:T(8,128)(2,1)S(1)}, u32[]{:S(2)}, u32[]{:S(2)}) collective-permute-start(bf16[1,1,1,1,1,128,896]{6,5,4,3,2,1,0:T(8,128)(2,1)S(1)} %fusion.25), channel_id=1, source_target_pairs={{0,2},{1,3},{2,0},{3,1},{4,6},{5,7},{6,4},{7,5},{8,10},{9,11},{10,... | collective-permute-start | bytes 688136 | tf_op jit(solution)/shard_map/ppermute | solution.py:35
  31.1 19.0 %collective-permute-start.1 = (bf16[1,1,1,2,1,128,896]{6,5,4,3,2,1,0:T(8,128)(2,1)S(1)}, bf16[1,1,1,2,1,128,896]{6,5,4,3,2,1,0:T(8,128)(2,1)S(1)}, u32[]{:S(2)}, u32[]{:S(2)}) collective-permute-start(bf16[1,1,1,2,1,128,896]{6,5,4,3,2,1,0:T(8,128)(2,1)S(1)} %constant_dynamic-update-slice_fusion), channel_id=1, source_target_pairs={{0,1},{1,0},{2,3},{3,2},{4,5},{5,4},{6,7},{7,6},{8,9},{9,8},{10,11... | collective-permute-start | bytes 1376264 | tf_op jit(solution)/shard_map/ppermute | solution.py:35
  32.7 26.3 %collective-permute-start.4 = (bf16[1,1,1,1,1,128,1280]{6,5,4,3,2,1,0:T(8,128)(2,1)S(1)}, bf16[1,1,1,1,1,128,1280]{6,5,4,3,2,1,0:T(8,128)(2,1)S(1)}, u32[]{:S(2)}, u32[]{:S(2)}) collective-permute-start(bf16[1,1,1,1,1,128,1280]{6,5,4,3,2,1,0:T(8,128)(2,1)S(1)} %maximum_bitcast_fusion.1), channel_id=1, source_target_pairs={{0,2},{1,3},{2,0},{3,1},{4,6},{5,7},{6,4},{7,5},{8,10},{9,11},{10,... | collective-permute-start | bytes 983048 | tf_op jit(solution)/shard_map/ppermute | solution.py:35
  51.6 18.4 %collective-permute-start.3 = (bf16[128,1024]{1,0:T(8,128)(2,1)S(1)}, bf16[128,1024]{1,0:T(8,128)(2,1)S(1)}, u32[]{:S(2)}, u32[]{:S(2)}) collective-permute-start(bf16[128,1024]{1,0:T(8,128)(2,1)S(1)} %slice.396), channel_id=1, source_target_pairs={{0,1},{1,2},{2,3},{4,5},{5,6},{6,7},{8,9},{9,10},{10,11},{12,13},{... | collective-permute-start | bytes 786440 | tf_op jit(solution)/shard_map/ppermute | solution.py:1107
  69.5 22.2 %collective-permute-start.8 = (bf16[1,2,1,2,2,128,512]{6,5,4,3,2,1,0:T(8,128)(2,1)S(1)}, bf16[1,2,1,2,2,128,512]{6,5,4,3,2,1,0:T(8,128)(2,1)S(1)}, u32[]{:S(2)}, u32[]{:S(2)}) collective-permute-start(bf16[1,2,1,2,2,128,512]{6,5,4,3,2,1,0:T(8,128)(2,1)S(1)} %constant_dynamic-update-slice_fusion.6), channel_id=1, source_target_pairs={{0,16},{4,20},{8,24},{12,28},{16,0},{20,4},{24,8},{28,12},{1,17},{... | collective-permute-start | bytes 3145736 | tf_op jit(solution)/shard_map/ppermute | solution.py:35
  70.2 21.6 %collective-permute-start.9 = (bf16[1,1,2,2,2,128,384]{6,5,4,3,2,1,0:T(8,128)(2,1)S(1)}, bf16[1,1,2,2,2,128,384]{6,5,4,3,2,1,0:T(8,128)(2,1)S(1)}, u32[]{:S(2)}, u32[]{:S(2)}) collective-permute-start(bf16[1,1,2,2,2,128,384]{6,5,4,3,2,1,0:T(8,128)(2,1)S(1)} %constant_dynamic-update-slice_fusion.8), channel_id=1, source_target_pairs={{0,8},{4,12},{8,0},{12,4},{16,24},{20,28},{24,16},{28,20},{1,9},{5... | collective-permute-start | bytes 2359304 | tf_op jit(solution)/shard_map/ppermute | solution.py:35
  76.9 25.3 %collective-permute-start.10 = (bf16[1,1,1,1,1,128,2048]{6,5,4,3,2,1,0:T(8,128)(2,1)}, bf16[1,1,1,1,1,128,2048]{6,5,4,3,2,1,0:T(8,128)(2,1)}, u32[]{:S(2)}, u32[]{:S(2)}) collective-permute-start(bf16[1,1,1,1,1,128,2048]{6,5,4,3,2,1,0:T(8,128)(2,1)} %maximum_bitcast_fusion), channel_id=1, source_target_pairs={{0,2},{1,3},{2,0},{3,1},{4,6},{5,7},{6,4},{7,5},{8,10},{9,11},{10,... | collective-permute-start | bytes 1572872 | tf_op jit(solution)/shard_map/ppermute | solution.py:35
  95.9 21.2 %collective-permute-start.13 = (bf16[1,1,1,2,2,128,768]{6,5,4,3,2,1,0:T(8,128)(2,1)S(1)}, bf16[1,1,1,2,2,128,768]{6,5,4,3,2,1,0:T(8,128)(2,1)S(1)}, u32[]{:S(2)}, u32[]{:S(2)}) collective-permute-start(bf16[1,1,1,2,2,128,768]{6,5,4,3,2,1,0:T(8,128)(2,1)S(1)} %slice.399), channel_id=1, source_target_pairs={{0,8},{4,12},{8,0},{12,4},{16,24},{20,28},{24,16},{28,20},{1,9},{5... | collective-permute-start | bytes 2359304 | tf_op jit(solution)/shard_map/ppermute | solution.py:35
  97.3 18.8 %collective-permute-start.12 = (bf16[1,1,1,2,2,128,512]{6,5,4,3,2,1,0:T(8,128)(2,1)S(1)}, bf16[1,1,1,2,2,128,512]{6,5,4,3,2,1,0:T(8,128)(2,1)S(1)}, u32[]{:S(2)}, u32[]{:S(2)}) collective-permute-start(bf16[1,1,1,2,2,128,512]{6,5,4,3,2,1,0:T(8,128)(2,1)S(1)} %slice.400), channel_id=1, source_target_pairs={{0,16},{4,20},{8,24},{12,28},{16,0},{20,4},{24,8},{28,12},{1,17},{... | collective-permute-start | bytes 1572872 | tf_op jit(solution)/shard_map/ppermute | solution.py:35
  103.2 24.1 %collective-permute-start.14 = (bf16[1,1,1,2,1,128,2048]{6,5,4,3,2,1,0:T(8,128)(2,1)S(1)}, bf16[1,1,1,2,1,128,2048]{6,5,4,3,2,1,0:T(8,128)(2,1)S(1)}, u32[]{:S(2)}, u32[]{:S(2)}) collective-permute-start(bf16[1,1,1,2,1,128,2048]{6,5,4,3,2,1,0:T(8,128)(2,1)S(1)} %constant_dynamic-update-slice_fusion.19), channel_id=1, source_target_pairs={{0,1},{1,0},{2,3},{3,2},{4,5},{5,4},{6,7},{7,6},{8,9},{9,8},{10,11... | collective-permute-start | bytes 3145736 | tf_op jit(solution)/shard_map/ppermute | solution.py:35
  128.5 282.7 %all-gather.5.cloned.1.call-start = ((), (), s32[]{:S(2)}) async-start(), calls=%async_computation.1 | async-start | bytes 3932160 | tf_op jit(solution)/shard_map/all_gather | solution.py:1223
  130.1 59.6 %collective-permute-start.18 = (bf16[1,2,1,2,2,128,768]{6,5,4,3,2,1,0:T(8,128)(2,1)}, bf16[1,2,1,2,2,128,768]{6,5,4,3,2,1,0:T(8,128)(2,1)}, u32[]{:S(2)}, u32[]{:S(2)}) collective-permute-start(bf16[1,2,1,2,2,128,768]{6,5,4,3,2,1,0:T(8,128)(2,1)} %constant_dynamic-update-slice_fusion.29), channel_id=1, source_target_pairs={{0,16},{4,20},{8,24},{12,28},{16,0},{20,4},{24,8},{28,12},{1,17},{... | collective-permute-start | bytes 4718600 | tf_op jit(solution)/shard_map/ppermute | solution.py:35
  131.7 49.3 %collective-permute-start.17 = (bf16[1,1,2,2,2,128,512]{6,5,4,3,2,1,0:T(8,128)(2,1)S(1)}, bf16[1,1,2,2,2,128,512]{6,5,4,3,2,1,0:T(8,128)(2,1)}, u32[]{:S(2)}, u32[]{:S(2)}) collective-permute-start(bf16[1,1,2,2,2,128,512]{6,5,4,3,2,1,0:T(8,128)(2,1)S(1)} %constant_dynamic-update-slice_fusion.27), channel_id=1, source_target_pairs={{0,8},{4,12},{8,0},{12,4},{16,24},{20,28},{24,16},{28,20},{1,9},{5... | collective-permute-start | bytes 3145736 | tf_op jit(solution)/shard_map/ppermute | solution.py:35
  133.1 27.0 %collective-permute-start.16 = (bf16[256,1024]{1,0:T(8,128)(2,1)}, bf16[256,1024]{1,0:T(8,128)(2,1)}, u32[]{:S(2)}, u32[]{:S(2)}) collective-permute-start(bf16[256,1024]{1,0:T(8,128)(2,1)} %reorder.6), channel_id=1, source_target_pairs={{0,2},{1,3},{2,0},{3,1},{4,6},{5,7},{6,4},{7,5},{8,10},{9,11},{10,... | collective-permute-start | bytes 1572872 | tf_op jit(solution)/shard_map/ppermute | solution.py:35
  191.2 40.1 %collective-permute-start.21 = (bf16[1,2,2,2,2,128,768]{6,5,4,3,2,1,0:T(8,128)(2,1)S(1)}, bf16[1,2,2,2,2,128,768]{6,5,4,3,2,1,0:T(8,128)(2,1)}, u32[]{:S(2)}, u32[]{:S(2)}) collective-permute-start(bf16[1,2,2,2,2,128,768]{6,5,4,3,2,1,0:T(8,128)(2,1)S(1)} %constant_dynamic-update-slice_fusion.37), channel_id=1, source_target_pairs={{0,4},{4,0},{8,12},{12,8},{16,20},{20,16},{24,28},{28,24},{1,5},{5... | collective-permute-start | bytes 9437192 | tf_op jit(solution)/shard_map/ppermute | solution.py:35
  191.3 28.0 %collective-permute-start.20 = (bf16[1,2,2,2,2,128,512]{6,5,4,3,2,1,0:T(8,128)(2,1)}, bf16[1,2,2,2,2,128,512]{6,5,4,3,2,1,0:T(8,128)(2,1)}, u32[]{:S(2)}, u32[]{:S(2)}) collective-permute-start(bf16[1,2,2,2,2,128,512]{6,5,4,3,2,1,0:T(8,128)(2,1)} %constant_dynamic-update-slice_fusion.35), channel_id=1, source_target_pairs={{0,4},{4,0},{8,12},{12,8},{16,20},{20,16},{24,28},{28,24},{1,5},{5... | collective-permute-start | bytes 6291464 | tf_op jit(solution)/shard_map/ppermute | solution.py:35
  192.4 25.5 %collective-permute-start.19 = (bf16[512,1024]{1,0:T(8,128)(2,1)}, bf16[512,1024]{1,0:T(8,128)(2,1)}, u32[]{:S(2)}, u32[]{:S(2)}) collective-permute-start(bf16[512,1024]{1,0:T(8,128)(2,1)} %constant_dynamic-update-slice_fusion.33), channel_id=1, source_target_pairs={{0,1},{1,0},{2,3},{3,2},{4,5},{5,4},{6,7},{7,6},{8,9},{9,8},{10,11... | collective-permute-start | bytes 3145736 | tf_op jit(solution)/shard_map/ppermute | solution.py:35
  286.3 20.0 %collective-permute-start.22 = (bf16[4,4,128,1024]{3,2,1,0:T(8,128)(2,1)}, bf16[4,4,128,1024]{3,2,1,0:T(8,128)(2,1)}, u32[]{:S(2)}, u32[]{:S(2)}) collective-permute-start(bf16[4,4,128,1024]{3,2,1,0:T(8,128)(2,1)} %down_grad_send.1), channel_id=1, source_target_pairs={{0,4},{4,0},{8,12},{12,8},{16,20},{20,16},{24,28},{28,24},{1,5},{5... | collective-permute-start | bytes 12582920 | tf_op jit(solution)/shard_map/ppermute | solution.py:35
  319.4 25.6 %collective-permute-start.23 = (bf16[4,4,128,1024]{3,2,1,0:T(8,128)(2,1)}, bf16[4,4,128,1024]{3,2,1,0:T(8,128)(2,1)}, u32[]{:S(2)}, u32[]{:S(2)}) collective-permute-start(bf16[4,4,128,1024]{3,2,1,0:T(8,128)(2,1)} %up_grad_send.1), channel_id=1, source_target_pairs={{0,4},{4,0},{8,12},{12,8},{16,20},{20,16},{24,28},{28,24},{1,5},{5... | collective-permute-start | bytes 12582920 | tf_op jit(solution)/shard_map/ppermute | solution.py:35
  319.9 32.2 %collective-permute-start.25 = (bf16[2,4,128,512]{3,2,1,0:T(8,128)(2,1)}, bf16[2,4,128,512]{3,2,1,0:T(8,128)(2,1)S(1)}, u32[]{:S(2)}, u32[]{:S(2)}) collective-permute-start(bf16[2,4,128,512]{3,2,1,0:T(8,128)(2,1)} %get-tuple-element.287), channel_id=1, source_target_pairs={{0,16},{4,20},{8,24},{12,28},{16,0},{20,4},{24,8},{28,12},{1,17},{... | collective-permute-start | bytes 3145736 | tf_op jit(solution)/shard_map/ppermute | solution.py:35
  321.4 31.7 %collective-permute-start.24 = (bf16[2,4,128,512]{3,2,1,0:T(8,128)(2,1)S(1)}, bf16[2,4,128,512]{3,2,1,0:T(8,128)(2,1)}, u32[]{:S(2)}, u32[]{:S(2)}) collective-permute-start(bf16[2,4,128,512]{3,2,1,0:T(8,128)(2,1)S(1)} %copy-done.54), channel_id=1, source_target_pairs={{0,8},{4,12},{8,0},{12,4},{16,24},{20,28},{24,16},{28,20},{1,9},{5... | collective-permute-start | bytes 3145736 | tf_op jit(solution)/shard_map/ppermute | solution.py:35
  365.9 34.5 %collective-permute-start.26 = (bf16[4,4,128,1024]{3,2,1,0:T(8,128)(2,1)}, bf16[4,4,128,1024]{3,2,1,0:T(8,128)(2,1)S(1)}, u32[]{:S(2)}, u32[]{:S(2)}) collective-permute-start(bf16[4,4,128,1024]{3,2,1,0:T(8,128)(2,1)} %cross_grad_send.1), channel_id=1, source_target_pairs={{0,4},{4,0},{8,12},{12,8},{16,20},{20,16},{24,28},{28,24},{1,5},{5... | collective-permute-start | bytes 12582920 | tf_op jit(solution)/shard_map/ppermute | solution.py:35
  365.9 45.2 %collective-permute-start.28 = (bf16[2,4,128,512]{3,2,1,0:T(8,128)(2,1)}, bf16[2,4,128,512]{3,2,1,0:T(8,128)(2,1)S(1)}, u32[]{:S(2)}, u32[]{:S(2)}) collective-permute-start(bf16[2,4,128,512]{3,2,1,0:T(8,128)(2,1)} %get-tuple-element.306), channel_id=1, source_target_pairs={{0,16},{4,20},{8,24},{12,28},{16,0},{20,4},{24,8},{28,12},{1,17},{... | collective-permute-start | bytes 3145736 | tf_op jit(solution)/shard_map/ppermute | solution.py:35
  366.0 46.1 %collective-permute-start.27 = (bf16[2,4,128,512]{3,2,1,0:T(8,128)(2,1)}, bf16[2,4,128,512]{3,2,1,0:T(8,128)(2,1)}, u32[]{:S(2)}, u32[]{:S(2)}) collective-permute-start(bf16[2,4,128,512]{3,2,1,0:T(8,128)(2,1)} %get-tuple-element.282), channel_id=1, source_target_pairs={{0,8},{4,12},{8,0},{12,4},{16,24},{20,28},{24,16},{28,20},{1,9},{5... | collective-permute-start | bytes 3145736 | tf_op jit(solution)/shard_map/ppermute | solution.py:35
  367.3 49.8 %collective-permute-start.29 = (bf16[1,4,128,512]{3,2,1,0:T(8,128)(2,1)}, bf16[1,4,128,512]{3,2,1,0:T(8,128)(2,1)}, u32[]{:S(2)}, u32[]{:S(2)}) collective-permute-start(bf16[1,4,128,512]{3,2,1,0:T(8,128)(2,1)} %get-tuple-element.497), channel_id=1, source_target_pairs={{0,16},{4,20},{8,24},{12,28},{16,0},{20,4},{24,8},{28,12},{1,17},{... | collective-permute-start | bytes 1572872 | tf_op jit(solution)/shard_map/ppermute | solution.py:35
  368.8 49.5 %collective-permute-start.30 = (bf16[1,4,128,512]{3,2,1,0:T(8,128)(2,1)}, bf16[1,4,128,512]{3,2,1,0:T(8,128)(2,1)}, u32[]{:S(2)}, u32[]{:S(2)}) collective-permute-start(bf16[1,4,128,512]{3,2,1,0:T(8,128)(2,1)} %get-tuple-element.495), channel_id=1, source_target_pairs={{0,8},{4,12},{8,0},{12,4},{16,24},{20,28},{24,16},{28,20},{1,9},{5... | collective-permute-start | bytes 1572872 | tf_op jit(solution)/shard_map/ppermute | solution.py:35
  428.3 32.3 %collective-permute-start.31 = (bf16[4,4,128,1152]{3,2,1,0:T(8,128)(2,1)}, bf16[4,4,128,1152]{3,2,1,0:T(8,128)(2,1)}, u32[]{:S(2)}, u32[]{:S(2)}) collective-permute-start(bf16[4,4,128,1152]{3,2,1,0:T(8,128)(2,1)} %self_grad_send.1), channel_id=1, source_target_pairs={{0,4},{4,0},{8,12},{12,8},{16,20},{20,16},{24,28},{28,24},{1,5},{5... | collective-permute-start | bytes 14155784 | tf_op jit(solution)/shard_map/ppermute | solution.py:35
  431.3 40.9 %collective-permute-start.32 = (bf16[2,4,128,512]{3,2,1,0:T(8,128)(2,1)}, bf16[2,4,128,512]{3,2,1,0:T(8,128)(2,1)}, u32[]{:S(2)}, u32[]{:S(2)}) collective-permute-start(bf16[2,4,128,512]{3,2,1,0:T(8,128)(2,1)} %get-tuple-element.299), channel_id=1, source_target_pairs={{0,8},{4,12},{8,0},{12,4},{16,24},{20,28},{24,16},{28,20},{1,9},{5... | collective-permute-start | bytes 3145736 | tf_op jit(solution)/shard_map/ppermute | solution.py:35
  431.5 39.4 %collective-permute-start.33 = (bf16[2,4,128,512]{3,2,1,0:T(8,128)(2,1)}, bf16[2,4,128,512]{3,2,1,0:T(8,128)(2,1)}, u32[]{:S(2)}, u32[]{:S(2)}) collective-permute-start(bf16[2,4,128,512]{3,2,1,0:T(8,128)(2,1)} %get-tuple-element.325), channel_id=1, source_target_pairs={{0,16},{4,20},{8,24},{12,28},{16,0},{20,4},{24,8},{28,12},{1,17},{... | collective-permute-start | bytes 3145736 | tf_op jit(solution)/shard_map/ppermute | solution.py:35
  432.8 45.9 %collective-permute-start.34 = (bf16[1,4,128,512]{3,2,1,0:T(8,128)(2,1)}, bf16[1,4,128,512]{3,2,1,0:T(8,128)(2,1)S(1)}, u32[]{:S(2)}, u32[]{:S(2)}) collective-permute-start(bf16[1,4,128,512]{3,2,1,0:T(8,128)(2,1)} %get-tuple-element.493), channel_id=1, source_target_pairs={{0,16},{4,20},{8,24},{12,28},{16,0},{20,4},{24,8},{28,12},{1,17},{... | collective-permute-start | bytes 1572872 | tf_op jit(solution)/shard_map/ppermute | solution.py:35
  434.4 47.1 %collective-permute-start.35 = (bf16[1,4,128,512]{3,2,1,0:T(8,128)(2,1)}, bf16[1,4,128,512]{3,2,1,0:T(8,128)(2,1)S(1)}, u32[]{:S(2)}, u32[]{:S(2)}) collective-permute-start(bf16[1,4,128,512]{3,2,1,0:T(8,128)(2,1)} %get-tuple-element.491), channel_id=1, source_target_pairs={{0,8},{4,12},{8,0},{12,4},{16,24},{20,28},{24,16},{28,20},{1,9},{5... | collective-permute-start | bytes 1572872 | tf_op jit(solution)/shard_map/ppermute | solution.py:35
  460.6 22.0 %collective-permute-start.36 = (bf16[2,128,1024]{2,1,0:T(8,128)(2,1)S(1)}, bf16[2,128,1024]{2,1,0:T(8,128)(2,1)S(1)}, u32[]{:S(2)}, u32[]{:S(2)}) collective-permute-start(bf16[2,128,1024]{2,1,0:T(8,128)(2,1)S(1)} %copy-done.27), channel_id=1, source_target_pairs={{0,1},{1,0},{2,3},{3,2},{4,5},{5,4},{6,7},{7,6},{8,9},{9,8},{10,11... | collective-permute-start | bytes 1572872 | tf_op jit(solution)/shard_map/ppermute | solution.py:35
  470.9 18.4 %collective-permute-start.37 = (bf16[128,1024]{1,0:T(8,128)(2,1)}, bf16[128,1024]{1,0:T(8,128)(2,1)}, u32[]{:S(2)}, u32[]{:S(2)}) collective-permute-start(bf16[128,1024]{1,0:T(8,128)(2,1)} %get-tuple-element.516), channel_id=1, source_target_pairs={{1,0},{2,1},{3,2},{5,4},{6,5},{7,6},{9,8},{10,9},{11,10},{13,12},{... | collective-permute-start | bytes 786440 | tf_op jit(solution)/shard_map/ppermute | solution.py:1262
  472.2 23.0 %collective-permute-start.38 = (bf16[128,1024]{1,0:T(8,128)(2,1)S(1)}, bf16[128,1024]{1,0:T(8,128)(2,1)}, u32[]{:S(2)}, u32[]{:S(2)}) collective-permute-start(bf16[128,1024]{1,0:T(8,128)(2,1)S(1)} %get-tuple-element.517), channel_id=1, source_target_pairs={{2,0},{3,1},{6,4},{7,5},{10,8},{11,9},{14,12},{15,13},{18,16},{19,... | collective-permute-start | bytes 786440 | tf_op jit(solution)/shard_map/ppermute | solution.py:1261
  478.7 47.7 %collective-permute-start.42 = (bf16[2,256,1024]{2,1,0:T(8,128)(2,1)}, bf16[2,256,1024]{2,1,0:T(8,128)(2,1)}, u32[]{:S(2)}, u32[]{:S(2)}) collective-permute-start(bf16[2,256,1024]{2,1,0:T(8,128)(2,1)} %bitcast.66), channel_id=1, source_target_pairs={{0,1},{1,0},{2,3},{3,2},{4,5},{5,4},{6,7},{7,6},{8,9},{9,8},{10,11... | collective-permute-start | bytes 3145736 | tf_op jit(solution)/shard_map/ppermute | solution.py:35
  482.6 43.2 %collective-permute-start.41 = (bf16[2,128,1024]{2,1,0:T(8,128)(2,1)}, bf16[2,128,1024]{2,1,0:T(8,128)(2,1)S(1)}, u32[]{:S(2)}, u32[]{:S(2)}) collective-permute-start(bf16[2,128,1024]{2,1,0:T(8,128)(2,1)} %get-tuple-element.503), channel_id=1, source_target_pairs={{0,1},{1,0},{2,3},{3,2},{4,5},{5,4},{6,7},{7,6},{8,9},{9,8},{10,11... | collective-permute-start | bytes 1572872 | tf_op jit(solution)/shard_map/ppermute | solution.py:35
  483.5 36.4 %collective-permute-start.40 = (bf16[1,128,1024]{2,1,0:T(8,128)(2,1)}, bf16[1,128,1024]{2,1,0:T(8,128)(2,1)}, u32[]{:S(2)}, u32[]{:S(2)}) collective-permute-start(bf16[1,128,1024]{2,1,0:T(8,128)(2,1)} %get-tuple-element.519), channel_id=1, source_target_pairs={{0,2},{1,3},{2,0},{3,1},{4,6},{5,7},{6,4},{7,5},{8,10},{9,11},{10,... | collective-permute-start | bytes 786440 | tf_op jit(solution)/shard_map/ppermute | solution.py:35
  489.3 39.4 %collective-permute-start.44 = (bf16[1,4,128,512]{3,2,1,0:T(8,128)(2,1)}, bf16[1,4,128,512]{3,2,1,0:T(8,128)(2,1)}, u32[]{:S(2)}, u32[]{:S(2)}) collective-permute-start(bf16[1,4,128,512]{3,2,1,0:T(8,128)(2,1)} %get-tuple-element.487), channel_id=1, source_target_pairs={{0,8},{4,12},{8,0},{12,4},{16,24},{20,28},{24,16},{28,20},{1,9},{5... | collective-permute-start | bytes 1572872 | tf_op jit(solution)/shard_map/ppermute | solution.py:35
  501.2 28.3 %collective-permute-start.43 = (bf16[1,4,128,512]{3,2,1,0:T(8,128)(2,1)S(1)}, bf16[1,4,128,512]{3,2,1,0:T(8,128)(2,1)S(1)}, u32[]{:S(2)}, u32[]{:S(2)}) collective-permute-start(bf16[1,4,128,512]{3,2,1,0:T(8,128)(2,1)S(1)} %copy-done.28), channel_id=1, source_target_pairs={{0,16},{4,20},{8,24},{12,28},{16,0},{20,4},{24,8},{28,12},{1,17},{... | collective-permute-start | bytes 1572872 | tf_op jit(solution)/shard_map/ppermute | solution.py:35
  519.9 24.0 %collective-permute-start.45 = (bf16[2,4,128,512]{3,2,1,0:T(8,128)(2,1)}, bf16[2,4,128,512]{3,2,1,0:T(8,128)(2,1)S(1)}, u32[]{:S(2)}, u32[]{:S(2)}) collective-permute-start(bf16[2,4,128,512]{3,2,1,0:T(8,128)(2,1)} %get-tuple-element.320), channel_id=1, source_target_pairs={{0,8},{4,12},{8,0},{12,4},{16,24},{20,28},{24,16},{28,20},{1,9},{5... | collective-permute-start | bytes 3145736 | tf_op jit(solution)/shard_map/ppermute | solution.py:35
  525.8 29.6 %collective-permute-start.46 = (bf16[2,4,128,640]{3,2,1,0:T(8,128)(2,1)}, bf16[2,4,128,640]{3,2,1,0:T(8,128)(2,1)S(1)}, u32[]{:S(2)}, u32[]{:S(2)}) collective-permute-start(bf16[2,4,128,640]{3,2,1,0:T(8,128)(2,1)} %get-tuple-element.360), channel_id=1, source_target_pairs={{0,16},{4,20},{8,24},{12,28},{16,0},{20,4},{24,8},{28,12},{1,17},{... | collective-permute-start | bytes 3932168 | tf_op jit(solution)/shard_map/ppermute | solution.py:35
  526.4 29.7 %collective-permute-start.47 = (f32[17920]{0:T(1024)S(1)}, f32[17920]{0:T(1024)S(1)}, u32[]{:S(2)}, u32[]{:S(2)}) collective-permute-start(f32[17920]{0:T(1024)S(1)} %add.226), channel_id=1, source_target_pairs={{0,8},{4,12},{8,0},{12,4},{16,24},{20,28},{24,16},{28,20},{1,9},{5... | collective-permute-start | bytes 215048 | tf_op jit(solution)/shard_map/ppermute | solution.py:35
  528.6 28.0 %collective-permute-start.48 = (bf16[1,128,1024]{2,1,0:T(8,128)(2,1)S(1)}, bf16[1,128,1024]{2,1,0:T(8,128)(2,1)S(1)}, u32[]{:S(2)}, u32[]{:S(2)}) collective-permute-start(bf16[1,128,1024]{2,1,0:T(8,128)(2,1)S(1)} %get-tuple-element.515), channel_id=1, source_target_pairs={{0,2},{1,3},{2,0},{3,1},{4,6},{5,7},{6,4},{7,5},{8,10},{9,11},{10,... | collective-permute-start | bytes 786440 | tf_op jit(solution)/shard_map/ppermute | solution.py:35
  531.0 26.5 %collective-permute-start.49 = (bf16[2,128,1024]{2,1,0:T(8,128)(2,1)S(1)}, bf16[2,128,1024]{2,1,0:T(8,128)(2,1)S(1)}, u32[]{:S(2)}, u32[]{:S(2)}) collective-permute-start(bf16[2,128,1024]{2,1,0:T(8,128)(2,1)S(1)} %get-tuple-element.501), channel_id=1, source_target_pairs={{0,1},{1,0},{2,3},{3,2},{4,5},{5,4},{6,7},{7,6},{8,9},{9,8},{10,11... | collective-permute-start | bytes 1572872 | tf_op jit(solution)/shard_map/ppermute | solution.py:35
  543.9 23.2 %collective-permute-start.50 = (bf16[256,1024]{1,0:T(8,128)(2,1)S(1)}, bf16[256,1024]{1,0:T(8,128)(2,1)S(1)}, u32[]{:S(2)}, u32[]{:S(2)}) collective-permute-start(bf16[256,1024]{1,0:T(8,128)(2,1)S(1)} %slice_bitcast_fusion), channel_id=1, source_target_pairs={{0,2},{1,3},{2,0},{3,1},{4,6},{5,7},{6,4},{7,5},{8,10},{9,11},{10,... | collective-permute-start | bytes 1572872 | tf_op jit(solution)/shard_map/ppermute | solution.py:35
  571.7 21.6 %collective-permute-start.55 = (bf16[2,128,1152]{2,1,0:T(8,128)(2,1)S(1)}, bf16[2,128,1152]{2,1,0:T(8,128)(2,1)S(1)}, u32[]{:S(2)}, u32[]{:S(2)}) collective-permute-start(bf16[2,128,1152]{2,1,0:T(8,128)(2,1)S(1)} %get-tuple-element.499), channel_id=1, source_target_pairs={{0,1},{1,0},{2,3},{3,2},{4,5},{5,4},{6,7},{7,6},{8,9},{9,8},{10,11... | collective-permute-start | bytes 1769480 | tf_op jit(solution)/shard_map/ppermute | solution.py:35
  574.5 17.9 %collective-permute-start.54 = (bf16[1,128,1024]{2,1,0:T(8,128)(2,1)S(1)}, bf16[1,128,1024]{2,1,0:T(8,128)(2,1)S(1)}, u32[]{:S(2)}, u32[]{:S(2)}) collective-permute-start(bf16[1,128,1024]{2,1,0:T(8,128)(2,1)S(1)} %copy-done.30), channel_id=1, source_target_pairs={{0,2},{1,3},{2,0},{3,1},{4,6},{5,7},{6,4},{7,5},{8,10},{9,11},{10,... | collective-permute-start | bytes 786440 | tf_op jit(solution)/shard_map/ppermute | solution.py:35
  (68 other events, 454.4 us)
Sparse Core Ops, SparseCore 0:
  128.6 114.6 all-gather.2
  323.3 63.5 all-gather.4

commit v3 on v2

--- a/solution.py
+++ b/solution.py
@@ -59,6 +59,58 @@
         return values[0]
 
 
+def chunk_of(rows):
+    return rows // 4 if rows % 64 == 0 else rows
+
+
+def stack_rows(*arrays):
+    rows = [array.shape[0] for array in arrays]
+
+    def body(*refs):
+        at = 0
+        for ref, count in zip(refs, rows):
+            refs[-1][at : at + count] = ref[...]
+            at += count
+
+    return pl.pallas_call(
+        body,
+        out_shape=jax.ShapeDtypeStruct((sum(rows), arrays[0].shape[1]), arrays[0].dtype),
+        compiler_params=params(),
+        name="stack_rows",
+    )(*arrays)
+
+
+def add_blocks(parts, outs, dtype):
+    rows = parts[0][0].shape[1]
+    chunk = chunk_of(rows) if parts[0][0].size >= 1 << 20 else rows
+    widths = [mine.shape[2] for mine, _ in parts]
+
+    def body(*refs):
+        ins, out_refs = refs[: 2 * len(parts)], refs[2 * len(parts) :]
+        for out_ref, (members, chosen) in zip(out_refs, outs):
+            at = 0
+            for part in chosen:
+                mine_ref, came_ref = ins[2 * part], ins[2 * part + 1]
+                for place, block in enumerate(members):
+                    total = mine_ref[block].astype(F32) + came_ref[block].astype(F32)
+                    out_ref[place, :, at : at + widths[part]] = total.astype(dtype)
+                at += widths[part]
+
+    def spec(count, width):
+        return pl.BlockSpec((count, chunk, width), lambda i: (0, i, 0))
+
+    shapes = [(len(members), sum(widths[part] for part in chosen)) for members, chosen in outs]
+    return pl.pallas_call(
+        body,
+        grid=(rows // chunk,),
+        in_specs=[spec(array.shape[0], array.shape[2]) for pair in parts for array in pair],
+        out_specs=[spec(*shape) for shape in shapes],
+        out_shape=[jax.ShapeDtypeStruct((count, rows, width), dtype) for count, width in shapes],
+        compiler_params=params(),
+        name="add_blocks",
+    )(*[array for pair in parts for array in pair])
+
+
 class Gather:
     def __init__(self, line, shard):
         self.line = line
@@ -71,7 +123,7 @@
 
     def take(self):
         mine = self.line.tie(self.buf)
-        self.buf = self.line.mark(jnp.concatenate([mine, self.came], self.axis))
+        self.buf = self.line.mark(jnp.concatenate([mine, after(self.came, mine)], self.axis))
 
     def columns(self, first, count):
         part = Gather.__new__(Gather)
@@ -85,11 +137,11 @@
 
 
 class Scatter:
-    def __init__(self, line, parts, orders):
+    def __init__(self, line, parts, orders, natural=False):
+        self.natural = natural
         nb, self.nz = bits_of("batch"), bits_of("head")
         self.line = line
-        self.groups = parts[0][1].shape[1]
-        self.blk = parts[0][1].shape[2]
+        self.groups, self.blk = parts[0][1].shape[1:3]
         self.left = [list(order) for order in orders]
         self.names = [sorted(order) for order in orders]
         self.heads = list(range(self.nz))
@@ -106,34 +158,58 @@
     def step(self):
         tied = [self.line.tie(mine) for mine in self.mine]
         came = [after(came, mine) for came, mine in zip(self.came, tied)]
+        pairs = [
+            (one.reshape(-1, self.blk, one.shape[-1]), two.reshape(-1, self.blk, one.shape[-1]))
+            for one, two in zip(tied, came)
+        ]
+        blocks = range(pairs[0][0].shape[0])
+        everyone = list(range(len(pairs)))
         if self.left[0]:
-            halves = []
-            for number, (old, new) in enumerate(zip(tied, came)):
-                inner = (2,) * len(self.names[number]) + (self.groups, self.blk, old.shape[-1])
-                axis = self.names[number].index(self.left[number][0])
-
-                def added(side):
-                    one = lax.index_in_dim(old.reshape(inner), side, axis, keepdims=False)
-                    two = lax.index_in_dim(new.reshape(inner), side, axis, keepdims=False)
-                    total = (one.astype(F32) + two.astype(F32)).astype(BF)
-                    return pin(total.reshape(-1, self.groups, self.blk, old.shape[-1]))
-
-                halves.append((added(1), added(0)))
-            self.line.mark(*[half for pair in halves for half in pair])
-            for number, (theirs, mine) in enumerate(halves):
-                self.send(number, theirs, mine)
+            outs = []
+            for number in everyone:
+                place = self.names[number].index(self.left[number][0])
+                bit = len(self.names[number]) - 1 - place
+                for side in (1, 0):
+                    chosen = [k for k in blocks if (k // self.groups >> bit & 1) == side]
+                    outs.append((chosen, [number]))
+            sums = add_blocks(pairs, outs, BF)
+            self.line.mark(*sums)
+            for number in everyone:
+                self.send(number, sums[2 * number], sums[2 * number + 1])
             return
-        sums = [one.astype(F32) + two.astype(F32) for one, two in zip(tied, came)]
-        total = sums[0] if len(sums) == 1 else jnp.concatenate(sums, -1)
+        if self.natural:
+            (total,) = add_blocks(pairs, [(list(blocks), everyone)], BF)
+            total = lax.psum_scatter(
+                self.line.mark(total), "head", scatter_dimension=0, tiled=False
+            )
+            self.total = total.astype(F32)
+            return
         if not self.heads:
-            self.total = self.line.mark(pin(total.reshape(self.blk, -1)))
+            (total,) = add_blocks(pairs, [([0], everyone)], F32)
+            self.total = self.line.mark(total).reshape(self.blk, -1)
             return
         bit = self.heads.pop(0)
-        total = total.astype(BF).reshape((-1, 2, self.blk, total.shape[-1]))
-        theirs, mine = pin(total[:, 1]), pin(total[:, 0])
+        sides = [[k for k in blocks if (k & 1) == side] for side in (1, 0)]
+        theirs, mine = add_blocks(pairs, [(side, everyone) for side in sides], BF)
         self.line.mark(theirs, mine)
         self.mine = [mine]
         self.came = [swap(theirs, "head", 1 << bit)]
+
+
+def add_halo(own, one, two):
+    count = one.shape[0]
+
+    def body(own_ref, one_ref, two_ref, out_ref):
+        out_ref[count:] = own_ref[count:]
+        came = one_ref[...].astype(F32) + two_ref[...].astype(F32)
+        out_ref[0:count] = own_ref[0:count] + came
+
+    return pl.pallas_call(
+        body,
+        out_shape=jax.ShapeDtypeStruct(own.shape, own.dtype),
+        compiler_params=params(),
+        name="add_halo",
+    )(own, one, two)
 
 
 def bit_reverse(number, width):
@@ -536,7 +612,7 @@
 
     def body(left_ref, *refs):
         piece_refs = refs[:count]
-        out_ref, acc_ref = refs[count:]
+        low_ref, high_ref, acc_ref = refs[count:]
         step = pl.program_id(0)
 
         @pl.when(step == 0)
@@ -547,15 +623,16 @@
 
         @pl.when(step == groups - 1)
         def _():
-            out_ref[...] = acc_ref[...].astype(BF)
+            low_ref[...] = acc_ref[0 : rows // 2].astype(BF)
+            high_ref[...] = acc_ref[rows // 2 :].astype(BF)
 
     return pl.pallas_call(
         body,
         grid=(groups,),
         in_specs=[pl.BlockSpec((rows, cols), lambda j: (0, j))]
         + piece_specs(pieces, cols, first_col // cols),
-        out_specs=whole((rows, features)),
-        out_shape=jax.ShapeDtypeStruct((rows, features), BF),
+        out_specs=[whole((rows // 2, features))] * 2,
+        out_shape=[jax.ShapeDtypeStruct((rows // 2, features), BF)] * 2,
         scratch_shapes=[pltpu.VMEM((rows, features), F32)],
         compiler_params=params(),
         name=name,
@@ -573,7 +650,7 @@
 
     def body(query_ref, kv_ref, rel_ref, *refs):
         parts = [refs[count * k : count * (k + 1)] for k in range(4)]
-        first_ref, halo_ref, own_ref, acc_ref = refs[4 * count :]
+        first_ref, two_ref, one_ref, own_ref, acc_ref = refs[4 * count :]
         step = pl.program_id(0)
 
         @pl.when(step == 0)
@@ -589,7 +666,8 @@
 
         @pl.when(step == groups - 1)
         def _():
-            halo_ref[...] = acc_ref[0:halo].astype(BF)
+            two_ref[...] = acc_ref[0 : halo // 2].astype(BF)
+            one_ref[...] = acc_ref[halo // 2 : halo].astype(BF)
             own_ref[...] = acc_ref[halo:]
 
     return pl.pallas_call(
@@ -605,9 +683,10 @@
         + piece_specs(others, width, 0)
         + piece_specs(others, rel_width, width // rel_width)
         + [whole((rows, features))],
-        out_specs=[whole((halo, features)), whole((rows, features))],
+        out_specs=[whole((halo // 2, features))] * 2 + [whole((rows, features))],
         out_shape=[
-            jax.ShapeDtypeStruct((halo, features), BF),
+            jax.ShapeDtypeStruct((halo // 2, features), BF),
+            jax.ShapeDtypeStruct((halo // 2, features), BF),
             jax.ShapeDtypeStruct((rows, features), F32),
         ],
         scratch_shapes=[pltpu.VMEM((long_rows, features), F32)],
@@ -616,7 +695,7 @@
     )(grad_query, grad_kv, grad_rel, *pieces, *pieces, *others, *others, first)
 
 
-def weight_products(entries, half, extra, parts, pieces, groups, name):
+def weight_products(order, entries, half, extra, parts, pieces, groups, name):
     features = entries[0][0].shape[1]
     depth = features // 2
     blk = depth // pieces
@@ -633,7 +712,7 @@
                 outs.append((at, width, [p for p in range(pieces) if (p >> bit & 1) == side]))
             at += width
 
-    def body(*refs):
+    def body(order_ref, *refs):
         lefts, rights = refs[:count], refs[count : 2 * count]
         out_refs = refs[len(refs) - len(outs) :]
         at = 0
@@ -653,11 +732,13 @@
             at += width
 
     def block(number, width):
-        return pl.BlockSpec((number, 1, blk, width), lambda j: (0, j, 0, 0))
-
-    in_specs = [pl.BlockSpec((left.shape[0], depth), lambda j: (0, half)) for left, _ in entries]
+        return pl.BlockSpec((number, 1, blk, width), lambda j, order: (0, j, 0, 0))
+
+    in_specs = [
+        pl.BlockSpec((left.shape[0], depth), lambda j, order: (0, half)) for left, _ in entries
+    ]
     in_specs += [
-        pl.BlockSpec((right.shape[0], width), lambda j: (0, j))
+        pl.BlockSpec((right.shape[0], width), lambda j, order: (0, order[j]))
         for (_, right), width in zip(entries, widths)
     ]
     operands = [left for left, _ in entries] + [right for _, right in entries]
@@ -666,16 +747,19 @@
         operands.append(extra)
     return pl.pallas_call(
         body,
-        grid=(groups,),
-        in_specs=in_specs,
-        out_specs=[block(len(members), width) for _, width, members in outs],
+        grid_spec=pltpu.PrefetchScalarGridSpec(
+            num_scalar_prefetch=1,
+            grid=(groups,),
+            in_specs=in_specs,
+            out_specs=[block(len(members), width) for _, width, members in outs],
+        ),
         out_shape=[
             jax.ShapeDtypeStruct((len(members), groups, blk, width), BF)
             for _, width, members in outs
         ],
         compiler_params=params(),
         name=name,
-    )(*operands)
+    )(order, *operands)
 
 
 def half_masks(rows):
@@ -686,13 +770,48 @@
     ]
 
 
-def skew(array_in, share):
-    rows, width = array_in.shape
-    parts = [
-        pltpu.roll(array_in[n * share : (n + 1) * share], width - share + 1, 1, stride=1, stride_axis=0)
-        for n in range(rows // share)
-    ]
-    return jnp.concatenate(parts, 0)
+def lanes_and_rows(share):
+    lane = lax.broadcasted_iota(jnp.int32, (share, share), 1)
+    row = lax.broadcasted_iota(jnp.int32, (share, share), 0)
+    return lane > row
+
+
+def turn_right(block):
+    return pltpu.roll(block, 1, 1, stride=1, stride_axis=0)
+
+
+def skew(distance, later):
+    share = later.shape[0]
+    tracks = []
+    for n in range(distance.shape[0] // share):
+        rows = slice(n * share, (n + 1) * share)
+        far, near = turn_right(distance[rows, 0:share]), turn_right(distance[rows, share:])
+        tracks.append(jnp.concatenate([far, jnp.where(later, near, far), near], 1))
+    return jnp.concatenate(tracks, 0)
+
+
+def unskew_sources(grid, later):
+    share = later.shape[0]
+    tracks = []
+    for n in range(grid.shape[0] // share):
+        old, mid, new = [
+            grid[n * share : (n + 1) * share, c * share : (c + 1) * share] for c in range(3)
+        ]
+        tracks.append(jnp.concatenate([jnp.where(later, old, mid), jnp.where(later, mid, new)], 1))
+    return jnp.concatenate(tracks, 0)
+
+
+def turn_blocks(array_in, share):
+    rows = array_in.shape[0]
+    return jnp.concatenate(
+        [
+            jnp.concatenate(
+                [turn_right(array_in[r : r + share, c : c + share]) for c in (0, share)], 1
+            )
+            for r in range(0, rows, share)
+        ],
+        0,
+    )
 
 
 def self_attention(qk, values, relpos, mask, turned, share):
@@ -701,13 +820,15 @@
     long_rows = qk.shape[0]
     halo = long_rows - rows
 
-    def body(q_ref, k_ref, v_ref, rel_ref, mask_ref, turned_ref, ctx_ref, probs_ref, own_ref):
+    def body(q_ref, k_ref, v_ref, rel_ref, mask_ref, turned_ref, ctx_ref, raised_ref, own_ref):
         halves = half_masks(rows)
+        later = lanes_and_rows(share)
         lane = lax.broadcasted_iota(jnp.int32, (rows, 128), 1)
         rel = rel_ref[...]
         high = rel.astype(BF)
         split = jnp.concatenate([high, (rel - high.astype(F32)).astype(BF)], 1)
-        row_id = lax.broadcasted_iota(jnp.int32, (256, window), 0) & 127
+        row_id = lax.broadcasted_iota(jnp.int32, (256, 2 * share), 0) & 127
+        track = lax.broadcasted_iota(jnp.int32, (rows, 1), 0) >= share
         own_all = jnp.zeros((rows, 128), F32)
         for pair in range(2):
             cols = slice(128 * pair, 128 * pair + 128)
@@ -721,21 +842,20 @@
                 head = 2 * pair + half
                 scores = dot(q * halves[half].astype(BF), k, 1, 1)
                 table = jnp.where(row_id == turned_ref[...] + 32 * head, 1.0, 0.0).astype(BF)
-                scores = scores + skew(dot(split, table, 1, 0), share) + mask_ref[...]
+                scores = scores + skew(dot(split, table, 1, 0), later) + mask_ref[...]
                 own = jnp.sum(
                     product * halves[half] + jnp.where(lane == 32 * head, rel, 0.0), -1, keepdims=True
                 )
-                track = lax.broadcasted_iota(jnp.int32, (rows, 1), 0) >= share
                 own = jnp.where(track, own, MASKED)
                 top = jnp.maximum(jnp.max(scores, -1, keepdims=True), own)
                 raised = jnp.exp(scores - top)
                 own_raised = jnp.exp(own - top)
                 scale = 1.0 / (jnp.sum(raised, -1, keepdims=True) + own_raised)
-                probs = (raised * scale).astype(BF)
-                own_probs = (own_raised * scale).astype(BF).astype(F32)
-                probs_ref[head] = probs
-                own_all = jnp.where(lane == head, own_probs, own_all)
-                mixed = mixed + (dot(probs, v, 1, 0) + own_probs * own_v) * halves[half]
+                raised = raised.astype(BF)
+                raised_ref[head] = raised
+                own_all = jnp.where(lane == head, own_raised, own_all)
+                own_all = jnp.where(lane == head + 4, scale, own_all)
+                mixed = mixed + (dot(raised, v, 1, 0) + own_raised * own_v) * (scale * halves[half])
             ctx_ref[:, cols] = mixed.astype(BF)
         own_ref[...] = own_all
 
@@ -748,7 +868,7 @@
             pl.BlockSpec((long_rows, 256), lambda j: (0, j)),
             pl.BlockSpec((rows, 128), lambda j: (0, j)),
             whole((rows, window)),
-            whole((1, window)),
+            whole((1, 2 * share)),
         ],
         out_specs=[
             pl.BlockSpec((rows, 256), lambda j: (0, j)),
@@ -765,35 +885,43 @@
     )(qk, qk, values, relpos, mask, turned)
 
 
-def self_attention_back(qk, values, probs, own_probs, grad_ctx, straight, share):
+def self_attention_back(qk, values, raised, own_raised, grad_ctx, straight, share):
     rows, window = 3 * share, 3 * share
     groups = values.shape[1] // 256
     long_rows = qk.shape[0]
     halo = long_rows - rows
 
     def body(
-        q_ref, k_ref, v_ref, probs_ref, own_ref, grad_ref, straight_ref,
+        q_ref, k_ref, v_ref, raised_ref, own_ref, grad_ref, straight_ref,
         gq_ref, gkv_ref, grel_ref, sums_ref, rel_sums_ref,
     ):
         halves = half_masks(rows)
+        later = lanes_and_rows(share)
         lane = lax.broadcasted_iota(jnp.int32, (rows, 128), 1)
         turn = jnp.where(
-            lax.broadcasted_iota(jnp.int32, (window, window), 0)
-            + lax.broadcasted_iota(jnp.int32, (window, window), 1)
-            == window - 1,
+            lax.broadcasted_iota(jnp.int32, (2 * share, 2 * share), 0)
+            + lax.broadcasted_iota(jnp.int32, (2 * share, 2 * share), 1)
+            == 2 * share - 1,
             1.0,
             0.0,
         ).astype(BF)
-        column = lax.broadcasted_iota(jnp.int32, (window, 128), 1)
+        column = lax.broadcasted_iota(jnp.int32, (2 * share, 128), 1)
         grel = jnp.zeros((rows, 128), F32)
+        own_all = own_ref[...]
+
+        def pick(number):
+            return jnp.sum(jnp.where(lane == number, own_all, 0.0), -1, keepdims=True)
+
         for pair in range(2):
             cols = slice(128 * pair, 128 * pair + 128)
             q = q_ref[halo:, cols]
             k, v = k_ref[0:window, cols], v_ref[0:window, cols]
             own_k = k_ref[halo:, cols].astype(F32)
             own_v = v_ref[halo:, cols].astype(F32)
-            grad = grad_ref[:, cols]
-            grad_wide = grad.astype(F32)
+            scales = [pick(2 * pair + half + 4) for half in range(2)]
+            grad_wide = grad_ref[:, cols].astype(F32)
+            grad_wide = grad_wide * (scales[0] * halves[0] + scales[1] * halves[1])
+            grad = grad_wide.astype(BF)
             own_product = grad_wide * own_v
             gq = jnp.zeros((rows, 128), F32)
             own_spread = jnp.zeros((rows, 128), F32)
@@ -802,14 +930,17 @@
             for half in range(2):
                 head = 2 * pair + half
                 low_half = halves[half].astype(BF)
-                p = probs_ref[head]
+                p = raised_ref[head]
                 p_wide = p.astype(F32)
                 grad_half = grad * low_half
                 grad_probs = dot(grad_half, v, 1, 1)
-                own_p = jnp.sum(jnp.where(lane == head, own_ref[...], 0.0), -1, keepdims=True)
+                own_p = pick(head)
                 own_grad = jnp.sum(own_product * halves[half], -1, keepdims=True)
                 row_dot = jnp.sum(p_wide * grad_probs, -1, keepdims=True) + own_p * own_grad
-                grad_scores = (p_wide * (grad_probs - row_dot)).astype(BF)
+                row_dot = row_dot * scales[half]
+                grad_scores = p_wide * (grad_probs - row_dot)
+                source = unskew_sources(grad_scores, later).astype(BF)
+                grad_scores = grad_scores.astype(BF)
                 grad_own = (own_p * (own_grad - row_dot)).astype(BF).astype(F32)
                 gq = gq + (dot(grad_scores, k, 1, 0) + grad_own * own_k) * halves[half]
                 own_spread = own_spread + grad_own * halves[half]
@@ -818,7 +949,7 @@
                 prob_parts.append(p)
                 q_parts.append(q * low_half)
                 g_parts.append(grad_half)
-                turned = skew(dot(grad_scores, turn, 1, 0), share).astype(BF)
+                turned = turn_blocks(dot(source, turn, 1, 0), share).astype(BF)
                 table = jnp.where(column == straight_ref[...] + 32 * head, 1.0, 0.0).astype(BF)
                 grel = grel + dot(turned, table, 1, 0) + jnp.where(lane == 32 * head, grad_own, 0.0)
             gk = dot(
@@ -851,7 +982,7 @@
             pl.BlockSpec((4, rows, window), lambda j: (j, 0, 0)),
             pl.BlockSpec((rows, 128), lambda j: (0, j)),
             pl.BlockSpec((rows, 256), lambda j: (0, j)),
-            whole((window, 1)),
+            whole((2 * share, 1)),
         ],
         out_specs=[
             pl.BlockSpec((rows, 256), lambda j: (0, j)),
@@ -869,26 +1000,32 @@
         ],
         compiler_params=params(),
         name="self_attention_back",
-    )(qk, qk, values, probs, own_probs, grad_ctx, straight)
+    )(qk, qk, values, raised, own_raised, grad_ctx, straight)
 
 
 def cross_attention(queries, kv):
     rows, places = queries.shape[0], kv.shape[0]
     groups = queries.shape[1] // 256
 
-    def body(q_ref, k_ref, v_ref, ctx_ref, probs_ref):
+    def body(q_ref, k_ref, v_ref, ctx_ref, raised_ref, scale_ref):
         halves = half_masks(rows)
+        lane = lax.broadcasted_iota(jnp.int32, (rows, 128), 1)
+        scales = jnp.zeros((rows, 128), F32)
         for pair in range(2):
             cols = slice(128 * pair, 128 * pair + 128)
             q, k, v = q_ref[:, cols], k_ref[:, cols], v_ref[:, cols]
             mixed = jnp.zeros((rows, 128), F32)
             for half in range(2):
+                head = 2 * pair + half
                 scores = dot(q * halves[half].astype(BF), k, 1, 1)
                 raised = jnp.exp(scores - jnp.max(scores, -1, keepdims=True))
-                probs = (raised * (1.0 / jnp.sum(raised, -1, keepdims=True))).astype(BF)
-                probs_ref[2 * pair + half] = probs
-                mixed = mixed + dot(probs, v, 1, 0) * halves[half]
+                scale = 1.0 / jnp.sum(raised, -1, keepdims=True)
+                raised = raised.astype(BF)
+                raised_ref[head] = raised
+                scales = jnp.where(lane == head, scale, scales)
+                mixed = mixed + dot(raised, v, 1, 0) * (scale * halves[half])
             ctx_ref[:, cols] = mixed.astype(BF)
+        scale_ref[...] = scales
 
     return pl.pallas_call(
         body,
@@ -901,34 +1038,44 @@
         out_specs=[
             pl.BlockSpec((rows, 256), lambda j: (0, j)),
             pl.BlockSpec((4, rows, places), lambda j: (j, 0, 0)),
+            pl.BlockSpec((rows, 128), lambda j: (0, j)),
         ],
         out_shape=[
             jax.ShapeDtypeStruct((rows, groups * 256), BF),
             jax.ShapeDtypeStruct((4 * groups, rows, places), BF),
+            jax.ShapeDtypeStruct((rows, groups * 128), F32),
         ],
         compiler_params=params(),
         name="cross_attention",
     )(queries, kv, kv)
 
 
-def cross_attention_back(queries, kv, probs, grad_ctx):
+def cross_attention_back(queries, kv, raised, scales, grad_ctx):
     rows, places = queries.shape[0], kv.shape[0]
     groups = queries.shape[1] // 256
 
-    def body(q_ref, k_ref, v_ref, probs_ref, grad_ref, gq_ref, gkv_ref, sums_ref):
+    def body(q_ref, k_ref, v_ref, raised_ref, scale_ref, grad_ref, gq_ref, gkv_ref, sums_ref):
         halves = half_masks(rows)
+        lane = lax.broadcasted_iota(jnp.int32, (rows, 128), 1)
+        scale_all = scale_ref[...]
         for pair in range(2):
             cols = slice(128 * pair, 128 * pair + 128)
-            q, k, v, grad = q_ref[:, cols], k_ref[:, cols], v_ref[:, cols], grad_ref[:, cols]
+            q, k, v = q_ref[:, cols], k_ref[:, cols], v_ref[:, cols]
+            scale = [
+                jnp.sum(jnp.where(lane == 2 * pair + half, scale_all, 0.0), -1, keepdims=True)
+                for half in range(2)
+            ]
+            grad = grad_ref[:, cols].astype(F32) * (scale[0] * halves[0] + scale[1] * halves[1])
+            grad = grad.astype(BF)
             gq = jnp.zeros((rows, 128), F32)
             score_parts, prob_parts, q_parts, g_parts = [], [], [], []
             for half in range(2):
                 low_half = halves[half].astype(BF)
-                p = probs_ref[2 * pair + half]
+                p = raised_ref[2 * pair + half]
                 p_wide = p.astype(F32)
                 grad_half = grad * low_half
                 grad_probs = dot(grad_half, v, 1, 1)
-                row_dot = jnp.sum(p_wide * grad_probs, -1, keepdims=True)
+                row_dot = jnp.sum(p_wide * grad_probs, -1, keepdims=True) * scale[half]
                 grad_scores = (p_wide * (grad_probs - row_dot)).astype(BF)
                 gq = gq + dot(grad_scores, k, 1, 0) * halves[half]
                 score_parts.append(grad_scores)
@@ -957,6 +1104,7 @@
             pl.BlockSpec((places, 256), lambda j: (0, 2 * j)),
             pl.BlockSpec((places, 256), lambda j: (0, 2 * j + 1)),
             pl.BlockSpec((4, rows, places), lambda j: (j, 0, 0)),
+            pl.BlockSpec((rows, 128), lambda j: (0, j)),
             pl.BlockSpec((rows, 256), lambda j: (0, j)),
         ],
         out_specs=[
@@ -971,7 +1119,7 @@
         ],
         compiler_params=params(),
         name="cross_attention_back",
-    )(queries, kv, kv, probs, grad_ctx)
+    )(queries, kv, kv, raised, scales, grad_ctx)
 
 
 def per_device(
@@ -1021,10 +1169,15 @@
         return jnp.take(blocks, to_exchange, axis=1).reshape(count, features)
 
     blk = self_weight.shape[0]
+    assert nb >= 2 and bits_of("head") == 2
     line = Line()
     self_shard = jnp.concatenate([self_weight.reshape(blk, -1), relpos_weight], 1).astype(BF)
     gather_self = Gather(line, line.mark(pin(self_shard)))
     gather_self.send("head", 1)
+    ffn_shard = line.mark(
+        pin(jnp.concatenate([line.tie(up_weight), down_weight], 1).astype(BF))
+    )
+    gather_ffn = Gather(line, ffn_shard)
 
     columns = jnp.concatenate(
         [
@@ -1044,7 +1197,6 @@
     up_row = columns[:, 1152:].reshape(1, -1)
 
     memory_own = line.mark(reorder_blocks(line.tie(memory[0]), to_exchange))
-    ffn_shard = jnp.concatenate([up_weight, down_weight], 1).astype(BF)
     own = jnp.transpose(line.tie(hidden[0]), (1, 0, 2)).reshape(rows, features)
     own = line.mark(reorder_blocks(own, to_exchange))
     upstream = lax.dynamic_slice_in_dim(line.tie(grad_out[0]), z * share, share, 0)
@@ -1084,7 +1236,7 @@
     allowed_pred = joined & (key_at < query_at)
     mask = jnp.where(jnp.stack([allowed_main, allowed_pred, allowed_pred]), 0.0, MASKED)
     mask = mask.reshape(rows, window).astype(F32)
-    straight = buckets[0:window]
+    straight = buckets[0 : 2 * share]
     turned = straight[::-1]
 
     mask = line.mark(line.tie(mask))
@@ -1097,34 +1249,34 @@
     )
     gather_self.take()
     gather_self.send("head", 0)
-    gather_cross.send("head", 1)
+    gather_ffn.send("head", 1)
     gather_self.take()
     parts_self = [gather_self.columns(0, 512), gather_self.columns(512, 384)]
     orders_self = [near, far]
     for part, part_order in zip(parts_self, orders_self):
         part.send("batch", part_order[0])
+    gather_ffn.take()
+    gather_ffn.send("head", 0)
+    for number in range(1, nb - 1):
+        for part, part_order in zip(parts_self, orders_self):
+            part.take()
+            part.send("batch", part_order[number])
+    gather_cross.send("head", 1)
+    gather_ffn.take()
+    for part in parts_self:
+        part.take()
+        part.send("batch", 0)
+    gather_cross.take()
+    gather_cross.send("head", 0)
     main = line.tie(own[0:share])
     before_one = lax.ppermute(main, "head", [(i, i + 1) for i in chain[:-1]])
     before_two = lax.ppermute(main, "head", [(i, i + 2) for i in chain[:-2]])
     gather_cross.take()
-    gather_cross.send("head", 0)
-    for number in range(1, nb - 1):
-        for part, part_order in zip(parts_self, orders_self):
-            part.take()
-            part.send("batch", part_order[number])
-    extended = line.mark(jnp.concatenate([before_two, before_one, line.tie(own)], 0))
-    gather_cross.take()
     parts_cross = [gather_cross.columns(0, 512), gather_cross.columns(512, 768)]
     orders_cross = [far, near]
-    gather_ffn = Gather(line, ffn_shard)
-    gather_ffn.send("head", 1)
-    for part in parts_self:
-        part.take()
-        part.send("batch", 0)
     for part, part_order in zip(parts_cross, orders_cross):
         part.send("batch", part_order[0])
-    gather_ffn.take()
-    gather_ffn.send("head", 0)
+    extended = line.mark(stack_rows(before_two, before_one, line.tie(own)))
     memory_came = swap(line.tie(memory_own), "head", 2)
     weights_qk, weights_vr = [part.close() for part in parts_self]
 
@@ -1139,12 +1291,11 @@
         for part, part_order in zip(parts_cross, orders_cross):
             part.take()
             part.send("batch", part_order[number])
-    gather_ffn.take()
-    weights_ffn = gather_ffn.buf.reshape((groups,) + ffn_shard.shape)
+    weights_ffn = line.tie(gather_ffn.buf).reshape((groups,) + ffn_shard.shape)
     weights_ffn = lax.all_gather(weights_ffn, "batch", axis=0)
     if blk % 128:
         weights_ffn = jnp.take(weights_ffn, to_exchange, axis=0)
-    qk = line.mark(project(line.tie(extended), weights_qk, 0, 512, 256, qk_affine, BF, "self_qk"))
+    qk = line.mark(project(line.tie(extended), weights_qk, 0, 512, 512, qk_affine, BF, "self_qk"))
     memory_half = line.mark(jnp.concatenate([line.tie(memory_own), memory_came], 0))
     memory_came = swap(memory_half, "head", 1)
     context, self_probs, self_own = self_attention(
@@ -1154,7 +1305,6 @@
     for part in parts_cross:
         part.take()
         part.send("batch", 0)
-    memory_all = line.mark(jnp.concatenate([line.tie(memory_half), memory_came], 0))
     weights_out, weights_kv = [part.close() for part in parts_cross]
     normed1, normed1_low, unit1, spread1 = close_sublayer(
         line.tie(context), weights_out, 0, 256, own, vectors[0], "self_out"
@@ -1165,10 +1315,11 @@
             line.tie(normed1_low), weights_out, 256, 256, 256, cross_query_affine, BF, "cross_q"
         )
     )
+    memory_all = line.mark(jnp.concatenate([line.tie(memory_half), memory_came], 0))
     cross_kv = line.mark(
-        project(line.tie(memory_all), weights_kv, 0, 512, 256, cross_kv_affine, BF, "cross_kv")
-    )
-    cross_context, cross_probs = cross_attention(line.tie(cross_q), cross_kv)
+        project(line.tie(memory_all), weights_kv, 0, 512, 512, cross_kv_affine, BF, "cross_kv")
+    )
+    cross_context, cross_probs, cross_scales = cross_attention(line.tie(cross_q), cross_kv)
     line.mark(cross_context)
     normed2, normed2_low, unit2, spread2 = close_sublayer(
         line.tie(cross_context), weights_kv, 512, 256, normed1, vectors[1], "cross_out"
@@ -1179,20 +1330,27 @@
     )
     line.mark(third)
 
-    def send(entries, name):
+    straight_order = lax.iota(jnp.int32, groups)
+
+    def send(entries, name, natural=False):
         left, right = entries[0]
         entries = [(line.tie(left), right)] + entries[1:]
-        (sent,) = weight_products(entries, 1, None, None, batches // 2, groups, name + "_send")
+        turn = group_order if natural else straight_order
+        (sent,) = weight_products(
+            turn, entries, 1, None, None, batches // 2, groups, name + "_send"
+        )
         return swap(line.mark(sent), "batch", 1)
 
-    def keep(entries, came, widths, name):
+    def keep(entries, came, parts, name, natural=False):
         left, right = entries[0]
         entries = [(line.tie(left), right)] + entries[1:]
-        orders = (near, far)
-        parts = [(width, nb - 1 - order[0]) for width, order in zip(widths, orders)]
-        outs = weight_products(entries, 0, came, parts, batches // 2, groups, name + "_keep")
+        parts = [(width, nb - 1 - part_order[0]) for width, part_order in parts]
+        turn = group_order if natural else straight_order
+        outs = weight_products(
+            turn, entries, 0, came, parts, batches // 2, groups, name + "_keep"
+        )
         line.mark(outs[0])
-        return Scatter(line, [outs[0:2], outs[2:4]], orders)
+        return [outs[k : k + 2] for k in range(0, len(outs), 2)]
 
     def natural_groups(block):
         return jnp.take(block.reshape(-1, groups, block.shape[1] // groups), group_order, axis=1)
@@ -1213,62 +1371,74 @@
         )
 
     down_entries = [(third_low, active)]
-    down_came = send(down_entries, "down_grad")
-    upper_low, up_sums, second, second_low, sums_second = feed_forward_back(
-        order, line.tie(third_low), third, slope, weights_ffn, unit2, spread2, vectors[1][0:1]
-    )
-    line.mark(second)
     out_low = line.mark(reorder_blocks(line.tie(out_low), to_natural))
     out_low = out_low.reshape(3, share, features)
     layer_out = lax.all_gather(jnp.transpose(out_low, (1, 0, 2)), "head", axis=0, tiled=True)[None]
-    scatter_down = keep(down_entries, down_came, (512, 512), "down_grad")
+    down_came = send(down_entries, "down_grad", True)
+    upper_low, up_sums, second, second_low, sums_second = feed_forward_back(
+        order, line.tie(third_low), third, slope, weights_ffn, unit2, spread2, vectors[1][0:1]
+    )
+    line.mark(second)
     up_entries = [(normed2_low, upper_low)]
-    up_came = send(up_entries, "up_grad")
+    up_came = send(up_entries, "up_grad", True)
     grad_cross_ctx = project_plain(line.tie(second_low), weights_kv, 512, 256, "cross_ctx_back")
     line.mark(grad_cross_ctx)
+    down_halves = keep(down_entries, down_came, [(1024, near)], "down_grad", True)
+    up_halves = keep(up_entries, up_came, [(1024, far)], "up_grad", True)
+    scatter_ffn = Scatter(line, down_halves + up_halves, (near, far), True)
     grad_cross_q, grad_cross_kv, cross_sums = cross_attention_back(
-        cross_q, cross_kv, cross_probs, line.tie(grad_cross_ctx)
+        cross_q, cross_kv, cross_probs, cross_scales, line.tie(grad_cross_ctx)
     )
     line.mark(grad_cross_q)
-    scatter_up = keep(up_entries, up_came, (512, 512), "up_grad")
-    scatter_down.step()
+    memory_part = rows_back(line.tie(grad_cross_kv), weights_kv, 0, 512, "memory_back")
+    span = memory.shape[1]
+    line.mark(*memory_part)
+    memory_mine, memory_came = memory_part[0], swap(memory_part[1], "head", 1)
+    first, first_low, sums_first = cross_query_back(
+        line.tie(grad_cross_q), weights_out, 256, 256, second, unit1, spread1, vectors[0][0:1]
+    )
+    line.mark(first)
+    grad_context = project_plain(line.tie(first_low), weights_out, 0, 256, "self_ctx_back")
+    line.mark(grad_context)
+    layer_out = line.tie(layer_out)
+    line.mark(layer_out, grad_context)
+    scatter_ffn.step()
+    grad_q, grad_kv, grad_rel, self_sums, rel_sums = self_attention_back(
+        qk, values, self_probs, self_own, line.tie(grad_context), straight.reshape(-1, 1), share
+    )
+    line.mark(grad_q)
+    scatter_ffn.step()
+    memory_mine, memory_came = line.tie(memory_mine), after(memory_came, *line.last)
+    pair = (memory_mine.reshape(2, span, features), memory_came.reshape(2, span, features))
+    theirs, memory_mine = add_blocks([pair], [([1], [0]), ([0], [0])], BF)
+    line.mark(theirs, memory_mine)
+    memory_came = swap(theirs, "head", 2)
     cross_entries = [
         (normed1_low, grad_cross_q),
         (memory_all, grad_cross_kv),
         (second_low, cross_context),
+        (first_low, context),
     ]
     cross_came = send(cross_entries, "cross_grad")
-    first, first_low, sums_first = cross_query_back(
-        line.tie(grad_cross_q), weights_out, 256, 256, second, unit1, spread1, vectors[0][0:1]
-    )
-    line.mark(first)
-    grad_context = project_plain(line.tie(first_low), weights_out, 0, 256, "self_ctx_back")
-    line.mark(grad_context)
-    grad_q, grad_kv, grad_rel, self_sums, rel_sums = self_attention_back(
-        qk, values, self_probs, self_own, line.tie(grad_context), straight.reshape(-1, 1), share
-    )
-    line.mark(grad_q)
-    scatter_cross = keep(cross_entries, cross_came, (512, 512), "cross_grad")
-    layer_out = line.mark(line.tie(layer_out))
-    scatter_up.step()
-    scatter_down.step()
-    self_entries = [(own, grad_q), (first_low, context), (extended, grad_kv), (own, grad_rel)]
+    self_entries = [(own, grad_q), (extended, grad_kv), (own, grad_rel)]
     self_came = send(self_entries, "self_grad")
-    halo_grad, own_grad = input_back(
+    halves = keep(cross_entries, cross_came, [(640, near), (640, far)], "cross_grad")
+    scatter_cross = Scatter(line, halves, (near, far))
+    halves = keep(self_entries, self_came, [(512, near), (384, far)], "self_grad")
+    scatter_self = Scatter(line, halves, (near, far))
+    while not hasattr(scatter_ffn, "total"):
+        scatter_ffn.step()
+    two_grad, one_grad, own_grad = input_back(
         line.tie(grad_q), grad_kv, grad_rel, weights_qk, weights_vr, first
     )
     line.mark(own_grad)
-    from_two = lax.ppermute(halo_grad[0:share], "head", [(i + 2, i) for i in chain[:-2]])
-    from_one = lax.ppermute(halo_grad[share:], "head", [(i + 1, i) for i in chain[:-1]])
-    memory_part = rows_back(line.tie(grad_cross_kv), weights_kv, 0, 512, "memory_back")
-    span = memory.shape[1]
-    memory_part = line.mark(memory_part).reshape(2, 2, span, features)
-    memory_came = swap(memory_part[1], "head", 1)
-    scatter_self = keep(self_entries, self_came, (512, 640), "self_grad")
+    from_two = lax.ppermute(two_grad, "head", [(i + 2, i) for i in chain[:-2]])
+    from_one = lax.ppermute(one_grad, "head", [(i + 1, i) for i in chain[:-1]])
+    scatter_ffn.total = line.tie(scatter_ffn.total)
+    line.mark(scatter_ffn.total, *line.last)
     scatter_cross.step()
-    scatter_up.step()
-    scatter_down.step()
-    packed = pack_sums(line.last[0])
+    scatter_self.step()
+    packed = line.mark(pack_sums(line.last[0]))
     packed_bits = [("batch", bit) for bit in range(nb)] + [("head", 0), ("head", 1)]
 
     def add_packed(packed):
@@ -1277,38 +1447,32 @@
         packed = line.tie(packed)
         return line.mark(packed + after(came, packed))
 
-    main_grad = line.tie(own_grad[0:share]) + from_one.astype(F32) + from_two.astype(F32)
-    own_grad = jnp.concatenate([main_grad, own_grad[share:]], 0)
-    own_grad = line.mark(reorder_blocks(own_grad, to_natural)).reshape(3, share, features)
+    own_grad = line.mark(add_halo(line.tie(own_grad), from_one, from_two))
+    own_grad = line.mark(reorder_blocks(line.tie(own_grad), to_natural)).reshape(
+        3, share, features
+    )
     grad_hidden = jnp.transpose(own_grad, (1, 0, 2))[None]
+    scatter_cross.step()
     packed = add_packed(packed)
-    scatter_down.step()
-    scatter_up.step()
-    memory_part, memory_came = line.tie(memory_part), after(memory_came, *line.last)
-    memory_mine = (memory_part[0].astype(F32) + memory_came.astype(F32)).astype(BF)
-    memory_mine = line.mark(memory_mine)
-    memory_came = swap(pin(memory_mine[1]), "head", 2)
-    scatter_cross.step()
     scatter_self.step()
     packed = add_packed(packed)
-    scatter_up.step()
+    memory_mine, memory_came = line.tie(memory_mine), after(memory_came, *line.last)
+    (memory_grad,) = add_blocks([(memory_mine, memory_came)], [([0], [0])], F32)
+    memory_grad = line.mark(memory_grad)[0]
+    grad_memory = line.mark(reorder_blocks(line.tie(memory_grad), to_natural))[None]
     scatter_cross.step()
-    memory_mine, memory_came = line.tie(memory_mine), after(memory_came, *line.last)
-    memory_grad = memory_mine[0].astype(F32) + memory_came.astype(F32)
-    grad_memory = line.mark(reorder_blocks(memory_grad, to_natural))[None]
+    packed = add_packed(packed)
     scatter_self.step()
     packed = add_packed(packed)
     scatter_cross.step()
     scatter_self.step()
-    packed = add_packed(packed)
-    scatter_self.step()
     while packed_bits:
         packed = add_packed(packed)
-    scatters = (scatter_down, scatter_up, scatter_cross, scatter_self)
+    scatters = (scatter_ffn, scatter_cross, scatter_self)
     for scatter in scatters:
         while not hasattr(scatter, "total"):
             scatter.step()
-    grad_down, grad_up, grads_cross, grads_self = [scatter.total for scatter in scatters]
+    grads_ffn, grads_cross, grads_self = [scatter.total for scatter in scatters]
 
     ends = [0]
     for size in (2 * features, groups * 128, 2 * features, up_bias.shape[0], 9 * features):
@@ -1323,14 +1487,14 @@
         layer_out,
         grad_hidden,
         grad_memory,
-        jnp.concatenate([grads_self[:, 0:256], grads_self[:, 512:1024]], 1).reshape(blk, 3, 256),
-        grads_self[:, 1024:1152],
-        grads_self[:, 256:512],
+        grads_self[:, 0:768].reshape(blk, 3, 256),
+        grads_self[:, 768:896],
+        grads_cross[:, 1024:1280],
         grads_cross[:, 0:256],
         grads_cross[:, 256:768].reshape(blk, 2, 256),
         grads_cross[:, 768:1024],
-        grad_up,
-        grad_down,
+        grads_ffn[:, 1024:],
+        grads_ffn[:, 0:1024],
         self_bias_grad,
         relpos_bias_grad,
         cross_bias_grad,

time: 639 us -> 617 us (0.966)
  Pallas kernels: 262 us -> 296 us
  other arithmetic: 39.7 us -> 9.08 us
  starting transfers between devices: 86.7 us -> 63.3 us
  waiting for transfers between devices: 161 us -> 154 us
  local copies, waits for them, and re-layouts: 65.5 us -> 72 us
    pallas_call x8 -> x22, Pallas kernels: 59.8 us -> 106 us  [the longest x8 65.2 us: weight_products(): pl.pallas_call(body, grid_spec=pltpu.PrefetchScalarGridSpec(num_scalar_pr...]
    ppermute x55 -> x47, starting transfers between devices: 77.7 us -> 55.4 us  [swap(): return lax.ppermute(array_in, axis, [(i, i ^ bit) for i in range(count)])]
    ppermute x55 -> x47, waiting for transfers between devices: 156 us -> 136 us  [swap(): return lax.ppermute(array_in, axis, [(i, i ^ bit) for i in range(count)])]
    convert_element_type x9 -> x1, other arithmetic: 17.8 us -> 1.13 us  [step(): self.total = total.astype(F32)]
    reduce_scatter x0 -> x1, waiting for transfers between devices: none -> 9.39 us  [step(): lax.psum_scatter(self.line.mark(total), 'head', scatter_dimension=0, tile...]
    unnamed x154 -> x148, local copies, waits for them, and re-layouts: 24.6 us -> 31.6 us
    pallas_call x1, Pallas kernels: 17.9 us -> 11.2 us  [self_attention(): pl.pallas_call(body, grid=(groups,), in_specs=[pl.BlockSpec((long_rows, 2...]
  transfers between devices with their start and end apart: 61 -> 54, of which waited for: 21 -> 27; matrix products, arithmetic and copies ran while one was open for 12% -> 7% of each run, Pallas kernels for 35% -> 41%
where the time goes in v3:
time: 617 us; the launch traced here: 610 us
  Pallas kernels  296 us (48%)
  waiting for transfers between devices  154 us (25%)
  local copies, waits for them, and re-layouts  72 us (12%)
  starting transfers between devices  63.3 us (10%)
  between operations  15.1 us (2%)
  other arithmetic  9.08 us (1%)
    ppermute x47, waiting for transfers between devices, swap(): return lax.ppermute(array_in, axis, [(i, i ^ bit) for i in range(count)])  136 us
    pallas_call x8, Pallas kernels, weight_products(): pl.pallas_call(body, grid_spec=pltpu.PrefetchScalarGridSpec(num_scalar_pr...  65.2 us
    ppermute x47, starting transfers between devices, swap(): return lax.ppermute(array_in, axis, [(i, i ^ bit) for i in range(count)])  55.4 us
    pallas_call x7, Pallas kernels, project(): pl.pallas_call(body, grid=(groups, per), in_specs=[whole((rows, features)...  39.9 us
    pallas_call x12, Pallas kernels, add_blocks(): pl.pallas_call(body, grid=(rows // chunk,), in_specs=[spec(array.shape[0]...  35.8 us
    unnamed x148, local copies, waits for them, and re-layouts  31.6 us
    pallas_call x6, Pallas kernels, reorder_blocks(): pl.pallas_call(body, out_shape=jax.ShapeDtypeStruct(array_in.shape, array...  18.6 us
    pallas_call x1, Pallas kernels, feed_forward(): pl.pallas_call(body, grid_spec=pltpu.PrefetchScalarGridSpec(num_scalar_pr...  17.4 us
  transfers between devices with their start and end apart: 54, of which 27 were waited for; matrix products, arithmetic and copies ran while one was open for 7% of the time, Pallas kernels for 41%

profile of v3, /device:TPU:0, one launch (start us, length us, event | category | flops | bytes accessed | tf_op | source)
XLA Modules:
  0.0 609.7 jit_solution(13640382682282430114)
XLA Ops:
  9.4 4.1 collective-permute-start
  24.8 3.7 reorder.8.grad_ref
  33.2 16.3 %collective-permute-done.1 = bf16[1,1,1,2,1,128,896]{6,5,4,3,2,1,0:T(8,128)(2,1)} collective-permute-done((bf16[1,1,1,2,1,128,896]{6,5,4,3,2,1,0:T(8,128)(2,1)S(1)}, bf16[1,1,1,2,1,128,896]{6,5,4,3,2,1,0:T(8,128)(2,1)}, u32[]{:S(2)}, u32[]{:S(2)}) %collective-permute-start.1) | collective-permute-done | bytes 458784 | tf_op jit(solution)/shard_map/ppermute | solution.py:35
  52.3 4.8 collective-permute-done.2
  58.9 4.2 collective-permute-done.3
  65.0 4.3 collective-permute-done.4
  72.1 15.5 %collective-permute-done.5 = bf16[1,1,1,2,1,128,2048]{6,5,4,3,2,1,0:T(8,128)(2,1)S(1)} collective-permute-done((bf16[1,1,1,2,1,128,2048]{6,5,4,3,2,1,0:T(8,128)(2,1)S(1)}, bf16[1,1,1,2,1,128,2048]{6,5,4,3,2,1,0:T(8,128)(2,1)S(1)}, u32[]{:S(2)}, u32[]{:S(2)}) %collective-permute-start.5) | collective-permute-done | bytes 1048608 | tf_op jit(solution)/shard_map/ppermute | solution.py:35
  99.6 8.9 %collective-permute-done.11 = bf16[1,1,1,2,1,128,1280]{6,5,4,3,2,1,0:T(8,128)(2,1)} collective-permute-done((bf16[1,1,1,2,1,128,1280]{6,5,4,3,2,1,0:T(8,128)(2,1)}, bf16[1,1,1,2,1,128,1280]{6,5,4,3,2,1,0:T(8,128)(2,1)}, u32[]{:S(2)}, u32[]{:S(2)}) %collective-permute-start.11) | collective-permute-done | bytes 655392 | tf_op jit(solution)/shard_map/ppermute | solution.py:35
  120.0 5.2 self_v.1.v_ref
  125.2 4.5 self_rel.1.rel_ref
  140.4 7.4 %self_qk.1.q_ref.k_ref = bf16[640,2048]{1,0:T(8,128)(2,1)} custom-call(bf16[640,1024]{1,0:T(8,128)(2,1)} %stack_rows.1.x_ref.refs_1_, bf16[4,4,128,512]{3,2,1,0:T(8,128)(2,1)} %bitcast.162, bf16[4,4,128,512]{3,2,1,0:T(8,128)(2,1)} %bitcast.21.refs_1_.refs_3_, f32[2,2048]{1,0:T(2,128)} %pad_maximum_fusion.4.refs_2_), custom_call_target="tpu_custom_call" | custom-call | tf_op jit(solution)/shard_map/self_qk/pallas_call | solution.py:279
  148.7 14.0 %collective-permute-done.16 = bf16[256,1024]{1,0:T(8,128)(2,1)} collective-permute-done((bf16[256,1024]{1,0:T(8,128)(2,1)}, bf16[256,1024]{1,0:T(8,128)(2,1)}, u32[]{:S(2)}, u32[]{:S(2)}) %collective-permute-start.16) | collective-permute-done | bytes 524320 | tf_op jit(solution)/shard_map/ppermute | solution.py:35
  164.6 11.2 %self_attention.1 = (bf16[384,1024]{1,0:T(8,128)(2,1)}, bf16[16,384,384]{2,1,0:T(8,128)(2,1)}, f32[384,512]{1,0:T(8,128)}) custom-call(bf16[640,2048]{1,0:T(8,128)(2,1)} %self_qk.1.q_ref.k_ref, bf16[640,2048]{1,0:T(8,128)(2,1)} %self_qk.1.q_ref.k_ref, bf16[640,1024]{1,0:T(8,128)(2,1)} %self_v.1.v_ref, f32[384,512]{1,0:T(8,128)} %self_rel.1.rel_ref, ...), custom_call_target="tpu_custom_call" | custom-call | tf_op jit(solution)/shard_map/self_attention/pallas_call | solution.py:862
  180.7 11.6 %collective-permute-done.18 = bf16[1,2,1,2,2,128,768]{6,5,4,3,2,1,0:T(8,128)(2,1)} collective-permute-done((bf16[1,2,1,2,2,128,768]{6,5,4,3,2,1,0:T(8,128)(2,1)}, bf16[1,2,1,2,2,128,768]{6,5,4,3,2,1,0:T(8,128)(2,1)}, u32[]{:S(2)}, u32[]{:S(2)}) %collective-permute-start.18) | collective-permute-done | bytes 1572896 | tf_op jit(solution)/shard_map/ppermute | solution.py:35
  201.0 4.5 collective-permute-done.19
  205.6 6.6 %self_out.1 = (f32[384,1024]{1,0:T(8,128)}, bf16[384,1024]{1,0:T(8,128)(2,1)}, f32[384,1024]{1,0:T(8,128)}, f32[384,1]{1,0:T(8,128)}) custom-call(bf16[384,1024]{1,0:T(8,128)(2,1)} %get-tuple-element.284.left_ref.refs_7_, bf16[4,4,128,512]{3,2,1,0:T(8,128)(2,1)} %bitcast.23.refs_0_, bf16[4,4,128,512]{3,2,1,0:T(8,128)(2,1)} %bitcast.24.refs_1_, ...), custom_call_target="tpu_custom_call" | custom-call | tf_op jit(solution)/shard_map/self_out/pallas_call | solution.py:350
  212.2 4.6 cross_q.1.q_ref
  222.8 8.5 %cross_kv.1.k_ref.v_ref = bf16[1024,2048]{1,0:T(8,128)(2,1)} custom-call(bf16[1024,1024]{1,0:T(8,128)(2,1)} %copy-done.4, bf16[4,4,128,768]{3,2,1,0:T(8,128)(2,1)} %bitcast.154, bf16[4,4,128,768]{3,2,1,0:T(8,128)(2,1)} %bitcast.29.refs_1_, f32[2,2048]{1,0:T(2,128)} %stack.26.refs_2_), custom_call_target="tpu_custom_call" | custom-call | tf_op jit(solution)/shard_map/cross_kv/pallas_call | solution.py:279
  231.3 13.5 %cross_attention.1 = (bf16[384,1024]{1,0:T(8,128)(2,1)}, bf16[16,384,1024]{2,1,0:T(8,128)(2,1)}, f32[384,512]{1,0:T(8,128)}) custom-call(bf16[384,1024]{1,0:T(8,128)(2,1)} %cross_q.1.q_ref, bf16[1024,2048]{1,0:T(8,128)(2,1)} %cross_kv.1.k_ref.v_ref, bf16[1024,2048]{1,0:T(8,128)(2,1)} %cross_kv.1.k_ref.v_ref), custom_call_target="tpu_custom_call" | custom-call | tf_op jit(solution)/shard_map/cross_attention/pallas_call | solution.py:1030
  244.8 7.0 %cross_out.1 = (f32[384,1024]{1,0:T(8,128)}, bf16[384,1024]{1,0:T(8,128)(2,1)}, f32[384,1024]{1,0:T(8,128)}, f32[384,1]{1,0:T(8,128)}) custom-call(bf16[384,1024]{1,0:T(8,128)(2,1)} %get-tuple-element.294.left_ref.refs_6_, bf16[4,4,128,768]{3,2,1,0:T(8,128)(2,1)} %bitcast.155, bf16[4,4,128,768]{3,2,1,0:T(8,128)(2,1)} %bitcast.29.refs_1_, ...), custom_call_target="tpu_custom_call" | custom-call | tf_op jit(solution)/shard_map/cross_out/pallas_call | solution.py:350
  251.7 17.4 %feed_forward.1 = (bf16[384,4096]{1,0:T(8,128)(2,1)}, bf16[384,4096]{1,0:T(8,128)(2,1)}, bf16[384,1024]{1,0:T(8,128)(2,1)}, f32[384,1024]{1,0:T(8,128)}, bf16[384,1024]{1,0:T(8,128)(2,1)}, /*index=5*/f32[3,1024]{1,0:T(4,128)}) custom-call(s32[12]{0:T(128)} %pad_add_fusion.order_ref, bf16[384,1024]{1,0:T(8,128)(2,1)} %get-tuple-element.318.low_ref.refs_0_, ...), custom_call_target="tpu_custom_call" | custom-call | tf_op jit(solution)/shard_map/feed_forward/pallas_call | solution.py:432
  272.0 6.7 %down_grad_send.1 = bf16[4,4,128,1024]{3,2,1,0:T(8,128)(2,1)} custom-call(s32[4]{0:T(128)} %copy-done.41, bf16[384,1024]{1,0:T(8,128)(2,1)} %get-tuple-element.316.refs_0_.third_low_ref, bf16[384,4096]{1,0:T(8,128)(2,1)} %get-tuple-element.306.refs_1_), custom_call_target="tpu_custom_call" | custom-call | tf_op jit(solution)/shard_map/down_grad_send/pallas_call | solution.py:748
  278.8 16.0 %feed_forward_back.1 = (bf16[384,4096]{1,0:T(8,128)(2,1)}, f32[1,4096]{1,0:T(1,128)}, f32[384,1024]{1,0:T(8,128)}, bf16[384,1024]{1,0:T(8,128)(2,1)}, f32[3,1024]{1,0:T(4,128)}) custom-call(s32[12]{0:T(128)} %pad_add_fusion.order_ref, bf16[384,1024]{1,0:T(8,128)(2,1)} %get-tuple-element.316.refs_0_.third_low_ref, f32[384,1024]{1,0:T(8,128)} %get-tuple-element.300.third_ref, ...), custom_call_target="tpu_custom_call" | custom-call | tf_op jit(solution)/shard_map/feed_forward_back/pallas_call | solution.py:519
  294.7 6.7 %up_grad_send.1 = bf16[4,4,128,1024]{3,2,1,0:T(8,128)(2,1)} custom-call(s32[4]{0:T(128)} %copy-done.41, bf16[384,1024]{1,0:T(8,128)(2,1)} %get-tuple-element.318.low_ref.refs_0_, bf16[384,4096]{1,0:T(8,128)(2,1)} %get-tuple-element.314.refs_1_), custom_call_target="tpu_custom_call" | custom-call | tf_op jit(solution)/shard_map/up_grad_send/pallas_call | solution.py:748
  302.0 5.1 cross_ctx_back.1.grad_ref
  307.1 7.8 %down_grad_keep.1 = (bf16[2,4,128,1024]{3,2,1,0:T(8,128)(2,1)}, bf16[2,4,128,1024]{3,2,1,0:T(8,128)(2,1)}) custom-call(s32[4]{0:T(128)} %copy-done.41, bf16[384,1024]{1,0:T(8,128)(2,1)} %get-tuple-element.316.refs_0_.third_low_ref, bf16[384,4096]{1,0:T(8,128)(2,1)} %get-tuple-element.306.refs_1_, bf16[4,4,128,1024]{3,2,1,0:T(8,128)(2,1)} %collective-permute-done.22.refs_2_), custom_call_target="tpu_custom_call" | custom-call | tf_op jit(solution)/shard_map/down_grad_keep/pallas_call | solution.py:748
  314.9 7.8 %up_grad_keep.1 = (bf16[2,4,128,1024]{3,2,1,0:T(8,128)(2,1)}, bf16[2,4,128,1024]{3,2,1,0:T(8,128)(2,1)}) custom-call(s32[4]{0:T(128)} %copy-done.41, bf16[384,1024]{1,0:T(8,128)(2,1)} %get-tuple-element.318.low_ref.refs_0_, bf16[384,4096]{1,0:T(8,128)(2,1)} %get-tuple-element.314.refs_1_, bf16[4,4,128,1024]{3,2,1,0:T(8,128)(2,1)} %collective-permute-done.23.refs_2_), custom_call_target="tpu_custom_call" | custom-call | tf_op jit(solution)/shard_map/up_grad_keep/pallas_call | solution.py:748
  325.7 17.3 %cross_attention_back.1 = (bf16[384,1024]{1,0:T(8,128)(2,1)}, bf16[1024,2048]{1,0:T(8,128)(2,1)}, f32[2,1024]{1,0:T(2,128)}) custom-call(bf16[384,1024]{1,0:T(8,128)(2,1)} %cross_q.1.q_ref, bf16[1024,2048]{1,0:T(8,128)(2,1)} %cross_kv.1.k_ref.v_ref, bf16[1024,2048]{1,0:T(8,128)(2,1)} %cross_kv.1.k_ref.v_ref, ...), custom_call_target="tpu_custom_call" | custom-call | tf_op jit(solution)/shard_map/cross_attention_back/pallas_call | solution.py:1099
  343.0 8.9 %memory_back.1 = (bf16[512,1024]{1,0:T(8,128)(2,1)}, bf16[512,1024]{1,0:T(8,128)(2,1)}) custom-call(bf16[1024,2048]{1,0:T(8,128)(2,1)} %get-tuple-element.323.left_ref.refs_5_, bf16[4,4,128,768]{3,2,1,0:T(8,128)(2,1)} %bitcast.157, bf16[4,4,128,768]{3,2,1,0:T(8,128)(2,1)} %bitcast.29.refs_1_), custom_call_target="tpu_custom_call" | custom-call | tf_op jit(solution)/shard_map/memory_back/pallas_call | solution.py:629
  351.9 7.0 %cross_query_back.1 = (f32[384,1024]{1,0:T(8,128)}, bf16[384,1024]{1,0:T(8,128)(2,1)}, f32[3,1024]{1,0:T(4,128)}) custom-call(bf16[384,1024]{1,0:T(8,128)(2,1)} %get-tuple-element.326.left_ref.refs_4_, bf16[4,4,128,512]{3,2,1,0:T(8,128)(2,1)} %bitcast.23.refs_0_, bf16[4,4,128,512]{3,2,1,0:T(8,128)(2,1)} %bitcast.24.refs_1_, ...), custom_call_target="tpu_custom_call" | custom-call | tf_op jit(solution)/shard_map/cross_query_back/pallas_call | solution.py:589
  359.0 4.6 self_ctx_back.1.grad_ref
  363.6 4.2 all-gather.5.cloned.1.call-done
  372.0 6.0 add_blocks.12
  381.8 16.7 %self_attention_back.1 = (bf16[384,1024]{1,0:T(8,128)(2,1)}, bf16[640,2048]{1,0:T(8,128)(2,1)}, bf16[384,512]{1,0:T(8,128)(2,1)}, f32[2,1024]{1,0:T(2,128)}, f32[1,512]{1,0:T(1,128)}) custom-call(bf16[640,2048]{1,0:T(8,128)(2,1)} %self_qk.1.q_ref.k_ref, bf16[640,2048]{1,0:T(8,128)(2,1)} %self_qk.1.q_ref.k_ref, bf16[640,1024]{1,0:T(8,128)(2,1)} %self_v.1.v_ref, ...), custom_call_target="tpu_custom_call" | custom-call | tf_op jit(solution)/shard_map/self_attention_back/pallas_call | solution.py:975
  398.5 3.9 collective-permute-done.27.refs_3_
  404.5 3.9 add_blocks.13
  412.5 9.4 %cross_grad_send.1 = bf16[4,4,128,1280]{3,2,1,0:T(8,128)(2,1)} custom-call(s32[4]{0:T(128)} %iota.57.order_ref, bf16[384,1024]{1,0:T(8,128)(2,1)} %get-tuple-element.359.x_ref.refs_0_, bf16[1024,1024]{1,0:T(8,128)(2,1)} %copy-done.4, bf16[384,1024]{1,0:T(8,128)(2,1)} %get-tuple-element.315.x_ref.refs_2_, bf16[384,1024]{1,0:T(8,128)(2,1)} %get-tuple-element.331.x_ref.refs_3_, ...), custom_call_target="tpu_custom_call" | custom-call | tf_op jit(solution)/shard_map/cross_grad_send/pallas_call | solution.py:748
  422.5 7.8 %self_grad_send.1 = bf16[4,4,128,896]{3,2,1,0:T(8,128)(2,1)} custom-call(s32[4]{0:T(128)} %iota.56.order_ref, bf16[384,1024]{1,0:T(8,128)(2,1)} %reorder.7.refs_2_.x_ref.refs_0_, bf16[640,1024]{1,0:T(8,128)(2,1)} %stack_rows.1.x_ref.refs_1_, bf16[384,1024]{1,0:T(8,128)(2,1)} %reorder.7.refs_2_.x_ref.refs_0_, ...), custom_call_target="tpu_custom_call" | custom-call | tf_op jit(solution)/shard_map/self_grad_send/pallas_call | solution.py:748
  431.5 10.6 %cross_grad_keep.1 = (bf16[2,4,128,640]{3,2,1,0:T(8,128)(2,1)}, bf16[2,4,128,640]{3,2,1,0:T(8,128)(2,1)}, bf16[2,4,128,640]{3,2,1,0:T(8,128)(2,1)}, bf16[2,4,128,640]{3,2,1,0:T(8,128)(2,1)}) custom-call(s32[4]{0:T(128)} %iota.55.order_ref, bf16[384,1024]{1,0:T(8,128)(2,1)} %get-tuple-element.359.x_ref.refs_0_, bf16[1024,1024]{1,0:T(8,128)(2,1)} %copy-done.4, ...), custom_call_target="tpu_custom_call" | custom-call | tf_op jit(solution)/shard_map/cross_grad_keep/pallas_call | solution.py:748
  449.1 8.3 %self_grad_keep.1 = (bf16[2,4,128,512]{3,2,1,0:T(8,128)(2,1)}, bf16[2,4,128,512]{3,2,1,0:T(8,128)(2,1)}, bf16[2,4,128,384]{3,2,1,0:T(8,128)(2,1)}, bf16[2,4,128,384]{3,2,1,0:T(8,128)(2,1)}) custom-call(s32[4]{0:T(128)} %iota.54.order_ref, bf16[384,1024]{1,0:T(8,128)(2,1)} %reorder.7.refs_2_.x_ref.refs_0_, bf16[640,1024]{1,0:T(8,128)(2,1)} %stack_rows.1.x_ref.refs_1_, ...), custom_call_target="tpu_custom_call" | custom-call | tf_op jit(solution)/shard_map/self_grad_keep/pallas_call | solution.py:748
  458.8 9.4 %reduce-scatter.2.cloned.1.call-done = bf16[1,128,2048]{2,1,0:T(8,128)(2,1)} async-done(((bf16[4,128,2048]{2,1,0:T(8,128)(2,1)}), bf16[1,128,2048]{2,1,0:T(8,128)(2,1)}) %reduce-scatter.2.cloned.1.call-update) | async-done | bytes 524304 | tf_op jit(solution)/shard_map/reduce_scatter | solution.py:182
  469.3 9.7 %input_back.1 = (bf16[128,1024]{1,0:T(8,128)(2,1)}, bf16[128,1024]{1,0:T(8,128)(2,1)}, f32[384,1024]{1,0:T(8,128)}) custom-call(bf16[384,1024]{1,0:T(8,128)(2,1)} %get-tuple-element.363.refs_3_.query_ref, bf16[640,2048]{1,0:T(8,128)(2,1)} %get-tuple-element.357.refs_4_.kv_ref, bf16[384,512]{1,0:T(8,128)(2,1)} %get-tuple-element.358.refs_5_.rel_ref, ...), custom_call_target="tpu_custom_call" | custom-call | tf_op jit(solution)/shard_map/input_back/pallas_call | solution.py:673
  480.1 4.1 add_blocks.15
  492.4 5.5 collective-permute-done.33
  511.1 3.5 reorder.10
  533.9 11.9 %collective-permute-done.43.refs_1_ = bf16[1,256,1024]{2,1,0:T(8,128)(2,1)S(1)} collective-permute-done((bf16[1,256,1024]{2,1,0:T(8,128)(2,1)S(1)}, bf16[1,256,1024]{2,1,0:T(8,128)(2,1)S(1)}, u32[]{:S(2)}, u32[]{:S(2)}) %collective-permute-start.43) | collective-permute-done | bytes 524320 | tf_op jit(solution)/shard_map/ppermute | solution.py:35
  554.9 3.7 collective-permute-start.47
  565.4 13.8 %collective-permute-done.48.refs_1_ = bf16[1,128,1280]{2,1,0:T(8,128)(2,1)S(1)} collective-permute-done((bf16[1,128,1280]{2,1,0:T(8,128)(2,1)}, bf16[1,128,1280]{2,1,0:T(8,128)(2,1)S(1)}, u32[]{:S(2)}, u32[]{:S(2)}) %collective-permute-start.48) | collective-permute-done | bytes 327712 | tf_op jit(solution)/shard_map/ppermute | solution.py:35
  (383 shorter events, 196.4 us)
Async XLA Ops:
  7.2 244.5 %all-gather.3.cloned.1.call-start = ((), (), s32[]{:S(2)}) async-start(), calls=%async_computation.1 | async-start | bytes 18874368 | tf_op jit(solution)/shard_map/all_gather | solution.py:1295
  9.4 20.7 %collective-permute-start = (bf16[1,1,1,1,1,128,896]{6,5,4,3,2,1,0:T(8,128)(2,1)S(1)}, bf16[1,1,1,1,1,128,896]{6,5,4,3,2,1,0:T(8,128)(2,1)S(1)}, u32[]{:S(2)}, u32[]{:S(2)}) collective-permute-start(bf16[1,1,1,1,1,128,896]{6,5,4,3,2,1,0:T(8,128)(2,1)S(1)} %pad_maximum_fusion.1), channel_id=1, source_target_pairs={{0,2},{1,3},{2,0},{3,1},{4,6},{5,7},{6,4},{7,5},{8,10},{9,11},{10,... | collective-permute-start | bytes 688136 | tf_op jit(solution)/shard_map/ppermute | solution.py:35
  30.1 19.4 %collective-permute-start.1 = (bf16[1,1,1,2,1,128,896]{6,5,4,3,2,1,0:T(8,128)(2,1)S(1)}, bf16[1,1,1,2,1,128,896]{6,5,4,3,2,1,0:T(8,128)(2,1)}, u32[]{:S(2)}, u32[]{:S(2)}) collective-permute-start(bf16[1,1,1,2,1,128,896]{6,5,4,3,2,1,0:T(8,128)(2,1)S(1)} %constant_dynamic-update-slice_fusion), channel_id=1, source_target_pairs={{0,1},{1,0},{2,3},{3,2},{4,5},{5,4},{6,7},{7,6},{8,9},{9,8},{10,11... | collective-permute-start | bytes 1376264 | tf_op jit(solution)/shard_map/ppermute | solution.py:35
  31.8 25.3 %collective-permute-start.2 = (bf16[1,1,1,1,1,128,2048]{6,5,4,3,2,1,0:T(8,128)(2,1)S(1)}, bf16[1,1,1,1,1,128,2048]{6,5,4,3,2,1,0:T(8,128)(2,1)S(1)}, u32[]{:S(2)}, u32[]{:S(2)}) collective-permute-start(bf16[1,1,1,1,1,128,2048]{6,5,4,3,2,1,0:T(8,128)(2,1)S(1)} %fusion.9), channel_id=1, source_target_pairs={{0,2},{1,3},{2,0},{3,1},{4,6},{5,7},{6,4},{7,5},{8,10},{9,11},{10,... | collective-permute-start | bytes 1572872 | tf_op jit(solution)/shard_map/ppermute | solution.py:35
  50.7 12.5 %collective-permute-start.3 = (bf16[1,1,1,2,2,128,512]{6,5,4,3,2,1,0:T(8,128)(2,1)S(1)}, bf16[1,1,1,2,2,128,512]{6,5,4,3,2,1,0:T(8,128)(2,1)S(1)}, u32[]{:S(2)}, u32[]{:S(2)}) collective-permute-start(bf16[1,1,1,2,2,128,512]{6,5,4,3,2,1,0:T(8,128)(2,1)S(1)} %slice.177), channel_id=1, source_target_pairs={{0,8},{4,12},{8,0},{12,4},{16,24},{20,28},{24,16},{28,20},{1,9},{5... | collective-permute-start | bytes 1572872 | tf_op jit(solution)/shard_map/ppermute | solution.py:35
  57.1 30.5 %collective-permute-start.5 = (bf16[1,1,1,2,1,128,2048]{6,5,4,3,2,1,0:T(8,128)(2,1)S(1)}, bf16[1,1,1,2,1,128,2048]{6,5,4,3,2,1,0:T(8,128)(2,1)S(1)}, u32[]{:S(2)}, u32[]{:S(2)}) collective-permute-start(bf16[1,1,1,2,1,128,2048]{6,5,4,3,2,1,0:T(8,128)(2,1)S(1)} %constant_dynamic-update-slice_fusion.4), channel_id=1, source_target_pairs={{0,1},{1,0},{2,3},{3,2},{4,5},{5,4},{6,7},{7,6},{8,9},{9,8},{10,11... | collective-permute-start | bytes 3145736 | tf_op jit(solution)/shard_map/ppermute | solution.py:35
  57.2 12.1 %collective-permute-start.4 = (bf16[1,1,1,2,2,128,384]{6,5,4,3,2,1,0:T(8,128)(2,1)S(1)}, bf16[1,1,1,2,2,128,384]{6,5,4,3,2,1,0:T(8,128)(2,1)S(1)}, u32[]{:S(2)}, u32[]{:S(2)}) collective-permute-start(bf16[1,1,1,2,2,128,384]{6,5,4,3,2,1,0:T(8,128)(2,1)S(1)} %slice.176), channel_id=1, source_target_pairs={{0,16},{4,20},{8,24},{12,28},{16,0},{20,4},{24,8},{28,12},{1,17},{... | collective-permute-start | bytes 1179656 | tf_op jit(solution)/shard_map/ppermute | solution.py:35
  63.2 26.0 %collective-permute-start.6 = (bf16[1,2,1,2,2,128,512]{6,5,4,3,2,1,0:T(8,128)(2,1)S(1)}, bf16[1,2,1,2,2,128,512]{6,5,4,3,2,1,0:T(8,128)(2,1)S(1)}, u32[]{:S(2)}, u32[]{:S(2)}) collective-permute-start(bf16[1,2,1,2,2,128,512]{6,5,4,3,2,1,0:T(8,128)(2,1)S(1)} %constant_dynamic-update-slice_fusion.6), channel_id=1, source_target_pairs={{0,16},{4,20},{8,24},{12,28},{16,0},{20,4},{24,8},{28,12},{1,17},{... | collective-permute-start | bytes 3145736 | tf_op jit(solution)/shard_map/ppermute | solution.py:35
  69.5 19.8 %collective-permute-start.7 = (bf16[1,1,2,2,2,128,384]{6,5,4,3,2,1,0:T(8,128)(2,1)S(1)}, bf16[1,1,2,2,2,128,384]{6,5,4,3,2,1,0:T(8,128)(2,1)S(1)}, u32[]{:S(2)}, u32[]{:S(2)}) collective-permute-start(bf16[1,1,2,2,2,128,384]{6,5,4,3,2,1,0:T(8,128)(2,1)S(1)} %constant_dynamic-update-slice_fusion.8), channel_id=1, source_target_pairs={{0,8},{4,12},{8,0},{12,4},{16,24},{20,28},{24,16},{28,20},{1,9},{5... | collective-permute-start | bytes 2359304 | tf_op jit(solution)/shard_map/ppermute | solution.py:35
  71.0 19.4 %collective-permute-start.8 = (bf16[1,1,1,1,1,128,1280]{6,5,4,3,2,1,0:T(8,128)(2,1)S(1)}, bf16[1,1,1,1,1,128,1280]{6,5,4,3,2,1,0:T(8,128)(2,1)S(1)}, u32[]{:S(2)}, u32[]{:S(2)}) collective-permute-start(bf16[1,1,1,1,1,128,1280]{6,5,4,3,2,1,0:T(8,128)(2,1)S(1)} %maximum_bitcast_fusion), channel_id=1, source_target_pairs={{0,2},{1,3},{2,0},{3,1},{4,6},{5,7},{6,4},{7,5},{8,10},{9,11},{10,... | collective-permute-start | bytes 983048 | tf_op jit(solution)/shard_map/ppermute | solution.py:35
  91.2 17.2 %collective-permute-start.11 = (bf16[1,1,1,2,1,128,1280]{6,5,4,3,2,1,0:T(8,128)(2,1)}, bf16[1,1,1,2,1,128,1280]{6,5,4,3,2,1,0:T(8,128)(2,1)}, u32[]{:S(2)}, u32[]{:S(2)}) collective-permute-start(bf16[1,1,1,2,1,128,1280]{6,5,4,3,2,1,0:T(8,128)(2,1)} %constant_dynamic-update-slice_fusion.16), channel_id=1, source_target_pairs={{0,1},{1,0},{2,3},{3,2},{4,5},{5,4},{6,7},{7,6},{8,9},{9,8},{10,11... | collective-permute-start | bytes 1966088 | tf_op jit(solution)/shard_map/ppermute | solution.py:35
  93.0 25.9 %collective-permute-start.12 = (bf16[1,2,2,2,2,128,384]{6,5,4,3,2,1,0:T(8,128)(2,1)S(1)}, bf16[1,2,2,2,2,128,384]{6,5,4,3,2,1,0:T(8,128)(2,1)S(1)}, u32[]{:S(2)}, u32[]{:S(2)}) collective-permute-start(bf16[1,2,2,2,2,128,384]{6,5,4,3,2,1,0:T(8,128)(2,1)S(1)} %constant_dynamic-update-slice_fusion.14), channel_id=1, source_target_pairs={{0,4},{4,0},{8,12},{12,8},{16,20},{20,16},{24,28},{28,24},{1,5},{5... | collective-permute-start | bytes 4718600 | tf_op jit(solution)/shard_map/ppermute | solution.py:35
  93.7 20.5 %collective-permute-start.10 = (bf16[128,1024]{1,0:T(8,128)(2,1)S(1)}, bf16[128,1024]{1,0:T(8,128)(2,1)S(1)}, u32[]{:S(2)}, u32[]{:S(2)}) collective-permute-start(bf16[128,1024]{1,0:T(8,128)(2,1)S(1)} %slice.175), channel_id=1, source_target_pairs={{0,1},{1,2},{2,3},{4,5},{5,6},{6,7},{8,9},{9,10},{10,11},{12,13},{... | collective-permute-start | bytes 786440 | tf_op jit(solution)/shard_map/ppermute | solution.py:1272
  95.9 19.8 %collective-permute-start.9 = (bf16[128,1024]{1,0:T(8,128)(2,1)S(1)}, bf16[128,1024]{1,0:T(8,128)(2,1)S(1)}, u32[]{:S(2)}, u32[]{:S(2)}) collective-permute-start(bf16[128,1024]{1,0:T(8,128)(2,1)S(1)} %slice.175), channel_id=1, source_target_pairs={{0,2},{1,3},{4,6},{5,7},{8,10},{9,11},{12,14},{13,15},{16,18},{17,... | collective-permute-start | bytes 786440 | tf_op jit(solution)/shard_map/ppermute | solution.py:1273
  109.7 21.0 %collective-permute-start.14 = (bf16[1,1,1,2,2,128,768]{6,5,4,3,2,1,0:T(8,128)(2,1)S(1)}, bf16[1,1,1,2,2,128,768]{6,5,4,3,2,1,0:T(8,128)(2,1)S(1)}, u32[]{:S(2)}, u32[]{:S(2)}) collective-permute-start(bf16[1,1,1,2,2,128,768]{6,5,4,3,2,1,0:T(8,128)(2,1)S(1)} %slice.178), channel_id=1, source_target_pairs={{0,8},{4,12},{8,0},{12,4},{16,24},{20,28},{24,16},{28,20},{1,9},{5... | collective-permute-start | bytes 2359304 | tf_op jit(solution)/shard_map/ppermute | solution.py:35
  111.3 18.3 %collective-permute-start.13 = (bf16[1,1,1,2,2,128,512]{6,5,4,3,2,1,0:T(8,128)(2,1)S(1)}, bf16[1,1,1,2,2,128,512]{6,5,4,3,2,1,0:T(8,128)(2,1)S(1)}, u32[]{:S(2)}, u32[]{:S(2)}) collective-permute-start(bf16[1,1,1,2,2,128,512]{6,5,4,3,2,1,0:T(8,128)(2,1)S(1)} %slice.179), channel_id=1, source_target_pairs={{0,16},{4,20},{8,24},{12,28},{16,0},{20,4},{24,8},{28,12},{1,17},{... | collective-permute-start | bytes 1572872 | tf_op jit(solution)/shard_map/ppermute | solution.py:35
  131.7 236.0 %all-gather.5.cloned.1.call-start = ((), (), s32[]{:S(2)}) async-start(), calls=%async_computation.2 | async-start | bytes 3932160 | tf_op jit(solution)/shard_map/all_gather | solution.py:1376
  132.6 59.7 %collective-permute-start.18 = (bf16[1,2,1,2,2,128,768]{6,5,4,3,2,1,0:T(8,128)(2,1)}, bf16[1,2,1,2,2,128,768]{6,5,4,3,2,1,0:T(8,128)(2,1)}, u32[]{:S(2)}, u32[]{:S(2)}) collective-permute-start(bf16[1,2,1,2,2,128,768]{6,5,4,3,2,1,0:T(8,128)(2,1)} %constant_dynamic-update-slice_fusion.28), channel_id=1, source_target_pairs={{0,16},{4,20},{8,24},{12,28},{16,0},{20,4},{24,8},{28,12},{1,17},{... | collective-permute-start | bytes 4718600 | tf_op jit(solution)/shard_map/ppermute | solution.py:35
  134.5 42.4 %collective-permute-start.17 = (bf16[1,1,2,2,2,128,512]{6,5,4,3,2,1,0:T(8,128)(2,1)S(1)}, bf16[1,1,2,2,2,128,512]{6,5,4,3,2,1,0:T(8,128)(2,1)}, u32[]{:S(2)}, u32[]{:S(2)}) collective-permute-start(bf16[1,1,2,2,2,128,512]{6,5,4,3,2,1,0:T(8,128)(2,1)S(1)} %constant_dynamic-update-slice_fusion.26), channel_id=1, source_target_pairs={{0,8},{4,12},{8,0},{12,4},{16,24},{20,28},{24,16},{28,20},{1,9},{5... | collective-permute-start | bytes 3145736 | tf_op jit(solution)/shard_map/ppermute | solution.py:35
  135.7 27.0 %collective-permute-start.16 = (bf16[256,1024]{1,0:T(8,128)(2,1)}, bf16[256,1024]{1,0:T(8,128)(2,1)}, u32[]{:S(2)}, u32[]{:S(2)}) collective-permute-start(bf16[256,1024]{1,0:T(8,128)(2,1)} %reorder.6), channel_id=1, source_target_pairs={{0,2},{1,3},{2,0},{3,1},{4,6},{5,7},{6,4},{7,5},{8,10},{9,11},{10,... | collective-permute-start | bytes 1572872 | tf_op jit(solution)/shard_map/ppermute | solution.py:35
  193.9 27.6 %collective-permute-start.21 = (bf16[1,2,2,2,2,128,768]{6,5,4,3,2,1,0:T(8,128)(2,1)S(1)}, bf16[1,2,2,2,2,128,768]{6,5,4,3,2,1,0:T(8,128)(2,1)}, u32[]{:S(2)}, u32[]{:S(2)}) collective-permute-start(bf16[1,2,2,2,2,128,768]{6,5,4,3,2,1,0:T(8,128)(2,1)S(1)} %constant_dynamic-update-slice_fusion.34), channel_id=1, source_target_pairs={{0,4},{4,0},{8,12},{12,8},{16,20},{20,16},{24,28},{28,24},{1,5},{5... | collective-permute-start | bytes 9437192 | tf_op jit(solution)/shard_map/ppermute | solution.py:35
  196.0 25.4 %collective-permute-start.20 = (bf16[512,1024]{1,0:T(8,128)(2,1)}, bf16[512,1024]{1,0:T(8,128)(2,1)S(1)}, u32[]{:S(2)}, u32[]{:S(2)}) collective-permute-start(bf16[512,1024]{1,0:T(8,128)(2,1)} %constant_dynamic-update-slice_fusion.30), channel_id=1, source_target_pairs={{0,1},{1,0},{2,3},{3,2},{4,5},{5,4},{6,7},{7,6},{8,9},{9,8},{10,11... | collective-permute-start | bytes 3145736 | tf_op jit(solution)/shard_map/ppermute | solution.py:35
  278.7 28.3 %collective-permute-start.22 = (bf16[4,4,128,1024]{3,2,1,0:T(8,128)(2,1)}, bf16[4,4,128,1024]{3,2,1,0:T(8,128)(2,1)}, u32[]{:S(2)}, u32[]{:S(2)}) collective-permute-start(bf16[4,4,128,1024]{3,2,1,0:T(8,128)(2,1)} %down_grad_send.1), channel_id=1, source_target_pairs={{0,4},{4,0},{8,12},{12,8},{16,20},{20,16},{24,28},{28,24},{1,5},{5... | collective-permute-start | bytes 12582920 | tf_op jit(solution)/shard_map/ppermute | solution.py:35
  301.5 13.5 %collective-permute-start.23 = (bf16[4,4,128,1024]{3,2,1,0:T(8,128)(2,1)}, bf16[4,4,128,1024]{3,2,1,0:T(8,128)(2,1)}, u32[]{:S(2)}, u32[]{:S(2)}) collective-permute-start(bf16[4,4,128,1024]{3,2,1,0:T(8,128)(2,1)} %up_grad_send.1), channel_id=1, source_target_pairs={{0,4},{4,0},{8,12},{12,8},{16,20},{20,16},{24,28},{28,24},{1,5},{5... | collective-permute-start | bytes 12582920 | tf_op jit(solution)/shard_map/ppermute | solution.py:35
  302.0 166.2 %reduce-scatter.2.cloned.1.call-start = ((), (), s32[]{:S(2)}) async-start(), calls=%async_computation.3 | async-start | bytes 2621440 | tf_op jit(solution)/shard_map/reduce_scatter | solution.py:182
  322.7 47.8 %collective-permute-start.25 = (bf16[2,4,128,1024]{3,2,1,0:T(8,128)(2,1)}, bf16[2,4,128,1024]{3,2,1,0:T(8,128)(2,1)S(1)}, u32[]{:S(2)}, u32[]{:S(2)}) collective-permute-start(bf16[2,4,128,1024]{3,2,1,0:T(8,128)(2,1)} %get-tuple-element.319), channel_id=1, source_target_pairs={{0,16},{4,20},{8,24},{12,28},{16,0},{20,4},{24,8},{28,12},{1,17},{... | collective-permute-start | bytes 6291464 | tf_op jit(solution)/shard_map/ppermute | solution.py:35
  324.4 47.6 %collective-permute-start.24 = (bf16[2,4,128,1024]{3,2,1,0:T(8,128)(2,1)}, bf16[2,4,128,1024]{3,2,1,0:T(8,128)(2,1)}, u32[]{:S(2)}, u32[]{:S(2)}) collective-permute-start(bf16[2,4,128,1024]{3,2,1,0:T(8,128)(2,1)} %get-tuple-element.317), channel_id=1, source_target_pairs={{0,8},{4,12},{8,0},{12,4},{16,24},{20,28},{24,16},{28,20},{1,9},{5... | collective-permute-start | bytes 6291464 | tf_op jit(solution)/shard_map/ppermute | solution.py:35
  378.0 24.4 %collective-permute-start.27 = (bf16[4,128,1024]{2,1,0:T(8,128)(2,1)}, bf16[4,128,1024]{2,1,0:T(8,128)(2,1)S(1)}, u32[]{:S(2)}, u32[]{:S(2)}) collective-permute-start(bf16[4,128,1024]{2,1,0:T(8,128)(2,1)} %get-tuple-element.343), channel_id=1, source_target_pairs={{0,8},{4,12},{8,0},{12,4},{16,24},{20,28},{24,16},{28,20},{1,9},{5... | collective-permute-start | bytes 3145736 | tf_op jit(solution)/shard_map/ppermute | solution.py:35
  379.3 24.2 %collective-permute-start.26 = (bf16[4,128,1024]{2,1,0:T(8,128)(2,1)}, bf16[4,128,1024]{2,1,0:T(8,128)(2,1)S(1)}, u32[]{:S(2)}, u32[]{:S(2)}) collective-permute-start(bf16[4,128,1024]{2,1,0:T(8,128)(2,1)} %get-tuple-element.341), channel_id=1, source_target_pairs={{0,16},{4,20},{8,24},{12,28},{16,0},{20,4},{24,8},{28,12},{1,17},{... | collective-permute-start | bytes 3145736 | tf_op jit(solution)/shard_map/ppermute | solution.py:35
  380.7 27.7 %collective-permute-start.28 = (bf16[512,1024]{1,0:T(8,128)(2,1)}, bf16[512,1024]{1,0:T(8,128)(2,1)S(1)}, u32[]{:S(2)}, u32[]{:S(2)}) collective-permute-start(bf16[512,1024]{1,0:T(8,128)(2,1)} %get-tuple-element.325), channel_id=1, source_target_pairs={{0,1},{1,0},{2,3},{3,2},{4,5},{5,4},{6,7},{7,6},{8,9},{9,8},{10,11... | collective-permute-start | bytes 3145736 | tf_op jit(solution)/shard_map/ppermute | solution.py:35
  430.3 18.3 %collective-permute-start.30 = (bf16[4,4,128,896]{3,2,1,0:T(8,128)(2,1)}, bf16[4,4,128,896]{3,2,1,0:T(8,128)(2,1)}, u32[]{:S(2)}, u32[]{:S(2)}) collective-permute-start(bf16[4,4,128,896]{3,2,1,0:T(8,128)(2,1)} %self_grad_send.1), channel_id=1, source_target_pairs={{0,4},{4,0},{8,12},{12,8},{16,20},{20,16},{24,28},{28,24},{1,5},{5... | collective-permute-start | bytes 11010056 | tf_op jit(solution)/shard_map/ppermute | solution.py:35
  442.1 36.9 %collective-permute-start.32 = (bf16[2,4,128,640]{3,2,1,0:T(8,128)(2,1)}, bf16[2,4,128,640]{3,2,1,0:T(8,128)(2,1)S(1)}, u32[]{:S(2)}, u32[]{:S(2)}) collective-permute-start(bf16[2,4,128,640]{3,2,1,0:T(8,128)(2,1)} %get-tuple-element.377), channel_id=1, source_target_pairs={{0,16},{4,20},{8,24},{12,28},{16,0},{20,4},{24,8},{28,12},{1,17},{... | collective-permute-start | bytes 3932168 | tf_op jit(solution)/shard_map/ppermute | solution.py:35
  443.6 35.4 %collective-permute-start.31 = (bf16[2,4,128,640]{3,2,1,0:T(8,128)(2,1)}, bf16[2,4,128,640]{3,2,1,0:T(8,128)(2,1)}, u32[]{:S(2)}, u32[]{:S(2)}) collective-permute-start(bf16[2,4,128,640]{3,2,1,0:T(8,128)(2,1)} %get-tuple-element.360), channel_id=1, source_target_pairs={{0,8},{4,12},{8,0},{12,4},{16,24},{20,28},{24,16},{28,20},{1,9},{5... | collective-permute-start | bytes 3932168 | tf_op jit(solution)/shard_map/ppermute | solution.py:35
  457.4 40.6 %collective-permute-start.33 = (bf16[2,4,128,512]{3,2,1,0:T(8,128)(2,1)}, bf16[2,4,128,512]{3,2,1,0:T(8,128)(2,1)S(1)}, u32[]{:S(2)}, u32[]{:S(2)}) collective-permute-start(bf16[2,4,128,512]{3,2,1,0:T(8,128)(2,1)} %get-tuple-element.362), channel_id=1, source_target_pairs={{0,8},{4,12},{8,0},{12,4},{16,24},{20,28},{24,16},{28,20},{1,9},{5... | collective-permute-start | bytes 3145736 | tf_op jit(solution)/shard_map/ppermute | solution.py:35
  458.3 32.7 %collective-permute-start.34 = (bf16[2,4,128,384]{3,2,1,0:T(8,128)(2,1)}, bf16[2,4,128,384]{3,2,1,0:T(8,128)(2,1)}, u32[]{:S(2)}, u32[]{:S(2)}) collective-permute-start(bf16[2,4,128,384]{3,2,1,0:T(8,128)(2,1)} %get-tuple-element.387), channel_id=1, source_target_pairs={{0,16},{4,20},{8,24},{12,28},{16,0},{20,4},{24,8},{28,12},{1,17},{... | collective-permute-start | bytes 2359304 | tf_op jit(solution)/shard_map/ppermute | solution.py:35
  484.3 30.3 %collective-permute-start.38 = (bf16[4,128,640]{2,1,0:T(8,128)(2,1)}, bf16[4,128,640]{2,1,0:T(8,128)(2,1)S(1)}, u32[]{:S(2)}, u32[]{:S(2)}) collective-permute-start(bf16[4,128,640]{2,1,0:T(8,128)(2,1)} %get-tuple-element.381), channel_id=1, source_target_pairs={{0,8},{4,12},{8,0},{12,4},{16,24},{20,28},{24,16},{28,20},{1,9},{5... | collective-permute-start | bytes 1966088 | tf_op jit(solution)/shard_map/ppermute | solution.py:35
  485.8 28.8 %collective-permute-start.37 = (bf16[4,128,640]{2,1,0:T(8,128)(2,1)}, bf16[4,128,640]{2,1,0:T(8,128)(2,1)S(1)}, u32[]{:S(2)}, u32[]{:S(2)}) collective-permute-start(bf16[4,128,640]{2,1,0:T(8,128)(2,1)} %get-tuple-element.379), channel_id=1, source_target_pairs={{0,16},{4,20},{8,24},{12,28},{16,0},{20,4},{24,8},{28,12},{1,17},{... | collective-permute-start | bytes 1966088 | tf_op jit(solution)/shard_map/ppermute | solution.py:35
  487.3 16.3 %collective-permute-start.35 = (bf16[128,1024]{1,0:T(8,128)(2,1)}, bf16[128,1024]{1,0:T(8,128)(2,1)}, u32[]{:S(2)}, u32[]{:S(2)}) collective-permute-start(bf16[128,1024]{1,0:T(8,128)(2,1)} %get-tuple-element.394), channel_id=1, source_target_pairs={{1,0},{2,1},{3,2},{5,4},{6,5},{7,6},{9,8},{10,9},{11,10},{13,12},{... | collective-permute-start | bytes 786440 | tf_op jit(solution)/shard_map/ppermute | solution.py:1436
  490.9 17.3 %collective-permute-start.36 = (bf16[128,1024]{1,0:T(8,128)(2,1)}, bf16[128,1024]{1,0:T(8,128)(2,1)}, u32[]{:S(2)}, u32[]{:S(2)}) collective-permute-start(bf16[128,1024]{1,0:T(8,128)(2,1)} %get-tuple-element.395), channel_id=1, source_target_pairs={{2,0},{3,1},{6,4},{7,5},{10,8},{11,9},{14,12},{15,13},{18,16},{19,... | collective-permute-start | bytes 786440 | tf_op jit(solution)/shard_map/ppermute | solution.py:1435
  502.3 21.0 %collective-permute-start.40 = (bf16[4,128,512]{2,1,0:T(8,128)(2,1)}, bf16[4,128,512]{2,1,0:T(8,128)(2,1)S(1)}, u32[]{:S(2)}, u32[]{:S(2)}) collective-permute-start(bf16[4,128,512]{2,1,0:T(8,128)(2,1)} %get-tuple-element.389), channel_id=1, source_target_pairs={{0,16},{4,20},{8,24},{12,28},{16,0},{20,4},{24,8},{28,12},{1,17},{... | collective-permute-start | bytes 1572872 | tf_op jit(solution)/shard_map/ppermute | solution.py:35
  503.6 19.7 %collective-permute-start.41 = (bf16[4,128,384]{2,1,0:T(8,128)(2,1)}, bf16[4,128,384]{2,1,0:T(8,128)(2,1)S(1)}, u32[]{:S(2)}, u32[]{:S(2)}) collective-permute-start(bf16[4,128,384]{2,1,0:T(8,128)(2,1)} %get-tuple-element.409), channel_id=1, source_target_pairs={{0,8},{4,12},{8,0},{12,4},{16,24},{20,28},{24,16},{28,20},{1,9},{5... | collective-permute-start | bytes 1179656 | tf_op jit(solution)/shard_map/ppermute | solution.py:35
  519.1 32.7 %collective-permute-start.44 = (bf16[2,128,1280]{2,1,0:T(8,128)(2,1)}, bf16[2,128,1280]{2,1,0:T(8,128)(2,1)S(1)}, u32[]{:S(2)}, u32[]{:S(2)}) collective-permute-start(bf16[2,128,1280]{2,1,0:T(8,128)(2,1)} %get-tuple-element.400), channel_id=1, source_target_pairs={{0,1},{1,0},{2,3},{3,2},{4,5},{5,4},{6,7},{7,6},{8,9},{9,8},{10,11... | collective-permute-start | bytes 1966088 | tf_op jit(solution)/shard_map/ppermute | solution.py:35
  519.1 26.6 %collective-permute-start.43 = (bf16[1,256,1024]{2,1,0:T(8,128)(2,1)S(1)}, bf16[1,256,1024]{2,1,0:T(8,128)(2,1)S(1)}, u32[]{:S(2)}, u32[]{:S(2)}) collective-permute-start(bf16[1,256,1024]{2,1,0:T(8,128)(2,1)S(1)} %copy-done.52), channel_id=1, source_target_pairs={{0,2},{1,3},{2,0},{3,1},{4,6},{5,7},{6,4},{7,5},{8,10},{9,11},{10,... | collective-permute-start | bytes 1572872 | tf_op jit(solution)/shard_map/ppermute | solution.py:35
  527.4 31.2 %collective-permute-start.46 = (bf16[2,128,896]{2,1,0:T(8,128)(2,1)}, bf16[2,128,896]{2,1,0:T(8,128)(2,1)S(1)}, u32[]{:S(2)}, u32[]{:S(2)}) collective-permute-start(bf16[2,128,896]{2,1,0:T(8,128)(2,1)} %get-tuple-element.411), channel_id=1, source_target_pairs={{0,1},{1,0},{2,3},{3,2},{4,5},{5,4},{6,7},{7,6},{8,9},{9,8},{10,11... | collective-permute-start | bytes 1376264 | tf_op jit(solution)/shard_map/ppermute | solution.py:35
  531.9 23.0 %collective-permute-start.45 = (f32[17920]{0:T(1024)S(1)}, f32[17920]{0:T(1024)S(1)}, u32[]{:S(2)}, u32[]{:S(2)}) collective-permute-start(f32[17920]{0:T(1024)S(1)} %add.86), channel_id=1, source_target_pairs={{0,16},{4,20},{8,24},{12,28},{16,0},{20,4},{24,8},{28,12},{1,17},{... | collective-permute-start | bytes 215048 | tf_op jit(solution)/shard_map/ppermute | solution.py:35
  558.6 20.7 %collective-permute-start.48 = (bf16[1,128,1280]{2,1,0:T(8,128)(2,1)}, bf16[1,128,1280]{2,1,0:T(8,128)(2,1)S(1)}, u32[]{:S(2)}, u32[]{:S(2)}) collective-permute-start(bf16[1,128,1280]{2,1,0:T(8,128)(2,1)} %get-tuple-element.420), channel_id=1, source_target_pairs={{0,2},{1,3},{2,0},{3,1},{4,6},{5,7},{6,4},{7,5},{8,10},{9,11},{10,... | collective-permute-start | bytes 983048 | tf_op jit(solution)/shard_map/ppermute | solution.py:35
  561.4 21.3 %collective-permute-start.49 = (bf16[1,128,896]{2,1,0:T(8,128)(2,1)}, bf16[1,128,896]{2,1,0:T(8,128)(2,1)S(1)}, u32[]{:S(2)}, u32[]{:S(2)}) collective-permute-start(bf16[1,128,896]{2,1,0:T(8,128)(2,1)} %get-tuple-element.427), channel_id=1, source_target_pairs={{0,2},{1,3},{2,0},{3,1},{4,6},{5,7},{6,4},{7,5},{8,10},{9,11},{10,... | collective-permute-start | bytes 688136 | tf_op jit(solution)/shard_map/ppermute | solution.py:35
  564.3 20.9 %collective-permute-start.50 = (f32[17920]{0:T(1024)S(1)}, f32[17920]{0:T(1024)S(1)}, u32[]{:S(2)}, u32[]{:S(2)}) collective-permute-start(f32[17920]{0:T(1024)S(1)} %add.88), channel_id=1, source_target_pairs={{0,2},{1,3},{2,0},{3,1},{4,6},{5,7},{6,4},{7,5},{8,10},{9,11},{10,... | collective-permute-start | bytes 215048 | tf_op jit(solution)/shard_map/ppermute | solution.py:35
  (59 other events, 401.6 us)
Sparse Core Ops, SparseCore 0:
  131.8 114.5 all-gather.2
  302.1 65.5 all-gather.4
  422.1 46.0 reduce-scatter.1

commit v4 on v3

--- a/solution.py
+++ b/solution.py
@@ -111,6 +111,30 @@
     )(*[array for pair in parts for array in pair])
 
 
+def split_sum(mine, came, cuts):
+    rows = mine.shape[0]
+
+    def body(mine_ref, came_ref, *out_refs):
+        for out_ref, (first, width, copies) in zip(out_refs, cuts):
+            for k in range(copies):
+                cols = slice(first + k * width, first + (k + 1) * width)
+                total = mine_ref[:, cols].astype(F32) + came_ref[:, cols].astype(F32)
+                if copies > 1:
+                    out_ref[k] = total
+                else:
+                    out_ref[...] = total
+
+    return pl.pallas_call(
+        body,
+        out_shape=[
+            jax.ShapeDtypeStruct((copies, rows, width) if copies > 1 else (rows, width), F32)
+            for _, width, copies in cuts
+        ],
+        compiler_params=params(),
+        name="split_sum",
+    )(mine, came)
+
+
 class Gather:
     def __init__(self, line, shard):
         self.line = line
@@ -137,8 +161,8 @@
 
 
 class Scatter:
-    def __init__(self, line, parts, orders, natural=False):
-        self.natural = natural
+    def __init__(self, line, parts, orders, natural=False, cuts=()):
+        self.natural, self.cuts = natural, cuts
         nb, self.nz = bits_of("batch"), bits_of("head")
         self.line = line
         self.groups, self.blk = parts[0][1].shape[1:3]
@@ -185,8 +209,8 @@
             self.total = total.astype(F32)
             return
         if not self.heads:
-            (total,) = add_blocks(pairs, [([0], everyone)], F32)
-            self.total = self.line.mark(total).reshape(self.blk, -1)
+            self.total = split_sum(pairs[0][0][0], pairs[0][1][0], self.cuts)
+            self.line.mark(*self.total)
             return
         bit = self.heads.pop(0)
         sides = [[k for k in blocks if (k & 1) == side] for side in (1, 0)]
@@ -219,21 +243,23 @@
     return turned
 
 
-def reorder_blocks(array_in, table):
+def reorder_blocks(array_in, table, dtype=None):
     count = table.shape[0]
     rows, features = array_in.shape
     blk = features // count
+    dtype = dtype or array_in.dtype
     if blk % 128:
-        return jnp.take(array_in.reshape(rows, count, blk), table, axis=1).reshape(rows, features)
+        blocks = jnp.take(array_in.reshape(rows, count, blk), table, axis=1)
+        return blocks.reshape(rows, features).astype(dtype)
 
     def body(table_ref, in_ref, out_ref):
         for p in range(count):
             start = pl.multiple_of(table_ref[p] * blk, blk)
-            out_ref[:, p * blk : (p + 1) * blk] = in_ref[:, pl.ds(start, blk)]
+            out_ref[:, p * blk : (p + 1) * blk] = in_ref[:, pl.ds(start, blk)].astype(dtype)
 
     return pl.pallas_call(
         body,
-        out_shape=jax.ShapeDtypeStruct(array_in.shape, array_in.dtype),
+        out_shape=jax.ShapeDtypeStruct(array_in.shape, dtype),
         grid_spec=pltpu.PrefetchScalarGridSpec(
             num_scalar_prefetch=1,
             grid=(1,),
@@ -384,92 +410,6 @@
         to_ref[:, p * blk : (p + 1) * blk] = from_ref[:, pl.ds(start, blk)]
 
 
-def flat_natural(ref):
-    count, _, blk, cols = ref.shape
-    return ref[...].reshape(count * blk, cols)
-
-
-def feed_forward(order, low, normed, weights, up_bias, vectors, grad_out):
-    rows, features = normed.shape
-    batches, groups, blk, both = weights.shape
-    cols = both // 2
-
-    def body(
-        order_ref, low_ref, normed_ref, up_ref, down_ref, bias_ref, vectors_ref, grad_ref,
-        active_ref, slope_ref, out_ref, third_ref, third_low_ref, sums_ref,
-        natural_ref, acc_ref, turned_ref,
-    ):
-        step = pl.program_id(0)
-
-        @pl.when(step == 0)
-        def _():
-            natural_from_exchange(order_ref, groups, low_ref, natural_ref, blk)
-            acc_ref[...] = jnp.zeros_like(acc_ref)
-
-        upper = dot(natural_ref[...], flat_natural(up_ref), 1, 0) + bias_ref[...]
-        cdf = 0.5 * (1.0 + lax.erf(upper * 0.7071067811865476))
-        active = (upper * cdf).astype(BF)
-        slope = cdf + upper * jnp.exp(-0.5 * upper * upper) * 0.3989422804014327
-        active_ref[...] = active
-        slope_ref[...] = slope.astype(BF)
-        acc_ref[...] += dot(active, flat_natural(down_ref), 1, 1)
-
-        @pl.when(step == groups - 1)
-        def _():
-            exchange_from_natural(order_ref, groups, acc_ref, turned_ref, blk)
-            v = normed_ref[...] + (turned_ref[...] + vectors_ref[2:3])
-            unit, spread = normalize(v)
-            gain = vectors_ref[0:1]
-            out_ref[...] = (unit * gain + vectors_ref[1:2]).astype(BF)
-            upstream = grad_ref[...]
-            third = normalize_back(upstream, unit, spread, gain)
-            third_ref[...] = third
-            third_low_ref[...] = third.astype(BF)
-            sums_ref[0:1] = column_sum(upstream * unit)
-            sums_ref[1:2] = column_sum(upstream)
-            sums_ref[2:3] = column_sum(third)
-
-    return pl.pallas_call(
-        body,
-        grid_spec=pltpu.PrefetchScalarGridSpec(
-            num_scalar_prefetch=1,
-            grid=(groups,),
-            in_specs=[
-                whole((rows, features)),
-                whole((rows, features)),
-                pl.BlockSpec((batches, 1, blk, cols), lambda j, order: (0, j, 0, 0)),
-                pl.BlockSpec((batches, 1, blk, cols), lambda j, order: (0, j, 0, 1)),
-                pl.BlockSpec((1, cols), lambda j, order: (0, j)),
-                whole((3, features)),
-                whole((rows, features)),
-            ],
-            out_specs=[
-                pl.BlockSpec((rows, cols), lambda j, order: (0, j)),
-                pl.BlockSpec((rows, cols), lambda j, order: (0, j)),
-                whole((rows, features)),
-                whole((rows, features)),
-                whole((rows, features)),
-                whole((3, features)),
-            ],
-            scratch_shapes=[
-                pltpu.VMEM((rows, features), BF),
-                pltpu.VMEM((rows, features), F32),
-                pltpu.VMEM((rows, features), F32),
-            ],
-        ),
-        out_shape=[
-            jax.ShapeDtypeStruct((rows, groups * cols), BF),
-            jax.ShapeDtypeStruct((rows, groups * cols), BF),
-            jax.ShapeDtypeStruct((rows, features), BF),
-            jax.ShapeDtypeStruct((rows, features), F32),
-            jax.ShapeDtypeStruct((rows, features), BF),
-            jax.ShapeDtypeStruct((3, features), F32),
-        ],
-        compiler_params=params(),
-        name="feed_forward",
-    )(order, low, normed, weights, weights, up_bias, vectors, grad_out)
-
-
 def norm_back_outputs(upstream, unit, spread, gain, grad_ref, grad_low_ref, sums_ref):
     grad = normalize_back(upstream, unit, spread, gain)
     grad_ref[...] = grad
@@ -479,31 +419,88 @@
     sums_ref[2:3] = column_sum(grad)
 
 
-def feed_forward_back(order, third_low, third, slope, weights, unit, spread, gain):
-    rows, features = third.shape
+def held(shape):
+    return pl.BlockSpec(shape, lambda *_: (0,) * len(shape), pipeline_mode=pl.Buffered(1))
+
+
+def feed_forward(
+    order, low, normed, weights, up_bias, vectors, grad_out, unit, spread, gain, out_pieces, out_col
+):
+    rows, features = normed.shape
     batches, groups, blk, both = weights.shape
     cols = both // 2
-
-    def body(
-        order_ref, third_low_ref, third_ref, slope_ref, up_ref, down_ref, unit_ref, spread_ref, gain_ref,
-        upper_ref, bias_ref, grad_ref, grad_low_ref, sums_ref,
-        natural_ref, acc_ref, turned_ref,
-    ):
+    width = out_pieces[0].shape[3] - out_col
+    count = len(out_pieces)
+
+    def body(order_ref, low_ref, normed_ref, weights_ref, bias_ref, vectors_ref, grad_ref, unit_ref,
+             spread_ref, gain_ref, *refs):
+        piece_refs = refs[:count]
+        (
+            active_ref, out_ref, third_low_ref, third_sums_ref, upper_ref, bias_sum_ref,
+            second_ref, second_low_ref, second_sums_ref, ctx_ref,
+            held_ref, natural_ref, acc_ref, turned_ref, third_ref, slope_ref, sems,
+        ) = refs[count:]
         step = pl.program_id(0)
+
+        def copy(j):
+            return pltpu.make_async_copy(weights_ref.at[:, j], held_ref.at[j], sems.at[j])
 
         @pl.when(step == 0)
         def _():
+            for j in range(groups):
+                copy(j).start()
+            natural_from_exchange(order_ref, groups, low_ref, natural_ref, blk)
+            acc_ref[...] = jnp.zeros_like(acc_ref)
+
+        for j in range(groups):
+
+            @pl.when(step == j)
+            def _():
+                copy(j).wait()
+
+        @pl.when(step < groups)
+        def _():
+            up = held_ref[step, :, :, 0:cols].reshape(features, cols)
+            upper = dot(natural_ref[...], up, 1, 0) + bias_ref[...]
+            cdf = 0.5 * (1.0 + lax.erf(upper * 0.7071067811865476))
+            active = (upper * cdf).astype(BF)
+            slope = cdf + upper * jnp.exp(-0.5 * upper * upper) * 0.3989422804014327
+            active_ref[...] = active
+            slope_ref[step] = slope.astype(BF)
+            down = held_ref[step, :, :, cols:].reshape(features, cols)
+            acc_ref[...] += dot(active, down, 1, 1)
+
+        @pl.when(step == groups - 1)
+        def _():
+            exchange_from_natural(order_ref, groups, acc_ref, turned_ref, blk)
+            v = normed_ref[...] + (turned_ref[...] + vectors_ref[2:3])
+            unit3, spread3 = normalize(v)
+            gain3 = vectors_ref[0:1]
+            turned_ref[...] = unit3 * gain3 + vectors_ref[1:2]
+            natural_from_exchange(order_ref, groups, turned_ref, acc_ref, blk)
+            out_ref[...] = acc_ref[...].astype(BF)
+            upstream = grad_ref[...]
+            third = normalize_back(upstream, unit3, spread3, gain3)
+            third_ref[...] = third
+            third_low_ref[...] = third.astype(BF)
+            third_sums_ref[0:1] = column_sum(upstream * unit3)
+            third_sums_ref[1:2] = column_sum(upstream)
+            third_sums_ref[2:3] = column_sum(third)
             natural_from_exchange(order_ref, groups, third_low_ref, natural_ref, blk)
             acc_ref[...] = jnp.zeros_like(acc_ref)
 
-        grad_upper = dot(natural_ref[...], flat_natural(down_ref), 1, 0)
-        grad_upper = grad_upper * slope_ref[...].astype(F32)
-        bias_ref[...] = column_sum(grad_upper)
-        low = grad_upper.astype(BF)
-        upper_ref[...] = low
-        acc_ref[...] += dot(low, flat_natural(up_ref), 1, 1)
-
-        @pl.when(step == groups - 1)
+        @pl.when((step >= groups) & (step < 2 * groups))
+        def _():
+            j = step - groups
+            down = held_ref[j, :, :, cols:].reshape(features, cols)
+            grad_upper = dot(natural_ref[...], down, 1, 0) * slope_ref[j].astype(F32)
+            bias_sum_ref[...] = column_sum(grad_upper)
+            low = grad_upper.astype(BF)
+            upper_ref[...] = low
+            up = held_ref[j, :, :, 0:cols].reshape(features, cols)
+            acc_ref[...] += dot(low, up, 1, 1)
+
+        @pl.when(step == 2 * groups - 1)
         def _():
             exchange_from_natural(order_ref, groups, acc_ref, turned_ref, blk)
             norm_back_outputs(
@@ -511,49 +508,91 @@
                 unit_ref[...],
                 spread_ref[...],
                 gain_ref[...],
-                grad_ref,
-                grad_low_ref,
-                sums_ref,
+                second_ref,
+                second_low_ref,
+                second_sums_ref,
             )
 
+        @pl.when(step == 2 * groups)
+        def _():
+            low = second_low_ref[...]
+            for j in range(groups):
+                total = None
+                depth = features // count
+                for number, ref in enumerate(piece_refs):
+                    piece = ref[:, j].reshape(depth, width)
+                    term = dot(low[:, number * depth : (number + 1) * depth], piece, 1, 0)
+                    total = term if total is None else total + term
+                ctx_ref[:, j * width : (j + 1) * width] = total.astype(BF)
+
+    def forward_block(j, order):
+        return (0, jnp.minimum(j, groups - 1))
+
+    def backward_block(j, order):
+        return (0, jnp.clip(j - groups, 0, groups - 1))
+
+    piece_rows = out_pieces[0].shape[0]
     return pl.pallas_call(
         body,
         grid_spec=pltpu.PrefetchScalarGridSpec(
             num_scalar_prefetch=1,
-            grid=(groups,),
+            grid=(2 * groups + 1,),
             in_specs=[
-                whole((rows, features)),
-                whole((rows, features)),
-                pl.BlockSpec((rows, cols), lambda j, order: (0, j)),
-                pl.BlockSpec((batches, 1, blk, cols), lambda j, order: (0, j, 0, 0)),
-                pl.BlockSpec((batches, 1, blk, cols), lambda j, order: (0, j, 0, 1)),
-                whole((rows, features)),
-                whole((rows, 1)),
-                whole((1, features)),
+                held((rows, features)),
+                held((rows, features)),
+                pl.BlockSpec(memory_space=pl.ANY),
+                pl.BlockSpec((1, cols), forward_block),
+                held((3, features)),
+                held((rows, features)),
+                held((rows, features)),
+                held((rows, 1)),
+                held((1, features)),
+            ]
+            + [
+                pl.BlockSpec(
+                    (piece_rows, groups, blk, width),
+                    lambda j, order: (0, 0, 0, out_col // width),
+                    pipeline_mode=pl.Buffered(1),
+                )
+                for _ in out_pieces
             ],
             out_specs=[
-                pl.BlockSpec((rows, cols), lambda j, order: (0, j)),
-                pl.BlockSpec((1, cols), lambda j, order: (0, j)),
+                pl.BlockSpec((rows, cols), forward_block),
                 whole((rows, features)),
                 whole((rows, features)),
                 whole((3, features)),
+                pl.BlockSpec((rows, cols), backward_block),
+                pl.BlockSpec((1, cols), backward_block),
+                whole((rows, features)),
+                whole((rows, features)),
+                whole((3, features)),
+                whole((rows, groups * width)),
             ],
             scratch_shapes=[
+                pltpu.VMEM((groups, batches, blk, both), BF),
                 pltpu.VMEM((rows, features), BF),
                 pltpu.VMEM((rows, features), F32),
                 pltpu.VMEM((rows, features), F32),
+                pltpu.VMEM((rows, features), F32),
+                pltpu.VMEM((groups, rows, cols), BF),
+                pltpu.SemaphoreType.DMA((groups,)),
             ],
         ),
         out_shape=[
+            jax.ShapeDtypeStruct((rows, groups * cols), BF),
+            jax.ShapeDtypeStruct((rows, features), BF),
+            jax.ShapeDtypeStruct((rows, features), BF),
+            jax.ShapeDtypeStruct((3, features), F32),
             jax.ShapeDtypeStruct((rows, groups * cols), BF),
             jax.ShapeDtypeStruct((1, groups * cols), F32),
             jax.ShapeDtypeStruct((rows, features), F32),
             jax.ShapeDtypeStruct((rows, features), BF),
             jax.ShapeDtypeStruct((3, features), F32),
+            jax.ShapeDtypeStruct((rows, groups * width), BF),
         ],
         compiler_params=params(),
-        name="feed_forward_back",
-    )(order, third_low, third, slope, weights, weights, unit, spread, gain)
+        name="feed_forward",
+    )(order, low, normed, weights, up_bias, vectors, grad_out, unit, spread, gain, *out_pieces)
 
 
 def cross_query_back(grad_query, pieces, first_col, cols, second, unit, spread, gain):
@@ -604,15 +643,16 @@
     )(grad_query, *pieces, second, unit, spread, gain)
 
 
-def rows_back(left, pieces, first_col, cols, name):
+def rows_back(order, left, pieces, first_col, cols, name):
     rows = left.shape[0]
     count = len(pieces)
     groups = pieces[0].shape[1]
     features = count * pieces[0].shape[0] * pieces[0].shape[2]
-
-    def body(left_ref, *refs):
+    span = rows // groups
+
+    def body(order_ref, left_ref, *refs):
         piece_refs = refs[:count]
-        low_ref, high_ref, acc_ref = refs[count:]
+        out_ref, acc_ref = refs[count:]
         step = pl.program_id(0)
 
         @pl.when(step == 0)
@@ -623,20 +663,30 @@
 
         @pl.when(step == groups - 1)
         def _():
-            low_ref[...] = acc_ref[0 : rows // 2].astype(BF)
-            high_ref[...] = acc_ref[rows // 2 :].astype(BF)
-
+            for k in range(groups):
+                start = pl.multiple_of(order_ref[k] * span, span)
+                out_ref[pl.ds(start, span)] = acc_ref[k * span : (k + 1) * span].astype(BF)
+
+    piece_count, _, blk, _ = pieces[0].shape
     return pl.pallas_call(
         body,
-        grid=(groups,),
-        in_specs=[pl.BlockSpec((rows, cols), lambda j: (0, j))]
-        + piece_specs(pieces, cols, first_col // cols),
-        out_specs=[whole((rows // 2, features))] * 2,
-        out_shape=[jax.ShapeDtypeStruct((rows // 2, features), BF)] * 2,
-        scratch_shapes=[pltpu.VMEM((rows, features), F32)],
+        grid_spec=pltpu.PrefetchScalarGridSpec(
+            num_scalar_prefetch=1,
+            grid=(groups,),
+            in_specs=[pl.BlockSpec((rows, cols), lambda j, order: (0, j))]
+            + [
+                pl.BlockSpec(
+                    (piece_count, 1, blk, cols), lambda j, order: (0, j, 0, first_col // cols)
+                )
+                for _ in pieces
+            ],
+            out_specs=whole((rows, features)),
+            scratch_shapes=[pltpu.VMEM((rows, features), F32)],
+        ),
+        out_shape=jax.ShapeDtypeStruct((rows, features), BF),
         compiler_params=params(),
         name=name,
-    )(left, *pieces)
+    )(order, left, *pieces)
 
 
 def input_back(grad_query, grad_kv, grad_rel, pieces, others, first):
@@ -1325,10 +1375,14 @@
         line.tie(cross_context), weights_kv, 512, 256, normed1, vectors[1], "cross_out"
     )
     line.mark(normed2)
-    active, slope, out_low, third, third_low, sums_third = feed_forward(
-        order, line.tie(normed2_low), normed2, weights_ffn, up_row, vectors[2], upstream
-    )
-    line.mark(third)
+    (
+        active, out_low, third_low, sums_third, upper_low, up_sums,
+        second, second_low, sums_second, grad_cross_ctx,
+    ) = feed_forward(
+        order, line.tie(normed2_low), normed2, weights_ffn, up_row, vectors[2], upstream,
+        unit2, spread2, vectors[1][0:1], weights_kv, 512,
+    )
+    line.mark(second)
 
     straight_order = lax.iota(jnp.int32, groups)
 
@@ -1371,18 +1425,14 @@
         )
 
     down_entries = [(third_low, active)]
-    out_low = line.mark(reorder_blocks(line.tie(out_low), to_natural))
+    if blk % 128:
+        out_low = reorder_blocks(out_low, to_natural)
     out_low = out_low.reshape(3, share, features)
     layer_out = lax.all_gather(jnp.transpose(out_low, (1, 0, 2)), "head", axis=0, tiled=True)[None]
+    down_entries = [(third_low, active)]
     down_came = send(down_entries, "down_grad", True)
-    upper_low, up_sums, second, second_low, sums_second = feed_forward_back(
-        order, line.tie(third_low), third, slope, weights_ffn, unit2, spread2, vectors[1][0:1]
-    )
-    line.mark(second)
     up_entries = [(normed2_low, upper_low)]
     up_came = send(up_entries, "up_grad", True)
-    grad_cross_ctx = project_plain(line.tie(second_low), weights_kv, 512, 256, "cross_ctx_back")
-    line.mark(grad_cross_ctx)
     down_halves = keep(down_entries, down_came, [(1024, near)], "down_grad", True)
     up_halves = keep(up_entries, up_came, [(1024, far)], "up_grad", True)
     scatter_ffn = Scatter(line, down_halves + up_halves, (near, far), True)
@@ -1390,29 +1440,27 @@
         cross_q, cross_kv, cross_probs, cross_scales, line.tie(grad_cross_ctx)
     )
     line.mark(grad_cross_q)
-    memory_part = rows_back(line.tie(grad_cross_kv), weights_kv, 0, 512, "memory_back")
-    span = memory.shape[1]
-    line.mark(*memory_part)
-    memory_mine, memory_came = memory_part[0], swap(memory_part[1], "head", 1)
     first, first_low, sums_first = cross_query_back(
         line.tie(grad_cross_q), weights_out, 256, 256, second, unit1, spread1, vectors[0][0:1]
     )
     line.mark(first)
     grad_context = project_plain(line.tie(first_low), weights_out, 0, 256, "self_ctx_back")
     line.mark(grad_context)
-    layer_out = line.tie(layer_out)
-    line.mark(layer_out, grad_context)
     scatter_ffn.step()
     grad_q, grad_kv, grad_rel, self_sums, rel_sums = self_attention_back(
         qk, values, self_probs, self_own, line.tie(grad_context), straight.reshape(-1, 1), share
     )
     line.mark(grad_q)
     scatter_ffn.step()
-    memory_mine, memory_came = line.tie(memory_mine), after(memory_came, *line.last)
-    pair = (memory_mine.reshape(2, span, features), memory_came.reshape(2, span, features))
-    theirs, memory_mine = add_blocks([pair], [([1], [0]), ([0], [0])], BF)
-    line.mark(theirs, memory_mine)
-    memory_came = swap(theirs, "head", 2)
+    layer_out = line.tie(layer_out)
+    line.mark(layer_out, *line.last)
+    memory_order = z ^ jnp.array([0, 2, 1, 3], jnp.int32)
+    memory_part = rows_back(
+        memory_order, line.tie(grad_cross_kv), weights_kv, 0, 512, "memory_back"
+    )
+    memory_grad = lax.psum_scatter(
+        line.mark(memory_part), "head", scatter_dimension=0, tiled=True
+    )
     cross_entries = [
         (normed1_low, grad_cross_q),
         (memory_all, grad_cross_kv),
@@ -1423,9 +1471,10 @@
     self_entries = [(own, grad_q), (extended, grad_kv), (own, grad_rel)]
     self_came = send(self_entries, "self_grad")
     halves = keep(cross_entries, cross_came, [(640, near), (640, far)], "cross_grad")
-    scatter_cross = Scatter(line, halves, (near, far))
+    cross_cuts = ((0, 256, 1), (256, 512, 1), (768, 256, 1), (1024, 256, 1))
+    scatter_cross = Scatter(line, halves, (near, far), cuts=cross_cuts)
     halves = keep(self_entries, self_came, [(512, near), (384, far)], "self_grad")
-    scatter_self = Scatter(line, halves, (near, far))
+    scatter_self = Scatter(line, halves, (near, far), cuts=((0, 256, 3), (768, 128, 1)))
     while not hasattr(scatter_ffn, "total"):
         scatter_ffn.step()
     two_grad, one_grad, own_grad = input_back(
@@ -1447,6 +1496,8 @@
         packed = line.tie(packed)
         return line.mark(packed + after(came, packed))
 
+    memory_grad = line.tie(memory_grad)
+    line.mark(memory_grad, *line.last)
     own_grad = line.mark(add_halo(line.tie(own_grad), from_one, from_two))
     own_grad = line.mark(reorder_blocks(line.tie(own_grad), to_natural)).reshape(
         3, share, features
@@ -1456,10 +1507,7 @@
     packed = add_packed(packed)
     scatter_self.step()
     packed = add_packed(packed)
-    memory_mine, memory_came = line.tie(memory_mine), after(memory_came, *line.last)
-    (memory_grad,) = add_blocks([(memory_mine, memory_came)], [([0], [0])], F32)
-    memory_grad = line.mark(memory_grad)[0]
-    grad_memory = line.mark(reorder_blocks(line.tie(memory_grad), to_natural))[None]
+    grad_memory = line.mark(reorder_blocks(line.tie(memory_grad), to_natural, F32))[None]
     scatter_cross.step()
     packed = add_packed(packed)
     scatter_self.step()
@@ -1487,12 +1535,12 @@
         layer_out,
         grad_hidden,
         grad_memory,
-        grads_self[:, 0:768].reshape(blk, 3, 256),
-        grads_self[:, 768:896],
-        grads_cross[:, 1024:1280],
-        grads_cross[:, 0:256],
-        grads_cross[:, 256:768].reshape(blk, 2, 256),
-        grads_cross[:, 768:1024],
+        jnp.transpose(grads_self[0], (1, 0, 2)),
+        grads_self[1],
+        grads_cross[3],
+        grads_cross[0],
+        grads_cross[1].reshape(blk, 2, 256),
+        grads_cross[2],
         grads_ffn[:, 1024:],
         grads_ffn[:, 0:1024],
         self_bias_grad,

time: 617 us -> 592 us (0.959)
  Pallas kernels: 296 us -> 281 us
  local copies, waits for them, and re-layouts: 72 us -> 64.6 us
    pallas_call x8, Pallas kernels: 43.5 us -> 29.1 us  [the longest x5 15.5 us: reorder_blocks(): pl.pallas_call(body, out_shape=jax.ShapeDtypeStruct(array_in.shape, dtype...]
    ppermute x47 -> x45, waiting for transfers between devices: 136 us -> 150 us  [swap(): return lax.ppermute(array_in, axis, [(i, i ^ bit) for i in range(count)])]
    pallas_call x1, Pallas kernels: 17.4 us -> 29.7 us  [feed_forward(): pl.pallas_call(body, grid_spec=pltpu.PrefetchScalarGridSpec(num_scalar_pr...]
    reduce_scatter x1, waiting for transfers between devices: 9.39 us -> 0.01 us  [step(): lax.psum_scatter(self.line.mark(total), 'head', scatter_dimension=0, tile...]
    pallas_call x12 -> x8, Pallas kernels: 35.8 us -> 27 us  [add_blocks(): pl.pallas_call(body, grid=(rows // chunk,), in_specs=[spec(array.shape[0]...]
    pallas_call x7 -> x6, Pallas kernels: 39.9 us -> 34.5 us  [project(): pl.pallas_call(body, grid=(groups, per), in_specs=[whole((rows, features)...]
    ppermute x47 -> x45, starting transfers between devices: 55.4 us -> 51.9 us  [swap(): return lax.ppermute(array_in, axis, [(i, i ^ bit) for i in range(count)])]
    unnamed x148 -> x143, local copies, waits for them, and re-layouts: 31.6 us -> 31 us
  transfers between devices with their start and end apart: 54 -> 53, of which waited for: 27 -> 29; matrix products, arithmetic and copies ran while one was open for 7% -> 8% of each run, Pallas kernels for 41% -> 42%
where the time goes in v4:
time: 592 us; the launch traced here: 584 us
  Pallas kernels  281 us (47%)
  waiting for transfers between devices  155 us (26%)
  local copies, waits for them, and re-layouts  64.6 us (11%)
  starting transfers between devices  59.8 us (10%)
  between operations  15.1 us (3%)
  other arithmetic  9.57 us (2%)
    ppermute x45, waiting for transfers between devices, swap(): return lax.ppermute(array_in, axis, [(i, i ^ bit) for i in range(count)])  150 us
    pallas_call x8, Pallas kernels, weight_products(): pl.pallas_call(body, grid_spec=pltpu.PrefetchScalarGridSpec(num_scalar_pr...  66 us
    ppermute x45, starting transfers between devices, swap(): return lax.ppermute(array_in, axis, [(i, i ^ bit) for i in range(count)])  51.9 us
    pallas_call x6, Pallas kernels, project(): pl.pallas_call(body, grid=(groups, per), in_specs=[whole((rows, features)...  34.5 us
    unnamed x143, local copies, waits for them, and re-layouts  31 us
    pallas_call x1, Pallas kernels, feed_forward(): pl.pallas_call(body, grid_spec=pltpu.PrefetchScalarGridSpec(num_scalar_pr...  29.7 us
    pallas_call x8, Pallas kernels, add_blocks(): pl.pallas_call(body, grid=(rows // chunk,), in_specs=[spec(array.shape[0]...  27 us
    pallas_call x1, Pallas kernels, cross_attention_back(): pl.pallas_call(body, grid=(groups,), in_specs=[pl.BlockSpec((rows, 256),...  17.3 us
  transfers between devices with their start and end apart: 53, of which 29 were waited for; matrix products, arithmetic and copies ran while one was open for 8% of the time, Pallas kernels for 42%

profile of v4, /device:TPU:0, one launch (start us, length us, event | category | flops | bytes accessed | tf_op | source)
XLA Modules:
  0.0 584.3 jit_solution(9260521118779900805)
XLA Ops:
  9.4 4.1 collective-permute-start
  24.8 3.7 reorder.7.grad_ref
  33.2 16.3 %collective-permute-done.1 = bf16[1,1,1,2,1,128,896]{6,5,4,3,2,1,0:T(8,128)(2,1)} collective-permute-done((bf16[1,1,1,2,1,128,896]{6,5,4,3,2,1,0:T(8,128)(2,1)S(1)}, bf16[1,1,1,2,1,128,896]{6,5,4,3,2,1,0:T(8,128)(2,1)}, u32[]{:S(2)}, u32[]{:S(2)}) %collective-permute-start.1) | collective-permute-done | bytes 458784 | tf_op jit(solution)/shard_map/ppermute | solution.py:35
  52.3 4.8 collective-permute-done.2
  58.9 4.2 collective-permute-done.3
  65.0 4.3 collective-permute-done.4
  72.1 15.5 %collective-permute-done.5 = bf16[1,1,1,2,1,128,2048]{6,5,4,3,2,1,0:T(8,128)(2,1)S(1)} collective-permute-done((bf16[1,1,1,2,1,128,2048]{6,5,4,3,2,1,0:T(8,128)(2,1)S(1)}, bf16[1,1,1,2,1,128,2048]{6,5,4,3,2,1,0:T(8,128)(2,1)S(1)}, u32[]{:S(2)}, u32[]{:S(2)}) %collective-permute-start.5) | collective-permute-done | bytes 1048608 | tf_op jit(solution)/shard_map/ppermute | solution.py:35
  99.5 8.9 %collective-permute-done.11 = bf16[1,1,1,2,1,128,1280]{6,5,4,3,2,1,0:T(8,128)(2,1)} collective-permute-done((bf16[1,1,1,2,1,128,1280]{6,5,4,3,2,1,0:T(8,128)(2,1)}, bf16[1,1,1,2,1,128,1280]{6,5,4,3,2,1,0:T(8,128)(2,1)}, u32[]{:S(2)}, u32[]{:S(2)}) %collective-permute-start.11) | collective-permute-done | bytes 655392 | tf_op jit(solution)/shard_map/ppermute | solution.py:35
  120.0 5.1 self_v.1.v_ref
  125.2 4.4 self_rel.1.rel_ref
  135.6 3.4 collective-permute-start.16
  140.3 7.3 %self_qk.1.q_ref.k_ref = bf16[640,2048]{1,0:T(8,128)(2,1)} custom-call(bf16[640,1024]{1,0:T(8,128)(2,1)} %stack_rows.1.x_ref.refs_1_, bf16[4,4,128,512]{3,2,1,0:T(8,128)(2,1)} %bitcast.161, bf16[4,4,128,512]{3,2,1,0:T(8,128)(2,1)} %bitcast.21.refs_1_.refs_3_, f32[2,2048]{1,0:T(2,128)} %pad_maximum_fusion.4.refs_2_), custom_call_target="tpu_custom_call" | custom-call | tf_op jit(solution)/shard_map/self_qk/pallas_call | solution.py:305
  148.5 14.1 %collective-permute-done.16 = bf16[256,1024]{1,0:T(8,128)(2,1)} collective-permute-done((bf16[256,1024]{1,0:T(8,128)(2,1)}, bf16[256,1024]{1,0:T(8,128)(2,1)}, u32[]{:S(2)}, u32[]{:S(2)}) %collective-permute-start.16) | collective-permute-done | bytes 524320 | tf_op jit(solution)/shard_map/ppermute | solution.py:35
  164.5 11.1 %self_attention.1 = (bf16[384,1024]{1,0:T(8,128)(2,1)}, bf16[16,384,384]{2,1,0:T(8,128)(2,1)}, f32[384,512]{1,0:T(8,128)}) custom-call(bf16[640,2048]{1,0:T(8,128)(2,1)} %self_qk.1.q_ref.k_ref, bf16[640,2048]{1,0:T(8,128)(2,1)} %self_qk.1.q_ref.k_ref, bf16[640,1024]{1,0:T(8,128)(2,1)} %self_v.1.v_ref, f32[384,512]{1,0:T(8,128)} %self_rel.1.rel_ref, ...), custom_call_target="tpu_custom_call" | custom-call | tf_op jit(solution)/shard_map/self_attention/pallas_call | solution.py:912
  180.5 11.7 %collective-permute-done.18 = bf16[1,2,1,2,2,128,768]{6,5,4,3,2,1,0:T(8,128)(2,1)} collective-permute-done((bf16[1,2,1,2,2,128,768]{6,5,4,3,2,1,0:T(8,128)(2,1)}, bf16[1,2,1,2,2,128,768]{6,5,4,3,2,1,0:T(8,128)(2,1)}, u32[]{:S(2)}, u32[]{:S(2)}) %collective-permute-start.18) | collective-permute-done | bytes 1572896 | tf_op jit(solution)/shard_map/ppermute | solution.py:35
  200.4 5.0 collective-permute-done.19
  205.5 6.6 %self_out.1 = (f32[384,1024]{1,0:T(8,128)}, bf16[384,1024]{1,0:T(8,128)(2,1)}, f32[384,1024]{1,0:T(8,128)}, f32[384,1]{1,0:T(8,128)}) custom-call(bf16[384,1024]{1,0:T(8,128)(2,1)} %get-tuple-element.279.left_ref.refs_7_, bf16[4,4,128,512]{3,2,1,0:T(8,128)(2,1)} %bitcast.23.refs_0_, bf16[4,4,128,512]{3,2,1,0:T(8,128)(2,1)} %bitcast.24.refs_1_, ...), custom_call_target="tpu_custom_call" | custom-call | tf_op jit(solution)/shard_map/self_out/pallas_call | solution.py:376
  212.1 4.6 cross_q.1.q_ref
  223.3 8.5 %cross_kv.1.k_ref.v_ref = bf16[1024,2048]{1,0:T(8,128)(2,1)} custom-call(bf16[1024,1024]{1,0:T(8,128)(2,1)} %copy-done.4, bf16[4,4,128,768]{3,2,1,0:T(8,128)(2,1)} %bitcast.153, bf16[4,4,128,768]{3,2,1,0:T(8,128)(2,1)} %bitcast.29.refs_1_, f32[2,2048]{1,0:T(2,128)} %stack.26.refs_2_), custom_call_target="tpu_custom_call" | custom-call | tf_op jit(solution)/shard_map/cross_kv/pallas_call | solution.py:305
  231.7 13.5 %cross_attention.1 = (bf16[384,1024]{1,0:T(8,128)(2,1)}, bf16[16,384,1024]{2,1,0:T(8,128)(2,1)}, f32[384,512]{1,0:T(8,128)}) custom-call(bf16[384,1024]{1,0:T(8,128)(2,1)} %cross_q.1.q_ref, bf16[1024,2048]{1,0:T(8,128)(2,1)} %cross_kv.1.k_ref.v_ref, bf16[1024,2048]{1,0:T(8,128)(2,1)} %cross_kv.1.k_ref.v_ref), custom_call_target="tpu_custom_call" | custom-call | tf_op jit(solution)/shard_map/cross_attention/pallas_call | solution.py:1080
  245.2 6.9 %cross_out.1 = (f32[384,1024]{1,0:T(8,128)}, bf16[384,1024]{1,0:T(8,128)(2,1)}, f32[384,1024]{1,0:T(8,128)}, f32[384,1]{1,0:T(8,128)}) custom-call(bf16[384,1024]{1,0:T(8,128)(2,1)} %get-tuple-element.289.left_ref.refs_6_, bf16[4,4,128,768]{3,2,1,0:T(8,128)(2,1)} %bitcast.154, bf16[4,4,128,768]{3,2,1,0:T(8,128)(2,1)} %bitcast.29.refs_1_, ...), custom_call_target="tpu_custom_call" | custom-call | tf_op jit(solution)/shard_map/cross_out/pallas_call | solution.py:376
  252.1 29.7 %feed_forward.1 = (bf16[384,4096]{1,0:T(8,128)(2,1)}, bf16[384,1024]{1,0:T(8,128)(2,1)}, bf16[384,1024]{1,0:T(8,128)(2,1)}, f32[3,1024]{1,0:T(4,128)}, bf16[384,...) custom-call(s32[12]{0:T(128)} %pad_add_fusion.order_ref, ...), custom_call_target="tpu_custom_call" | custom-call | tf_op jit(solution)/shard_map/feed_forward/pallas_call | solution.py:535
  281.8 6.7 %down_grad_send.1 = bf16[4,4,128,1024]{3,2,1,0:T(8,128)(2,1)} custom-call(s32[4]{0:T(128)} %copy-done.38, bf16[384,1024]{1,0:T(8,128)(2,1)} %get-tuple-element.303.refs_0_, bf16[384,4096]{1,0:T(8,128)(2,1)} %get-tuple-element.300.refs_1_), custom_call_target="tpu_custom_call" | custom-call | tf_op jit(solution)/shard_map/down_grad_send/pallas_call | solution.py:798
  288.5 6.7 %up_grad_send.1 = bf16[4,4,128,1024]{3,2,1,0:T(8,128)(2,1)} custom-call(s32[4]{0:T(128)} %copy-done.38, bf16[384,1024]{1,0:T(8,128)(2,1)} %get-tuple-element.309.low_ref.refs_0_, bf16[384,4096]{1,0:T(8,128)(2,1)} %get-tuple-element.302.refs_1_), custom_call_target="tpu_custom_call" | custom-call | tf_op jit(solution)/shard_map/up_grad_send/pallas_call | solution.py:798
  296.0 8.1 %down_grad_keep.1 = (bf16[2,4,128,1024]{3,2,1,0:T(8,128)(2,1)}, bf16[2,4,128,1024]{3,2,1,0:T(8,128)(2,1)}) custom-call(s32[4]{0:T(128)} %copy-done.38, bf16[384,1024]{1,0:T(8,128)(2,1)} %get-tuple-element.303.refs_0_, bf16[384,4096]{1,0:T(8,128)(2,1)} %get-tuple-element.300.refs_1_, bf16[4,4,128,1024]{3,2,1,0:T(8,128)(2,1)} %collective-permute-done.22.refs_2_), custom_call_target="tpu_custom_call" | custom-call | tf_op jit(solution)/shard_map/down_grad_keep/pallas_call | solution.py:798
  304.2 8.1 %up_grad_keep.1 = (bf16[2,4,128,1024]{3,2,1,0:T(8,128)(2,1)}, bf16[2,4,128,1024]{3,2,1,0:T(8,128)(2,1)}) custom-call(s32[4]{0:T(128)} %copy-done.38, bf16[384,1024]{1,0:T(8,128)(2,1)} %get-tuple-element.309.low_ref.refs_0_, bf16[384,4096]{1,0:T(8,128)(2,1)} %get-tuple-element.302.refs_1_, bf16[4,4,128,1024]{3,2,1,0:T(8,128)(2,1)} %collective-permute-done.23.refs_2_), custom_call_target="tpu_custom_call" | custom-call | tf_op jit(solution)/shard_map/up_grad_keep/pallas_call | solution.py:798
  315.3 17.3 %cross_attention_back.1 = (bf16[384,1024]{1,0:T(8,128)(2,1)}, bf16[1024,2048]{1,0:T(8,128)(2,1)}, f32[2,1024]{1,0:T(2,128)}) custom-call(bf16[384,1024]{1,0:T(8,128)(2,1)} %cross_q.1.q_ref, bf16[1024,2048]{1,0:T(8,128)(2,1)} %cross_kv.1.k_ref.v_ref, bf16[1024,2048]{1,0:T(8,128)(2,1)} %cross_kv.1.k_ref.v_ref, ...), custom_call_target="tpu_custom_call" | custom-call | tf_op jit(solution)/shard_map/cross_attention_back/pallas_call | solution.py:1149
  332.7 7.0 %cross_query_back.1 = (f32[384,1024]{1,0:T(8,128)}, bf16[384,1024]{1,0:T(8,128)(2,1)}, f32[3,1024]{1,0:T(4,128)}) custom-call(bf16[384,1024]{1,0:T(8,128)(2,1)} %get-tuple-element.313.left_ref.refs_4_, bf16[4,4,128,512]{3,2,1,0:T(8,128)(2,1)} %bitcast.23.refs_0_, bf16[4,4,128,512]{3,2,1,0:T(8,128)(2,1)} %bitcast.24.refs_1_, ...), custom_call_target="tpu_custom_call" | custom-call | tf_op jit(solution)/shard_map/cross_query_back/pallas_call | solution.py:628
  339.7 4.6 self_ctx_back.1.grad_ref
  344.3 15.9 %collective-permute-done.25 = bf16[2,4,128,1024]{3,2,1,0:T(8,128)(2,1)S(1)} collective-permute-done((bf16[2,4,128,1024]{3,2,1,0:T(8,128)(2,1)}, bf16[2,4,128,1024]{3,2,1,0:T(8,128)(2,1)S(1)}, u32[]{:S(2)}, u32[]{:S(2)}) %collective-permute-start.25) | collective-permute-done | bytes 2097184 | tf_op jit(solution)/shard_map/ppermute | solution.py:35
  362.8 6.0 %add_blocks.8 = (bf16[4,128,1024]{2,1,0:T(8,128)(2,1)}, bf16[4,128,1024]{2,1,0:T(8,128)(2,1)}, bf16[4,128,1024]{2,1,0:T(8,128)(2,1)}, bf16[4,128,1024]{2,1,0:T(8,128)(2,1)}) custom-call(bf16[8,128,1024]{2,1,0:T(8,128)(2,1)} %bitcast.171, bf16[8,128,1024]{2,1,0:T(8,128)(2,1)} %bitcast.174, bf16[8,128,1024]{2,1,0:T(8,128)(2,1)} %bitcast.172, ...), custom_call_target="tpu_custom_call" | custom-call | tf_op jit(solution)/shard_map/add_blocks/pallas_call | solution.py:103
  372.0 16.5 %self_attention_back.1 = (bf16[384,1024]{1,0:T(8,128)(2,1)}, bf16[640,2048]{1,0:T(8,128)(2,1)}, bf16[384,512]{1,0:T(8,128)(2,1)}, f32[2,1024]{1,0:T(2,128)}, f32[1,512]{1,0:T(1,128)}) custom-call(bf16[640,2048]{1,0:T(8,128)(2,1)} %self_qk.1.q_ref.k_ref, bf16[640,2048]{1,0:T(8,128)(2,1)} %self_qk.1.q_ref.k_ref, bf16[640,1024]{1,0:T(8,128)(2,1)} %self_v.1.v_ref, ...), custom_call_target="tpu_custom_call" | custom-call | tf_op jit(solution)/shard_map/self_attention_back/pallas_call | solution.py:1025
  388.5 4.7 collective-permute-done.27.refs_3_
  395.1 4.0 add_blocks.9
  400.3 9.8 %memory_back.1 = bf16[1024,1024]{1,0:T(8,128)(2,1)} custom-call(s32[4]{0:T(128)} %broadcast_xor_fusion.1.order_ref, bf16[1024,2048]{1,0:T(8,128)(2,1)} %get-tuple-element.338.left_ref.refs_5_, bf16[4,4,128,768]{3,2,1,0:T(8,128)(2,1)} %bitcast.156, bf16[4,4,128,768]{3,2,1,0:T(8,128)(2,1)} %bitcast.29.refs_1_), custom_call_target="tpu_custom_call" | custom-call | tf_op jit(solution)/shard_map/memory_back/pallas_call | solution.py:671
  410.6 9.5 %cross_grad_send.1 = bf16[4,4,128,1280]{3,2,1,0:T(8,128)(2,1)} custom-call(s32[4]{0:T(128)} %iota.57.order_ref, bf16[384,1024]{1,0:T(8,128)(2,1)} %get-tuple-element.344.x_ref.refs_0_, bf16[1024,1024]{1,0:T(8,128)(2,1)} %copy-done.4, bf16[384,1024]{1,0:T(8,128)(2,1)} %get-tuple-element.340.refs_2_, bf16[384,1024]{1,0:T(8,128)(2,1)} %get-tuple-element.318.x_ref.refs_3_, ...), custom_call_target="tpu_custom_call" | custom-call | tf_op jit(solution)/shard_map/cross_grad_send/pallas_call | solution.py:798
  420.6 7.7 %self_grad_send.1 = bf16[4,4,128,896]{3,2,1,0:T(8,128)(2,1)} custom-call(s32[4]{0:T(128)} %iota.56.order_ref, bf16[384,1024]{1,0:T(8,128)(2,1)} %reorder.6.refs_2_.x_ref.refs_0_, bf16[640,1024]{1,0:T(8,128)(2,1)} %stack_rows.1.x_ref.refs_1_, bf16[384,1024]{1,0:T(8,128)(2,1)} %reorder.6.refs_2_.x_ref.refs_0_, ...), custom_call_target="tpu_custom_call" | custom-call | tf_op jit(solution)/shard_map/self_grad_send/pallas_call | solution.py:798
  429.6 10.6 %cross_grad_keep.1 = (bf16[2,4,128,640]{3,2,1,0:T(8,128)(2,1)}, bf16[2,4,128,640]{3,2,1,0:T(8,128)(2,1)}, bf16[2,4,128,640]{3,2,1,0:T(8,128)(2,1)}, bf16[2,4,128,640]{3,2,1,0:T(8,128)(2,1)}) custom-call(s32[4]{0:T(128)} %iota.55.order_ref, bf16[384,1024]{1,0:T(8,128)(2,1)} %get-tuple-element.344.x_ref.refs_0_, bf16[1024,1024]{1,0:T(8,128)(2,1)} %copy-done.4, ...), custom_call_target="tpu_custom_call" | custom-call | tf_op jit(solution)/shard_map/cross_grad_keep/pallas_call | solution.py:798
  447.5 8.6 %self_grad_keep.1 = (bf16[2,4,128,512]{3,2,1,0:T(8,128)(2,1)}, bf16[2,4,128,512]{3,2,1,0:T(8,128)(2,1)}, bf16[2,4,128,384]{3,2,1,0:T(8,128)(2,1)}, bf16[2,4,128,384]{3,2,1,0:T(8,128)(2,1)}) custom-call(s32[4]{0:T(128)} %iota.54.order_ref, bf16[384,1024]{1,0:T(8,128)(2,1)} %reorder.6.refs_2_.x_ref.refs_0_, bf16[640,1024]{1,0:T(8,128)(2,1)} %stack_rows.1.x_ref.refs_1_, ...), custom_call_target="tpu_custom_call" | custom-call | tf_op jit(solution)/shard_map/self_grad_keep/pallas_call | solution.py:798
  458.4 9.8 %input_back.1 = (bf16[128,1024]{1,0:T(8,128)(2,1)}, bf16[128,1024]{1,0:T(8,128)(2,1)}, f32[384,1024]{1,0:T(8,128)}) custom-call(bf16[384,1024]{1,0:T(8,128)(2,1)} %get-tuple-element.348.refs_3_.query_ref, bf16[640,2048]{1,0:T(8,128)(2,1)} %get-tuple-element.342.refs_4_.kv_ref, bf16[384,512]{1,0:T(8,128)(2,1)} %get-tuple-element.343.refs_5_.rel_ref, ...), custom_call_target="tpu_custom_call" | custom-call | tf_op jit(solution)/shard_map/input_back/pallas_call | solution.py:723
  468.3 3.8 collective-permute-done.31
  473.5 4.2 add_blocks.10
  481.3 7.7 %collective-permute-done.33 = bf16[2,4,128,384]{3,2,1,0:T(8,128)(2,1)} collective-permute-done((bf16[2,4,128,384]{3,2,1,0:T(8,128)(2,1)}, bf16[2,4,128,384]{3,2,1,0:T(8,128)(2,1)}, u32[]{:S(2)}, u32[]{:S(2)}) %collective-permute-start.33) | collective-permute-done | bytes 786464 | tf_op jit(solution)/shard_map/ppermute | solution.py:35
  490.5 5.4 collective-permute-done.32
  508.7 3.5 reorder.8
  541.0 7.2 %collective-permute-done.44.refs_1_ = bf16[2,128,896]{2,1,0:T(8,128)(2,1)S(1)} collective-permute-done((bf16[2,128,896]{2,1,0:T(8,128)(2,1)}, bf16[2,128,896]{2,1,0:T(8,128)(2,1)S(1)}, u32[]{:S(2)}, u32[]{:S(2)}) %collective-permute-start.44) | collective-permute-done | bytes 458784 | tf_op jit(solution)/shard_map/ppermute | solution.py:35
  554.9 6.0 %collective-permute-done.46 = bf16[1,128,1280]{2,1,0:T(8,128)(2,1)S(1)} collective-permute-done((bf16[1,128,1280]{2,1,0:T(8,128)(2,1)}, bf16[1,128,1280]{2,1,0:T(8,128)(2,1)S(1)}, u32[]{:S(2)}, u32[]{:S(2)}) %collective-permute-start.46) | collective-permute-done | bytes 327712 | tf_op jit(solution)/shard_map/ppermute | solution.py:35
  573.7 3.9 copy.142
  (368 shorter events, 172.3 us)
Async XLA Ops:
  7.2 244.9 %all-gather.3.cloned.1.call-start = ((), (), s32[]{:S(2)}) async-start(), calls=%async_computation.2 | async-start | bytes 18874368 | tf_op jit(solution)/shard_map/all_gather | solution.py:1345
  9.4 20.6 %collective-permute-start = (bf16[1,1,1,1,1,128,896]{6,5,4,3,2,1,0:T(8,128)(2,1)S(1)}, bf16[1,1,1,1,1,128,896]{6,5,4,3,2,1,0:T(8,128)(2,1)S(1)}, u32[]{:S(2)}, u32[]{:S(2)}) collective-permute-start(bf16[1,1,1,1,1,128,896]{6,5,4,3,2,1,0:T(8,128)(2,1)S(1)} %pad_maximum_fusion.1), channel_id=1, source_target_pairs={{0,2},{1,3},{2,0},{3,1},{4,6},{5,7},{6,4},{7,5},{8,10},{9,11},{10,... | collective-permute-start | bytes 688136 | tf_op jit(solution)/shard_map/ppermute | solution.py:35
  30.1 19.4 %collective-permute-start.1 = (bf16[1,1,1,2,1,128,896]{6,5,4,3,2,1,0:T(8,128)(2,1)S(1)}, bf16[1,1,1,2,1,128,896]{6,5,4,3,2,1,0:T(8,128)(2,1)}, u32[]{:S(2)}, u32[]{:S(2)}) collective-permute-start(bf16[1,1,1,2,1,128,896]{6,5,4,3,2,1,0:T(8,128)(2,1)S(1)} %constant_dynamic-update-slice_fusion), channel_id=1, source_target_pairs={{0,1},{1,0},{2,3},{3,2},{4,5},{5,4},{6,7},{7,6},{8,9},{9,8},{10,11... | collective-permute-start | bytes 1376264 | tf_op jit(solution)/shard_map/ppermute | solution.py:35
  31.8 25.3 %collective-permute-start.2 = (bf16[1,1,1,1,1,128,2048]{6,5,4,3,2,1,0:T(8,128)(2,1)S(1)}, bf16[1,1,1,1,1,128,2048]{6,5,4,3,2,1,0:T(8,128)(2,1)S(1)}, u32[]{:S(2)}, u32[]{:S(2)}) collective-permute-start(bf16[1,1,1,1,1,128,2048]{6,5,4,3,2,1,0:T(8,128)(2,1)S(1)} %fusion.9), channel_id=1, source_target_pairs={{0,2},{1,3},{2,0},{3,1},{4,6},{5,7},{6,4},{7,5},{8,10},{9,11},{10,... | collective-permute-start | bytes 1572872 | tf_op jit(solution)/shard_map/ppermute | solution.py:35
  50.6 12.5 %collective-permute-start.3 = (bf16[1,1,1,2,2,128,512]{6,5,4,3,2,1,0:T(8,128)(2,1)S(1)}, bf16[1,1,1,2,2,128,512]{6,5,4,3,2,1,0:T(8,128)(2,1)S(1)}, u32[]{:S(2)}, u32[]{:S(2)}) collective-permute-start(bf16[1,1,1,2,2,128,512]{6,5,4,3,2,1,0:T(8,128)(2,1)S(1)} %slice.153), channel_id=1, source_target_pairs={{0,8},{4,12},{8,0},{12,4},{16,24},{20,28},{24,16},{28,20},{1,9},{5... | collective-permute-start | bytes 1572872 | tf_op jit(solution)/shard_map/ppermute | solution.py:35
  57.1 30.5 %collective-permute-start.5 = (bf16[1,1,1,2,1,128,2048]{6,5,4,3,2,1,0:T(8,128)(2,1)S(1)}, bf16[1,1,1,2,1,128,2048]{6,5,4,3,2,1,0:T(8,128)(2,1)S(1)}, u32[]{:S(2)}, u32[]{:S(2)}) collective-permute-start(bf16[1,1,1,2,1,128,2048]{6,5,4,3,2,1,0:T(8,128)(2,1)S(1)} %constant_dynamic-update-slice_fusion.4), channel_id=1, source_target_pairs={{0,1},{1,0},{2,3},{3,2},{4,5},{5,4},{6,7},{7,6},{8,9},{9,8},{10,11... | collective-permute-start | bytes 3145736 | tf_op jit(solution)/shard_map/ppermute | solution.py:35
  57.2 12.1 %collective-permute-start.4 = (bf16[1,1,1,2,2,128,384]{6,5,4,3,2,1,0:T(8,128)(2,1)S(1)}, bf16[1,1,1,2,2,128,384]{6,5,4,3,2,1,0:T(8,128)(2,1)S(1)}, u32[]{:S(2)}, u32[]{:S(2)}) collective-permute-start(bf16[1,1,1,2,2,128,384]{6,5,4,3,2,1,0:T(8,128)(2,1)S(1)} %slice.152), channel_id=1, source_target_pairs={{0,16},{4,20},{8,24},{12,28},{16,0},{20,4},{24,8},{28,12},{1,17},{... | collective-permute-start | bytes 1179656 | tf_op jit(solution)/shard_map/ppermute | solution.py:35
  63.1 26.0 %collective-permute-start.6 = (bf16[1,2,1,2,2,128,512]{6,5,4,3,2,1,0:T(8,128)(2,1)S(1)}, bf16[1,2,1,2,2,128,512]{6,5,4,3,2,1,0:T(8,128)(2,1)S(1)}, u32[]{:S(2)}, u32[]{:S(2)}) collective-permute-start(bf16[1,2,1,2,2,128,512]{6,5,4,3,2,1,0:T(8,128)(2,1)S(1)} %constant_dynamic-update-slice_fusion.6), channel_id=1, source_target_pairs={{0,16},{4,20},{8,24},{12,28},{16,0},{20,4},{24,8},{28,12},{1,17},{... | collective-permute-start | bytes 3145736 | tf_op jit(solution)/shard_map/ppermute | solution.py:35
  69.5 19.8 %collective-permute-start.7 = (bf16[1,1,2,2,2,128,384]{6,5,4,3,2,1,0:T(8,128)(2,1)S(1)}, bf16[1,1,2,2,2,128,384]{6,5,4,3,2,1,0:T(8,128)(2,1)S(1)}, u32[]{:S(2)}, u32[]{:S(2)}) collective-permute-start(bf16[1,1,2,2,2,128,384]{6,5,4,3,2,1,0:T(8,128)(2,1)S(1)} %constant_dynamic-update-slice_fusion.8), channel_id=1, source_target_pairs={{0,8},{4,12},{8,0},{12,4},{16,24},{20,28},{24,16},{28,20},{1,9},{5... | collective-permute-start | bytes 2359304 | tf_op jit(solution)/shard_map/ppermute | solution.py:35
  71.0 19.4 %collective-permute-start.8 = (bf16[1,1,1,1,1,128,1280]{6,5,4,3,2,1,0:T(8,128)(2,1)S(1)}, bf16[1,1,1,1,1,128,1280]{6,5,4,3,2,1,0:T(8,128)(2,1)S(1)}, u32[]{:S(2)}, u32[]{:S(2)}) collective-permute-start(bf16[1,1,1,1,1,128,1280]{6,5,4,3,2,1,0:T(8,128)(2,1)S(1)} %maximum_bitcast_fusion), channel_id=1, source_target_pairs={{0,2},{1,3},{2,0},{3,1},{4,6},{5,7},{6,4},{7,5},{8,10},{9,11},{10,... | collective-permute-start | bytes 983048 | tf_op jit(solution)/shard_map/ppermute | solution.py:35
  91.2 17.2 %collective-permute-start.11 = (bf16[1,1,1,2,1,128,1280]{6,5,4,3,2,1,0:T(8,128)(2,1)}, bf16[1,1,1,2,1,128,1280]{6,5,4,3,2,1,0:T(8,128)(2,1)}, u32[]{:S(2)}, u32[]{:S(2)}) collective-permute-start(bf16[1,1,1,2,1,128,1280]{6,5,4,3,2,1,0:T(8,128)(2,1)} %constant_dynamic-update-slice_fusion.16), channel_id=1, source_target_pairs={{0,1},{1,0},{2,3},{3,2},{4,5},{5,4},{6,7},{7,6},{8,9},{9,8},{10,11... | collective-permute-start | bytes 1966088 | tf_op jit(solution)/shard_map/ppermute | solution.py:35
  92.9 25.9 %collective-permute-start.12 = (bf16[1,2,2,2,2,128,384]{6,5,4,3,2,1,0:T(8,128)(2,1)S(1)}, bf16[1,2,2,2,2,128,384]{6,5,4,3,2,1,0:T(8,128)(2,1)S(1)}, u32[]{:S(2)}, u32[]{:S(2)}) collective-permute-start(bf16[1,2,2,2,2,128,384]{6,5,4,3,2,1,0:T(8,128)(2,1)S(1)} %constant_dynamic-update-slice_fusion.14), channel_id=1, source_target_pairs={{0,4},{4,0},{8,12},{12,8},{16,20},{20,16},{24,28},{28,24},{1,5},{5... | collective-permute-start | bytes 4718600 | tf_op jit(solution)/shard_map/ppermute | solution.py:35
  93.6 20.5 %collective-permute-start.10 = (bf16[128,1024]{1,0:T(8,128)(2,1)S(1)}, bf16[128,1024]{1,0:T(8,128)(2,1)S(1)}, u32[]{:S(2)}, u32[]{:S(2)}) collective-permute-start(bf16[128,1024]{1,0:T(8,128)(2,1)S(1)} %slice.151), channel_id=1, source_target_pairs={{0,1},{1,2},{2,3},{4,5},{5,6},{6,7},{8,9},{9,10},{10,11},{12,13},{... | collective-permute-start | bytes 786440 | tf_op jit(solution)/shard_map/ppermute | solution.py:1322
  95.9 19.8 %collective-permute-start.9 = (bf16[128,1024]{1,0:T(8,128)(2,1)S(1)}, bf16[128,1024]{1,0:T(8,128)(2,1)S(1)}, u32[]{:S(2)}, u32[]{:S(2)}) collective-permute-start(bf16[128,1024]{1,0:T(8,128)(2,1)S(1)} %slice.151), channel_id=1, source_target_pairs={{0,2},{1,3},{4,6},{5,7},{8,10},{9,11},{12,14},{13,15},{16,18},{17,... | collective-permute-start | bytes 786440 | tf_op jit(solution)/shard_map/ppermute | solution.py:1323
  109.7 20.9 %collective-permute-start.14 = (bf16[1,1,1,2,2,128,768]{6,5,4,3,2,1,0:T(8,128)(2,1)S(1)}, bf16[1,1,1,2,2,128,768]{6,5,4,3,2,1,0:T(8,128)(2,1)S(1)}, u32[]{:S(2)}, u32[]{:S(2)}) collective-permute-start(bf16[1,1,1,2,2,128,768]{6,5,4,3,2,1,0:T(8,128)(2,1)S(1)} %slice.154), channel_id=1, source_target_pairs={{0,8},{4,12},{8,0},{12,4},{16,24},{20,28},{24,16},{28,20},{1,9},{5... | collective-permute-start | bytes 2359304 | tf_op jit(solution)/shard_map/ppermute | solution.py:35
  111.3 18.3 %collective-permute-start.13 = (bf16[1,1,1,2,2,128,512]{6,5,4,3,2,1,0:T(8,128)(2,1)S(1)}, bf16[1,1,1,2,2,128,512]{6,5,4,3,2,1,0:T(8,128)(2,1)S(1)}, u32[]{:S(2)}, u32[]{:S(2)}) collective-permute-start(bf16[1,1,1,2,2,128,512]{6,5,4,3,2,1,0:T(8,128)(2,1)S(1)} %slice.155), channel_id=1, source_target_pairs={{0,16},{4,20},{8,24},{12,28},{16,0},{20,4},{24,8},{28,12},{1,17},{... | collective-permute-start | bytes 1572872 | tf_op jit(solution)/shard_map/ppermute | solution.py:35
  131.6 268.7 %all-gather.5.cloned.1.call-start = ((), (), s32[]{:S(2)}) async-start(), calls=%async_computation.3 | async-start | bytes 3932160 | tf_op jit(solution)/shard_map/all_gather | solution.py:1431
  132.5 59.7 %collective-permute-start.18 = (bf16[1,2,1,2,2,128,768]{6,5,4,3,2,1,0:T(8,128)(2,1)}, bf16[1,2,1,2,2,128,768]{6,5,4,3,2,1,0:T(8,128)(2,1)}, u32[]{:S(2)}, u32[]{:S(2)}) collective-permute-start(bf16[1,2,1,2,2,128,768]{6,5,4,3,2,1,0:T(8,128)(2,1)} %constant_dynamic-update-slice_fusion.28), channel_id=1, source_target_pairs={{0,16},{4,20},{8,24},{12,28},{16,0},{20,4},{24,8},{28,12},{1,17},{... | collective-permute-start | bytes 4718600 | tf_op jit(solution)/shard_map/ppermute | solution.py:35
  134.4 42.4 %collective-permute-start.17 = (bf16[1,1,2,2,2,128,512]{6,5,4,3,2,1,0:T(8,128)(2,1)S(1)}, bf16[1,1,2,2,2,128,512]{6,5,4,3,2,1,0:T(8,128)(2,1)}, u32[]{:S(2)}, u32[]{:S(2)}) collective-permute-start(bf16[1,1,2,2,2,128,512]{6,5,4,3,2,1,0:T(8,128)(2,1)S(1)} %constant_dynamic-update-slice_fusion.26), channel_id=1, source_target_pairs={{0,8},{4,12},{8,0},{12,4},{16,24},{20,28},{24,16},{28,20},{1,9},{5... | collective-permute-start | bytes 3145736 | tf_op jit(solution)/shard_map/ppermute | solution.py:35
  135.6 27.0 %collective-permute-start.16 = (bf16[256,1024]{1,0:T(8,128)(2,1)}, bf16[256,1024]{1,0:T(8,128)(2,1)}, u32[]{:S(2)}, u32[]{:S(2)}) collective-permute-start(bf16[256,1024]{1,0:T(8,128)(2,1)} %reorder.5), channel_id=1, source_target_pairs={{0,2},{1,3},{2,0},{3,1},{4,6},{5,7},{6,4},{7,5},{8,10},{9,11},{10,... | collective-permute-start | bytes 1572872 | tf_op jit(solution)/shard_map/ppermute | solution.py:35
  193.8 28.2 %collective-permute-start.21 = (bf16[1,2,2,2,2,128,768]{6,5,4,3,2,1,0:T(8,128)(2,1)S(1)}, bf16[1,2,2,2,2,128,768]{6,5,4,3,2,1,0:T(8,128)(2,1)}, u32[]{:S(2)}, u32[]{:S(2)}) collective-permute-start(bf16[1,2,2,2,2,128,768]{6,5,4,3,2,1,0:T(8,128)(2,1)S(1)} %constant_dynamic-update-slice_fusion.34), channel_id=1, source_target_pairs={{0,4},{4,0},{8,12},{12,8},{16,20},{20,16},{24,28},{28,24},{1,5},{5... | collective-permute-start | bytes 9437192 | tf_op jit(solution)/shard_map/ppermute | solution.py:35
  193.8 11.6 %collective-permute-start.19 = (bf16[1,2,2,2,2,128,512]{6,5,4,3,2,1,0:T(8,128)(2,1)}, bf16[1,2,2,2,2,128,512]{6,5,4,3,2,1,0:T(8,128)(2,1)}, u32[]{:S(2)}, u32[]{:S(2)}) collective-permute-start(bf16[1,2,2,2,2,128,512]{6,5,4,3,2,1,0:T(8,128)(2,1)} %constant_dynamic-update-slice_fusion.32), channel_id=1, source_target_pairs={{0,4},{4,0},{8,12},{12,8},{16,20},{20,16},{24,28},{28,24},{1,5},{5... | collective-permute-start | bytes 6291464 | tf_op jit(solution)/shard_map/ppermute | solution.py:35
  195.1 25.5 %collective-permute-start.20 = (bf16[512,1024]{1,0:T(8,128)(2,1)}, bf16[512,1024]{1,0:T(8,128)(2,1)}, u32[]{:S(2)}, u32[]{:S(2)}) collective-permute-start(bf16[512,1024]{1,0:T(8,128)(2,1)} %constant_dynamic-update-slice_fusion.30), channel_id=1, source_target_pairs={{0,1},{1,0},{2,3},{3,2},{4,5},{5,4},{6,7},{7,6},{8,9},{9,8},{10,11... | collective-permute-start | bytes 3145736 | tf_op jit(solution)/shard_map/ppermute | solution.py:35
  295.8 161.5 %reduce-scatter.5.cloned.1.call-start = ((), (), s32[]{:S(2)}) async-start(), calls=%async_computation.5 | async-start | bytes 2621440 | tf_op jit(solution)/shard_map/reduce_scatter | solution.py:206
  312.2 48.0 %collective-permute-start.25 = (bf16[2,4,128,1024]{3,2,1,0:T(8,128)(2,1)}, bf16[2,4,128,1024]{3,2,1,0:T(8,128)(2,1)S(1)}, u32[]{:S(2)}, u32[]{:S(2)}) collective-permute-start(bf16[2,4,128,1024]{3,2,1,0:T(8,128)(2,1)} %get-tuple-element.310), channel_id=1, source_target_pairs={{0,16},{4,20},{8,24},{12,28},{16,0},{20,4},{24,8},{28,12},{1,17},{... | collective-permute-start | bytes 6291464 | tf_op jit(solution)/shard_map/ppermute | solution.py:35
  314.0 47.4 %collective-permute-start.24 = (bf16[2,4,128,1024]{3,2,1,0:T(8,128)(2,1)S(1)}, bf16[2,4,128,1024]{3,2,1,0:T(8,128)(2,1)S(1)}, u32[]{:S(2)}, u32[]{:S(2)}) collective-permute-start(bf16[2,4,128,1024]{3,2,1,0:T(8,128)(2,1)S(1)} %copy-done.49), channel_id=1, source_target_pairs={{0,8},{4,12},{8,0},{12,4},{16,24},{20,28},{24,16},{28,20},{1,9},{5... | collective-permute-start | bytes 6291464 | tf_op jit(solution)/shard_map/ppermute | solution.py:35
  368.8 24.4 %collective-permute-start.27 = (bf16[4,128,1024]{2,1,0:T(8,128)(2,1)}, bf16[4,128,1024]{2,1,0:T(8,128)(2,1)S(1)}, u32[]{:S(2)}, u32[]{:S(2)}) collective-permute-start(bf16[4,128,1024]{2,1,0:T(8,128)(2,1)} %get-tuple-element.328), channel_id=1, source_target_pairs={{0,8},{4,12},{8,0},{12,4},{16,24},{20,28},{24,16},{28,20},{1,9},{5... | collective-permute-start | bytes 3145736 | tf_op jit(solution)/shard_map/ppermute | solution.py:35
  370.0 24.1 %collective-permute-start.26 = (bf16[4,128,1024]{2,1,0:T(8,128)(2,1)}, bf16[4,128,1024]{2,1,0:T(8,128)(2,1)S(1)}, u32[]{:S(2)}, u32[]{:S(2)}) collective-permute-start(bf16[4,128,1024]{2,1,0:T(8,128)(2,1)} %get-tuple-element.327), channel_id=1, source_target_pairs={{0,16},{4,20},{8,24},{12,28},{16,0},{20,4},{24,8},{28,12},{1,17},{... | collective-permute-start | bytes 3145736 | tf_op jit(solution)/shard_map/ppermute | solution.py:35
  399.1 103.8 %reduce-scatter.3.cloned.1.call-start = ((), (), s32[]{:S(2)}) async-start(), calls=%async_computation.4 | async-start | bytes 2621440 | tf_op jit(solution)/shard_map/reduce_scatter | solution.py:1461
  420.1 9.0 %collective-permute-start.28 = (bf16[4,4,128,1280]{3,2,1,0:T(8,128)(2,1)}, bf16[4,4,128,1280]{3,2,1,0:T(8,128)(2,1)}, u32[]{:S(2)}, u32[]{:S(2)}) collective-permute-start(bf16[4,4,128,1280]{3,2,1,0:T(8,128)(2,1)} %cross_grad_send.1), channel_id=1, source_target_pairs={{0,4},{4,0},{8,12},{12,8},{16,20},{20,16},{24,28},{28,24},{1,5},{5... | collective-permute-start | bytes 15728648 | tf_op jit(solution)/shard_map/ppermute | solution.py:35
  428.4 18.6 %collective-permute-start.29 = (bf16[4,4,128,896]{3,2,1,0:T(8,128)(2,1)}, bf16[4,4,128,896]{3,2,1,0:T(8,128)(2,1)}, u32[]{:S(2)}, u32[]{:S(2)}) collective-permute-start(bf16[4,4,128,896]{3,2,1,0:T(8,128)(2,1)} %self_grad_send.1), channel_id=1, source_target_pairs={{0,4},{4,0},{8,12},{12,8},{16,20},{20,16},{24,28},{28,24},{1,5},{5... | collective-permute-start | bytes 11010056 | tf_op jit(solution)/shard_map/ppermute | solution.py:35
  440.2 31.9 %collective-permute-start.31 = (bf16[2,4,128,640]{3,2,1,0:T(8,128)(2,1)}, bf16[2,4,128,640]{3,2,1,0:T(8,128)(2,1)S(1)}, u32[]{:S(2)}, u32[]{:S(2)}) collective-permute-start(bf16[2,4,128,640]{3,2,1,0:T(8,128)(2,1)} %get-tuple-element.362), channel_id=1, source_target_pairs={{0,16},{4,20},{8,24},{12,28},{16,0},{20,4},{24,8},{28,12},{1,17},{... | collective-permute-start | bytes 3932168 | tf_op jit(solution)/shard_map/ppermute | solution.py:35
  441.6 32.0 %collective-permute-start.30 = (bf16[2,4,128,640]{3,2,1,0:T(8,128)(2,1)}, bf16[2,4,128,640]{3,2,1,0:T(8,128)(2,1)}, u32[]{:S(2)}, u32[]{:S(2)}) collective-permute-start(bf16[2,4,128,640]{3,2,1,0:T(8,128)(2,1)} %get-tuple-element.345), channel_id=1, source_target_pairs={{0,8},{4,12},{8,0},{12,4},{16,24},{20,28},{24,16},{28,20},{1,9},{5... | collective-permute-start | bytes 3932168 | tf_op jit(solution)/shard_map/ppermute | solution.py:35
  456.1 39.8 %collective-permute-start.32 = (bf16[2,4,128,512]{3,2,1,0:T(8,128)(2,1)}, bf16[2,4,128,512]{3,2,1,0:T(8,128)(2,1)S(1)}, u32[]{:S(2)}, u32[]{:S(2)}) collective-permute-start(bf16[2,4,128,512]{3,2,1,0:T(8,128)(2,1)} %get-tuple-element.347), channel_id=1, source_target_pairs={{0,8},{4,12},{8,0},{12,4},{16,24},{20,28},{24,16},{28,20},{1,9},{5... | collective-permute-start | bytes 3145736 | tf_op jit(solution)/shard_map/ppermute | solution.py:35
  456.9 32.2 %collective-permute-start.33 = (bf16[2,4,128,384]{3,2,1,0:T(8,128)(2,1)}, bf16[2,4,128,384]{3,2,1,0:T(8,128)(2,1)}, u32[]{:S(2)}, u32[]{:S(2)}) collective-permute-start(bf16[2,4,128,384]{3,2,1,0:T(8,128)(2,1)} %get-tuple-element.372), channel_id=1, source_target_pairs={{0,16},{4,20},{8,24},{12,28},{16,0},{20,4},{24,8},{28,12},{1,17},{... | collective-permute-start | bytes 2359304 | tf_op jit(solution)/shard_map/ppermute | solution.py:35
  477.7 34.5 %collective-permute-start.37 = (bf16[4,128,640]{2,1,0:T(8,128)(2,1)}, bf16[4,128,640]{2,1,0:T(8,128)(2,1)S(1)}, u32[]{:S(2)}, u32[]{:S(2)}) collective-permute-start(bf16[4,128,640]{2,1,0:T(8,128)(2,1)} %get-tuple-element.366), channel_id=1, source_target_pairs={{0,8},{4,12},{8,0},{12,4},{16,24},{20,28},{24,16},{28,20},{1,9},{5... | collective-permute-start | bytes 1966088 | tf_op jit(solution)/shard_map/ppermute | solution.py:35
  479.1 33.2 %collective-permute-start.36 = (bf16[4,128,640]{2,1,0:T(8,128)(2,1)}, bf16[4,128,640]{2,1,0:T(8,128)(2,1)S(1)}, u32[]{:S(2)}, u32[]{:S(2)}) collective-permute-start(bf16[4,128,640]{2,1,0:T(8,128)(2,1)} %get-tuple-element.364), channel_id=1, source_target_pairs={{0,16},{4,20},{8,24},{12,28},{16,0},{20,4},{24,8},{28,12},{1,17},{... | collective-permute-start | bytes 1966088 | tf_op jit(solution)/shard_map/ppermute | solution.py:35
  480.0 21.6 %collective-permute-start.34 = (bf16[128,1024]{1,0:T(8,128)(2,1)}, bf16[128,1024]{1,0:T(8,128)(2,1)}, u32[]{:S(2)}, u32[]{:S(2)}) collective-permute-start(bf16[128,1024]{1,0:T(8,128)(2,1)} %get-tuple-element.380), channel_id=1, source_target_pairs={{1,0},{2,1},{3,2},{5,4},{6,5},{7,6},{9,8},{10,9},{11,10},{13,12},{... | collective-permute-start | bytes 786440 | tf_op jit(solution)/shard_map/ppermute | solution.py:1485
  489.0 16.9 %collective-permute-start.35 = (bf16[128,1024]{1,0:T(8,128)(2,1)}, bf16[128,1024]{1,0:T(8,128)(2,1)}, u32[]{:S(2)}, u32[]{:S(2)}) collective-permute-start(bf16[128,1024]{1,0:T(8,128)(2,1)} %get-tuple-element.381), channel_id=1, source_target_pairs={{2,0},{3,1},{6,4},{7,5},{10,8},{11,9},{14,12},{15,13},{18,16},{19,... | collective-permute-start | bytes 786440 | tf_op jit(solution)/shard_map/ppermute | solution.py:1484
  500.2 17.9 %collective-permute-start.39 = (bf16[4,128,512]{2,1,0:T(8,128)(2,1)}, bf16[4,128,512]{2,1,0:T(8,128)(2,1)S(1)}, u32[]{:S(2)}, u32[]{:S(2)}) collective-permute-start(bf16[4,128,512]{2,1,0:T(8,128)(2,1)} %get-tuple-element.374), channel_id=1, source_target_pairs={{0,16},{4,20},{8,24},{12,28},{16,0},{20,4},{24,8},{28,12},{1,17},{... | collective-permute-start | bytes 1572872 | tf_op jit(solution)/shard_map/ppermute | solution.py:35
  501.7 16.4 %collective-permute-start.40 = (bf16[4,128,384]{2,1,0:T(8,128)(2,1)}, bf16[4,128,384]{2,1,0:T(8,128)(2,1)S(1)}, u32[]{:S(2)}, u32[]{:S(2)}) collective-permute-start(bf16[4,128,384]{2,1,0:T(8,128)(2,1)} %get-tuple-element.395), channel_id=1, source_target_pairs={{0,8},{4,12},{8,0},{12,4},{16,24},{20,28},{24,16},{28,20},{1,9},{5... | collective-permute-start | bytes 1179656 | tf_op jit(solution)/shard_map/ppermute | solution.py:35
  516.8 17.9 %collective-permute-start.42 = (bf16[2,128,1280]{2,1,0:T(8,128)(2,1)}, bf16[2,128,1280]{2,1,0:T(8,128)(2,1)S(1)}, u32[]{:S(2)}, u32[]{:S(2)}) collective-permute-start(bf16[2,128,1280]{2,1,0:T(8,128)(2,1)} %get-tuple-element.386), channel_id=1, source_target_pairs={{0,1},{1,0},{2,3},{3,2},{4,5},{5,4},{6,7},{7,6},{8,9},{9,8},{10,11... | collective-permute-start | bytes 1966088 | tf_op jit(solution)/shard_map/ppermute | solution.py:35
  522.1 26.0 %collective-permute-start.44 = (bf16[2,128,896]{2,1,0:T(8,128)(2,1)}, bf16[2,128,896]{2,1,0:T(8,128)(2,1)S(1)}, u32[]{:S(2)}, u32[]{:S(2)}) collective-permute-start(bf16[2,128,896]{2,1,0:T(8,128)(2,1)} %get-tuple-element.397), channel_id=1, source_target_pairs={{0,1},{1,0},{2,3},{3,2},{4,5},{5,4},{6,7},{7,6},{8,9},{9,8},{10,11... | collective-permute-start | bytes 1376264 | tf_op jit(solution)/shard_map/ppermute | solution.py:35
  528.5 9.2 %collective-permute-start.43 = (f32[17920]{0:T(1024)S(1)}, f32[17920]{0:T(1024)S(1)}, u32[]{:S(2)}, u32[]{:S(2)}) collective-permute-start(f32[17920]{0:T(1024)S(1)} %add.88), channel_id=1, source_target_pairs={{0,16},{4,20},{8,24},{12,28},{16,0},{20,4},{24,8},{28,12},{1,17},{... | collective-permute-start | bytes 215048 | tf_op jit(solution)/shard_map/ppermute | solution.py:35
  537.8 13.1 %collective-permute-start.45 = (f32[17920]{0:T(1024)S(1)}, f32[17920]{0:T(1024)S(1)}, u32[]{:S(2)}, u32[]{:S(2)}) collective-permute-start(f32[17920]{0:T(1024)S(1)} %add.89), channel_id=1, source_target_pairs={{0,1},{1,0},{2,3},{3,2},{4,5},{5,4},{6,7},{7,6},{8,9},{9,8},{10,11... | collective-permute-start | bytes 215048 | tf_op jit(solution)/shard_map/ppermute | solution.py:35
  537.8 23.0 %collective-permute-start.46 = (bf16[1,128,1280]{2,1,0:T(8,128)(2,1)}, bf16[1,128,1280]{2,1,0:T(8,128)(2,1)S(1)}, u32[]{:S(2)}, u32[]{:S(2)}) collective-permute-start(bf16[1,128,1280]{2,1,0:T(8,128)(2,1)} %get-tuple-element.404), channel_id=1, source_target_pairs={{0,2},{1,3},{2,0},{3,1},{4,6},{5,7},{6,4},{7,5},{8,10},{9,11},{10,... | collective-permute-start | bytes 983048 | tf_op jit(solution)/shard_map/ppermute | solution.py:35
  550.9 14.1 %collective-permute-start.47 = (bf16[1,128,896]{2,1,0:T(8,128)(2,1)}, bf16[1,128,896]{2,1,0:T(8,128)(2,1)S(1)}, u32[]{:S(2)}, u32[]{:S(2)}) collective-permute-start(bf16[1,128,896]{2,1,0:T(8,128)(2,1)} %get-tuple-element.411), channel_id=1, source_target_pairs={{0,2},{1,3},{2,0},{3,1},{4,6},{5,7},{6,4},{7,5},{8,10},{9,11},{10,... | collective-permute-start | bytes 688136 | tf_op jit(solution)/shard_map/ppermute | solution.py:35
  550.9 16.6 %collective-permute-start.48 = (f32[17920]{0:T(1024)S(1)}, f32[17920]{0:T(1024)S(1)}, u32[]{:S(2)}, u32[]{:S(2)}) collective-permute-start(f32[17920]{0:T(1024)S(1)} %add.90), channel_id=1, source_target_pairs={{0,2},{1,3},{2,0},{3,1},{4,6},{5,7},{6,4},{7,5},{8,10},{9,11},{10,... | collective-permute-start | bytes 215048 | tf_op jit(solution)/shard_map/ppermute | solution.py:35
  (56 other events, 387.4 us)
Sparse Core Ops, SparseCore 0:
  131.7 114.5 all-gather.2
  295.9 65.3 all-gather.4
  399.2 45.4 reduce-scatter.4
  447.0 45.5 reduce-scatter.2

commit v5 on v4

--- a/solution.py
+++ b/solution.py
@@ -236,6 +236,23 @@
     )(own, one, two)
 
 
+def copy_tracks(array_in):
+    tracks, rows, features = array_in.shape
+
+    def body(in_ref, out_ref):
+        out_ref[...] = in_ref[...]
+
+    return pl.pallas_call(
+        body,
+        grid=(tracks,),
+        in_specs=[pl.BlockSpec((1, rows, features), lambda n: (n, 0, 0))],
+        out_specs=pl.BlockSpec((1, rows, features), lambda n: (n, 0, 0)),
+        out_shape=jax.ShapeDtypeStruct(array_in.shape, array_in.dtype),
+        compiler_params=params(),
+        name="copy_tracks",
+    )(array_in)
+
+
 def bit_reverse(number, width):
     turned = 0
     for bit in range(width):
@@ -296,19 +313,40 @@
     rows, features = x.shape
     groups = pieces[0].shape[1]
     per = cols // tile
+    paired = per == 1 and tile <= 256
 
     def body(x_ref, *refs):
         *piece_refs, affine_ref, out_ref = refs
-        acc = over_features(x_ref[...], piece_refs)
-        out_ref[...] = ((acc + affine_ref[0:1]) * affine_ref[1:2]).astype(out_ref.dtype)
-
+        depth = features // len(pieces)
+        for k in range(2 if paired else 1):
+            total = None
+            for number, ref in enumerate(piece_refs):
+                piece = ref[:, k].reshape(depth, tile)
+                term = dot(x_ref[:, number * depth : (number + 1) * depth], piece, 1, 0)
+                total = term if total is None else total + term
+            where = slice(k * tile, (k + 1) * tile)
+            total = (total + affine_ref[0:1, where]) * affine_ref[1:2, where]
+            out_ref[:, where] = total.astype(out_ref.dtype)
+
+    if paired:
+        grid, wide = (groups // 2, 1), 2 * tile
+        weight_specs = [
+            pl.BlockSpec(
+                (pieces[0].shape[0], 2, pieces[0].shape[2], tile),
+                lambda j, c: (0, j, 0, first_col // tile),
+            )
+            for _ in pieces
+        ]
+    else:
+        grid, wide = (groups, per), tile
+        weight_specs = piece_specs(pieces, tile, first_col // tile)
     return pl.pallas_call(
         body,
-        grid=(groups, per),
+        grid=grid,
         in_specs=[whole((rows, features))]
-        + piece_specs(pieces, tile, first_col // tile)
-        + [pl.BlockSpec((2, tile), lambda j, c: (0, j * per + c))],
-        out_specs=pl.BlockSpec((rows, tile), lambda j, c: (0, j * per + c)),
+        + weight_specs
+        + [pl.BlockSpec((2, wide), lambda j, c: (0, j * per + c))],
+        out_specs=pl.BlockSpec((rows, wide), lambda j, c: (0, j * per + c)),
         out_shape=jax.ShapeDtypeStruct((rows, groups * cols), out_dtype),
         compiler_params=params(),
         name=name,
@@ -319,6 +357,23 @@
     groups = pieces[0].shape[1]
     affine = jnp.stack([jnp.zeros((groups * cols,), F32), jnp.ones((groups * cols,), F32)])
     return project(x, pieces, first_col, cols, cols, affine, BF, name)
+
+
+def paired_specs(pieces, cols, col_block):
+    count, _, blk, _ = pieces[0].shape
+    return [pl.BlockSpec((count, 2, blk, cols), lambda i: (0, i, 0, col_block)) for _ in pieces]
+
+
+def add_paired_rows(acc_ref, left_ref, piece_refs, cols):
+    depth = acc_ref.shape[1] // len(piece_refs)
+    for number, ref in enumerate(piece_refs):
+        where = slice(number * depth, (number + 1) * depth)
+        total = None
+        for k in range(2):
+            piece = ref[:, k].reshape(depth, cols)
+            term = dot(left_ref[:, k * cols : (k + 1) * cols], piece, 1, 1)
+            total = term if total is None else total + term
+        acc_ref[:, where] += total
 
 
 def add_rows(acc_ref, left, piece_refs):
@@ -361,9 +416,9 @@
         def _():
             acc_ref[...] = jnp.zeros_like(acc_ref)
 
-        add_rows(acc_ref, left_ref[...], piece_refs)
-
-        @pl.when(step == groups - 1)
+        add_paired_rows(acc_ref, left_ref, piece_refs, cols)
+
+        @pl.when(step == groups // 2 - 1)
         def _():
             v = residual_ref[...].astype(F32) + (acc_ref[...] + vectors_ref[2:3])
             unit, spread = normalize(v)
@@ -375,9 +430,9 @@
 
     return pl.pallas_call(
         body,
-        grid=(groups,),
-        in_specs=[pl.BlockSpec((rows, cols), lambda j: (0, j))]
-        + piece_specs(pieces, cols, first_col // cols)
+        grid=(groups // 2,),
+        in_specs=[pl.BlockSpec((rows, 2 * cols), lambda j: (0, j))]
+        + paired_specs(pieces, cols, first_col // cols)
         + [whole((rows, features)), whole((3, features))],
         out_specs=[whole((rows, features))] * 3 + [whole((rows, 1))],
         out_shape=[
@@ -611,9 +666,9 @@
         def _():
             acc_ref[...] = second_ref[...]
 
-        add_rows(acc_ref, left_ref[...], piece_refs)
-
-        @pl.when(step == groups - 1)
+        add_paired_rows(acc_ref, left_ref, piece_refs, cols)
+
+        @pl.when(step == groups // 2 - 1)
         def _():
             norm_back_outputs(
                 acc_ref[...],
@@ -627,9 +682,9 @@
 
     return pl.pallas_call(
         body,
-        grid=(groups,),
-        in_specs=[pl.BlockSpec((rows, cols), lambda j: (0, j))]
-        + piece_specs(pieces, cols, first_col // cols)
+        grid=(groups // 2,),
+        in_specs=[pl.BlockSpec((rows, 2 * cols), lambda j: (0, j))]
+        + paired_specs(pieces, cols, first_col // cols)
         + [whole((rows, features)), whole((rows, features)), whole((rows, 1)), whole((1, features))],
         out_specs=[whole((rows, features)), whole((rows, features)), whole((3, features))],
         out_shape=[
@@ -765,30 +820,33 @@
     def body(order_ref, *refs):
         lefts, rights = refs[:count], refs[count : 2 * count]
         out_refs = refs[len(refs) - len(outs) :]
-        at = 0
-        for left_ref, right_ref, width in zip(lefts, rights, widths):
-            term = dot(left_ref[...], right_ref[...], 0, 0).reshape(pieces, blk, width)
-            if extra is not None:
-                term = term + refs[2 * count][:, 0, :, at : at + width].astype(F32)
-            term = term.astype(BF)
-            for out_ref, (first, size, members) in zip(out_refs, outs):
-                low, high = max(at, first), min(at + width, first + size)
-                if low >= high:
-                    continue
-                for place, piece in enumerate(members):
-                    out_ref[place, 0, :, low - first : high - first] = term[
-                        piece, :, low - at : high - at
-                    ]
-            at += width
+        for k in range(2):
+            odd = order_ref[2 * pl.program_id(0) + k] & 1
+            at = 0
+            for left_ref, right_ref, width in zip(lefts, rights, widths):
+                right = right_ref[:, pl.ds(pl.multiple_of(odd * width, 128), width)]
+                term = dot(left_ref[...], right, 0, 0).reshape(pieces, blk, width)
+                if extra is not None:
+                    term = term + refs[2 * count][:, k, :, at : at + width].astype(F32)
+                term = term.astype(BF)
+                for out_ref, (first, size, members) in zip(out_refs, outs):
+                    low, high = max(at, first), min(at + width, first + size)
+                    if low >= high:
+                        continue
+                    for place, piece in enumerate(members):
+                        out_ref[place, k, :, low - first : high - first] = term[
+                            piece, :, low - at : high - at
+                        ]
+                at += width
 
     def block(number, width):
-        return pl.BlockSpec((number, 1, blk, width), lambda j, order: (0, j, 0, 0))
+        return pl.BlockSpec((number, 2, blk, width), lambda i, order: (0, i, 0, 0))
 
     in_specs = [
-        pl.BlockSpec((left.shape[0], depth), lambda j, order: (0, half)) for left, _ in entries
+        pl.BlockSpec((left.shape[0], depth), lambda i, order: (0, half)) for left, _ in entries
     ]
     in_specs += [
-        pl.BlockSpec((right.shape[0], width), lambda j, order: (0, order[j]))
+        pl.BlockSpec((right.shape[0], 2 * width), lambda i, order: (0, order[2 * i] // 2))
         for (_, right), width in zip(entries, widths)
     ]
     operands = [left for left, _ in entries] + [right for _, right in entries]
@@ -799,7 +857,7 @@
         body,
         grid_spec=pltpu.PrefetchScalarGridSpec(
             num_scalar_prefetch=1,
-            grid=(groups,),
+            grid=(groups // 2,),
             in_specs=in_specs,
             out_specs=[block(len(members), width) for _, width, members in outs],
         ),
@@ -1428,7 +1486,7 @@
     if blk % 128:
         out_low = reorder_blocks(out_low, to_natural)
     out_low = out_low.reshape(3, share, features)
-    layer_out = lax.all_gather(jnp.transpose(out_low, (1, 0, 2)), "head", axis=0, tiled=True)[None]
+    layer_out = lax.all_gather(out_low, "head", axis=1, tiled=True)
     down_entries = [(third_low, active)]
     down_came = send(down_entries, "down_grad", True)
     up_entries = [(normed2_low, upper_low)]
@@ -1446,14 +1504,13 @@
     line.mark(first)
     grad_context = project_plain(line.tie(first_low), weights_out, 0, 256, "self_ctx_back")
     line.mark(grad_context)
-    scatter_ffn.step()
     grad_q, grad_kv, grad_rel, self_sums, rel_sums = self_attention_back(
         qk, values, self_probs, self_own, line.tie(grad_context), straight.reshape(-1, 1), share
     )
     line.mark(grad_q)
-    scatter_ffn.step()
     layer_out = line.tie(layer_out)
     line.mark(layer_out, *line.last)
+    scatter_ffn.step()
     memory_order = z ^ jnp.array([0, 2, 1, 3], jnp.int32)
     memory_part = rows_back(
         memory_order, line.tie(grad_cross_kv), weights_kv, 0, 512, "memory_back"
@@ -1477,16 +1534,8 @@
     scatter_self = Scatter(line, halves, (near, far), cuts=((0, 256, 3), (768, 128, 1)))
     while not hasattr(scatter_ffn, "total"):
         scatter_ffn.step()
-    two_grad, one_grad, own_grad = input_back(
-        line.tie(grad_q), grad_kv, grad_rel, weights_qk, weights_vr, first
-    )
-    line.mark(own_grad)
-    from_two = lax.ppermute(two_grad, "head", [(i + 2, i) for i in chain[:-2]])
-    from_one = lax.ppermute(one_grad, "head", [(i + 1, i) for i in chain[:-1]])
-    scatter_ffn.total = line.tie(scatter_ffn.total)
-    line.mark(scatter_ffn.total, *line.last)
-    scatter_cross.step()
-    scatter_self.step()
+    memory_grad = line.tie(memory_grad)
+    line.mark(memory_grad, *line.last)
     packed = line.mark(pack_sums(line.last[0]))
     packed_bits = [("batch", bit) for bit in range(nb)] + [("head", 0), ("head", 1)]
 
@@ -1496,32 +1545,33 @@
         packed = line.tie(packed)
         return line.mark(packed + after(came, packed))
 
-    memory_grad = line.tie(memory_grad)
-    line.mark(memory_grad, *line.last)
+    two_grad, one_grad, own_grad = input_back(
+        line.tie(grad_q), grad_kv, grad_rel, weights_qk, weights_vr, first
+    )
+    line.mark(own_grad)
+    from_two = lax.ppermute(two_grad, "head", [(i + 2, i) for i in chain[:-2]])
+    from_one = lax.ppermute(one_grad, "head", [(i + 1, i) for i in chain[:-1]])
+    scatter_cross.step()
+    scatter_self.step()
+    scatter_ffn.total = line.tie(scatter_ffn.total)
+    line.mark(scatter_ffn.total, *line.last)
     own_grad = line.mark(add_halo(line.tie(own_grad), from_one, from_two))
     own_grad = line.mark(reorder_blocks(line.tie(own_grad), to_natural)).reshape(
         3, share, features
     )
     grad_hidden = jnp.transpose(own_grad, (1, 0, 2))[None]
     scatter_cross.step()
-    packed = add_packed(packed)
     scatter_self.step()
     packed = add_packed(packed)
     grad_memory = line.mark(reorder_blocks(line.tie(memory_grad), to_natural, F32))[None]
+    packed = add_packed(packed)
+    layer_out = line.mark(copy_tracks(line.tie(layer_out)))
+    layer_out = jnp.transpose(layer_out, (1, 0, 2))[None]
     scatter_cross.step()
     packed = add_packed(packed)
     scatter_self.step()
-    packed = add_packed(packed)
-    scatter_cross.step()
-    scatter_self.step()
     while packed_bits:
         packed = add_packed(packed)
-    scatters = (scatter_ffn, scatter_cross, scatter_self)
-    for scatter in scatters:
-        while not hasattr(scatter, "total"):
-            scatter.step()
-    grads_ffn, grads_cross, grads_self = [scatter.total for scatter in scatters]
-
     ends = [0]
     for size in (2 * features, groups * 128, 2 * features, up_bias.shape[0], 9 * features):
         ends.append(ends[-1] + size)
@@ -1530,6 +1580,25 @@
     cross_bias_grad = packed[ends[2] : ends[3]].reshape(2, -1)
     up_bias_grad = packed[ends[3] : ends[4]]
     feature_sums = packed[ends[4] : ends[5]].reshape(3, 3, features)
+    small = (
+        self_bias_grad,
+        relpos_bias_grad,
+        cross_bias_grad,
+        up_bias_grad,
+        feature_sums[:, 0],
+        feature_sums[:, 1],
+        feature_sums[:, 2],
+    )
+    small = lax.optimization_barrier(small + line.last)[: len(small)]
+    line.mark(*small)
+    while not hasattr(scatter_cross, "total"):
+        scatter_cross.step()
+    cross_kv_grad = line.mark(line.tie(scatter_cross.total[1]).reshape(blk, 2, 256))
+    while not hasattr(scatter_self, "total"):
+        scatter_self.step()
+    grads_ffn, grads_cross, grads_self = [
+        scatter.total for scatter in (scatter_ffn, scatter_cross, scatter_self)
+    ]
 
     return (
         layer_out,
@@ -1539,18 +1608,11 @@
         grads_self[1],
         grads_cross[3],
         grads_cross[0],
-        grads_cross[1].reshape(blk, 2, 256),
+        cross_kv_grad,
         grads_cross[2],
         grads_ffn[:, 1024:],
         grads_ffn[:, 0:1024],
-        self_bias_grad,
-        relpos_bias_grad,
-        cross_bias_grad,
-        up_bias_grad,
-        feature_sums[:, 0],
-        feature_sums[:, 1],
-        feature_sums[:, 2],
-    )
+    ) + tuple(small)
 
 
 def solution(mesh):

time: 592 us -> 575 us (0.971)
  waiting for transfers between devices: 155 us -> 144 us
  Pallas kernels: 281 us -> 272 us
    ppermute x45, waiting for transfers between devices: 150 us -> 139 us  [swap(): return lax.ppermute(array_in, axis, [(i, i ^ bit) for i in range(count)])]
    pallas_call x9 -> x10, Pallas kernels: 55.1 us -> 52.1 us  [the longest x6 30.2 us: project(): pl.pallas_call(body, grid=grid, in_specs=[whole((rows, features))] + weig...]
    unnamed x143 -> x152, local copies, waits for them, and re-layouts: 31 us -> 30.8 us
  transfers between devices with their start and end apart: 53 -> 53, of which waited for: 29 -> 26; matrix products, arithmetic and copies ran while one was open for 8% -> 10% of each run, Pallas kernels for 42% -> 37%
where the time goes in v5:
time: 575 us; the launch traced here: 568 us
  Pallas kernels  272 us (47%)
  waiting for transfers between devices  144 us (25%)
  local copies, waits for them, and re-layouts  65.9 us (11%)
  starting transfers between devices  58.1 us (10%)
  between operations  15 us (3%)
  other arithmetic  13.1 us (2%)
    ppermute x45, waiting for transfers between devices, swap(): return lax.ppermute(array_in, axis, [(i, i ^ bit) for i in range(count)])  139 us
    pallas_call x8, Pallas kernels, weight_products(): pl.pallas_call(body, grid_spec=pltpu.PrefetchScalarGridSpec(num_scalar_pr...  60.3 us
    ppermute x45, starting transfers between devices, swap(): return lax.ppermute(array_in, axis, [(i, i ^ bit) for i in range(count)])  49.9 us
    unnamed x152, local copies, waits for them, and re-layouts  30.8 us
    pallas_call x6, Pallas kernels, project(): pl.pallas_call(body, grid=grid, in_specs=[whole((rows, features))] + weig...  30.2 us
    pallas_call x1, Pallas kernels, feed_forward(): pl.pallas_call(body, grid_spec=pltpu.PrefetchScalarGridSpec(num_scalar_pr...  29.7 us
    pallas_call x8, Pallas kernels, add_blocks(): pl.pallas_call(body, grid=(rows // chunk,), in_specs=[spec(array.shape[0]...  27.1 us
    pallas_call x1, Pallas kernels, cross_attention_back(): pl.pallas_call(body, grid=(groups,), in_specs=[pl.BlockSpec((rows, 256),...  17.4 us
  transfers between devices with their start and end apart: 53, of which 26 were waited for; matrix products, arithmetic and copies ran while one was open for 10% of the time, Pallas kernels for 37%

profile of v5, /device:TPU:0, one launch (start us, length us, event | category | flops | bytes accessed | tf_op | source)
XLA Modules:
  0.0 567.7 jit_solution(3346889685503397693)
XLA Ops:
  9.4 4.1 collective-permute-start
  24.7 3.6 reorder.7.grad_ref
  33.1 16.3 %collective-permute-done.1 = bf16[1,1,1,2,1,128,896]{6,5,4,3,2,1,0:T(8,128)(2,1)} collective-permute-done((bf16[1,1,1,2,1,128,896]{6,5,4,3,2,1,0:T(8,128)(2,1)S(1)}, bf16[1,1,1,2,1,128,896]{6,5,4,3,2,1,0:T(8,128)(2,1)}, u32[]{:S(2)}, u32[]{:S(2)}) %collective-permute-start.1) | collective-permute-done | bytes 458784 | tf_op jit(solution)/shard_map/ppermute | solution.py:35
  52.2 4.8 collective-permute-done.2
  58.8 4.2 collective-permute-done.3
  64.9 4.3 collective-permute-done.4
  72.0 15.5 %collective-permute-done.5 = bf16[1,1,1,2,1,128,2048]{6,5,4,3,2,1,0:T(8,128)(2,1)S(1)} collective-permute-done((bf16[1,1,1,2,1,128,2048]{6,5,4,3,2,1,0:T(8,128)(2,1)S(1)}, bf16[1,1,1,2,1,128,2048]{6,5,4,3,2,1,0:T(8,128)(2,1)S(1)}, u32[]{:S(2)}, u32[]{:S(2)}) %collective-permute-start.5) | collective-permute-done | bytes 1048608 | tf_op jit(solution)/shard_map/ppermute | solution.py:35
  99.5 8.9 %collective-permute-done.11 = bf16[1,1,1,2,1,128,1280]{6,5,4,3,2,1,0:T(8,128)(2,1)} collective-permute-done((bf16[1,1,1,2,1,128,1280]{6,5,4,3,2,1,0:T(8,128)(2,1)}, bf16[1,1,1,2,1,128,1280]{6,5,4,3,2,1,0:T(8,128)(2,1)}, u32[]{:S(2)}, u32[]{:S(2)}) %collective-permute-start.11) | collective-permute-done | bytes 655392 | tf_op jit(solution)/shard_map/ppermute | solution.py:35
  120.0 4.3 self_v.1.v_ref
  124.3 3.3 self_rel.1.rel_ref
  133.6 3.4 collective-permute-start.16
  138.3 7.4 %self_qk.1.q_ref.k_ref = bf16[640,2048]{1,0:T(8,128)(2,1)} custom-call(bf16[640,1024]{1,0:T(8,128)(2,1)} %stack_rows.1.x_ref.refs_1_, bf16[4,4,128,512]{3,2,1,0:T(8,128)(2,1)} %bitcast.161, bf16[4,4,128,512]{3,2,1,0:T(8,128)(2,1)} %bitcast.21.refs_1_.refs_3_, f32[2,2048]{1,0:T(2,128)} %pad_maximum_fusion.4.refs_2_), custom_call_target="tpu_custom_call" | custom-call | tf_op jit(solution)/shard_map/self_qk/pallas_call | solution.py:343
  146.5 14.0 %collective-permute-done.16 = bf16[256,1024]{1,0:T(8,128)(2,1)} collective-permute-done((bf16[256,1024]{1,0:T(8,128)(2,1)}, bf16[256,1024]{1,0:T(8,128)(2,1)}, u32[]{:S(2)}, u32[]{:S(2)}) %collective-permute-start.16) | collective-permute-done | bytes 524320 | tf_op jit(solution)/shard_map/ppermute | solution.py:35
  162.5 11.1 %self_attention.1 = (bf16[384,1024]{1,0:T(8,128)(2,1)}, bf16[16,384,384]{2,1,0:T(8,128)(2,1)}, f32[384,512]{1,0:T(8,128)}) custom-call(bf16[640,2048]{1,0:T(8,128)(2,1)} %self_qk.1.q_ref.k_ref, bf16[640,2048]{1,0:T(8,128)(2,1)} %self_qk.1.q_ref.k_ref, bf16[640,1024]{1,0:T(8,128)(2,1)} %self_v.1.v_ref, f32[384,512]{1,0:T(8,128)} %self_rel.1.rel_ref, ...), custom_call_target="tpu_custom_call" | custom-call | tf_op jit(solution)/shard_map/self_attention/pallas_call | solution.py:970
  178.5 11.7 %collective-permute-done.18 = bf16[1,2,1,2,2,128,768]{6,5,4,3,2,1,0:T(8,128)(2,1)} collective-permute-done((bf16[1,2,1,2,2,128,768]{6,5,4,3,2,1,0:T(8,128)(2,1)}, bf16[1,2,1,2,2,128,768]{6,5,4,3,2,1,0:T(8,128)(2,1)}, u32[]{:S(2)}, u32[]{:S(2)}) %collective-permute-start.18) | collective-permute-done | bytes 1572896 | tf_op jit(solution)/shard_map/ppermute | solution.py:35
  198.4 5.0 collective-permute-done.19
  203.4 5.6 self_out.1
  209.1 3.4 cross_q.1.q_ref
  213.8 4.8 collective-permute-done.20
  221.2 8.4 %cross_kv.1.k_ref.v_ref = bf16[1024,2048]{1,0:T(8,128)(2,1)} custom-call(bf16[1024,1024]{1,0:T(8,128)(2,1)} %copy-done.4, bf16[4,4,128,768]{3,2,1,0:T(8,128)(2,1)} %bitcast.153, bf16[4,4,128,768]{3,2,1,0:T(8,128)(2,1)} %bitcast.29.refs_1_, f32[2,2048]{1,0:T(2,128)} %stack.26.refs_2_), custom_call_target="tpu_custom_call" | custom-call | tf_op jit(solution)/shard_map/cross_kv/pallas_call | solution.py:343
  229.7 13.5 %cross_attention.1 = (bf16[384,1024]{1,0:T(8,128)(2,1)}, bf16[16,384,1024]{2,1,0:T(8,128)(2,1)}, f32[384,512]{1,0:T(8,128)}) custom-call(bf16[384,1024]{1,0:T(8,128)(2,1)} %cross_q.1.q_ref, bf16[1024,2048]{1,0:T(8,128)(2,1)} %cross_kv.1.k_ref.v_ref, bf16[1024,2048]{1,0:T(8,128)(2,1)} %cross_kv.1.k_ref.v_ref), custom_call_target="tpu_custom_call" | custom-call | tf_op jit(solution)/shard_map/cross_attention/pallas_call | solution.py:1138
  243.2 5.9 %cross_out.1 = (f32[384,1024]{1,0:T(8,128)}, bf16[384,1024]{1,0:T(8,128)(2,1)}, f32[384,1024]{1,0:T(8,128)}, f32[384,1]{1,0:T(8,128)}) custom-call(bf16[384,1024]{1,0:T(8,128)(2,1)} %get-tuple-element.297.left_ref.refs_6_, bf16[4,4,128,768]{3,2,1,0:T(8,128)(2,1)} %bitcast.154, bf16[4,4,128,768]{3,2,1,0:T(8,128)(2,1)} %bitcast.29.refs_1_, ...), custom_call_target="tpu_custom_call" | custom-call | tf_op jit(solution)/shard_map/cross_out/pallas_call | solution.py:431
  249.0 29.7 %feed_forward.1 = (bf16[384,4096]{1,0:T(8,128)(2,1)}, bf16[384,1024]{1,0:T(8,128)(2,1)}, bf16[384,1024]{1,0:T(8,128)(2,1)}, f32[3,1024]{1,0:T(4,128)}, bf16[384,...) custom-call(s32[12]{0:T(128)} %pad_add_fusion.order_ref, ...), custom_call_target="tpu_custom_call" | custom-call | tf_op jit(solution)/shard_map/feed_forward/pallas_call | solution.py:590
  278.7 6.1 %down_grad_send.1 = bf16[4,4,128,1024]{3,2,1,0:T(8,128)(2,1)} custom-call(s32[4]{0:T(128)} %copy-done.40, bf16[384,1024]{1,0:T(8,128)(2,1)} %get-tuple-element.316.refs_0_, bf16[384,4096]{1,0:T(8,128)(2,1)} %get-tuple-element.313.refs_1_), custom_call_target="tpu_custom_call" | custom-call | tf_op jit(solution)/shard_map/down_grad_send/pallas_call | solution.py:856
  284.8 6.1 %up_grad_send.1 = bf16[4,4,128,1024]{3,2,1,0:T(8,128)(2,1)} custom-call(s32[4]{0:T(128)} %copy-done.40, bf16[384,1024]{1,0:T(8,128)(2,1)} %get-tuple-element.318.low_ref.refs_0_, bf16[384,4096]{1,0:T(8,128)(2,1)} %get-tuple-element.315.refs_1_), custom_call_target="tpu_custom_call" | custom-call | tf_op jit(solution)/shard_map/up_grad_send/pallas_call | solution.py:856
  292.3 6.9 %down_grad_keep.1 = (bf16[2,4,128,1024]{3,2,1,0:T(8,128)(2,1)}, bf16[2,4,128,1024]{3,2,1,0:T(8,128)(2,1)}) custom-call(s32[4]{0:T(128)} %copy-done.40, bf16[384,1024]{1,0:T(8,128)(2,1)} %get-tuple-element.316.refs_0_, bf16[384,4096]{1,0:T(8,128)(2,1)} %get-tuple-element.313.refs_1_, bf16[4,4,128,1024]{3,2,1,0:T(8,128)(2,1)} %collective-permute-done.22.refs_2_), custom_call_target="tpu_custom_call" | custom-call | tf_op jit(solution)/shard_map/down_grad_keep/pallas_call | solution.py:856
  299.2 7.3 %up_grad_keep.1 = (bf16[2,4,128,1024]{3,2,1,0:T(8,128)(2,1)}, bf16[2,4,128,1024]{3,2,1,0:T(8,128)(2,1)}) custom-call(s32[4]{0:T(128)} %copy-done.40, bf16[384,1024]{1,0:T(8,128)(2,1)} %get-tuple-element.318.low_ref.refs_0_, bf16[384,4096]{1,0:T(8,128)(2,1)} %get-tuple-element.315.refs_1_, bf16[4,4,128,1024]{3,2,1,0:T(8,128)(2,1)} %collective-permute-done.23.refs_2_), custom_call_target="tpu_custom_call" | custom-call | tf_op jit(solution)/shard_map/up_grad_keep/pallas_call | solution.py:856
  310.9 17.4 %cross_attention_back.1 = (bf16[384,1024]{1,0:T(8,128)(2,1)}, bf16[1024,2048]{1,0:T(8,128)(2,1)}, f32[2,1024]{1,0:T(2,128)}) custom-call(bf16[384,1024]{1,0:T(8,128)(2,1)} %cross_q.1.q_ref, bf16[1024,2048]{1,0:T(8,128)(2,1)} %cross_kv.1.k_ref.v_ref, bf16[1024,2048]{1,0:T(8,128)(2,1)} %cross_kv.1.k_ref.v_ref, ...), custom_call_target="tpu_custom_call" | custom-call | tf_op jit(solution)/shard_map/cross_attention_back/pallas_call | solution.py:1207
  328.3 6.0 %cross_query_back.1 = (f32[384,1024]{1,0:T(8,128)}, bf16[384,1024]{1,0:T(8,128)(2,1)}, f32[3,1024]{1,0:T(4,128)}) custom-call(bf16[384,1024]{1,0:T(8,128)(2,1)} %get-tuple-element.322.left_ref.refs_4_, bf16[4,4,128,512]{3,2,1,0:T(8,128)(2,1)} %bitcast.23.refs_0_, bf16[4,4,128,512]{3,2,1,0:T(8,128)(2,1)} %bitcast.24.refs_1_, ...), custom_call_target="tpu_custom_call" | custom-call | tf_op jit(solution)/shard_map/cross_query_back/pallas_call | solution.py:683
  334.3 3.4 self_ctx_back.1.grad_ref
  337.8 16.5 %self_attention_back.1 = (bf16[384,1024]{1,0:T(8,128)(2,1)}, bf16[640,2048]{1,0:T(8,128)(2,1)}, bf16[384,512]{1,0:T(8,128)(2,1)}, f32[2,1024]{1,0:T(2,128)}, f32[1,512]{1,0:T(1,128)}) custom-call(bf16[640,2048]{1,0:T(8,128)(2,1)} %self_qk.1.q_ref.k_ref, bf16[640,2048]{1,0:T(8,128)(2,1)} %self_qk.1.q_ref.k_ref, bf16[640,1024]{1,0:T(8,128)(2,1)} %self_v.1.v_ref, ...), custom_call_target="tpu_custom_call" | custom-call | tf_op jit(solution)/shard_map/self_attention_back/pallas_call | solution.py:1083
  358.4 6.0 %add_blocks.8 = (bf16[4,128,1024]{2,1,0:T(8,128)(2,1)}, bf16[4,128,1024]{2,1,0:T(8,128)(2,1)}, bf16[4,128,1024]{2,1,0:T(8,128)(2,1)}, bf16[4,128,1024]{2,1,0:T(8,128)(2,1)}) custom-call(bf16[8,128,1024]{2,1,0:T(8,128)(2,1)} %bitcast.171, bf16[8,128,1024]{2,1,0:T(8,128)(2,1)} %bitcast.45.refs_1_, bf16[8,128,1024]{2,1,0:T(8,128)(2,1)} %bitcast.172, ...), custom_call_target="tpu_custom_call" | custom-call | tf_op jit(solution)/shard_map/add_blocks/pallas_call | solution.py:103
  364.3 9.9 %memory_back.1 = bf16[1024,1024]{1,0:T(8,128)(2,1)} custom-call(s32[4]{0:T(128)} %broadcast_xor_fusion.1.order_ref, bf16[1024,2048]{1,0:T(8,128)(2,1)} %get-tuple-element.346.left_ref.refs_5_, bf16[4,4,128,768]{3,2,1,0:T(8,128)(2,1)} %bitcast.156, bf16[4,4,128,768]{3,2,1,0:T(8,128)(2,1)} %bitcast.29.refs_1_), custom_call_target="tpu_custom_call" | custom-call | tf_op jit(solution)/shard_map/memory_back/pallas_call | solution.py:726
  374.7 9.2 %cross_grad_send.1 = bf16[4,4,128,1280]{3,2,1,0:T(8,128)(2,1)} custom-call(s32[4]{0:T(128)} %iota.56.order_ref, bf16[384,1024]{1,0:T(8,128)(2,1)} %get-tuple-element.352.x_ref.refs_0_, bf16[1024,1024]{1,0:T(8,128)(2,1)} %copy-done.4, bf16[384,1024]{1,0:T(8,128)(2,1)} %get-tuple-element.348.refs_2_, bf16[384,1024]{1,0:T(8,128)(2,1)} %get-tuple-element.327.x_ref.refs_3_, ...), custom_call_target="tpu_custom_call" | custom-call | tf_op jit(solution)/shard_map/cross_grad_send/pallas_call | solution.py:856
  384.5 7.1 %self_grad_send.1 = bf16[4,4,128,896]{3,2,1,0:T(8,128)(2,1)} custom-call(s32[4]{0:T(128)} %iota.55.order_ref, bf16[384,1024]{1,0:T(8,128)(2,1)} %reorder.6.refs_2_.x_ref.refs_0_, bf16[640,1024]{1,0:T(8,128)(2,1)} %stack_rows.1.x_ref.refs_1_, bf16[384,1024]{1,0:T(8,128)(2,1)} %reorder.6.refs_2_.x_ref.refs_0_, ...), custom_call_target="tpu_custom_call" | custom-call | tf_op jit(solution)/shard_map/self_grad_send/pallas_call | solution.py:856
  395.6 10.0 %cross_grad_keep.1 = (bf16[2,4,128,640]{3,2,1,0:T(8,128)(2,1)}, bf16[2,4,128,640]{3,2,1,0:T(8,128)(2,1)}, bf16[2,4,128,640]{3,2,1,0:T(8,128)(2,1)}, bf16[2,4,128,640]{3,2,1,0:T(8,128)(2,1)}) custom-call(s32[4]{0:T(128)} %iota.54.order_ref, bf16[384,1024]{1,0:T(8,128)(2,1)} %get-tuple-element.352.x_ref.refs_0_, bf16[1024,1024]{1,0:T(8,128)(2,1)} %copy-done.4, ...), custom_call_target="tpu_custom_call" | custom-call | tf_op jit(solution)/shard_map/cross_grad_keep/pallas_call | solution.py:856
  407.5 7.6 %self_grad_keep.1 = (bf16[2,4,128,512]{3,2,1,0:T(8,128)(2,1)}, bf16[2,4,128,512]{3,2,1,0:T(8,128)(2,1)}, bf16[2,4,128,384]{3,2,1,0:T(8,128)(2,1)}, bf16[2,4,128,384]{3,2,1,0:T(8,128)(2,1)}) custom-call(s32[4]{0:T(128)} %iota.53.order_ref, bf16[384,1024]{1,0:T(8,128)(2,1)} %reorder.6.refs_2_.x_ref.refs_0_, bf16[640,1024]{1,0:T(8,128)(2,1)} %stack_rows.1.x_ref.refs_1_, ...), custom_call_target="tpu_custom_call" | custom-call | tf_op jit(solution)/shard_map/self_grad_keep/pallas_call | solution.py:856
  419.5 4.0 add_blocks.9
  438.2 9.8 %input_back.1 = (bf16[128,1024]{1,0:T(8,128)(2,1)}, bf16[128,1024]{1,0:T(8,128)(2,1)}, f32[384,1024]{1,0:T(8,128)}) custom-call(bf16[384,1024]{1,0:T(8,128)(2,1)} %get-tuple-element.366.refs_3_.query_ref, bf16[640,2048]{1,0:T(8,128)(2,1)} %get-tuple-element.350.refs_4_.kv_ref, bf16[384,512]{1,0:T(8,128)(2,1)} %get-tuple-element.351.refs_5_.rel_ref, ...), custom_call_target="tpu_custom_call" | custom-call | tf_op jit(solution)/shard_map/input_back/pallas_call | solution.py:778
  449.4 11.1 %collective-permute-done.31 = bf16[2,4,128,640]{3,2,1,0:T(8,128)(2,1)S(1)} collective-permute-done((bf16[2,4,128,640]{3,2,1,0:T(8,128)(2,1)}, bf16[2,4,128,640]{3,2,1,0:T(8,128)(2,1)S(1)}, u32[]{:S(2)}, u32[]{:S(2)}) %collective-permute-start.31) | collective-permute-done | bytes 1310752 | tf_op jit(solution)/shard_map/ppermute | solution.py:35
  462.0 4.2 add_blocks.10
  469.0 8.4 %collective-permute-done.33 = bf16[2,4,128,384]{3,2,1,0:T(8,128)(2,1)S(1)} collective-permute-done((bf16[2,4,128,384]{3,2,1,0:T(8,128)(2,1)}, bf16[2,4,128,384]{3,2,1,0:T(8,128)(2,1)S(1)}, u32[]{:S(2)}, u32[]{:S(2)}) %collective-permute-start.33) | collective-permute-done | bytes 786464 | tf_op jit(solution)/shard_map/ppermute | solution.py:35
  478.7 3.2 collective-permute-done.32
  481.8 3.3 add_blocks.11
  493.1 3.5 reorder.8
  515.4 4.4 copy_tracks.1
  524.3 3.1 collective-permute-done.44.refs_1_
  534.2 12.7 %collective-permute-done.46 = f32[17920]{0:T(1024)S(1)} collective-permute-done((f32[17920]{0:T(1024)S(1)}, f32[17920]{0:T(1024)S(1)}, u32[]{:S(2)}, u32[]{:S(2)}) %collective-permute-start.46) | collective-permute-done | bytes 71712 | tf_op jit(solution)/shard_map/ppermute | solution.py:35
  (378 shorter events, 172.3 us)
Async XLA Ops:
  7.2 241.9 %all-gather.3.cloned.1.call-start = ((), (), s32[]{:S(2)}) async-start(), calls=%async_computation.2 | async-start | bytes 18874368 | tf_op jit(solution)/shard_map/all_gather | solution.py:1403
  9.4 20.6 %collective-permute-start = (bf16[1,1,1,1,1,128,896]{6,5,4,3,2,1,0:T(8,128)(2,1)S(1)}, bf16[1,1,1,1,1,128,896]{6,5,4,3,2,1,0:T(8,128)(2,1)S(1)}, u32[]{:S(2)}, u32[]{:S(2)}) collective-permute-start(bf16[1,1,1,1,1,128,896]{6,5,4,3,2,1,0:T(8,128)(2,1)S(1)} %pad_maximum_fusion.1), channel_id=1, source_target_pairs={{0,2},{1,3},{2,0},{3,1},{4,6},{5,7},{6,4},{7,5},{8,10},{9,11},{10,... | collective-permute-start | bytes 688136 | tf_op jit(solution)/shard_map/ppermute | solution.py:35
  30.0 19.4 %collective-permute-start.1 = (bf16[1,1,1,2,1,128,896]{6,5,4,3,2,1,0:T(8,128)(2,1)S(1)}, bf16[1,1,1,2,1,128,896]{6,5,4,3,2,1,0:T(8,128)(2,1)}, u32[]{:S(2)}, u32[]{:S(2)}) collective-permute-start(bf16[1,1,1,2,1,128,896]{6,5,4,3,2,1,0:T(8,128)(2,1)S(1)} %constant_dynamic-update-slice_fusion), channel_id=1, source_target_pairs={{0,1},{1,0},{2,3},{3,2},{4,5},{5,4},{6,7},{7,6},{8,9},{9,8},{10,11... | collective-permute-start | bytes 1376264 | tf_op jit(solution)/shard_map/ppermute | solution.py:35
  31.7 25.3 %collective-permute-start.2 = (bf16[1,1,1,1,1,128,2048]{6,5,4,3,2,1,0:T(8,128)(2,1)S(1)}, bf16[1,1,1,1,1,128,2048]{6,5,4,3,2,1,0:T(8,128)(2,1)S(1)}, u32[]{:S(2)}, u32[]{:S(2)}) collective-permute-start(bf16[1,1,1,1,1,128,2048]{6,5,4,3,2,1,0:T(8,128)(2,1)S(1)} %fusion.9), channel_id=1, source_target_pairs={{0,2},{1,3},{2,0},{3,1},{4,6},{5,7},{6,4},{7,5},{8,10},{9,11},{10,... | collective-permute-start | bytes 1572872 | tf_op jit(solution)/shard_map/ppermute | solution.py:35
  50.6 12.5 %collective-permute-start.3 = (bf16[1,1,1,2,2,128,512]{6,5,4,3,2,1,0:T(8,128)(2,1)S(1)}, bf16[1,1,1,2,2,128,512]{6,5,4,3,2,1,0:T(8,128)(2,1)S(1)}, u32[]{:S(2)}, u32[]{:S(2)}) collective-permute-start(bf16[1,1,1,2,2,128,512]{6,5,4,3,2,1,0:T(8,128)(2,1)S(1)} %slice.153), channel_id=1, source_target_pairs={{0,8},{4,12},{8,0},{12,4},{16,24},{20,28},{24,16},{28,20},{1,9},{5... | collective-permute-start | bytes 1572872 | tf_op jit(solution)/shard_map/ppermute | solution.py:35
  57.0 30.5 %collective-permute-start.5 = (bf16[1,1,1,2,1,128,2048]{6,5,4,3,2,1,0:T(8,128)(2,1)S(1)}, bf16[1,1,1,2,1,128,2048]{6,5,4,3,2,1,0:T(8,128)(2,1)S(1)}, u32[]{:S(2)}, u32[]{:S(2)}) collective-permute-start(bf16[1,1,1,2,1,128,2048]{6,5,4,3,2,1,0:T(8,128)(2,1)S(1)} %constant_dynamic-update-slice_fusion.4), channel_id=1, source_target_pairs={{0,1},{1,0},{2,3},{3,2},{4,5},{5,4},{6,7},{7,6},{8,9},{9,8},{10,11... | collective-permute-start | bytes 3145736 | tf_op jit(solution)/shard_map/ppermute | solution.py:35
  57.1 12.1 %collective-permute-start.4 = (bf16[1,1,1,2,2,128,384]{6,5,4,3,2,1,0:T(8,128)(2,1)S(1)}, bf16[1,1,1,2,2,128,384]{6,5,4,3,2,1,0:T(8,128)(2,1)S(1)}, u32[]{:S(2)}, u32[]{:S(2)}) collective-permute-start(bf16[1,1,1,2,2,128,384]{6,5,4,3,2,1,0:T(8,128)(2,1)S(1)} %slice.152), channel_id=1, source_target_pairs={{0,16},{4,20},{8,24},{12,28},{16,0},{20,4},{24,8},{28,12},{1,17},{... | collective-permute-start | bytes 1179656 | tf_op jit(solution)/shard_map/ppermute | solution.py:35
  63.1 26.0 %collective-permute-start.6 = (bf16[1,2,1,2,2,128,512]{6,5,4,3,2,1,0:T(8,128)(2,1)S(1)}, bf16[1,2,1,2,2,128,512]{6,5,4,3,2,1,0:T(8,128)(2,1)S(1)}, u32[]{:S(2)}, u32[]{:S(2)}) collective-permute-start(bf16[1,2,1,2,2,128,512]{6,5,4,3,2,1,0:T(8,128)(2,1)S(1)} %constant_dynamic-update-slice_fusion.6), channel_id=1, source_target_pairs={{0,16},{4,20},{8,24},{12,28},{16,0},{20,4},{24,8},{28,12},{1,17},{... | collective-permute-start | bytes 3145736 | tf_op jit(solution)/shard_map/ppermute | solution.py:35
  69.4 19.8 %collective-permute-start.7 = (bf16[1,1,2,2,2,128,384]{6,5,4,3,2,1,0:T(8,128)(2,1)S(1)}, bf16[1,1,2,2,2,128,384]{6,5,4,3,2,1,0:T(8,128)(2,1)S(1)}, u32[]{:S(2)}, u32[]{:S(2)}) collective-permute-start(bf16[1,1,2,2,2,128,384]{6,5,4,3,2,1,0:T(8,128)(2,1)S(1)} %constant_dynamic-update-slice_fusion.8), channel_id=1, source_target_pairs={{0,8},{4,12},{8,0},{12,4},{16,24},{20,28},{24,16},{28,20},{1,9},{5... | collective-permute-start | bytes 2359304 | tf_op jit(solution)/shard_map/ppermute | solution.py:35
  70.9 19.5 %collective-permute-start.8 = (bf16[1,1,1,1,1,128,1280]{6,5,4,3,2,1,0:T(8,128)(2,1)S(1)}, bf16[1,1,1,1,1,128,1280]{6,5,4,3,2,1,0:T(8,128)(2,1)S(1)}, u32[]{:S(2)}, u32[]{:S(2)}) collective-permute-start(bf16[1,1,1,1,1,128,1280]{6,5,4,3,2,1,0:T(8,128)(2,1)S(1)} %maximum_bitcast_fusion), channel_id=1, source_target_pairs={{0,2},{1,3},{2,0},{3,1},{4,6},{5,7},{6,4},{7,5},{8,10},{9,11},{10,... | collective-permute-start | bytes 983048 | tf_op jit(solution)/shard_map/ppermute | solution.py:35
  91.2 17.2 %collective-permute-start.11 = (bf16[1,1,1,2,1,128,1280]{6,5,4,3,2,1,0:T(8,128)(2,1)}, bf16[1,1,1,2,1,128,1280]{6,5,4,3,2,1,0:T(8,128)(2,1)}, u32[]{:S(2)}, u32[]{:S(2)}) collective-permute-start(bf16[1,1,1,2,1,128,1280]{6,5,4,3,2,1,0:T(8,128)(2,1)} %constant_dynamic-update-slice_fusion.16), channel_id=1, source_target_pairs={{0,1},{1,0},{2,3},{3,2},{4,5},{5,4},{6,7},{7,6},{8,9},{9,8},{10,11... | collective-permute-start | bytes 1966088 | tf_op jit(solution)/shard_map/ppermute | solution.py:35
  92.9 25.9 %collective-permute-start.12 = (bf16[1,2,2,2,2,128,384]{6,5,4,3,2,1,0:T(8,128)(2,1)S(1)}, bf16[1,2,2,2,2,128,384]{6,5,4,3,2,1,0:T(8,128)(2,1)S(1)}, u32[]{:S(2)}, u32[]{:S(2)}) collective-permute-start(bf16[1,2,2,2,2,128,384]{6,5,4,3,2,1,0:T(8,128)(2,1)S(1)} %constant_dynamic-update-slice_fusion.14), channel_id=1, source_target_pairs={{0,4},{4,0},{8,12},{12,8},{16,20},{20,16},{24,28},{28,24},{1,5},{5... | collective-permute-start | bytes 4718600 | tf_op jit(solution)/shard_map/ppermute | solution.py:35
  93.6 20.5 %collective-permute-start.10 = (bf16[128,1024]{1,0:T(8,128)(2,1)S(1)}, bf16[128,1024]{1,0:T(8,128)(2,1)S(1)}, u32[]{:S(2)}, u32[]{:S(2)}) collective-permute-start(bf16[128,1024]{1,0:T(8,128)(2,1)S(1)} %slice.151), channel_id=1, source_target_pairs={{0,1},{1,2},{2,3},{4,5},{5,6},{6,7},{8,9},{9,10},{10,11},{12,13},{... | collective-permute-start | bytes 786440 | tf_op jit(solution)/shard_map/ppermute | solution.py:1380
  95.9 19.8 %collective-permute-start.9 = (bf16[128,1024]{1,0:T(8,128)(2,1)S(1)}, bf16[128,1024]{1,0:T(8,128)(2,1)S(1)}, u32[]{:S(2)}, u32[]{:S(2)}) collective-permute-start(bf16[128,1024]{1,0:T(8,128)(2,1)S(1)} %slice.151), channel_id=1, source_target_pairs={{0,2},{1,3},{4,6},{5,7},{8,10},{9,11},{12,14},{13,15},{16,18},{17,... | collective-permute-start | bytes 786440 | tf_op jit(solution)/shard_map/ppermute | solution.py:1381
  109.7 18.9 %collective-permute-start.14 = (bf16[1,1,1,2,2,128,768]{6,5,4,3,2,1,0:T(8,128)(2,1)S(1)}, bf16[1,1,1,2,2,128,768]{6,5,4,3,2,1,0:T(8,128)(2,1)S(1)}, u32[]{:S(2)}, u32[]{:S(2)}) collective-permute-start(bf16[1,1,1,2,2,128,768]{6,5,4,3,2,1,0:T(8,128)(2,1)S(1)} %slice.154), channel_id=1, source_target_pairs={{0,8},{4,12},{8,0},{12,4},{16,24},{20,28},{24,16},{28,20},{1,9},{5... | collective-permute-start | bytes 2359304 | tf_op jit(solution)/shard_map/ppermute | solution.py:35
  111.3 16.3 %collective-permute-start.13 = (bf16[1,1,1,2,2,128,512]{6,5,4,3,2,1,0:T(8,128)(2,1)S(1)}, bf16[1,1,1,2,2,128,512]{6,5,4,3,2,1,0:T(8,128)(2,1)S(1)}, u32[]{:S(2)}, u32[]{:S(2)}) collective-permute-start(bf16[1,1,1,2,2,128,512]{6,5,4,3,2,1,0:T(8,128)(2,1)S(1)} %slice.155), channel_id=1, source_target_pairs={{0,16},{4,20},{8,24},{12,28},{16,0},{20,4},{24,8},{28,12},{1,17},{... | collective-permute-start | bytes 1572872 | tf_op jit(solution)/shard_map/ppermute | solution.py:35
  129.6 227.4 %all-gather.5.cloned.1.call-start = ((), (), s32[]{:S(2)}) async-start(), calls=%async_computation.3 | async-start | bytes 3932160 | tf_op jit(solution)/shard_map/all_gather | solution.py:1489
  130.5 59.7 %collective-permute-start.18 = (bf16[1,2,1,2,2,128,768]{6,5,4,3,2,1,0:T(8,128)(2,1)}, bf16[1,2,1,2,2,128,768]{6,5,4,3,2,1,0:T(8,128)(2,1)}, u32[]{:S(2)}, u32[]{:S(2)}) collective-permute-start(bf16[1,2,1,2,2,128,768]{6,5,4,3,2,1,0:T(8,128)(2,1)} %constant_dynamic-update-slice_fusion.28), channel_id=1, source_target_pairs={{0,16},{4,20},{8,24},{12,28},{16,0},{20,4},{24,8},{28,12},{1,17},{... | collective-permute-start | bytes 4718600 | tf_op jit(solution)/shard_map/ppermute | solution.py:35
  132.4 42.3 %collective-permute-start.17 = (bf16[1,1,2,2,2,128,512]{6,5,4,3,2,1,0:T(8,128)(2,1)S(1)}, bf16[1,1,2,2,2,128,512]{6,5,4,3,2,1,0:T(8,128)(2,1)}, u32[]{:S(2)}, u32[]{:S(2)}) collective-permute-start(bf16[1,1,2,2,2,128,512]{6,5,4,3,2,1,0:T(8,128)(2,1)S(1)} %constant_dynamic-update-slice_fusion.26), channel_id=1, source_target_pairs={{0,8},{4,12},{8,0},{12,4},{16,24},{20,28},{24,16},{28,20},{1,9},{5... | collective-permute-start | bytes 3145736 | tf_op jit(solution)/shard_map/ppermute | solution.py:35
  133.6 27.0 %collective-permute-start.16 = (bf16[256,1024]{1,0:T(8,128)(2,1)}, bf16[256,1024]{1,0:T(8,128)(2,1)}, u32[]{:S(2)}, u32[]{:S(2)}) collective-permute-start(bf16[256,1024]{1,0:T(8,128)(2,1)} %reorder.5), channel_id=1, source_target_pairs={{0,2},{1,3},{2,0},{3,1},{4,6},{5,7},{6,4},{7,5},{8,10},{9,11},{10,... | collective-permute-start | bytes 1572872 | tf_op jit(solution)/shard_map/ppermute | solution.py:35
  191.7 28.2 %collective-permute-start.21 = (bf16[1,2,2,2,2,128,768]{6,5,4,3,2,1,0:T(8,128)(2,1)S(1)}, bf16[1,2,2,2,2,128,768]{6,5,4,3,2,1,0:T(8,128)(2,1)}, u32[]{:S(2)}, u32[]{:S(2)}) collective-permute-start(bf16[1,2,2,2,2,128,768]{6,5,4,3,2,1,0:T(8,128)(2,1)S(1)} %constant_dynamic-update-slice_fusion.34), channel_id=1, source_target_pairs={{0,4},{4,0},{8,12},{12,8},{16,20},{20,16},{24,28},{28,24},{1,5},{5... | collective-permute-start | bytes 9437192 | tf_op jit(solution)/shard_map/ppermute | solution.py:35
  191.8 11.6 %collective-permute-start.19 = (bf16[1,2,2,2,2,128,512]{6,5,4,3,2,1,0:T(8,128)(2,1)}, bf16[1,2,2,2,2,128,512]{6,5,4,3,2,1,0:T(8,128)(2,1)}, u32[]{:S(2)}, u32[]{:S(2)}) collective-permute-start(bf16[1,2,2,2,2,128,512]{6,5,4,3,2,1,0:T(8,128)(2,1)} %constant_dynamic-update-slice_fusion.32), channel_id=1, source_target_pairs={{0,4},{4,0},{8,12},{12,8},{16,20},{20,16},{24,28},{28,24},{1,5},{5... | collective-permute-start | bytes 6291464 | tf_op jit(solution)/shard_map/ppermute | solution.py:35
  193.1 25.5 %collective-permute-start.20 = (bf16[512,1024]{1,0:T(8,128)(2,1)}, bf16[512,1024]{1,0:T(8,128)(2,1)}, u32[]{:S(2)}, u32[]{:S(2)}) collective-permute-start(bf16[512,1024]{1,0:T(8,128)(2,1)} %constant_dynamic-update-slice_fusion.30), channel_id=1, source_target_pairs={{0,1},{1,0},{2,3},{3,2},{4,5},{5,4},{6,7},{7,6},{8,9},{9,8},{10,11... | collective-permute-start | bytes 3145736 | tf_op jit(solution)/shard_map/ppermute | solution.py:35
  290.9 8.3 %collective-permute-start.23 = (bf16[4,4,128,1024]{3,2,1,0:T(8,128)(2,1)}, bf16[4,4,128,1024]{3,2,1,0:T(8,128)(2,1)}, u32[]{:S(2)}, u32[]{:S(2)}) collective-permute-start(bf16[4,4,128,1024]{3,2,1,0:T(8,128)(2,1)} %up_grad_send.1), channel_id=1, source_target_pairs={{0,4},{4,0},{8,12},{12,8},{16,20},{20,16},{24,28},{28,24},{1,5},{5... | collective-permute-start | bytes 12582920 | tf_op jit(solution)/shard_map/ppermute | solution.py:35
  291.4 144.0 %reduce-scatter.3.cloned.1.call-start = ((), (), s32[]{:S(2)}) async-start(), calls=%async_computation.4 | async-start | bytes 2621440 | tf_op jit(solution)/shard_map/reduce_scatter | solution.py:1518
  306.5 50.5 %collective-permute-start.25 = (bf16[2,4,128,1024]{3,2,1,0:T(8,128)(2,1)}, bf16[2,4,128,1024]{3,2,1,0:T(8,128)(2,1)S(1)}, u32[]{:S(2)}, u32[]{:S(2)}) collective-permute-start(bf16[2,4,128,1024]{3,2,1,0:T(8,128)(2,1)} %get-tuple-element.319), channel_id=1, source_target_pairs={{0,16},{4,20},{8,24},{12,28},{16,0},{20,4},{24,8},{28,12},{1,17},{... | collective-permute-start | bytes 6291464 | tf_op jit(solution)/shard_map/ppermute | solution.py:35
  308.4 48.6 %collective-permute-start.24 = (bf16[2,4,128,1024]{3,2,1,0:T(8,128)(2,1)}, bf16[2,4,128,1024]{3,2,1,0:T(8,128)(2,1)}, u32[]{:S(2)}, u32[]{:S(2)}) collective-permute-start(bf16[2,4,128,1024]{3,2,1,0:T(8,128)(2,1)} %get-tuple-element.317), channel_id=1, source_target_pairs={{0,8},{4,12},{8,0},{12,4},{16,24},{20,28},{24,16},{28,20},{1,9},{5... | collective-permute-start | bytes 6291464 | tf_op jit(solution)/shard_map/ppermute | solution.py:35
  383.9 11.2 %collective-permute-start.26 = (bf16[4,4,128,1280]{3,2,1,0:T(8,128)(2,1)}, bf16[4,4,128,1280]{3,2,1,0:T(8,128)(2,1)}, u32[]{:S(2)}, u32[]{:S(2)}) collective-permute-start(bf16[4,4,128,1280]{3,2,1,0:T(8,128)(2,1)} %cross_grad_send.1), channel_id=1, source_target_pairs={{0,4},{4,0},{8,12},{12,8},{16,20},{20,16},{24,28},{28,24},{1,5},{5... | collective-permute-start | bytes 15728648 | tf_op jit(solution)/shard_map/ppermute | solution.py:35
  383.9 104.7 %reduce-scatter.5.cloned.1.call-start = ((), (), s32[]{:S(2)}) async-start(), calls=%async_computation.5 | async-start | bytes 2621440 | tf_op jit(solution)/shard_map/reduce_scatter | solution.py:206
  391.6 14.0 %collective-permute-start.27 = (bf16[4,4,128,896]{3,2,1,0:T(8,128)(2,1)}, bf16[4,4,128,896]{3,2,1,0:T(8,128)(2,1)S(1)}, u32[]{:S(2)}, u32[]{:S(2)}) collective-permute-start(bf16[4,4,128,896]{3,2,1,0:T(8,128)(2,1)} %self_grad_send.1), channel_id=1, source_target_pairs={{0,4},{4,0},{8,12},{12,8},{16,20},{20,16},{24,28},{28,24},{1,5},{5... | collective-permute-start | bytes 11010056 | tf_op jit(solution)/shard_map/ppermute | solution.py:35
  392.1 25.1 %collective-permute-start.29 = (bf16[4,128,1024]{2,1,0:T(8,128)(2,1)S(1)}, bf16[4,128,1024]{2,1,0:T(8,128)(2,1)S(1)}, u32[]{:S(2)}, u32[]{:S(2)}) collective-permute-start(bf16[4,128,1024]{2,1,0:T(8,128)(2,1)S(1)} %copy-done.52), channel_id=1, source_target_pairs={{0,8},{4,12},{8,0},{12,4},{16,24},{20,28},{24,16},{28,20},{1,9},{5... | collective-permute-start | bytes 3145736 | tf_op jit(solution)/shard_map/ppermute | solution.py:35
  393.6 24.9 %collective-permute-start.28 = (bf16[4,128,1024]{2,1,0:T(8,128)(2,1)S(1)}, bf16[4,128,1024]{2,1,0:T(8,128)(2,1)S(1)}, u32[]{:S(2)}, u32[]{:S(2)}) collective-permute-start(bf16[4,128,1024]{2,1,0:T(8,128)(2,1)S(1)} %copy-done.51), channel_id=1, source_target_pairs={{0,16},{4,20},{8,24},{12,28},{16,0},{20,4},{24,8},{28,12},{1,17},{... | collective-permute-start | bytes 3145736 | tf_op jit(solution)/shard_map/ppermute | solution.py:35
  427.3 33.3 %collective-permute-start.30 = (bf16[2,4,128,640]{3,2,1,0:T(8,128)(2,1)}, bf16[2,4,128,640]{3,2,1,0:T(8,128)(2,1)S(1)}, u32[]{:S(2)}, u32[]{:S(2)}) collective-permute-start(bf16[2,4,128,640]{3,2,1,0:T(8,128)(2,1)} %get-tuple-element.353), channel_id=1, source_target_pairs={{0,8},{4,12},{8,0},{12,4},{16,24},{20,28},{24,16},{28,20},{1,9},{5... | collective-permute-start | bytes 3932168 | tf_op jit(solution)/shard_map/ppermute | solution.py:35
  428.6 31.9 %collective-permute-start.31 = (bf16[2,4,128,640]{3,2,1,0:T(8,128)(2,1)}, bf16[2,4,128,640]{3,2,1,0:T(8,128)(2,1)S(1)}, u32[]{:S(2)}, u32[]{:S(2)}) collective-permute-start(bf16[2,4,128,640]{3,2,1,0:T(8,128)(2,1)} %get-tuple-element.372), channel_id=1, source_target_pairs={{0,16},{4,20},{8,24},{12,28},{16,0},{20,4},{24,8},{28,12},{1,17},{... | collective-permute-start | bytes 3932168 | tf_op jit(solution)/shard_map/ppermute | solution.py:35
  433.4 48.5 %collective-permute-start.32 = (bf16[2,4,128,512]{3,2,1,0:T(8,128)(2,1)}, bf16[2,4,128,512]{3,2,1,0:T(8,128)(2,1)}, u32[]{:S(2)}, u32[]{:S(2)}) collective-permute-start(bf16[2,4,128,512]{3,2,1,0:T(8,128)(2,1)} %get-tuple-element.355), channel_id=1, source_target_pairs={{0,8},{4,12},{8,0},{12,4},{16,24},{20,28},{24,16},{28,20},{1,9},{5... | collective-permute-start | bytes 3145736 | tf_op jit(solution)/shard_map/ppermute | solution.py:35
  435.5 41.9 %collective-permute-start.33 = (bf16[2,4,128,384]{3,2,1,0:T(8,128)(2,1)}, bf16[2,4,128,384]{3,2,1,0:T(8,128)(2,1)S(1)}, u32[]{:S(2)}, u32[]{:S(2)}) collective-permute-start(bf16[2,4,128,384]{3,2,1,0:T(8,128)(2,1)} %get-tuple-element.382), channel_id=1, source_target_pairs={{0,16},{4,20},{8,24},{12,28},{16,0},{20,4},{24,8},{28,12},{1,17},{... | collective-permute-start | bytes 2359304 | tf_op jit(solution)/shard_map/ppermute | solution.py:35
  448.0 38.5 %collective-permute-start.34 = (bf16[128,1024]{1,0:T(8,128)(2,1)}, bf16[128,1024]{1,0:T(8,128)(2,1)S(1)}, u32[]{:S(2)}, u32[]{:S(2)}) collective-permute-start(bf16[128,1024]{1,0:T(8,128)(2,1)} %get-tuple-element.390), channel_id=1, source_target_pairs={{1,0},{2,1},{3,2},{5,4},{6,5},{7,6},{9,8},{10,9},{11,10},{13,12},{... | collective-permute-start | bytes 786440 | tf_op jit(solution)/shard_map/ppermute | solution.py:1553
  466.3 30.3 %collective-permute-start.37 = (bf16[4,128,640]{2,1,0:T(8,128)(2,1)}, bf16[4,128,640]{2,1,0:T(8,128)(2,1)S(1)}, u32[]{:S(2)}, u32[]{:S(2)}) collective-permute-start(bf16[4,128,640]{2,1,0:T(8,128)(2,1)} %get-tuple-element.376), channel_id=1, source_target_pairs={{0,8},{4,12},{8,0},{12,4},{16,24},{20,28},{24,16},{28,20},{1,9},{5... | collective-permute-start | bytes 1966088 | tf_op jit(solution)/shard_map/ppermute | solution.py:35
  467.0 29.6 %collective-permute-start.36 = (bf16[4,128,640]{2,1,0:T(8,128)(2,1)}, bf16[4,128,640]{2,1,0:T(8,128)(2,1)S(1)}, u32[]{:S(2)}, u32[]{:S(2)}) collective-permute-start(bf16[4,128,640]{2,1,0:T(8,128)(2,1)} %get-tuple-element.374), channel_id=1, source_target_pairs={{0,16},{4,20},{8,24},{12,28},{16,0},{20,4},{24,8},{28,12},{1,17},{... | collective-permute-start | bytes 1966088 | tf_op jit(solution)/shard_map/ppermute | solution.py:35
  477.4 12.9 %collective-permute-start.35 = (bf16[128,1024]{1,0:T(8,128)(2,1)}, bf16[128,1024]{1,0:T(8,128)(2,1)}, u32[]{:S(2)}, u32[]{:S(2)}) collective-permute-start(bf16[128,1024]{1,0:T(8,128)(2,1)} %get-tuple-element.391), channel_id=1, source_target_pairs={{2,0},{3,1},{6,4},{7,5},{10,8},{11,9},{14,12},{15,13},{18,16},{19,... | collective-permute-start | bytes 786440 | tf_op jit(solution)/shard_map/ppermute | solution.py:1552
  485.2 17.1 %collective-permute-start.39 = (bf16[4,128,384]{2,1,0:T(8,128)(2,1)}, bf16[4,128,384]{2,1,0:T(8,128)(2,1)S(1)}, u32[]{:S(2)}, u32[]{:S(2)}) collective-permute-start(bf16[4,128,384]{2,1,0:T(8,128)(2,1)} %get-tuple-element.386), channel_id=1, source_target_pairs={{0,8},{4,12},{8,0},{12,4},{16,24},{20,28},{24,16},{28,20},{1,9},{5... | collective-permute-start | bytes 1179656 | tf_op jit(solution)/shard_map/ppermute | solution.py:35
  487.2 15.2 %collective-permute-start.38 = (bf16[4,128,512]{2,1,0:T(8,128)(2,1)}, bf16[4,128,512]{2,1,0:T(8,128)(2,1)S(1)}, u32[]{:S(2)}, u32[]{:S(2)}) collective-permute-start(bf16[4,128,512]{2,1,0:T(8,128)(2,1)} %get-tuple-element.385), channel_id=1, source_target_pairs={{0,16},{4,20},{8,24},{12,28},{16,0},{20,4},{24,8},{28,12},{1,17},{... | collective-permute-start | bytes 1572872 | tf_op jit(solution)/shard_map/ppermute | solution.py:35
  501.2 18.5 %collective-permute-start.42 = (bf16[2,128,1280]{2,1,0:T(8,128)(2,1)}, bf16[2,128,1280]{2,1,0:T(8,128)(2,1)S(1)}, u32[]{:S(2)}, u32[]{:S(2)}) collective-permute-start(bf16[2,128,1280]{2,1,0:T(8,128)(2,1)} %get-tuple-element.396), channel_id=1, source_target_pairs={{0,1},{1,0},{2,3},{3,2},{4,5},{5,4},{6,7},{7,6},{8,9},{9,8},{10,11... | collective-permute-start | bytes 1966088 | tf_op jit(solution)/shard_map/ppermute | solution.py:35
  506.3 21.0 %collective-permute-start.44 = (bf16[2,128,896]{2,1,0:T(8,128)(2,1)}, bf16[2,128,896]{2,1,0:T(8,128)(2,1)S(1)}, u32[]{:S(2)}, u32[]{:S(2)}) collective-permute-start(bf16[2,128,896]{2,1,0:T(8,128)(2,1)} %get-tuple-element.402), channel_id=1, source_target_pairs={{0,1},{1,0},{2,3},{3,2},{4,5},{5,4},{6,7},{7,6},{8,9},{9,8},{10,11... | collective-permute-start | bytes 1376264 | tf_op jit(solution)/shard_map/ppermute | solution.py:35
  514.1 8.7 %collective-permute-start.43 = (f32[17920]{0:T(1024)S(1)}, f32[17920]{0:T(1024)S(1)}, u32[]{:S(2)}, u32[]{:S(2)}) collective-permute-start(f32[17920]{0:T(1024)S(1)} %add.88), channel_id=1, source_target_pairs={{0,16},{4,20},{8,24},{12,28},{16,0},{20,4},{24,8},{28,12},{1,17},{... | collective-permute-start | bytes 215048 | tf_op jit(solution)/shard_map/ppermute | solution.py:35
  530.1 16.8 %collective-permute-start.46 = (f32[17920]{0:T(1024)S(1)}, f32[17920]{0:T(1024)S(1)}, u32[]{:S(2)}, u32[]{:S(2)}) collective-permute-start(f32[17920]{0:T(1024)S(1)} %add.90), channel_id=1, source_target_pairs={{0,2},{1,3},{2,0},{3,1},{4,6},{5,7},{6,4},{7,5},{8,10},{9,11},{10,... | collective-permute-start | bytes 215048 | tf_op jit(solution)/shard_map/ppermute | solution.py:35
  531.2 22.7 %collective-permute-start.47 = (bf16[1,128,1280]{2,1,0:T(8,128)(2,1)S(1)}, bf16[1,128,1280]{2,1,0:T(8,128)(2,1)S(1)}, u32[]{:S(2)}, u32[]{:S(2)}) collective-permute-start(bf16[1,128,1280]{2,1,0:T(8,128)(2,1)S(1)} %copy-done.53), channel_id=1, source_target_pairs={{0,2},{1,3},{2,0},{3,1},{4,6},{5,7},{6,4},{7,5},{8,10},{9,11},{10,... | collective-permute-start | bytes 983048 | tf_op jit(solution)/shard_map/ppermute | solution.py:35
  534.2 24.2 %collective-permute-start.48 = (bf16[1,128,896]{2,1,0:T(8,128)(2,1)S(1)}, bf16[1,128,896]{2,1,0:T(8,128)(2,1)S(1)}, u32[]{:S(2)}, u32[]{:S(2)}) collective-permute-start(bf16[1,128,896]{2,1,0:T(8,128)(2,1)S(1)} %copy-done.54), channel_id=1, source_target_pairs={{0,2},{1,3},{2,0},{3,1},{4,6},{5,7},{6,4},{7,5},{8,10},{9,11},{10,... | collective-permute-start | bytes 688136 | tf_op jit(solution)/shard_map/ppermute | solution.py:35
  (61 other events, 334.0 us)
Sparse Core Ops, SparseCore 0:
  129.7 114.5 all-gather.2
  291.5 65.3 all-gather.4
  384.1 43.2 reduce-scatter.2
  430.2 48.7 reduce-scatter.4

commit v6 on v5

--- a/solution.py
+++ b/solution.py
@@ -568,7 +568,7 @@
                 second_sums_ref,
             )
 
-        @pl.when(step == 2 * groups)
+        @pl.when(step == 2 * groups - 1)
         def _():
             low = second_low_ref[...]
             for j in range(groups):
@@ -591,7 +591,7 @@
         body,
         grid_spec=pltpu.PrefetchScalarGridSpec(
             num_scalar_prefetch=1,
-            grid=(2 * groups + 1,),
+            grid=(2 * groups,),
             in_specs=[
                 held((rows, features)),
                 held((rows, features)),
@@ -714,9 +714,9 @@
         def _():
             acc_ref[...] = jnp.zeros_like(acc_ref)
 
-        add_rows(acc_ref, left_ref[...], piece_refs)
-
-        @pl.when(step == groups - 1)
+        add_paired_rows(acc_ref, left_ref, piece_refs, cols)
+
+        @pl.when(step == groups // 2 - 1)
         def _():
             for k in range(groups):
                 start = pl.multiple_of(order_ref[k] * span, span)
@@ -727,11 +727,11 @@
         body,
         grid_spec=pltpu.PrefetchScalarGridSpec(
             num_scalar_prefetch=1,
-            grid=(groups,),
-            in_specs=[pl.BlockSpec((rows, cols), lambda j, order: (0, j))]
+            grid=(groups // 2,),
+            in_specs=[pl.BlockSpec((rows, 2 * cols), lambda j, order: (0, j))]
             + [
                 pl.BlockSpec(
-                    (piece_count, 1, blk, cols), lambda j, order: (0, j, 0, first_col // cols)
+                    (piece_count, 2, blk, cols), lambda j, order: (0, j, 0, first_col // cols)
                 )
                 for _ in pieces
             ],
@@ -764,12 +764,14 @@
             acc_ref[halo:] = first_ref[...]
 
         own_acc = acc_ref.at[halo:]
-        add_rows(own_acc, query_ref[...], parts[0])
-        add_rows(acc_ref, kv_ref[:, 0:width], parts[1])
-        add_rows(acc_ref, kv_ref[:, width : 2 * width], parts[2])
-        add_rows(own_acc, rel_ref[...], parts[3])
-
-        @pl.when(step == groups - 1)
+        add_paired_rows(own_acc, query_ref, parts[0], width)
+        keys = jnp.concatenate([kv_ref[:, 0:width], kv_ref[:, 2 * width : 3 * width]], 1)
+        add_paired_rows(acc_ref, keys, parts[1], width)
+        values = jnp.concatenate([kv_ref[:, width : 2 * width], kv_ref[:, 3 * width :]], 1)
+        add_paired_rows(acc_ref, values, parts[2], width)
+        add_paired_rows(own_acc, rel_ref, parts[3], rel_width)
+
+        @pl.when(step == groups // 2 - 1)
         def _():
             two_ref[...] = acc_ref[0 : halo // 2].astype(BF)
             one_ref[...] = acc_ref[halo // 2 : halo].astype(BF)
@@ -777,16 +779,16 @@
 
     return pl.pallas_call(
         body,
-        grid=(groups,),
+        grid=(groups // 2,),
         in_specs=[
-            pl.BlockSpec((rows, width), lambda j: (0, j)),
-            pl.BlockSpec((long_rows, 2 * width), lambda j: (0, j)),
-            pl.BlockSpec((rows, rel_width), lambda j: (0, j)),
+            pl.BlockSpec((rows, 2 * width), lambda j: (0, j)),
+            pl.BlockSpec((long_rows, 4 * width), lambda j: (0, j)),
+            pl.BlockSpec((rows, 2 * rel_width), lambda j: (0, j)),
         ]
-        + piece_specs(pieces, width, 0)
-        + piece_specs(pieces, width, 1)
-        + piece_specs(others, width, 0)
-        + piece_specs(others, rel_width, width // rel_width)
+        + paired_specs(pieces, width, 0)
+        + paired_specs(pieces, width, 1)
+        + paired_specs(others, width, 0)
+        + paired_specs(others, rel_width, width // rel_width)
         + [whole((rows, features))],
         out_specs=[whole((halo // 2, features))] * 2 + [whole((rows, features))],
         out_shape=[

time: 575 us -> 574 us (level)
  no operation moved by 1% of the time
where the time goes in v6:
time: 574 us; the launch traced here: 567 us
  Pallas kernels  271 us (47%)
  waiting for transfers between devices  144 us (25%)
  local copies, waits for them, and re-layouts  65.9 us (11%)
  starting transfers between devices  58.1 us (10%)
  between operations  15 us (3%)
  other arithmetic  13.1 us (2%)
    ppermute x45, waiting for transfers between devices, swap(): return lax.ppermute(array_in, axis, [(i, i ^ bit) for i in range(count)])  139 us
    pallas_call x8, Pallas kernels, weight_products(): pl.pallas_call(body, grid_spec=pltpu.PrefetchScalarGridSpec(num_scalar_pr...  60.3 us
    ppermute x45, starting transfers between devices, swap(): return lax.ppermute(array_in, axis, [(i, i ^ bit) for i in range(count)])  50 us
    unnamed x152, local copies, waits for them, and re-layouts  30.8 us
    pallas_call x6, Pallas kernels, project(): pl.pallas_call(body, grid=grid, in_specs=[whole((rows, features))] + weig...  30.2 us
    pallas_call x1, Pallas kernels, feed_forward(): pl.pallas_call(body, grid_spec=pltpu.PrefetchScalarGridSpec(num_scalar_pr...  29.4 us
    pallas_call x8, Pallas kernels, add_blocks(): pl.pallas_call(body, grid=(rows // chunk,), in_specs=[spec(array.shape[0]...  27.1 us
    pallas_call x1, Pallas kernels, cross_attention_back(): pl.pallas_call(body, grid=(groups,), in_specs=[pl.BlockSpec((rows, 256),...  17.4 us
  transfers between devices with their start and end apart: 53, of which 26 were waited for; matrix products, arithmetic and copies ran while one was open for 10% of the time, Pallas kernels for 37%

profile of v6, /device:TPU:0, one launch (start us, length us, event | category | flops | bytes accessed | tf_op | source)
XLA Modules:
  0.0 567.4 jit_solution(13450094144440976054)
XLA Ops:
  9.4 4.1 collective-permute-start
  24.7 3.6 reorder.7.grad_ref
  33.1 16.3 %collective-permute-done.1 = bf16[1,1,1,2,1,128,896]{6,5,4,3,2,1,0:T(8,128)(2,1)} collective-permute-done((bf16[1,1,1,2,1,128,896]{6,5,4,3,2,1,0:T(8,128)(2,1)S(1)}, bf16[1,1,1,2,1,128,896]{6,5,4,3,2,1,0:T(8,128)(2,1)}, u32[]{:S(2)}, u32[]{:S(2)}) %collective-permute-start.1) | collective-permute-done | bytes 458784 | tf_op jit(solution)/shard_map/ppermute | solution.py:35
  52.2 4.8 collective-permute-done.2
  58.8 4.2 collective-permute-done.3
  64.9 4.3 collective-permute-done.4
  72.0 15.5 %collective-permute-done.5 = bf16[1,1,1,2,1,128,2048]{6,5,4,3,2,1,0:T(8,128)(2,1)S(1)} collective-permute-done((bf16[1,1,1,2,1,128,2048]{6,5,4,3,2,1,0:T(8,128)(2,1)S(1)}, bf16[1,1,1,2,1,128,2048]{6,5,4,3,2,1,0:T(8,128)(2,1)S(1)}, u32[]{:S(2)}, u32[]{:S(2)}) %collective-permute-start.5) | collective-permute-done | bytes 1048608 | tf_op jit(solution)/shard_map/ppermute | solution.py:35
  99.5 8.9 %collective-permute-done.11 = bf16[1,1,1,2,1,128,1280]{6,5,4,3,2,1,0:T(8,128)(2,1)} collective-permute-done((bf16[1,1,1,2,1,128,1280]{6,5,4,3,2,1,0:T(8,128)(2,1)}, bf16[1,1,1,2,1,128,1280]{6,5,4,3,2,1,0:T(8,128)(2,1)}, u32[]{:S(2)}, u32[]{:S(2)}) %collective-permute-start.11) | collective-permute-done | bytes 655392 | tf_op jit(solution)/shard_map/ppermute | solution.py:35
  120.0 4.3 self_v.1.v_ref
  124.3 3.3 self_rel.1.rel_ref
  133.6 3.4 collective-permute-start.16
  138.3 7.4 %self_qk.1.q_ref.k_ref = bf16[640,2048]{1,0:T(8,128)(2,1)} custom-call(bf16[640,1024]{1,0:T(8,128)(2,1)} %stack_rows.1.x_ref.refs_1_, bf16[4,4,128,512]{3,2,1,0:T(8,128)(2,1)} %bitcast.161, bf16[4,4,128,512]{3,2,1,0:T(8,128)(2,1)} %bitcast.21.refs_1_.refs_3_, f32[2,2048]{1,0:T(2,128)} %pad_maximum_fusion.4.refs_2_), custom_call_target="tpu_custom_call" | custom-call | tf_op jit(solution)/shard_map/self_qk/pallas_call | solution.py:343
  146.5 14.0 %collective-permute-done.16 = bf16[256,1024]{1,0:T(8,128)(2,1)} collective-permute-done((bf16[256,1024]{1,0:T(8,128)(2,1)}, bf16[256,1024]{1,0:T(8,128)(2,1)}, u32[]{:S(2)}, u32[]{:S(2)}) %collective-permute-start.16) | collective-permute-done | bytes 524320 | tf_op jit(solution)/shard_map/ppermute | solution.py:35
  162.5 11.1 %self_attention.1 = (bf16[384,1024]{1,0:T(8,128)(2,1)}, bf16[16,384,384]{2,1,0:T(8,128)(2,1)}, f32[384,512]{1,0:T(8,128)}) custom-call(bf16[640,2048]{1,0:T(8,128)(2,1)} %self_qk.1.q_ref.k_ref, bf16[640,2048]{1,0:T(8,128)(2,1)} %self_qk.1.q_ref.k_ref, bf16[640,1024]{1,0:T(8,128)(2,1)} %self_v.1.v_ref, f32[384,512]{1,0:T(8,128)} %self_rel.1.rel_ref, ...), custom_call_target="tpu_custom_call" | custom-call | tf_op jit(solution)/shard_map/self_attention/pallas_call | solution.py:972
  178.5 11.7 %collective-permute-done.18 = bf16[1,2,1,2,2,128,768]{6,5,4,3,2,1,0:T(8,128)(2,1)} collective-permute-done((bf16[1,2,1,2,2,128,768]{6,5,4,3,2,1,0:T(8,128)(2,1)}, bf16[1,2,1,2,2,128,768]{6,5,4,3,2,1,0:T(8,128)(2,1)}, u32[]{:S(2)}, u32[]{:S(2)}) %collective-permute-start.18) | collective-permute-done | bytes 1572896 | tf_op jit(solution)/shard_map/ppermute | solution.py:35
  198.4 5.0 collective-permute-done.19
  203.4 5.6 self_out.1
  209.1 3.4 cross_q.1.q_ref
  213.8 4.8 collective-permute-done.20
  221.2 8.4 %cross_kv.1.k_ref.v_ref = bf16[1024,2048]{1,0:T(8,128)(2,1)} custom-call(bf16[1024,1024]{1,0:T(8,128)(2,1)} %copy-done.4, bf16[4,4,128,768]{3,2,1,0:T(8,128)(2,1)} %bitcast.153, bf16[4,4,128,768]{3,2,1,0:T(8,128)(2,1)} %bitcast.29.refs_1_, f32[2,2048]{1,0:T(2,128)} %stack.26.refs_2_), custom_call_target="tpu_custom_call" | custom-call | tf_op jit(solution)/shard_map/cross_kv/pallas_call | solution.py:343
  229.7 13.5 %cross_attention.1 = (bf16[384,1024]{1,0:T(8,128)(2,1)}, bf16[16,384,1024]{2,1,0:T(8,128)(2,1)}, f32[384,512]{1,0:T(8,128)}) custom-call(bf16[384,1024]{1,0:T(8,128)(2,1)} %cross_q.1.q_ref, bf16[1024,2048]{1,0:T(8,128)(2,1)} %cross_kv.1.k_ref.v_ref, bf16[1024,2048]{1,0:T(8,128)(2,1)} %cross_kv.1.k_ref.v_ref), custom_call_target="tpu_custom_call" | custom-call | tf_op jit(solution)/shard_map/cross_attention/pallas_call | solution.py:1140
  243.2 5.9 %cross_out.1 = (f32[384,1024]{1,0:T(8,128)}, bf16[384,1024]{1,0:T(8,128)(2,1)}, f32[384,1024]{1,0:T(8,128)}, f32[384,1]{1,0:T(8,128)}) custom-call(bf16[384,1024]{1,0:T(8,128)(2,1)} %get-tuple-element.297.left_ref.refs_6_, bf16[4,4,128,768]{3,2,1,0:T(8,128)(2,1)} %bitcast.154, bf16[4,4,128,768]{3,2,1,0:T(8,128)(2,1)} %bitcast.29.refs_1_, ...), custom_call_target="tpu_custom_call" | custom-call | tf_op jit(solution)/shard_map/cross_out/pallas_call | solution.py:431
  249.0 29.4 %feed_forward.1 = (bf16[384,4096]{1,0:T(8,128)(2,1)}, bf16[384,1024]{1,0:T(8,128)(2,1)}, bf16[384,1024]{1,0:T(8,128)(2,1)}, f32[3,1024]{1,0:T(4,128)}, bf16[384,...) custom-call(s32[12]{0:T(128)} %pad_add_fusion.order_ref, ...), custom_call_target="tpu_custom_call" | custom-call | tf_op jit(solution)/shard_map/feed_forward/pallas_call | solution.py:590
  278.5 6.1 %down_grad_send.1 = bf16[4,4,128,1024]{3,2,1,0:T(8,128)(2,1)} custom-call(s32[4]{0:T(128)} %copy-done.40, bf16[384,1024]{1,0:T(8,128)(2,1)} %get-tuple-element.316.refs_0_, bf16[384,4096]{1,0:T(8,128)(2,1)} %get-tuple-element.313.refs_1_), custom_call_target="tpu_custom_call" | custom-call | tf_op jit(solution)/shard_map/down_grad_send/pallas_call | solution.py:858
  284.6 6.1 %up_grad_send.1 = bf16[4,4,128,1024]{3,2,1,0:T(8,128)(2,1)} custom-call(s32[4]{0:T(128)} %copy-done.40, bf16[384,1024]{1,0:T(8,128)(2,1)} %get-tuple-element.318.low_ref.refs_0_, bf16[384,4096]{1,0:T(8,128)(2,1)} %get-tuple-element.315.refs_1_), custom_call_target="tpu_custom_call" | custom-call | tf_op jit(solution)/shard_map/up_grad_send/pallas_call | solution.py:858
  292.1 7.0 %down_grad_keep.1 = (bf16[2,4,128,1024]{3,2,1,0:T(8,128)(2,1)}, bf16[2,4,128,1024]{3,2,1,0:T(8,128)(2,1)}) custom-call(s32[4]{0:T(128)} %copy-done.40, bf16[384,1024]{1,0:T(8,128)(2,1)} %get-tuple-element.316.refs_0_, bf16[384,4096]{1,0:T(8,128)(2,1)} %get-tuple-element.313.refs_1_, bf16[4,4,128,1024]{3,2,1,0:T(8,128)(2,1)} %collective-permute-done.22.refs_2_), custom_call_target="tpu_custom_call" | custom-call | tf_op jit(solution)/shard_map/down_grad_keep/pallas_call | solution.py:858
  299.0 7.3 %up_grad_keep.1 = (bf16[2,4,128,1024]{3,2,1,0:T(8,128)(2,1)}, bf16[2,4,128,1024]{3,2,1,0:T(8,128)(2,1)}) custom-call(s32[4]{0:T(128)} %copy-done.40, bf16[384,1024]{1,0:T(8,128)(2,1)} %get-tuple-element.318.low_ref.refs_0_, bf16[384,4096]{1,0:T(8,128)(2,1)} %get-tuple-element.315.refs_1_, bf16[4,4,128,1024]{3,2,1,0:T(8,128)(2,1)} %collective-permute-done.23.refs_2_), custom_call_target="tpu_custom_call" | custom-call | tf_op jit(solution)/shard_map/up_grad_keep/pallas_call | solution.py:858
  310.7 17.4 %cross_attention_back.1 = (bf16[384,1024]{1,0:T(8,128)(2,1)}, bf16[1024,2048]{1,0:T(8,128)(2,1)}, f32[2,1024]{1,0:T(2,128)}) custom-call(bf16[384,1024]{1,0:T(8,128)(2,1)} %cross_q.1.q_ref, bf16[1024,2048]{1,0:T(8,128)(2,1)} %cross_kv.1.k_ref.v_ref, bf16[1024,2048]{1,0:T(8,128)(2,1)} %cross_kv.1.k_ref.v_ref, ...), custom_call_target="tpu_custom_call" | custom-call | tf_op jit(solution)/shard_map/cross_attention_back/pallas_call | solution.py:1209
  328.1 6.0 %cross_query_back.1 = (f32[384,1024]{1,0:T(8,128)}, bf16[384,1024]{1,0:T(8,128)(2,1)}, f32[3,1024]{1,0:T(4,128)}) custom-call(bf16[384,1024]{1,0:T(8,128)(2,1)} %get-tuple-element.322.left_ref.refs_4_, bf16[4,4,128,512]{3,2,1,0:T(8,128)(2,1)} %bitcast.23.refs_0_, bf16[4,4,128,512]{3,2,1,0:T(8,128)(2,1)} %bitcast.24.refs_1_, ...), custom_call_target="tpu_custom_call" | custom-call | tf_op jit(solution)/shard_map/cross_query_back/pallas_call | solution.py:683
  334.1 3.4 self_ctx_back.1.grad_ref
  337.6 16.5 %self_attention_back.1 = (bf16[384,1024]{1,0:T(8,128)(2,1)}, bf16[640,2048]{1,0:T(8,128)(2,1)}, bf16[384,512]{1,0:T(8,128)(2,1)}, f32[2,1024]{1,0:T(2,128)}, f32[1,512]{1,0:T(1,128)}) custom-call(bf16[640,2048]{1,0:T(8,128)(2,1)} %self_qk.1.q_ref.k_ref, bf16[640,2048]{1,0:T(8,128)(2,1)} %self_qk.1.q_ref.k_ref, bf16[640,1024]{1,0:T(8,128)(2,1)} %self_v.1.v_ref, ...), custom_call_target="tpu_custom_call" | custom-call | tf_op jit(solution)/shard_map/self_attention_back/pallas_call | solution.py:1085
  358.1 6.0 %add_blocks.8 = (bf16[4,128,1024]{2,1,0:T(8,128)(2,1)}, bf16[4,128,1024]{2,1,0:T(8,128)(2,1)}, bf16[4,128,1024]{2,1,0:T(8,128)(2,1)}, bf16[4,128,1024]{2,1,0:T(8,128)(2,1)}) custom-call(bf16[8,128,1024]{2,1,0:T(8,128)(2,1)} %bitcast.171, bf16[8,128,1024]{2,1,0:T(8,128)(2,1)} %bitcast.45.refs_1_, bf16[8,128,1024]{2,1,0:T(8,128)(2,1)} %bitcast.172, ...), custom_call_target="tpu_custom_call" | custom-call | tf_op jit(solution)/shard_map/add_blocks/pallas_call | solution.py:103
  364.1 9.8 %memory_back.1 = bf16[1024,1024]{1,0:T(8,128)(2,1)} custom-call(s32[4]{0:T(128)} %broadcast_xor_fusion.1.order_ref, bf16[1024,2048]{1,0:T(8,128)(2,1)} %get-tuple-element.346.left_ref.refs_5_, bf16[4,4,128,768]{3,2,1,0:T(8,128)(2,1)} %bitcast.156, bf16[4,4,128,768]{3,2,1,0:T(8,128)(2,1)} %bitcast.29.refs_1_), custom_call_target="tpu_custom_call" | custom-call | tf_op jit(solution)/shard_map/memory_back/pallas_call | solution.py:726
  374.5 9.2 %cross_grad_send.1 = bf16[4,4,128,1280]{3,2,1,0:T(8,128)(2,1)} custom-call(s32[4]{0:T(128)} %iota.56.order_ref, bf16[384,1024]{1,0:T(8,128)(2,1)} %get-tuple-element.352.x_ref.refs_0_, bf16[1024,1024]{1,0:T(8,128)(2,1)} %copy-done.4, bf16[384,1024]{1,0:T(8,128)(2,1)} %get-tuple-element.348.refs_2_, bf16[384,1024]{1,0:T(8,128)(2,1)} %get-tuple-element.327.x_ref.refs_3_, ...), custom_call_target="tpu_custom_call" | custom-call | tf_op jit(solution)/shard_map/cross_grad_send/pallas_call | solution.py:858
  384.2 7.1 %self_grad_send.1 = bf16[4,4,128,896]{3,2,1,0:T(8,128)(2,1)} custom-call(s32[4]{0:T(128)} %iota.55.order_ref, bf16[384,1024]{1,0:T(8,128)(2,1)} %reorder.6.refs_2_.x_ref.refs_0_, bf16[640,1024]{1,0:T(8,128)(2,1)} %stack_rows.1.x_ref.refs_1_, bf16[384,1024]{1,0:T(8,128)(2,1)} %reorder.6.refs_2_.x_ref.refs_0_, ...), custom_call_target="tpu_custom_call" | custom-call | tf_op jit(solution)/shard_map/self_grad_send/pallas_call | solution.py:858
  395.3 10.0 %cross_grad_keep.1 = (bf16[2,4,128,640]{3,2,1,0:T(8,128)(2,1)}, bf16[2,4,128,640]{3,2,1,0:T(8,128)(2,1)}, bf16[2,4,128,640]{3,2,1,0:T(8,128)(2,1)}, bf16[2,4,128,640]{3,2,1,0:T(8,128)(2,1)}) custom-call(s32[4]{0:T(128)} %iota.54.order_ref, bf16[384,1024]{1,0:T(8,128)(2,1)} %get-tuple-element.352.x_ref.refs_0_, bf16[1024,1024]{1,0:T(8,128)(2,1)} %copy-done.4, ...), custom_call_target="tpu_custom_call" | custom-call | tf_op jit(solution)/shard_map/cross_grad_keep/pallas_call | solution.py:858
  407.2 7.6 %self_grad_keep.1 = (bf16[2,4,128,512]{3,2,1,0:T(8,128)(2,1)}, bf16[2,4,128,512]{3,2,1,0:T(8,128)(2,1)}, bf16[2,4,128,384]{3,2,1,0:T(8,128)(2,1)}, bf16[2,4,128,384]{3,2,1,0:T(8,128)(2,1)}) custom-call(s32[4]{0:T(128)} %iota.53.order_ref, bf16[384,1024]{1,0:T(8,128)(2,1)} %reorder.6.refs_2_.x_ref.refs_0_, bf16[640,1024]{1,0:T(8,128)(2,1)} %stack_rows.1.x_ref.refs_1_, ...), custom_call_target="tpu_custom_call" | custom-call | tf_op jit(solution)/shard_map/self_grad_keep/pallas_call | solution.py:858
  419.2 4.0 add_blocks.9
  437.9 9.6 %input_back.1 = (bf16[128,1024]{1,0:T(8,128)(2,1)}, bf16[128,1024]{1,0:T(8,128)(2,1)}, f32[384,1024]{1,0:T(8,128)}) custom-call(bf16[384,1024]{1,0:T(8,128)(2,1)} %get-tuple-element.366.refs_3_.query_ref, bf16[640,2048]{1,0:T(8,128)(2,1)} %get-tuple-element.350.refs_4_.kv_ref, bf16[384,512]{1,0:T(8,128)(2,1)} %get-tuple-element.351.refs_5_.rel_ref, ...), custom_call_target="tpu_custom_call" | custom-call | tf_op jit(solution)/shard_map/input_back/pallas_call | solution.py:780
  448.8 11.5 %collective-permute-done.31 = bf16[2,4,128,640]{3,2,1,0:T(8,128)(2,1)S(1)} collective-permute-done((bf16[2,4,128,640]{3,2,1,0:T(8,128)(2,1)}, bf16[2,4,128,640]{3,2,1,0:T(8,128)(2,1)S(1)}, u32[]{:S(2)}, u32[]{:S(2)}) %collective-permute-start.31) | collective-permute-done | bytes 1310752 | tf_op jit(solution)/shard_map/ppermute | solution.py:35
  461.7 4.2 add_blocks.10
  468.7 8.4 %collective-permute-done.33 = bf16[2,4,128,384]{3,2,1,0:T(8,128)(2,1)S(1)} collective-permute-done((bf16[2,4,128,384]{3,2,1,0:T(8,128)(2,1)}, bf16[2,4,128,384]{3,2,1,0:T(8,128)(2,1)S(1)}, u32[]{:S(2)}, u32[]{:S(2)}) %collective-permute-start.33) | collective-permute-done | bytes 786464 | tf_op jit(solution)/shard_map/ppermute | solution.py:35
  478.6 3.0 collective-permute-done.32
  481.6 3.3 add_blocks.11
  492.8 3.5 reorder.8
  515.1 4.4 copy_tracks.1
  524.0 3.1 collective-permute-done.44.refs_1_
  534.0 12.7 %collective-permute-done.46 = f32[17920]{0:T(1024)S(1)} collective-permute-done((f32[17920]{0:T(1024)S(1)}, f32[17920]{0:T(1024)S(1)}, u32[]{:S(2)}, u32[]{:S(2)}) %collective-permute-start.46) | collective-permute-done | bytes 71712 | tf_op jit(solution)/shard_map/ppermute | solution.py:35
  (378 shorter events, 172.3 us)
Async XLA Ops:
  7.2 241.9 %all-gather.3.cloned.1.call-start = ((), (), s32[]{:S(2)}) async-start(), calls=%async_computation.2 | async-start | bytes 18874368 | tf_op jit(solution)/shard_map/all_gather | solution.py:1405
  9.4 20.6 %collective-permute-start = (bf16[1,1,1,1,1,128,896]{6,5,4,3,2,1,0:T(8,128)(2,1)S(1)}, bf16[1,1,1,1,1,128,896]{6,5,4,3,2,1,0:T(8,128)(2,1)S(1)}, u32[]{:S(2)}, u32[]{:S(2)}) collective-permute-start(bf16[1,1,1,1,1,128,896]{6,5,4,3,2,1,0:T(8,128)(2,1)S(1)} %pad_maximum_fusion.1), channel_id=1, source_target_pairs={{0,2},{1,3},{2,0},{3,1},{4,6},{5,7},{6,4},{7,5},{8,10},{9,11},{10,... | collective-permute-start | bytes 688136 | tf_op jit(solution)/shard_map/ppermute | solution.py:35
  30.0 19.4 %collective-permute-start.1 = (bf16[1,1,1,2,1,128,896]{6,5,4,3,2,1,0:T(8,128)(2,1)S(1)}, bf16[1,1,1,2,1,128,896]{6,5,4,3,2,1,0:T(8,128)(2,1)}, u32[]{:S(2)}, u32[]{:S(2)}) collective-permute-start(bf16[1,1,1,2,1,128,896]{6,5,4,3,2,1,0:T(8,128)(2,1)S(1)} %constant_dynamic-update-slice_fusion), channel_id=1, source_target_pairs={{0,1},{1,0},{2,3},{3,2},{4,5},{5,4},{6,7},{7,6},{8,9},{9,8},{10,11... | collective-permute-start | bytes 1376264 | tf_op jit(solution)/shard_map/ppermute | solution.py:35
  31.7 25.3 %collective-permute-start.2 = (bf16[1,1,1,1,1,128,2048]{6,5,4,3,2,1,0:T(8,128)(2,1)S(1)}, bf16[1,1,1,1,1,128,2048]{6,5,4,3,2,1,0:T(8,128)(2,1)S(1)}, u32[]{:S(2)}, u32[]{:S(2)}) collective-permute-start(bf16[1,1,1,1,1,128,2048]{6,5,4,3,2,1,0:T(8,128)(2,1)S(1)} %fusion.9), channel_id=1, source_target_pairs={{0,2},{1,3},{2,0},{3,1},{4,6},{5,7},{6,4},{7,5},{8,10},{9,11},{10,... | collective-permute-start | bytes 1572872 | tf_op jit(solution)/shard_map/ppermute | solution.py:35
  50.6 12.5 %collective-permute-start.3 = (bf16[1,1,1,2,2,128,512]{6,5,4,3,2,1,0:T(8,128)(2,1)S(1)}, bf16[1,1,1,2,2,128,512]{6,5,4,3,2,1,0:T(8,128)(2,1)S(1)}, u32[]{:S(2)}, u32[]{:S(2)}) collective-permute-start(bf16[1,1,1,2,2,128,512]{6,5,4,3,2,1,0:T(8,128)(2,1)S(1)} %slice.153), channel_id=1, source_target_pairs={{0,8},{4,12},{8,0},{12,4},{16,24},{20,28},{24,16},{28,20},{1,9},{5... | collective-permute-start | bytes 1572872 | tf_op jit(solution)/shard_map/ppermute | solution.py:35
  57.0 30.5 %collective-permute-start.5 = (bf16[1,1,1,2,1,128,2048]{6,5,4,3,2,1,0:T(8,128)(2,1)S(1)}, bf16[1,1,1,2,1,128,2048]{6,5,4,3,2,1,0:T(8,128)(2,1)S(1)}, u32[]{:S(2)}, u32[]{:S(2)}) collective-permute-start(bf16[1,1,1,2,1,128,2048]{6,5,4,3,2,1,0:T(8,128)(2,1)S(1)} %constant_dynamic-update-slice_fusion.4), channel_id=1, source_target_pairs={{0,1},{1,0},{2,3},{3,2},{4,5},{5,4},{6,7},{7,6},{8,9},{9,8},{10,11... | collective-permute-start | bytes 3145736 | tf_op jit(solution)/shard_map/ppermute | solution.py:35
  57.1 12.1 %collective-permute-start.4 = (bf16[1,1,1,2,2,128,384]{6,5,4,3,2,1,0:T(8,128)(2,1)S(1)}, bf16[1,1,1,2,2,128,384]{6,5,4,3,2,1,0:T(8,128)(2,1)S(1)}, u32[]{:S(2)}, u32[]{:S(2)}) collective-permute-start(bf16[1,1,1,2,2,128,384]{6,5,4,3,2,1,0:T(8,128)(2,1)S(1)} %slice.152), channel_id=1, source_target_pairs={{0,16},{4,20},{8,24},{12,28},{16,0},{20,4},{24,8},{28,12},{1,17},{... | collective-permute-start | bytes 1179656 | tf_op jit(solution)/shard_map/ppermute | solution.py:35
  63.1 26.0 %collective-permute-start.6 = (bf16[1,2,1,2,2,128,512]{6,5,4,3,2,1,0:T(8,128)(2,1)S(1)}, bf16[1,2,1,2,2,128,512]{6,5,4,3,2,1,0:T(8,128)(2,1)S(1)}, u32[]{:S(2)}, u32[]{:S(2)}) collective-permute-start(bf16[1,2,1,2,2,128,512]{6,5,4,3,2,1,0:T(8,128)(2,1)S(1)} %constant_dynamic-update-slice_fusion.6), channel_id=1, source_target_pairs={{0,16},{4,20},{8,24},{12,28},{16,0},{20,4},{24,8},{28,12},{1,17},{... | collective-permute-start | bytes 3145736 | tf_op jit(solution)/shard_map/ppermute | solution.py:35
  69.4 19.8 %collective-permute-start.7 = (bf16[1,1,2,2,2,128,384]{6,5,4,3,2,1,0:T(8,128)(2,1)S(1)}, bf16[1,1,2,2,2,128,384]{6,5,4,3,2,1,0:T(8,128)(2,1)S(1)}, u32[]{:S(2)}, u32[]{:S(2)}) collective-permute-start(bf16[1,1,2,2,2,128,384]{6,5,4,3,2,1,0:T(8,128)(2,1)S(1)} %constant_dynamic-update-slice_fusion.8), channel_id=1, source_target_pairs={{0,8},{4,12},{8,0},{12,4},{16,24},{20,28},{24,16},{28,20},{1,9},{5... | collective-permute-start | bytes 2359304 | tf_op jit(solution)/shard_map/ppermute | solution.py:35
  70.9 19.5 %collective-permute-start.8 = (bf16[1,1,1,1,1,128,1280]{6,5,4,3,2,1,0:T(8,128)(2,1)S(1)}, bf16[1,1,1,1,1,128,1280]{6,5,4,3,2,1,0:T(8,128)(2,1)S(1)}, u32[]{:S(2)}, u32[]{:S(2)}) collective-permute-start(bf16[1,1,1,1,1,128,1280]{6,5,4,3,2,1,0:T(8,128)(2,1)S(1)} %maximum_bitcast_fusion), channel_id=1, source_target_pairs={{0,2},{1,3},{2,0},{3,1},{4,6},{5,7},{6,4},{7,5},{8,10},{9,11},{10,... | collective-permute-start | bytes 983048 | tf_op jit(solution)/shard_map/ppermute | solution.py:35
  91.2 17.2 %collective-permute-start.11 = (bf16[1,1,1,2,1,128,1280]{6,5,4,3,2,1,0:T(8,128)(2,1)}, bf16[1,1,1,2,1,128,1280]{6,5,4,3,2,1,0:T(8,128)(2,1)}, u32[]{:S(2)}, u32[]{:S(2)}) collective-permute-start(bf16[1,1,1,2,1,128,1280]{6,5,4,3,2,1,0:T(8,128)(2,1)} %constant_dynamic-update-slice_fusion.16), channel_id=1, source_target_pairs={{0,1},{1,0},{2,3},{3,2},{4,5},{5,4},{6,7},{7,6},{8,9},{9,8},{10,11... | collective-permute-start | bytes 1966088 | tf_op jit(solution)/shard_map/ppermute | solution.py:35
  92.9 25.9 %collective-permute-start.12 = (bf16[1,2,2,2,2,128,384]{6,5,4,3,2,1,0:T(8,128)(2,1)S(1)}, bf16[1,2,2,2,2,128,384]{6,5,4,3,2,1,0:T(8,128)(2,1)S(1)}, u32[]{:S(2)}, u32[]{:S(2)}) collective-permute-start(bf16[1,2,2,2,2,128,384]{6,5,4,3,2,1,0:T(8,128)(2,1)S(1)} %constant_dynamic-update-slice_fusion.14), channel_id=1, source_target_pairs={{0,4},{4,0},{8,12},{12,8},{16,20},{20,16},{24,28},{28,24},{1,5},{5... | collective-permute-start | bytes 4718600 | tf_op jit(solution)/shard_map/ppermute | solution.py:35
  93.6 20.5 %collective-permute-start.10 = (bf16[128,1024]{1,0:T(8,128)(2,1)S(1)}, bf16[128,1024]{1,0:T(8,128)(2,1)S(1)}, u32[]{:S(2)}, u32[]{:S(2)}) collective-permute-start(bf16[128,1024]{1,0:T(8,128)(2,1)S(1)} %slice.151), channel_id=1, source_target_pairs={{0,1},{1,2},{2,3},{4,5},{5,6},{6,7},{8,9},{9,10},{10,11},{12,13},{... | collective-permute-start | bytes 786440 | tf_op jit(solution)/shard_map/ppermute | solution.py:1382
  95.9 19.8 %collective-permute-start.9 = (bf16[128,1024]{1,0:T(8,128)(2,1)S(1)}, bf16[128,1024]{1,0:T(8,128)(2,1)S(1)}, u32[]{:S(2)}, u32[]{:S(2)}) collective-permute-start(bf16[128,1024]{1,0:T(8,128)(2,1)S(1)} %slice.151), channel_id=1, source_target_pairs={{0,2},{1,3},{4,6},{5,7},{8,10},{9,11},{12,14},{13,15},{16,18},{17,... | collective-permute-start | bytes 786440 | tf_op jit(solution)/shard_map/ppermute | solution.py:1383
  109.7 18.9 %collective-permute-start.14 = (bf16[1,1,1,2,2,128,768]{6,5,4,3,2,1,0:T(8,128)(2,1)S(1)}, bf16[1,1,1,2,2,128,768]{6,5,4,3,2,1,0:T(8,128)(2,1)S(1)}, u32[]{:S(2)}, u32[]{:S(2)}) collective-permute-start(bf16[1,1,1,2,2,128,768]{6,5,4,3,2,1,0:T(8,128)(2,1)S(1)} %slice.154), channel_id=1, source_target_pairs={{0,8},{4,12},{8,0},{12,4},{16,24},{20,28},{24,16},{28,20},{1,9},{5... | collective-permute-start | bytes 2359304 | tf_op jit(solution)/shard_map/ppermute | solution.py:35
  111.3 16.3 %collective-permute-start.13 = (bf16[1,1,1,2,2,128,512]{6,5,4,3,2,1,0:T(8,128)(2,1)S(1)}, bf16[1,1,1,2,2,128,512]{6,5,4,3,2,1,0:T(8,128)(2,1)S(1)}, u32[]{:S(2)}, u32[]{:S(2)}) collective-permute-start(bf16[1,1,1,2,2,128,512]{6,5,4,3,2,1,0:T(8,128)(2,1)S(1)} %slice.155), channel_id=1, source_target_pairs={{0,16},{4,20},{8,24},{12,28},{16,0},{20,4},{24,8},{28,12},{1,17},{... | collective-permute-start | bytes 1572872 | tf_op jit(solution)/shard_map/ppermute | solution.py:35
  129.6 227.2 %all-gather.5.cloned.1.call-start = ((), (), s32[]{:S(2)}) async-start(), calls=%async_computation.3 | async-start | bytes 3932160 | tf_op jit(solution)/shard_map/all_gather | solution.py:1491
  130.5 59.7 %collective-permute-start.18 = (bf16[1,2,1,2,2,128,768]{6,5,4,3,2,1,0:T(8,128)(2,1)}, bf16[1,2,1,2,2,128,768]{6,5,4,3,2,1,0:T(8,128)(2,1)}, u32[]{:S(2)}, u32[]{:S(2)}) collective-permute-start(bf16[1,2,1,2,2,128,768]{6,5,4,3,2,1,0:T(8,128)(2,1)} %constant_dynamic-update-slice_fusion.28), channel_id=1, source_target_pairs={{0,16},{4,20},{8,24},{12,28},{16,0},{20,4},{24,8},{28,12},{1,17},{... | collective-permute-start | bytes 4718600 | tf_op jit(solution)/shard_map/ppermute | solution.py:35
  132.4 42.3 %collective-permute-start.17 = (bf16[1,1,2,2,2,128,512]{6,5,4,3,2,1,0:T(8,128)(2,1)S(1)}, bf16[1,1,2,2,2,128,512]{6,5,4,3,2,1,0:T(8,128)(2,1)}, u32[]{:S(2)}, u32[]{:S(2)}) collective-permute-start(bf16[1,1,2,2,2,128,512]{6,5,4,3,2,1,0:T(8,128)(2,1)S(1)} %constant_dynamic-update-slice_fusion.26), channel_id=1, source_target_pairs={{0,8},{4,12},{8,0},{12,4},{16,24},{20,28},{24,16},{28,20},{1,9},{5... | collective-permute-start | bytes 3145736 | tf_op jit(solution)/shard_map/ppermute | solution.py:35
  133.6 27.0 %collective-permute-start.16 = (bf16[256,1024]{1,0:T(8,128)(2,1)}, bf16[256,1024]{1,0:T(8,128)(2,1)}, u32[]{:S(2)}, u32[]{:S(2)}) collective-permute-start(bf16[256,1024]{1,0:T(8,128)(2,1)} %reorder.5), channel_id=1, source_target_pairs={{0,2},{1,3},{2,0},{3,1},{4,6},{5,7},{6,4},{7,5},{8,10},{9,11},{10,... | collective-permute-start | bytes 1572872 | tf_op jit(solution)/shard_map/ppermute | solution.py:35
  191.7 28.2 %collective-permute-start.21 = (bf16[1,2,2,2,2,128,768]{6,5,4,3,2,1,0:T(8,128)(2,1)S(1)}, bf16[1,2,2,2,2,128,768]{6,5,4,3,2,1,0:T(8,128)(2,1)}, u32[]{:S(2)}, u32[]{:S(2)}) collective-permute-start(bf16[1,2,2,2,2,128,768]{6,5,4,3,2,1,0:T(8,128)(2,1)S(1)} %constant_dynamic-update-slice_fusion.34), channel_id=1, source_target_pairs={{0,4},{4,0},{8,12},{12,8},{16,20},{20,16},{24,28},{28,24},{1,5},{5... | collective-permute-start | bytes 9437192 | tf_op jit(solution)/shard_map/ppermute | solution.py:35
  191.8 11.6 %collective-permute-start.19 = (bf16[1,2,2,2,2,128,512]{6,5,4,3,2,1,0:T(8,128)(2,1)}, bf16[1,2,2,2,2,128,512]{6,5,4,3,2,1,0:T(8,128)(2,1)}, u32[]{:S(2)}, u32[]{:S(2)}) collective-permute-start(bf16[1,2,2,2,2,128,512]{6,5,4,3,2,1,0:T(8,128)(2,1)} %constant_dynamic-update-slice_fusion.32), channel_id=1, source_target_pairs={{0,4},{4,0},{8,12},{12,8},{16,20},{20,16},{24,28},{28,24},{1,5},{5... | collective-permute-start | bytes 6291464 | tf_op jit(solution)/shard_map/ppermute | solution.py:35
  193.1 25.5 %collective-permute-start.20 = (bf16[512,1024]{1,0:T(8,128)(2,1)}, bf16[512,1024]{1,0:T(8,128)(2,1)}, u32[]{:S(2)}, u32[]{:S(2)}) collective-permute-start(bf16[512,1024]{1,0:T(8,128)(2,1)} %constant_dynamic-update-slice_fusion.30), channel_id=1, source_target_pairs={{0,1},{1,0},{2,3},{3,2},{4,5},{5,4},{6,7},{7,6},{8,9},{9,8},{10,11... | collective-permute-start | bytes 3145736 | tf_op jit(solution)/shard_map/ppermute | solution.py:35
  290.7 8.3 %collective-permute-start.23 = (bf16[4,4,128,1024]{3,2,1,0:T(8,128)(2,1)}, bf16[4,4,128,1024]{3,2,1,0:T(8,128)(2,1)}, u32[]{:S(2)}, u32[]{:S(2)}) collective-permute-start(bf16[4,4,128,1024]{3,2,1,0:T(8,128)(2,1)} %up_grad_send.1), channel_id=1, source_target_pairs={{0,4},{4,0},{8,12},{12,8},{16,20},{20,16},{24,28},{28,24},{1,5},{5... | collective-permute-start | bytes 12582920 | tf_op jit(solution)/shard_map/ppermute | solution.py:35
  291.2 144.0 %reduce-scatter.3.cloned.1.call-start = ((), (), s32[]{:S(2)}) async-start(), calls=%async_computation.4 | async-start | bytes 2621440 | tf_op jit(solution)/shard_map/reduce_scatter | solution.py:1520
  306.3 50.4 %collective-permute-start.25 = (bf16[2,4,128,1024]{3,2,1,0:T(8,128)(2,1)}, bf16[2,4,128,1024]{3,2,1,0:T(8,128)(2,1)S(1)}, u32[]{:S(2)}, u32[]{:S(2)}) collective-permute-start(bf16[2,4,128,1024]{3,2,1,0:T(8,128)(2,1)} %get-tuple-element.319), channel_id=1, source_target_pairs={{0,16},{4,20},{8,24},{12,28},{16,0},{20,4},{24,8},{28,12},{1,17},{... | collective-permute-start | bytes 6291464 | tf_op jit(solution)/shard_map/ppermute | solution.py:35
  308.2 48.6 %collective-permute-start.24 = (bf16[2,4,128,1024]{3,2,1,0:T(8,128)(2,1)}, bf16[2,4,128,1024]{3,2,1,0:T(8,128)(2,1)}, u32[]{:S(2)}, u32[]{:S(2)}) collective-permute-start(bf16[2,4,128,1024]{3,2,1,0:T(8,128)(2,1)} %get-tuple-element.317), channel_id=1, source_target_pairs={{0,8},{4,12},{8,0},{12,4},{16,24},{20,28},{24,16},{28,20},{1,9},{5... | collective-permute-start | bytes 6291464 | tf_op jit(solution)/shard_map/ppermute | solution.py:35
  383.6 11.2 %collective-permute-start.26 = (bf16[4,4,128,1280]{3,2,1,0:T(8,128)(2,1)}, bf16[4,4,128,1280]{3,2,1,0:T(8,128)(2,1)}, u32[]{:S(2)}, u32[]{:S(2)}) collective-permute-start(bf16[4,4,128,1280]{3,2,1,0:T(8,128)(2,1)} %cross_grad_send.1), channel_id=1, source_target_pairs={{0,4},{4,0},{8,12},{12,8},{16,20},{20,16},{24,28},{28,24},{1,5},{5... | collective-permute-start | bytes 15728648 | tf_op jit(solution)/shard_map/ppermute | solution.py:35
  383.7 104.7 %reduce-scatter.5.cloned.1.call-start = ((), (), s32[]{:S(2)}) async-start(), calls=%async_computation.5 | async-start | bytes 2621440 | tf_op jit(solution)/shard_map/reduce_scatter | solution.py:206
  391.4 14.0 %collective-permute-start.27 = (bf16[4,4,128,896]{3,2,1,0:T(8,128)(2,1)}, bf16[4,4,128,896]{3,2,1,0:T(8,128)(2,1)S(1)}, u32[]{:S(2)}, u32[]{:S(2)}) collective-permute-start(bf16[4,4,128,896]{3,2,1,0:T(8,128)(2,1)} %self_grad_send.1), channel_id=1, source_target_pairs={{0,4},{4,0},{8,12},{12,8},{16,20},{20,16},{24,28},{28,24},{1,5},{5... | collective-permute-start | bytes 11010056 | tf_op jit(solution)/shard_map/ppermute | solution.py:35
  391.9 25.1 %collective-permute-start.29 = (bf16[4,128,1024]{2,1,0:T(8,128)(2,1)S(1)}, bf16[4,128,1024]{2,1,0:T(8,128)(2,1)S(1)}, u32[]{:S(2)}, u32[]{:S(2)}) collective-permute-start(bf16[4,128,1024]{2,1,0:T(8,128)(2,1)S(1)} %copy-done.52), channel_id=1, source_target_pairs={{0,8},{4,12},{8,0},{12,4},{16,24},{20,28},{24,16},{28,20},{1,9},{5... | collective-permute-start | bytes 3145736 | tf_op jit(solution)/shard_map/ppermute | solution.py:35
  393.3 24.9 %collective-permute-start.28 = (bf16[4,128,1024]{2,1,0:T(8,128)(2,1)S(1)}, bf16[4,128,1024]{2,1,0:T(8,128)(2,1)S(1)}, u32[]{:S(2)}, u32[]{:S(2)}) collective-permute-start(bf16[4,128,1024]{2,1,0:T(8,128)(2,1)S(1)} %copy-done.51), channel_id=1, source_target_pairs={{0,16},{4,20},{8,24},{12,28},{16,0},{20,4},{24,8},{28,12},{1,17},{... | collective-permute-start | bytes 3145736 | tf_op jit(solution)/shard_map/ppermute | solution.py:35
  427.0 33.3 %collective-permute-start.30 = (bf16[2,4,128,640]{3,2,1,0:T(8,128)(2,1)}, bf16[2,4,128,640]{3,2,1,0:T(8,128)(2,1)S(1)}, u32[]{:S(2)}, u32[]{:S(2)}) collective-permute-start(bf16[2,4,128,640]{3,2,1,0:T(8,128)(2,1)} %get-tuple-element.353), channel_id=1, source_target_pairs={{0,8},{4,12},{8,0},{12,4},{16,24},{20,28},{24,16},{28,20},{1,9},{5... | collective-permute-start | bytes 3932168 | tf_op jit(solution)/shard_map/ppermute | solution.py:35
  428.3 31.9 %collective-permute-start.31 = (bf16[2,4,128,640]{3,2,1,0:T(8,128)(2,1)}, bf16[2,4,128,640]{3,2,1,0:T(8,128)(2,1)S(1)}, u32[]{:S(2)}, u32[]{:S(2)}) collective-permute-start(bf16[2,4,128,640]{3,2,1,0:T(8,128)(2,1)} %get-tuple-element.372), channel_id=1, source_target_pairs={{0,16},{4,20},{8,24},{12,28},{16,0},{20,4},{24,8},{28,12},{1,17},{... | collective-permute-start | bytes 3932168 | tf_op jit(solution)/shard_map/ppermute | solution.py:35
  433.1 48.5 %collective-permute-start.32 = (bf16[2,4,128,512]{3,2,1,0:T(8,128)(2,1)}, bf16[2,4,128,512]{3,2,1,0:T(8,128)(2,1)}, u32[]{:S(2)}, u32[]{:S(2)}) collective-permute-start(bf16[2,4,128,512]{3,2,1,0:T(8,128)(2,1)} %get-tuple-element.355), channel_id=1, source_target_pairs={{0,8},{4,12},{8,0},{12,4},{16,24},{20,28},{24,16},{28,20},{1,9},{5... | collective-permute-start | bytes 3145736 | tf_op jit(solution)/shard_map/ppermute | solution.py:35
  435.2 41.9 %collective-permute-start.33 = (bf16[2,4,128,384]{3,2,1,0:T(8,128)(2,1)}, bf16[2,4,128,384]{3,2,1,0:T(8,128)(2,1)S(1)}, u32[]{:S(2)}, u32[]{:S(2)}) collective-permute-start(bf16[2,4,128,384]{3,2,1,0:T(8,128)(2,1)} %get-tuple-element.382), channel_id=1, source_target_pairs={{0,16},{4,20},{8,24},{12,28},{16,0},{20,4},{24,8},{28,12},{1,17},{... | collective-permute-start | bytes 2359304 | tf_op jit(solution)/shard_map/ppermute | solution.py:35
  447.5 38.7 %collective-permute-start.34 = (bf16[128,1024]{1,0:T(8,128)(2,1)}, bf16[128,1024]{1,0:T(8,128)(2,1)S(1)}, u32[]{:S(2)}, u32[]{:S(2)}) collective-permute-start(bf16[128,1024]{1,0:T(8,128)(2,1)} %get-tuple-element.390), channel_id=1, source_target_pairs={{1,0},{2,1},{3,2},{5,4},{6,5},{7,6},{9,8},{10,9},{11,10},{13,12},{... | collective-permute-start | bytes 786440 | tf_op jit(solution)/shard_map/ppermute | solution.py:1555
  466.0 30.4 %collective-permute-start.37 = (bf16[4,128,640]{2,1,0:T(8,128)(2,1)}, bf16[4,128,640]{2,1,0:T(8,128)(2,1)S(1)}, u32[]{:S(2)}, u32[]{:S(2)}) collective-permute-start(bf16[4,128,640]{2,1,0:T(8,128)(2,1)} %get-tuple-element.376), channel_id=1, source_target_pairs={{0,8},{4,12},{8,0},{12,4},{16,24},{20,28},{24,16},{28,20},{1,9},{5... | collective-permute-start | bytes 1966088 | tf_op jit(solution)/shard_map/ppermute | solution.py:35
  466.7 29.6 %collective-permute-start.36 = (bf16[4,128,640]{2,1,0:T(8,128)(2,1)}, bf16[4,128,640]{2,1,0:T(8,128)(2,1)S(1)}, u32[]{:S(2)}, u32[]{:S(2)}) collective-permute-start(bf16[4,128,640]{2,1,0:T(8,128)(2,1)} %get-tuple-element.374), channel_id=1, source_target_pairs={{0,16},{4,20},{8,24},{12,28},{16,0},{20,4},{24,8},{28,12},{1,17},{... | collective-permute-start | bytes 1966088 | tf_op jit(solution)/shard_map/ppermute | solution.py:35
  477.1 12.9 %collective-permute-start.35 = (bf16[128,1024]{1,0:T(8,128)(2,1)}, bf16[128,1024]{1,0:T(8,128)(2,1)}, u32[]{:S(2)}, u32[]{:S(2)}) collective-permute-start(bf16[128,1024]{1,0:T(8,128)(2,1)} %get-tuple-element.391), channel_id=1, source_target_pairs={{2,0},{3,1},{6,4},{7,5},{10,8},{11,9},{14,12},{15,13},{18,16},{19,... | collective-permute-start | bytes 786440 | tf_op jit(solution)/shard_map/ppermute | solution.py:1554
  484.9 17.1 %collective-permute-start.39 = (bf16[4,128,384]{2,1,0:T(8,128)(2,1)}, bf16[4,128,384]{2,1,0:T(8,128)(2,1)S(1)}, u32[]{:S(2)}, u32[]{:S(2)}) collective-permute-start(bf16[4,128,384]{2,1,0:T(8,128)(2,1)} %get-tuple-element.386), channel_id=1, source_target_pairs={{0,8},{4,12},{8,0},{12,4},{16,24},{20,28},{24,16},{28,20},{1,9},{5... | collective-permute-start | bytes 1179656 | tf_op jit(solution)/shard_map/ppermute | solution.py:35
  486.9 15.2 %collective-permute-start.38 = (bf16[4,128,512]{2,1,0:T(8,128)(2,1)}, bf16[4,128,512]{2,1,0:T(8,128)(2,1)S(1)}, u32[]{:S(2)}, u32[]{:S(2)}) collective-permute-start(bf16[4,128,512]{2,1,0:T(8,128)(2,1)} %get-tuple-element.385), channel_id=1, source_target_pairs={{0,16},{4,20},{8,24},{12,28},{16,0},{20,4},{24,8},{28,12},{1,17},{... | collective-permute-start | bytes 1572872 | tf_op jit(solution)/shard_map/ppermute | solution.py:35
  500.9 18.5 %collective-permute-start.42 = (bf16[2,128,1280]{2,1,0:T(8,128)(2,1)}, bf16[2,128,1280]{2,1,0:T(8,128)(2,1)S(1)}, u32[]{:S(2)}, u32[]{:S(2)}) collective-permute-start(bf16[2,128,1280]{2,1,0:T(8,128)(2,1)} %get-tuple-element.396), channel_id=1, source_target_pairs={{0,1},{1,0},{2,3},{3,2},{4,5},{5,4},{6,7},{7,6},{8,9},{9,8},{10,11... | collective-permute-start | bytes 1966088 | tf_op jit(solution)/shard_map/ppermute | solution.py:35
  506.0 21.0 %collective-permute-start.44 = (bf16[2,128,896]{2,1,0:T(8,128)(2,1)}, bf16[2,128,896]{2,1,0:T(8,128)(2,1)S(1)}, u32[]{:S(2)}, u32[]{:S(2)}) collective-permute-start(bf16[2,128,896]{2,1,0:T(8,128)(2,1)} %get-tuple-element.402), channel_id=1, source_target_pairs={{0,1},{1,0},{2,3},{3,2},{4,5},{5,4},{6,7},{7,6},{8,9},{9,8},{10,11... | collective-permute-start | bytes 1376264 | tf_op jit(solution)/shard_map/ppermute | solution.py:35
  513.8 8.7 %collective-permute-start.43 = (f32[17920]{0:T(1024)S(1)}, f32[17920]{0:T(1024)S(1)}, u32[]{:S(2)}, u32[]{:S(2)}) collective-permute-start(f32[17920]{0:T(1024)S(1)} %add.88), channel_id=1, source_target_pairs={{0,16},{4,20},{8,24},{12,28},{16,0},{20,4},{24,8},{28,12},{1,17},{... | collective-permute-start | bytes 215048 | tf_op jit(solution)/shard_map/ppermute | solution.py:35
  529.8 16.8 %collective-permute-start.46 = (f32[17920]{0:T(1024)S(1)}, f32[17920]{0:T(1024)S(1)}, u32[]{:S(2)}, u32[]{:S(2)}) collective-permute-start(f32[17920]{0:T(1024)S(1)} %add.90), channel_id=1, source_target_pairs={{0,2},{1,3},{2,0},{3,1},{4,6},{5,7},{6,4},{7,5},{8,10},{9,11},{10,... | collective-permute-start | bytes 215048 | tf_op jit(solution)/shard_map/ppermute | solution.py:35
  531.0 22.7 %collective-permute-start.47 = (bf16[1,128,1280]{2,1,0:T(8,128)(2,1)S(1)}, bf16[1,128,1280]{2,1,0:T(8,128)(2,1)S(1)}, u32[]{:S(2)}, u32[]{:S(2)}) collective-permute-start(bf16[1,128,1280]{2,1,0:T(8,128)(2,1)S(1)} %copy-done.53), channel_id=1, source_target_pairs={{0,2},{1,3},{2,0},{3,1},{4,6},{5,7},{6,4},{7,5},{8,10},{9,11},{10,... | collective-permute-start | bytes 983048 | tf_op jit(solution)/shard_map/ppermute | solution.py:35
  533.9 24.3 %collective-permute-start.48 = (bf16[1,128,896]{2,1,0:T(8,128)(2,1)S(1)}, bf16[1,128,896]{2,1,0:T(8,128)(2,1)S(1)}, u32[]{:S(2)}, u32[]{:S(2)}) collective-permute-start(bf16[1,128,896]{2,1,0:T(8,128)(2,1)S(1)} %copy-done.54), channel_id=1, source_target_pairs={{0,2},{1,3},{2,0},{3,1},{4,6},{5,7},{6,4},{7,5},{8,10},{9,11},{10,... | collective-permute-start | bytes 688136 | tf_op jit(solution)/shard_map/ppermute | solution.py:35
  (61 other events, 334.0 us)
Sparse Core Ops, SparseCore 0:
  129.7 114.5 all-gather.2
  291.3 65.3 all-gather.4
  383.8 43.2 reduce-scatter.2
  429.9 48.7 reduce-scatter.4
